TPU v7x, 32 devices: a whole 2x2x4 slice. The times are simulated.
32 devices in a mesh: fsdp: 4 (over y, core), ctx: 2 (over x), tp: 4 (over z).
Axes of the slice: x: 2, y: 2, z: 4, core: 2. Of those that a mesh axis runs over, the one named last changes fastest.
Arguments:
- hidden_in: bfloat16 [16, 1024, 768], P('fsdp', 'ctx'), may hold values from -6 to 6
- prev_logits: bfloat16 [16, 12, 1024, 1024], P('fsdp', 'tp', 'ctx'), may hold values from -6 to 6
- w_query: bfloat16 [768, 768], P('fsdp', 'tp'), may hold values from -0.21875 to 0.21875
- w_key: bfloat16 [768, 768], P('fsdp', 'tp'), may hold values from -0.21875 to 0.21875
- w_value: bfloat16 [768, 768], P('fsdp', 'tp'), may hold values from -0.21875 to 0.21875
- w_out: bfloat16 [768, 768], P('fsdp', 'tp'), may hold values from -1.75 to 1.75
- w_inner: bfloat16 [768, 3072], P('fsdp', 'tp'), may hold values from -0.21875 to 0.21875
- w_outer: bfloat16 [768, 3072], P('fsdp', 'tp'), may hold values from -0.109375 to 0.109375
- b_query: float32 [768], P('tp'), may hold values from -3 to 3
- b_value: float32 [768], P('tp'), may hold values from -3 to 3
- b_out: float32 [768], replicated, may hold values from -3 to 3
- b_inner: float32 [3072], P('tp'), may hold values from -3 to 3
- b_outer: float32 [768], replicated, may hold values from -3 to 3
- gain_attn: float32 [768], replicated, may hold values from 0.25 to 1.75
- shift_attn: float32 [768], replicated, may hold values from -3 to 3
- gain_ffn: float32 [768], replicated, may hold values from 0.25 to 1.75
- shift_ffn: float32 [768], replicated, may hold values from -3 to 3
- d_output: bfloat16 [16, 1024, 768], P('fsdp', 'ctx'), may hold values from -6 to 6
- d_logits: bfloat16 [16, 12, 1024, 1024], P('fsdp', 'tp', 'ctx'), may hold values from -6 to 6
Outputs:
- output: bfloat16 [16, 1024, 768], P('fsdp', 'ctx')
- new_logits: bfloat16 [16, 12, 1024, 1024], P('fsdp', 'tp', 'ctx')
- d_hidden: float32 [16, 1024, 768], P('fsdp', 'ctx')
- d_prev: bfloat16 [16, 12, 1024, 1024], P('fsdp', 'tp', 'ctx')
- d_w_query: float32 [768, 768], P('fsdp', 'tp')
- d_w_key: float32 [768, 768], P('fsdp', 'tp')
- d_w_value: float32 [768, 768], P('fsdp', 'tp')
- d_w_out: float32 [768, 768], P('fsdp', 'tp')
- d_w_inner: float32 [768, 3072], P('fsdp', 'tp')
- d_w_outer: float32 [768, 3072], P('fsdp', 'tp')
- d_b_query: float32 [768], P('tp')
- d_b_value: float32 [768], P('tp')
- d_b_out: float32 [768], replicated
- d_b_inner: float32 [3072], P('tp')
- d_b_outer: float32 [768], replicated
- d_gain_attn: float32 [768], replicated
- d_shift_attn: float32 [768], replicated
- d_gain_ffn: float32 [768], replicated
- d_shift_ffn: float32 [768], replicated
All inputs are finite; a program needn't handle non-finite values.
Results may differ from a plain program's by a relative error of at most 0.017.
Values may be sent and summed in bfloat16 or wider, within the bound.
No kernel may reach another device: no remote copies, remote signals or barrier semaphores. Data moves between devices by JAX's collectives and lax.ppermute only.
A program may use at most 448 MiB of HBM per device.

v0:
```python
import jax
import jax.numpy as jnp
from jax import lax
from jax.sharding import PartitionSpec as P

BLOCK = 256


def layer_norm(value, gain, shift):
    mean = jnp.mean(value, axis=-1, keepdims=True)
    centered = value - mean
    variance = jnp.mean(centered * centered, axis=-1, keepdims=True)
    return centered * lax.rsqrt(variance + 1e-06) * gain + shift


def gelu_exact(value):
    return jax.nn.gelu(value, approximate=False)


def contract_rows(left, right):
    return lax.dot_general(
        left, right, (((0,), (0,)), ((), ())), preferred_element_type=jnp.float32
    )


def contract_cols(left, right):
    return lax.dot_general(
        left, right, (((1,), (1,)), ((), ())), preferred_element_type=jnp.float32
    )


def raw_scores(query_heads, key_heads, previous, allowed, scale):
    scores = (
        jnp.einsum("sqhd,skhd->shqk", query_heads, key_heads, preferred_element_type=jnp.float32)
        * scale
    )
    scores = scores + previous.astype(jnp.float32)
    return (scores, jnp.where(allowed[None, None], scores, -1e30))


def body(
    hidden_in,
    prev_logits,
    w_query,
    w_key,
    w_value,
    w_out,
    w_inner,
    w_outer,
    b_query,
    b_value,
    b_out,
    b_inner,
    b_outer,
    gain_attn,
    shift_attn,
    gain_ffn,
    shift_ffn,
    d_output,
    d_logits,
):
    seq_count, rows, width = hidden_in.shape
    heads_here = prev_logits.shape[1]
    full_len = prev_logits.shape[3]
    local_width = w_query.shape[1]
    head_size = local_width // heads_here
    scale = head_size ** (-0.5)
    tokens = seq_count * rows
    my_ctx = lax.axis_index("ctx")
    query_pos = my_ctx * rows + jnp.arange(rows, dtype=jnp.int32)
    key_pos = jnp.arange(full_len, dtype=jnp.int32)
    allowed = (key_pos // BLOCK)[None, :] <= (query_pos // BLOCK)[:, None]
    query_full, key_full, value_full, out_full, inner_full, outer_full = (
        lax.all_gather(w_query, "fsdp", axis=0, tiled=True),
        lax.all_gather(w_key, "fsdp", axis=0, tiled=True),
        lax.all_gather(w_value, "fsdp", axis=0, tiled=True),
        lax.all_gather(w_out, "fsdp", axis=0, tiled=True),
        lax.all_gather(w_inner, "fsdp", axis=0, tiled=True),
        lax.all_gather(w_outer, "fsdp", axis=0, tiled=True),
    )
    flat = hidden_in.reshape(tokens, width)
    flat_f = flat.astype(jnp.float32)
    query = (jnp.dot(flat, query_full, preferred_element_type=jnp.float32) + b_query).astype(
        jnp.bfloat16
    )
    keys = jnp.dot(flat, key_full, preferred_element_type=jnp.float32).astype(jnp.bfloat16)
    values = (jnp.dot(flat, value_full, preferred_element_type=jnp.float32) + b_value).astype(
        jnp.bfloat16
    )
    keys_all, values_all = (
        lax.all_gather(keys.reshape(seq_count, rows, local_width), "ctx", axis=1, tiled=True),
        lax.all_gather(values.reshape(seq_count, rows, local_width), "ctx", axis=1, tiled=True),
    )
    query_heads = query.reshape(seq_count, rows, heads_here, head_size)
    key_heads = keys_all.reshape(seq_count, full_len, heads_here, head_size)
    value_heads = values_all.reshape(seq_count, full_len, heads_here, head_size)
    scores, masked = raw_scores(query_heads, key_heads, prev_logits, allowed, scale)
    new_logits = jnp.where(allowed[None, None], scores, 0.0).astype(jnp.bfloat16)
    highest = jnp.max(masked, axis=-1, keepdims=True)
    unnorm = jnp.exp(masked - highest)
    total = jnp.sum(unnorm, axis=-1, keepdims=True)
    log_total = highest + jnp.log(total)
    probs_low = (unnorm / total).astype(jnp.bfloat16)
    mixed = jnp.einsum(
        "shqk,skhd->sqhd", probs_low, value_heads, preferred_element_type=jnp.float32
    )
    attended = mixed.reshape(tokens, local_width).astype(jnp.bfloat16)
    attn_part = contract_cols(attended, out_full)
    cotangent = d_output.reshape(tokens, width).astype(jnp.float32)
    first = flat_f + lax.psum(attn_part, "tp") + b_out
    normed_f, attn_pull = jax.vjp(layer_norm, first, gain_attn, shift_attn)
    normed = normed_f.astype(jnp.bfloat16)
    inner = jnp.dot(normed, inner_full, preferred_element_type=jnp.float32) + b_inner
    act_f, gelu_pull = jax.vjp(gelu_exact, inner)
    act = act_f.astype(jnp.bfloat16)
    ffn_part = contract_cols(act, outer_full)
    second = normed.astype(jnp.float32) + lax.psum(ffn_part, "tp") + b_outer
    result_f, ffn_pull = jax.vjp(layer_norm, second, gain_ffn, shift_ffn)
    output = result_f.astype(jnp.bfloat16).reshape(seq_count, rows, width)
    grad_second, grad_gain_ffn, grad_shift_ffn = ffn_pull(cotangent)
    grad_b_outer = jnp.sum(grad_second, axis=0)
    second_low = grad_second.astype(jnp.bfloat16)
    grad_w_outer = contract_rows(second_low, act)
    grad_act = jnp.dot(second_low, outer_full, preferred_element_type=jnp.float32)
    grad_inner = gelu_pull(grad_act)[0]
    grad_b_inner = jnp.sum(grad_inner, axis=0)
    inner_low = grad_inner.astype(jnp.bfloat16)
    grad_w_inner = contract_rows(normed, inner_low)
    normed_part = contract_cols(inner_low, inner_full)
    grad_normed = lax.psum(normed_part, "tp") + grad_second
    grad_first, grad_gain_attn, grad_shift_attn = attn_pull(grad_normed)
    grad_b_out = jnp.sum(grad_first, axis=0)
    first_low = grad_first.astype(jnp.bfloat16)
    grad_w_out = contract_rows(first_low, attended)
    grad_attended = jnp.dot(first_low, out_full, preferred_element_type=jnp.float32).astype(
        jnp.bfloat16
    )
    grad_heads = grad_attended.reshape(seq_count, rows, heads_here, head_size)
    probs = jnp.exp(masked - log_total)
    probs_again = probs.astype(jnp.bfloat16)
    grad_probs = jnp.einsum(
        "sqhd,skhd->shqk", grad_heads, value_heads, preferred_element_type=jnp.float32
    )
    delta = jnp.sum(probs * grad_probs, axis=-1, keepdims=True)
    grad_scores = probs * (grad_probs - delta) + jnp.where(
        allowed[None, None], d_logits.astype(jnp.float32), 0.0
    )
    d_prev = grad_scores.astype(jnp.bfloat16)
    grad_query = (
        jnp.einsum("shqk,skhd->sqhd", d_prev, key_heads, preferred_element_type=jnp.float32) * scale
    )
    grad_keys_all = (
        jnp.einsum("shqk,sqhd->skhd", d_prev, query_heads, preferred_element_type=jnp.float32)
        * scale
    )
    grad_values_all = jnp.einsum(
        "shqk,sqhd->skhd", probs_again, grad_heads, preferred_element_type=jnp.float32
    )
    grad_keys, grad_values = (
        lax.psum_scatter(
            grad_keys_all.reshape(seq_count, full_len, local_width).astype(jnp.bfloat16),
            "ctx",
            scatter_dimension=1,
            tiled=True,
        ).astype(jnp.float32),
        lax.psum_scatter(
            grad_values_all.reshape(seq_count, full_len, local_width).astype(jnp.bfloat16),
            "ctx",
            scatter_dimension=1,
            tiled=True,
        ).astype(jnp.float32),
    )
    grad_query = grad_query.reshape(tokens, local_width)
    grad_keys = grad_keys.reshape(tokens, local_width)
    grad_values = grad_values.reshape(tokens, local_width)
    grad_b_query = jnp.sum(grad_query, axis=0)
    grad_b_value = jnp.sum(grad_values, axis=0)
    query_low = grad_query.astype(jnp.bfloat16)
    keys_low = grad_keys.astype(jnp.bfloat16)
    values_low = grad_values.astype(jnp.bfloat16)
    grad_w_query = contract_rows(flat, query_low)
    grad_w_key = contract_rows(flat, keys_low)
    grad_w_value = contract_rows(flat, values_low)
    input_part = contract_cols(query_low, query_full) + contract_cols(keys_low, key_full)
    input_part = input_part + contract_cols(values_low, value_full)
    d_hidden = (
        lax.psum(input_part.astype(jnp.bfloat16), "tp").astype(jnp.float32) + grad_first
    ).reshape(seq_count, rows, width)
    small_sums = lax.psum(
        (
            grad_b_query,
            grad_b_value,
            grad_b_inner,
            grad_b_out,
            grad_b_outer,
            grad_gain_attn,
            grad_shift_attn,
            grad_gain_ffn,
            grad_shift_ffn,
        ),
        ("fsdp", "ctx"),
    )
    sum_query, sum_value, sum_inner = (small_sums[0], small_sums[1], small_sums[2])
    sum_out, sum_outer, sum_gain_attn, sum_shift_attn, sum_gain_ffn, sum_shift_ffn = small_sums[3:]
    weight_grads = (grad_w_query, grad_w_key, grad_w_value, grad_w_out, grad_w_inner, grad_w_outer)
    weight_grads = (
        lax.psum_scatter(
            weight_grads[0].astype(jnp.bfloat16), "fsdp", scatter_dimension=0, tiled=True
        ).astype(jnp.float32),
        lax.psum_scatter(
            weight_grads[1].astype(jnp.bfloat16), "fsdp", scatter_dimension=0, tiled=True
        ).astype(jnp.float32),
        lax.psum_scatter(
            weight_grads[2].astype(jnp.bfloat16), "fsdp", scatter_dimension=0, tiled=True
        ).astype(jnp.float32),
        lax.psum_scatter(
            weight_grads[3].astype(jnp.bfloat16), "fsdp", scatter_dimension=0, tiled=True
        ).astype(jnp.float32),
        lax.psum_scatter(
            weight_grads[4].astype(jnp.bfloat16), "fsdp", scatter_dimension=0, tiled=True
        ).astype(jnp.float32),
        lax.psum_scatter(
            weight_grads[5].astype(jnp.bfloat16), "fsdp", scatter_dimension=0, tiled=True
        ).astype(jnp.float32),
    )
    weight_grads = (
        lax.psum(weight_grads[0].astype(jnp.bfloat16), "ctx").astype(jnp.float32),
        lax.psum(weight_grads[1].astype(jnp.bfloat16), "ctx").astype(jnp.float32),
        lax.psum(weight_grads[2].astype(jnp.bfloat16), "ctx").astype(jnp.float32),
        lax.psum(weight_grads[3].astype(jnp.bfloat16), "ctx").astype(jnp.float32),
        lax.psum(weight_grads[4].astype(jnp.bfloat16), "ctx").astype(jnp.float32),
        lax.psum(weight_grads[5].astype(jnp.bfloat16), "ctx").astype(jnp.float32),
    )
    return (
        output,
        new_logits,
        d_hidden,
        d_prev,
        weight_grads[0],
        weight_grads[1],
        weight_grads[2],
        weight_grads[3],
        weight_grads[4],
        weight_grads[5],
        sum_query,
        sum_value,
        sum_out,
        sum_inner,
        sum_outer,
        sum_gain_attn,
        sum_shift_attn,
        sum_gain_ffn,
        sum_shift_ffn,
    )


def solution(mesh):
    in_specs = (
        P("fsdp", "ctx", None),
        P("fsdp", "tp", "ctx", None),
        P("fsdp", "tp"),
        P("fsdp", "tp"),
        P("fsdp", "tp"),
        P("fsdp", "tp"),
        P("fsdp", "tp"),
        P("fsdp", "tp"),
        P("tp"),
        P("tp"),
        P(),
        P("tp"),
        P(),
        P(),
        P(),
        P(),
        P(),
        P("fsdp", "ctx", None),
        P("fsdp", "tp", "ctx", None),
    )
    out_specs = (
        P("fsdp", "ctx", None),
        P("fsdp", "tp", "ctx", None),
        P("fsdp", "ctx", None),
        P("fsdp", "tp", "ctx", None),
        P("fsdp", "tp"),
        P("fsdp", "tp"),
        P("fsdp", "tp"),
        P("fsdp", "tp"),
        P("fsdp", "tp"),
        P("fsdp", "tp"),
        P("tp"),
        P("tp"),
        P(),
        P("tp"),
        P(),
        P(),
        P(),
        P(),
        P(),
    )
    return jax.shard_map(body, mesh=mesh, in_specs=in_specs, out_specs=out_specs, check_vma=False)
```

profile of v0, /device:TPU:0, one launch (start us, length us, event | category | flops | bytes accessed | tf_op | source)
XLA Modules:
  0.0 1649.4 jit_solution(8693518717527014616)
XLA Ops:
  8.1 8.3 all_gather.27
  17.2 4.0 convolution_convert_fusion.1
  24.2 6.6 all_gather.24
  36.7 6.6 all_gather.26
  43.3 6.8 all_gather.29
  58.6 16.1 select_reduce_fusion
  75.3 12.2 fusion.2
  89.3 12.2 fusion.40
  103.2 3.8 fusion.74
  108.2 11.1 all-reduce.10.cloned.1.call-start
  119.3 211.6 %all-reduce.8.cloned.1.call-done = f32[2048,768]{1,0:T(8,128)} async-done(((f32[2048,768]{1,0:T(8,128)}), f32[2048,768]{1,0:T(8,128)}) %all-reduce.8.cloned.1.call-update) | async-done | bytes 6291472 | tf_op jit(solution)/shard_map/psum | solution.py:110
  330.9 3.7 fusion.72
  338.5 19.8 %multiply_convert_fusion = (bf16[2048,768]{1,0:T(8,128)(2,1)}, f32[2048,768]{1,0:T(8,128)}, f32[2048,768]{1,0:T(8,128)}) fusion(f32[768]{0:T(1024)} %param.30, bf16[2048,768]{1,0:T(8,128)(2,1)S(1)} %add_convert_fusion.3, bf16[768,768]{1,0:T(8,128)(2,1)} %all-gather.9.cloned.1.call-done), kind=kOutput, calls=%fused_computation.39 | convolution fusion | flops 2519728128 | bytes 20057088 | tf_op jit(solution)/shard_map/dot_general | solution.py:113
  358.3 7.6 fusion.75
  366.0 221.9 %all-reduce.10.cloned.1.call-done = f32[2048,768]{1,0:T(8,128)} async-done(((f32[2048,768]{1,0:T(8,128)}), f32[2048,768]{1,0:T(8,128)}) %all-reduce.10.cloned.1.call-update) | async-done | bytes 6291472 | tf_op jit(solution)/shard_map/psum | solution.py:117
  587.9 5.7 fusion.70
  598.6 4.3 fusion.69
  603.0 5.6 fusion.73
  610.4 4.5 fusion.34
  615.7 221.2 %all-reduce.12.cloned.1.call-done = f32[2048,768]{1,0:T(8,128)} async-done(((f32[2048,768]{1,0:T(8,128)}), f32[2048,768]{1,0:T(8,128)}) %all-reduce.12.cloned.1.call-update) | async-done | bytes 6291472 | tf_op jit(solution)/shard_map/psum | solution.py:130
  836.9 8.7 multiply_reduce_fusion.1
  845.6 4.2 fusion.68
  855.6 36.6 %add_convert_fusion = bf16[4,3,512,1024]{3,2,1,0:T(8,128)(2,1)} fusion(bf16[4,3,512,1024]{3,2,1,0:T(8,128)(2,1)} %param.37, f32[4,3,512,1024]{3,2,1,0:T(8,128)} %get-tuple-element.112, f32[4,3,512]{2,1,0:T(4,128)S(1)} %log_add_fusion, pred[512,1024]{1,0:T(8,128)(4,1)S(1)} %copy-done.7, bf16[4,1024,3,64]{1,3,2,0:T(8,128)(2,1)S(1)} %bitcast.151, ...), kind=kOutput, calls=%fused_computation.1 | convolution fusion | flops 1679825920 | bytes 53239808 | tf_op jit(solution)/shard_map/sub | solution.py:145
  892.2 6.9 multiply_convert_fusion.1
  899.0 36.0 %copy.77 = bf16[4,1024,192]{0,2,1:T(8,128)(2,1)} copy(bf16[4,1024,192]{1,2,0:T(8,128)(2,1)S(1)} %bitcast.139) | data formatting | bytes 3145728
  935.0 91.2 %reshape.235 = bf16[1024,768]{1,0:T(8,128)(2,1)} reshape(bf16[1024,192,4]{2,1,0:T(8,128)(2,1)} %bitcast.128) | data formatting | bytes 3145728
  1026.2 11.7 fusion.29
  1038.0 35.9 %copy.79 = bf16[4,1024,192]{0,2,1:T(8,128)(2,1)} copy(bf16[4,1024,192]{1,2,0:T(8,128)(2,1)S(1)} %bitcast.149) | data formatting | bytes 3145728
  1073.9 90.9 %reshape.237 = bf16[1024,768]{1,0:T(8,128)(2,1)} reshape(bf16[1024,192,4]{2,1,0:T(8,128)(2,1)} %bitcast.129) | data formatting | bytes 3145728
  1165.1 10.6 bitcast_convert_fusion
  1179.3 56.7 %reshape.236 = bf16[512,192,4]{2,1,0:T(8,128)(2,1)} reshape(bf16[512,768]{1,0:T(8,128)(2,1)} %reduce-scatter.25.cloned.1.call-done) | data formatting | bytes 1572864
  1236.0 23.6 %copy.72 = bf16[4,512,192]{1,2,0:T(8,128)(2,1)} copy(bf16[4,512,192]{0,2,1:T(8,128)(2,1)} %bitcast.126) | data formatting | bytes 1572864 | tf_op jit(solution)/shard_map/reduce_scatter | solution.py:160
  1262.6 56.7 %reshape.238 = bf16[512,192,4]{2,1,0:T(8,128)(2,1)} reshape(bf16[512,768]{1,0:T(8,128)(2,1)} %reduce-scatter.27.cloned.1.call-done) | data formatting | bytes 1572864
  1319.3 23.6 %copy.73 = bf16[4,512,192]{1,2,0:T(8,128)(2,1)} copy(bf16[4,512,192]{0,2,1:T(8,128)(2,1)} %bitcast.124) | data formatting | bytes 1572864 | tf_op jit(solution)/shard_map/reduce_scatter | solution.py:166
  1346.2 6.5 fusion.36
  1352.9 7.6 convolution_convert_fusion.2
  1360.6 5.0 convolution_convert_fusion.3
  1365.7 3.8 fusion.76
  1371.1 23.7 %copy.78 = bf16[4,512,192]{1,0,2:T(4,128)(2,1)S(1)} copy(bf16[4,512,192]{0,2,1:T(8,128)(2,1)} %bitcast.127) | data formatting | bytes 1572864
  1398.3 23.7 %reduce-scatter.23.cloned.1.call-done = bf16[192,768]{1,0:T(8,128)(2,1)} async-done(((bf16[768,768]{1,0:T(8,128)(2,1)}), bf16[192,768]{1,0:T(8,128)(2,1)}) %reduce-scatter.23.cloned.1.call-update) | async-done | bytes 294928 | tf_op jit(solution)/shard_map/reduce_scatter | solution.py:222
  1422.0 23.3 %reduce-scatter.19.cloned.1.call-done = bf16[192,192]{1,0:T(8,128)(2,1)} async-done(((bf16[768,192]{1,0:T(8,128)(2,1)}), bf16[192,192]{1,0:T(8,128)(2,1)}) %reduce-scatter.19.cloned.1.call-update) | async-done | bytes 73744 | tf_op jit(solution)/shard_map/reduce_scatter | solution.py:216
  1445.6 3.7 fusion.77
  1449.3 23.5 %copy.80 = bf16[4,512,192]{1,0,2:T(4,128)(2,1)S(1)} copy(bf16[4,512,192]{0,2,1:T(8,128)(2,1)} %bitcast.125) | data formatting | bytes 1572864
  1473.8 7.9 add_convert_fusion.1
  1482.2 14.8 select_convert_fusion
  1508.6 102.9 %all-reduce.14.cloned.1.call-done = bf16[2048,768]{1,0:T(8,128)(2,1)} async-done(((bf16[2048,768]{1,0:T(8,128)(2,1)}), bf16[2048,768]{1,0:T(8,128)(2,1)}) %all-reduce.14.cloned.1.call-update) | async-done | bytes 3145744 | tf_op jit(solution)/shard_map/psum | solution.py:187
  1611.4 5.9 add_reduce_fusion
  1617.3 24.7 %all-reduce = (f32[192]{0:T(256)}, f32[192]{0:T(256)}, f32[768]{0:T(1024)}, f32[768]{0:T(1024)}, f32[768]{0:T(1024)}, /*index=5*/f32[768]{0:T(1024)}, f32[768]{0:T(1024)}, f32[768]{0:T(1024)}, f32[768]{0:T(1024)}) all-reduce(f32[192]{0:T(256)S(1)} %reduce_sum.216, ...), channel_id=1, replica_groups=mesh['fsdp'=4,'ctx'=2,'tp'=4] {'fsdp','ctx'}, use_global_device_ids=true, to_apply=%region_30.31 | all-reduce | flops 5760 | bytes 46080 | tf_op jit(solution)/shard_map/psum | solution.py:189
  (220 shorter events, 69.1 us)
Async XLA Ops:
  8.0 23.5 %copy-start.2 = (bf16[4,512,768]{2,1,0:T(8,128)(2,1)S(1)}, bf16[4,512,768]{2,1,0:T(8,128)(2,1)}, u32[]{:S(2)}) copy-start(bf16[4,512,768]{2,1,0:T(8,128)(2,1)} %param.19) | copy-start | bytes 9437188
  8.0 16.2 copy-start.31
  8.0 23.5 %copy-start.55 = (f32[192]{0:T(256)S(1)}, f32[192]{0:T(256)}, u32[]{:S(2)}) copy-start(f32[192]{0:T(256)} %param.28) | copy-start | bytes 2308
  8.1 48.6 %all-gather.7.cloned.1.call-start = ((), (), s32[]{:S(2)}) async-start(), calls=%async_computation.9 | async-start | bytes 2359296 | tf_op jit(solution)/shard_map/all_gather | solution.py:91
  17.2 19.6 %copy-start.32 = (bf16[192,192]{1,0:T(8,128)(2,1)S(1)}, bf16[192,192]{1,0:T(8,128)(2,1)}, u32[]{:S(2)}) copy-start(bf16[192,192]{1,0:T(8,128)(2,1)} %param.21) | copy-start | bytes 221188
  21.2 29.0 %copy-start.56 = (f32[192]{0:T(256)S(1)}, f32[192]{0:T(256)}, u32[]{:S(2)}) copy-start(f32[192]{0:T(256)} %param.27) | copy-start | bytes 2308
  24.2 63.3 %all-gather.5.cloned.1.call-start = ((), (), s32[]{:S(2)}) async-start(), calls=%async_computation.8 | async-start | bytes 2359296 | tf_op jit(solution)/shard_map/all_gather | solution.py:92
  36.7 294.2 %all-reduce.8.cloned.1.call-start = ((), (), s32[]{:S(2)}) async-start(), calls=%async_computation.10 | async-start | bytes 12582912 | tf_op jit(solution)/shard_map/psum | solution.py:110
  58.5 16.1 copy-start.9
  58.6 16.7 %copy-start.6 = (pred[512,1024]{1,0:T(8,128)(4,1)S(1)}, pred[512,1024]{1,0:T(8,128)(4,1)}, u32[]{:S(2)}) copy-start(pred[512,1024]{1,0:T(8,128)(4,1)} %broadcast_compare_fusion) | copy-start | bytes 1572868
  89.3 12.2 copy-start.23
  107.0 223.9 %copy-start.50 = (f32[768]{0:T(1024)S(1)}, f32[768]{0:T(1024)}, u32[]{:S(2)}) copy-start(f32[768]{0:T(1024)} %param.29) | copy-start | bytes 9220
  107.0 231.5 %all-gather.9.cloned.1.call-start = ((), (), s32[]{:S(2)}) async-start(), calls=%async_computation.11 | async-start | bytes 1474560 | tf_op jit(solution)/shard_map/all_gather | solution.py:78
  107.6 250.7 %all-gather.11.cloned.1.call-start = ((), (), s32[]{:S(2)}) async-start(), calls=%async_computation.12 | async-start | bytes 1474560 | tf_op jit(solution)/shard_map/all_gather | solution.py:79
  108.2 479.7 %all-reduce.10.cloned.1.call-start = ((), (), s32[]{:S(2)}) async-start(), calls=%async_computation.13 | async-start | bytes 12582912 | tf_op jit(solution)/shard_map/psum | solution.py:117
  338.4 19.9 %copy-start.20 = (bf16[2048,768]{1,0:T(8,128)(2,1)}, bf16[2048,768]{1,0:T(8,128)(2,1)S(1)}, u32[]{:S(2)}) copy-start(bf16[2048,768]{1,0:T(8,128)(2,1)S(1)} %add_convert_fusion.3) | copy-start | bytes 9437188
  365.9 222.0 %copy-start.38 = (f32[768]{0:T(1024)S(1)}, f32[768]{0:T(1024)}, u32[]{:S(2)}) copy-start(f32[768]{0:T(1024)} %param.32) | copy-start | bytes 9220
  365.9 222.0 %copy-start.44 = (f32[768]{0:T(1024)S(1)}, f32[768]{0:T(1024)}, u32[]{:S(2)}) copy-start(f32[768]{0:T(1024)} %param.33) | copy-start | bytes 9220
  365.9 222.0 %copy-start.51 = (f32[768]{0:T(1024)S(1)}, f32[768]{0:T(1024)}, u32[]{:S(2)}) copy-start(f32[768]{0:T(1024)} %param.31) | copy-start | bytes 9220
  365.9 471.0 %all-reduce.12.cloned.1.call-start = ((), (), s32[]{:S(2)}) async-start(), calls=%async_computation.14 | async-start | bytes 12582912 | tf_op jit(solution)/shard_map/psum | solution.py:130
  602.9 234.0 %copy-start.39 = (f32[2048]{0:T(1024)}, f32[2048]{0:T(1024)S(1)}, u32[]{:S(2)}) copy-start(f32[2048]{0:T(1024)S(1)} %negate_multiply_fusion.2) | copy-start | bytes 24580
  614.9 564.4 %reduce-scatter.25.cloned.1.call-start = ((), (), s32[]{:S(2)}) async-start(), calls=%async_computation.19 | async-start | bytes 2359296
  615.7 229.9 %copy-start.34 = (f32[2048]{0:T(1024)S(1)}, f32[2048]{0:T(1024)}, u32[]{:S(2)}) copy-start(f32[2048]{0:T(1024)} %copy-done.33) | copy-start | bytes 24580
  849.9 42.2 %copy-start.35 = (f32[2048]{0:T(1024)}, f32[2048]{0:T(1024)S(1)}, u32[]{:S(2)}) copy-start(f32[2048]{0:T(1024)S(1)} %negate_multiply_fusion.1) | copy-start | bytes 24580
  855.6 36.6 %copy-start.14 = (bf16[4,512,3,64]{1,0,3,2:T(4,128)(2,1)S(1)}, bf16[4,512,3,64]{1,0,3,2:T(4,128)(2,1)}, u32[]{:S(2)}) copy-start(bf16[4,512,3,64]{1,0,3,2:T(4,128)(2,1)} %reshape.226) | copy-start | bytes 2359300
  935.0 91.2 %copy-start.27 = (bf16[4,512,3,64]{1,0,3,2:T(4,128)(2,1)S(1)}, bf16[4,512,3,64]{1,0,3,2:T(4,128)(2,1)}, u32[]{:S(2)}) copy-start(bf16[4,512,3,64]{1,0,3,2:T(4,128)(2,1)} %reshape.230) | copy-start | bytes 2359300
  1026.2 236.4 %reduce-scatter.27.cloned.1.call-start = ((), (), s32[]{:S(2)}) async-start(), calls=%async_computation.20 | async-start | bytes 2359296
  1164.9 12.6 copy-start.3
  1164.9 204.6 %reduce-scatter.29.cloned.1.call-start = ((), (), s32[]{:S(2)}) async-start(), calls=%async_computation.21 | async-start | bytes 491520
  1179.2 215.8 %reduce-scatter.31.cloned.1.call-start = ((), (), s32[]{:S(2)}) async-start(), calls=%async_computation.22 | async-start | bytes 491520
  1262.5 134.2 %reduce-scatter.33.cloned.1.call-start = ((), (), s32[]{:S(2)}) async-start(), calls=%async_computation.23 | async-start | bytes 491520
  1344.8 8.0 copy-start.40
  1345.8 52.5 %reduce-scatter.21.cloned.1.call-start = ((), (), s32[]{:S(2)}) async-start(), calls=%async_computation.17 | async-start | bytes 1474560 | tf_op jit(solution)/shard_map/reduce_scatter | solution.py:219
  1352.8 7.8 copy-start.17
  1352.8 69.2 %reduce-scatter.23.cloned.1.call-start = ((), (), s32[]{:S(2)}) async-start(), calls=%async_computation.18 | async-start | bytes 1474560 | tf_op jit(solution)/shard_map/reduce_scatter | solution.py:222
  1360.5 84.9 %reduce-scatter.19.cloned.1.call-start = ((), (), s32[]{:S(2)}) async-start(), calls=%async_computation.16 | async-start | bytes 491520 | tf_op jit(solution)/shard_map/reduce_scatter | solution.py:216
  1365.6 132.7 %all-reduce.16.cloned.1.call-start = ((), (), s32[]{:S(2)}) async-start(), calls=%async_computation.24 | async-start | bytes 1966080 | tf_op jit(solution)/shard_map/psum | solution.py:227
  1371.1 74.5 %copy-start.19 = (bf16[768,192]{1,0:T(8,128)(2,1)S(1)}, bf16[768,192]{1,0:T(8,128)(2,1)}, u32[]{:S(2)}) copy-start(bf16[768,192]{1,0:T(8,128)(2,1)} %copy-done.18) | copy-start | bytes 884740
  1445.4 166.1 %all-reduce.14.cloned.1.call-start = ((), (), s32[]{:S(2)}) async-start(), calls=%async_computation.15 | async-start | bytes 6291456 | tf_op jit(solution)/shard_map/psum | solution.py:187
  1449.3 24.5 %copy-start.26 = (bf16[768,192]{1,0:T(8,128)(2,1)S(1)}, bf16[768,192]{1,0:T(8,128)(2,1)}, u32[]{:S(2)}) copy-start(bf16[768,192]{1,0:T(8,128)(2,1)} %copy-done.25) | copy-start | bytes 884740
  1473.8 7.9 copy-start.5
  1482.2 14.8 copy-start.15
  1482.2 15.0 copy-start.13
  1508.6 108.8 %copy-start.42 = (f32[768]{0:T(1024)S(1)}, f32[768]{0:T(1024)}, u32[]{:S(2)}) copy-start(f32[768]{0:T(1024)} %get-tuple-element.78) | copy-start | bytes 9220
  1508.6 108.8 %copy-start.45 = (f32[768]{0:T(1024)S(1)}, f32[768]{0:T(1024)}, u32[]{:S(2)}) copy-start(f32[768]{0:T(1024)} %get-tuple-element.76) | copy-start | bytes 9220
  1508.6 108.8 %copy-start.46 = (f32[768]{0:T(1024)S(1)}, f32[768]{0:T(1024)}, u32[]{:S(2)}) copy-start(f32[768]{0:T(1024)} %get-tuple-element.80) | copy-start | bytes 9220
  1508.6 108.8 %copy-start.47 = (f32[768]{0:T(1024)S(1)}, f32[768]{0:T(1024)}, u32[]{:S(2)}) copy-start(f32[768]{0:T(1024)} %get-tuple-element.108) | copy-start | bytes 9220
  1508.6 108.8 %copy-start.49 = (f32[768]{0:T(1024)S(1)}, f32[768]{0:T(1024)}, u32[]{:S(2)}) copy-start(f32[768]{0:T(1024)} %get-tuple-element.116) | copy-start | bytes 9220
  (31 other events, 109.9 us)
Sparse Core Ops, SparseCore 0:
  24.3 28.1 all-gather.6
  54.5 27.1 all-gather.4
  107.1 223.7 all-reduce.7
  366.0 221.7 all-reduce.9
  615.0 221.7 all-reduce.11
  1026.3 25.0 reduce-scatter.24
  1165.0 25.0 reduce-scatter.26
  1192.5 20.7 reduce-scatter.28
  1262.6 19.3 reduce-scatter.30
  1345.9 19.3 reduce-scatter.32
  1367.9 25.7 reduce-scatter.20
  1396.3 25.7 reduce-scatter.22
  1424.5 20.7 reduce-scatter.18
  1448.5 39.4 all-reduce.15
  1490.3 121.0 all-reduce.13
Sparse Core Ops, SparseCore 1:
  109.0 18.2 all-gather.8
  128.7 17.3 all-gather.10
where the time goes:
time: 1660 us; the launch traced here: 1650 us
  waiting for transfers between devices  806 us (49%)
  local copies, waits for them, and re-layouts  504 us (30%)
  matrix products  184 us (11%)
  other arithmetic  73.5 us (4%)
  blocking collectives  52.9 us (3%)
    unnamed x145, local copies, waits for them, and re-layouts  441 us
    psum x1, waiting for transfers between devices, body(): second = normed.astype(jnp.float32) + lax.psum(ffn_part, 'tp') + b_outer  222 us
    psum x1, waiting for transfers between devices, body(): grad_normed = lax.psum(normed_part, 'tp') + grad_second  221 us
    psum x1, waiting for transfers between devices, body(): first = flat_f + lax.psum(attn_part, 'tp') + b_out  212 us
    psum x1, waiting for transfers between devices, body(): lax.psum(input_part.astype(jnp.bfloat16), 'tp').astype(jnp.float32)  103 us
    sub x1, matrix products, body(): grad_probs - delta  36.6 us
  transfers between devices with their start and end apart: 17, of which 6 were waited for; matrix products, arithmetic and copies ran while one was open for 30% of the time, Pallas kernels for 0%

commit v1 on v0

v1 whole, which is shorter than its diff:
```python
import functools

import jax
import jax.numpy as jnp
from jax import lax
from jax.experimental import pallas as pl
from jax.experimental.pallas import tpu as pltpu
from jax.sharding import PartitionSpec as P

BLOCK = 256
EPS = 1e-6
BF = jnp.bfloat16
F32 = jnp.float32
VMEM_LIMIT = 63 * 1024 * 1024
ANY = pl.BlockSpec(memory_space=pl.ANY)

ERFC_P = 0.4
ERFC_Q = (
    0.22567586447289167,
    0.22566948029813316,
    0.20784439930786347,
    0.16853075364238013,
    0.14147089627243886,
    -0.0056861722734636855,
    0.16917441518538521,
    -0.18295470304963965,
    0.05027519140388732,
)

SWAP = ((0, 1), (1, 0), (2, 3), (3, 2))
FAR = ((0, 2), (2, 0), (1, 3), (3, 1))
MIDDLE = ((1, 2), (2, 1))
OUTWARD = ((1, 0), (2, 3))
INWARD = ((0, 1), (3, 2))


def params(**kw):
    return pltpu.CompilerParams(vmem_limit_bytes=VMEM_LIMIT, **kw)


def dot(left, right):
    return jnp.dot(left, right, preferred_element_type=F32)


def dot_nt(left, right):
    return lax.dot_general(left, right, (((1,), (1,)), ((), ())), preferred_element_type=F32)


def gelu_parts(u):
    t = 1.0 / (1.0 + jnp.abs(u) * (ERFC_P * 0.5**0.5))
    e = jnp.exp(-0.5 * (u * u))
    q = jnp.full_like(t, 0.5 * ERFC_Q[-1])
    for c in ERFC_Q[-2::-1]:
        q = q * t + 0.5 * c
    half = q * t * e
    cdf = jnp.where(u < 0.0, half, 1.0 - half)
    return u * cdf, cdf + u * (e * 0.3989422804014327)


def head_mask(value, offset, head, size):
    lane = lax.broadcasted_iota(jnp.int32, value.shape, 1)
    keep = (lane >= offset + head * size) & (lane < offset + (head + 1) * size)
    return jnp.where(keep, value, jnp.zeros_like(value))


def load_rows(ids, pieces, scratch, sems):
    f = ids[0]
    rows = pieces[0].shape[0]
    copies = []
    for k, piece in enumerate(pieces):
        at = pl.multiple_of((f ^ k) * rows, rows)
        copies.append(pltpu.make_async_copy(piece, scratch.at[pl.ds(at, rows)], sems.at[k]))
    return copies


def qkv_kernel(ids, x_ref, w0, w1, w2, w3, b_ref, q_ref, kv_ref, w_scr, sems, *, scale):
    copies = load_rows(ids, (w0, w1, w2, w3), w_scr, sems)
    for c in copies:
        c.start()
    for c in copies:
        c.wait()
    width = q_ref.shape[1]
    out = dot(x_ref[0], w_scr[...])
    bias = b_ref[...]
    query = (out[:, :width] + bias[:, :width]).astype(BF)
    q_ref[...] = (query.astype(F32) * scale).astype(BF)
    kv_ref[...] = (out[:, 256:] + bias[:, 256:]).astype(BF)


def qkv_call(ids, hidden, seq, pieces, bias, width, scale):
    _, rows, d = hidden.shape
    cols = pieces[0].shape[1]
    return pl.pallas_call(
        functools.partial(qkv_kernel, scale=scale),
        out_shape=(
            jax.ShapeDtypeStruct((rows, width), BF),
            jax.ShapeDtypeStruct((rows, 2 * width), BF),
        ),
        grid_spec=pltpu.PrefetchScalarGridSpec(
            num_scalar_prefetch=1,
            grid=(1,),
            in_specs=[pl.BlockSpec((1, rows, d), lambda i, s: (seq, 0, 0))]
            + [ANY] * 4
            + [pl.BlockSpec((1, cols), lambda i, s: (0, 0))],
            out_specs=[
                pl.BlockSpec((rows, width), lambda i, s: (0, 0)),
                pl.BlockSpec((rows, 2 * width), lambda i, s: (0, 0)),
            ],
            scratch_shapes=[pltpu.VMEM((d, cols), BF), pltpu.SemaphoreType.DMA((4,))],
        ),
        compiler_params=params(),
        cost_estimate=pl.CostEstimate(
            flops=2 * rows * d * cols, bytes_accessed=2 * (rows + d) * (d + cols), transcendentals=0
        ),
        name="qkv",
    )(ids, hidden, *pieces, bias)


def spread_heads(ids, kv_refs, k3, v3, heads, size):
    width = heads * size
    if len(kv_refs) == 2:
        low, own = kv_refs
        rows = own.shape[0]
        own_v = own[...]
        parts = ((0, jnp.where(ids[1] == 0, own_v, low[...])), (rows, own_v))
    else:
        parts = ((0, kv_refs[0][...]),)
    for at, part in parts:
        keys, values = part[:, :width], part[:, width:]
        for h in range(heads):
            k3[h, at : at + part.shape[0], :] = head_mask(keys, 0, h, size)
            v3[h, at : at + part.shape[0], :] = head_mask(values, 0, h, size)


def attn_fwd_kernel(ids, *refs, heads, size, nkv, chained):
    q_ref, prev_ref = refs[0], refs[1]
    kv_refs = refs[2 : 2 + nkv]
    outs = refs[2 + nkv + chained :]
    log_ref, p_ref, att_ref, k3, v3 = outs
    rb = pl.program_id(0)
    blocks = pl.num_programs(0)
    full = prev_ref.shape[3]

    @pl.when(rb == 0)
    def _():
        spread_heads(ids, kv_refs, k3, v3, heads, size)

    g = ids[1] * blocks + rb
    for i in range(full // BLOCK):
        n = (i + 1) * BLOCK

        @pl.when(g == i)
        def _(n=n):
            query = q_ref[...]
            total = None
            for h in range(heads):
                s = dot_nt(query, k3[h, :n, :]) + prev_ref[0, h, :, :n].astype(F32)
                log_ref[0, h, :, :n] = s.astype(BF)
                if n < full:
                    log_ref[0, h, :, n:] = jnp.zeros((BLOCK, full - n), BF)
                e = jnp.exp(s - jnp.max(s, axis=1, keepdims=True))
                p = (e * (1.0 / jnp.sum(e, axis=1, keepdims=True))).astype(BF)
                p_ref[h, :, :n] = p
                part = dot(p, v3[h, :n, :])
                total = part if total is None else total + part
            att_ref[...] = total.astype(BF)


def attn_fwd_call(ids, q, kvs, prev, seq, chain, heads, size):
    seqs, _, rows, full = prev.shape
    width = heads * size
    blocks = rows // BLOCK
    big = pl.BlockSpec((1, heads, BLOCK, full), lambda r, s: (seq, 0, r, 0))
    chained = [] if chain is None else [chain]
    tokens = 3 * full // 4
    return pl.pallas_call(
        functools.partial(
            attn_fwd_kernel, heads=heads, size=size, nkv=len(kvs), chained=len(chained)
        ),
        out_shape=(
            jax.ShapeDtypeStruct(prev.shape, BF),
            jax.ShapeDtypeStruct((heads, rows, full), BF),
            jax.ShapeDtypeStruct((rows, width), BF),
        ),
        grid_spec=pltpu.PrefetchScalarGridSpec(
            num_scalar_prefetch=1,
            grid=(blocks,),
            in_specs=[pl.BlockSpec((BLOCK, width), lambda r, s: (r, 0)), big]
            + [pl.BlockSpec(kv.shape, lambda r, s: (0, 0)) for kv in kvs]
            + [ANY] * len(chained),
            out_specs=[
                big,
                pl.BlockSpec((heads, BLOCK, full), lambda r, s: (0, r, 0)),
                pl.BlockSpec((BLOCK, width), lambda r, s: (r, 0)),
            ],
            scratch_shapes=[
                pltpu.VMEM((heads, full, width), BF),
                pltpu.VMEM((heads, full, width), BF),
            ],
        ),
        input_output_aliases={3 + len(kvs): 0} if chained else {},
        compiler_params=params(),
        cost_estimate=pl.CostEstimate(
            flops=4 * 4 * heads * rows * tokens * size,
            bytes_accessed=6 * heads * rows * full,
            transcendentals=heads * rows * tokens,
        ),
        name="attn_fwd",
    )(ids, q, prev, *kvs, *chained)


def attn_bwd_kernel(ids, *refs, heads, size, nkv, chained, scale):
    q_ref, p_ref, dl_ref, datt_ref, att_ref = refs[:5]
    kv_refs = refs[5 : 5 + nkv]
    dprev_ref, dq_ref, dkv_ref, k3, v3, dk_t, dv_t = refs[5 + nkv + chained :]
    rb = pl.program_id(0)
    blocks = pl.num_programs(0)
    full = dl_ref.shape[3]
    width = heads * size

    @pl.when(rb == 0)
    def _():
        spread_heads(ids, kv_refs, k3, v3, heads, size)
        dk_t[...] = jnp.zeros_like(dk_t)
        dv_t[...] = jnp.zeros_like(dv_t)

    g = ids[1] * blocks + rb
    for i in range(full // BLOCK):
        n = (i + 1) * BLOCK

        @pl.when(g == i)
        def _(n=n):
            datt = datt_ref[...]
            q_t = q_ref[...].T
            datt_t = datt.T
            weighted = datt.astype(F32) * att_ref[...].astype(F32)
            total = None
            for h in range(heads):
                at = h * size
                dp = dot_nt(datt, v3[h, :n, :])
                delta = jnp.sum(head_mask(weighted, 0, h, size), axis=1, keepdims=True)
                p = p_ref[h, :, :n]
                ds = p.astype(F32) * (dp - delta) + dl_ref[0, h, :, :n].astype(F32)
                low = ds.astype(BF)
                dprev_ref[0, h, :, :n] = low
                if n < full:
                    dprev_ref[0, h, :, n:] = jnp.zeros((BLOCK, full - n), BF)
                part = dot(low, k3[h, :n, :])
                total = part if total is None else total + part
                dk_t[at : at + size, :n] += dot(q_t[at : at + size], low)
                dv_t[at : at + size, :n] += dot(datt_t[at : at + size], p)
            dq_ref[...] = (total * scale).astype(BF)

    @pl.when(rb == blocks - 1)
    def _():
        dkv_ref[:, :width] = dk_t[...].T.astype(BF)
        dkv_ref[:, width:] = dv_t[...].T.astype(BF)


def attn_bwd_call(ids, q, probs, d_logits, datt, att, kvs, seq, chain, heads, size, scale):
    seqs, _, rows, full = d_logits.shape
    width = heads * size
    blocks = rows // BLOCK
    big = pl.BlockSpec((1, heads, BLOCK, full), lambda r, s: (seq, 0, r, 0))
    tile = pl.BlockSpec((BLOCK, width), lambda r, s: (r, 0))
    chained = [] if chain is None else [chain]
    tokens = 3 * full // 4
    return pl.pallas_call(
        functools.partial(
            attn_bwd_kernel,
            heads=heads,
            size=size,
            nkv=len(kvs),
            chained=len(chained),
            scale=scale,
        ),
        out_shape=(
            jax.ShapeDtypeStruct(d_logits.shape, BF),
            jax.ShapeDtypeStruct((rows, width), BF),
            jax.ShapeDtypeStruct((full, 2 * width), BF),
        ),
        grid_spec=pltpu.PrefetchScalarGridSpec(
            num_scalar_prefetch=1,
            grid=(blocks,),
            in_specs=[
                tile,
                pl.BlockSpec((heads, BLOCK, full), lambda r, s: (0, r, 0)),
                big,
                tile,
                tile,
            ]
            + [pl.BlockSpec(kv.shape, lambda r, s: (0, 0)) for kv in kvs]
            + [ANY] * len(chained),
            out_specs=[big, tile, pl.BlockSpec((full, 2 * width), lambda r, s: (0, 0))],
            scratch_shapes=[
                pltpu.VMEM((heads, full, width), BF),
                pltpu.VMEM((heads, full, width), BF),
                pltpu.VMEM((width, full), F32),
                pltpu.VMEM((width, full), F32),
            ],
        ),
        input_output_aliases={6 + len(kvs): 0} if chained else {},
        compiler_params=params(),
        cost_estimate=pl.CostEstimate(
            flops=4 * 8 * heads * rows * tokens * size,
            bytes_accessed=6 * heads * rows * full,
            transcendentals=0,
        ),
        name="attn_bwd",
    )(ids, q, probs, d_logits, datt, att, *kvs, *chained)


def slot_owner(rank, slot):
    if slot == 0:
        return rank
    if slot == 1:
        return rank ^ 1
    if slot == 2:
        return jnp.where(rank < 2, 2, 1)
    return jnp.where(rank < 2, 3, 0)


def row_mean(value):
    return jnp.mean(value, axis=1, keepdims=True)


def col_sum(value):
    return jnp.sum(value, axis=0, keepdims=True)


def ffn_kernel(ids, *refs, chained, width, units):
    x_ref, a0, a1, a2, a3, do_ref, vec_ref, bin_ref = refs[:8]
    pieces = refs[8:24]
    refs = refs[24:]
    if chained:
        gi_in, go_in, gw_in = refs[:3]
        refs = refs[4:]
    out_ref, dh1_ref, datt_ref, sum_ref, gi_hbm, go_hbm, gw_hbm = refs[:7]
    wi, wo, wa, act_s, gp_s, din_s, att_s, gi, go, gw, w_sem, g_sem = refs[7:]
    step = pl.program_id(0)
    last = pl.num_programs(0) - 1
    rank = ids[2]
    rows = pieces[0].shape[0]

    def copies(group):
        out = []
        for slot in range(4):
            owner = slot_owner(rank, slot)
            for k in range(4):
                piece = pieces[slot * 4 + k]
                at = pl.ds(pl.multiple_of((ids[0] ^ k) * rows, rows), rows)
                sem = w_sem.at[group, slot * 4 + k]
                if group == 0:
                    src, dst = piece.at[:, 2 * units : 2 * units + width], wa.at[owner, at]
                elif group == 1:
                    src, dst = piece.at[:, :units], wi.at[owner, at]
                else:
                    src, dst = piece.at[:, units : 2 * units], wo.at[owner, at]
                out.append(pltpu.make_async_copy(src, dst, sem))
        return out

    def grad_in():
        return [
            pltpu.make_async_copy(src, dst, g_sem.at[i])
            for i, (src, dst) in enumerate(((gi_in, gi), (go_in, go), (gw_in, gw)))
        ]

    @pl.when(step == 0)
    def _():
        for group in range(3):
            for c in copies(group):
                c.start()
        if chained:
            for c in grad_in():
                c.start()
        else:
            gi[...] = jnp.zeros_like(gi)
            go[...] = jnp.zeros_like(go)
            gw[...] = jnp.zeros_like(gw)
        sum_ref[...] = jnp.zeros_like(sum_ref)
        for c in copies(0):
            c.wait()

    for slot, a in enumerate((a0, a1, a2, a3)):
        att_s[slot_owner(rank, slot)] = a[...]
    b_out, gain_a, shift_a = vec_ref[0:1], vec_ref[1:2], vec_ref[2:3]
    b_outer, gain_f, shift_f = vec_ref[3:4], vec_ref[4:5], vec_ref[5:6]
    h1 = x_ref[0].astype(F32) + b_out
    for t in range(4):
        h1 = h1 + dot_nt(att_s[t], wa[t])
    c1 = h1 - row_mean(h1)
    r1 = lax.rsqrt(row_mean(c1 * c1) + EPS)
    n1 = c1 * r1
    normed = (n1 * gain_a + shift_a).astype(BF)

    @pl.when(step == 0)
    def _():
        for c in copies(1):
            c.wait()
        for c in copies(2):
            c.wait()
        if chained:
            for c in grad_in():
                c.wait()

    h2 = normed.astype(F32) + b_outer
    for t in range(4):
        inner = dot(normed, wi[t]) + bin_ref[t : t + 1]
        act, slope = gelu_parts(inner)
        low = act.astype(BF)
        act_s[t] = low
        gp_s[t] = slope.astype(BF)
        h2 = h2 + dot_nt(low, wo[t])
    c2 = h2 - row_mean(h2)
    r2 = lax.rsqrt(row_mean(c2 * c2) + EPS)
    n2 = c2 * r2
    out_ref[0] = (n2 * gain_f + shift_f).astype(BF)
    d_out = do_ref[0].astype(F32)
    e2 = d_out * gain_f
    dh2 = (e2 - row_mean(e2) - n2 * row_mean(e2 * n2)) * r2
    dh2_low = dh2.astype(BF)
    dn = dh2
    for t in range(4):
        din = dot(dh2_low, wo[t]) * gp_s[t].astype(F32)
        low = din.astype(BF)
        din_s[t] = low
        dn = dn + dot_nt(low, wi[t])
    e1 = dn * gain_a
    dh1 = (e1 - row_mean(e1) - n1 * row_mean(e1 * n1)) * r1
    dh1_ref[...] = dh1
    dh1_low = dh1.astype(BF)
    datt_ref[...] = dot(dh1_low, wa[rank]).astype(BF)
    din_own = din_s[rank]
    sum_ref[0:1] += col_sum(dh1)
    sum_ref[1:2] += col_sum(dn * n1)
    sum_ref[2:3] += col_sum(dn)
    sum_ref[3:4] += col_sum(dh2)
    sum_ref[4:5] += col_sum(d_out * n2)
    sum_ref[5:6] += col_sum(d_out)
    sum_ref[6:7] += col_sum(din_own.astype(F32))
    gi[...] += dot(normed.T, din_own)
    go[...] += dot(dh2_low.T, act_s[rank])
    gw[...] += dot(dh1_low.T, att_s[rank])

    @pl.when(step == last)
    def _():
        out = [
            pltpu.make_async_copy(src, dst, g_sem.at[i])
            for i, (src, dst) in enumerate(((gi, gi_hbm), (go, go_hbm), (gw, gw_hbm)))
        ]
        for c in out:
            c.start()
        for c in out:
            c.wait()


def ffn_call(ids, hidden, atts, d_output, vec, b_inner, pieces, seq, chain, units):
    _, rows, d = hidden.shape
    width = atts[0].shape[1]
    tile = min(rows, 256)
    whole = pl.BlockSpec((1, tile, d), lambda r, s: (seq, r, 0))
    att = pl.BlockSpec((tile, width), lambda r, s: (r, 0))
    fixed = lambda shape: pl.BlockSpec(shape, lambda r, s: (0, 0))
    chained = [] if chain is None else list(chain)
    base = 1 + 8 + 16
    return pl.pallas_call(
        functools.partial(ffn_kernel, chained=bool(chained), width=width, units=units),
        out_shape=(
            jax.ShapeDtypeStruct(hidden.shape, BF),
            jax.ShapeDtypeStruct((rows, d), F32),
            jax.ShapeDtypeStruct((rows, width), BF),
            jax.ShapeDtypeStruct((8, d), F32),
            jax.ShapeDtypeStruct((d, units), F32),
            jax.ShapeDtypeStruct((d, units), F32),
            jax.ShapeDtypeStruct((d, width), F32),
        ),
        grid_spec=pltpu.PrefetchScalarGridSpec(
            num_scalar_prefetch=1,
            grid=(rows // tile,),
            in_specs=[whole, att, att, att, att, whole, fixed((8, d)), fixed((4, units))]
            + [ANY] * 16
            + [ANY] * len(chained),
            out_specs=[
                whole,
                pl.BlockSpec((tile, d), lambda r, s: (r, 0)),
                att,
                fixed((8, d)),
                ANY,
                ANY,
                ANY,
            ],
            scratch_shapes=[
                pltpu.VMEM((4, d, units), BF),
                pltpu.VMEM((4, d, units), BF),
                pltpu.VMEM((4, d, width), BF),
                pltpu.VMEM((4, tile, units), BF),
                pltpu.VMEM((4, tile, units), BF),
                pltpu.VMEM((4, tile, units), BF),
                pltpu.VMEM((4, tile, width), BF),
                pltpu.VMEM((d, units), F32),
                pltpu.VMEM((d, units), F32),
                pltpu.VMEM((d, width), F32),
                pltpu.SemaphoreType.DMA((3, 16)),
                pltpu.SemaphoreType.DMA((3,)),
            ],
        ),
        input_output_aliases=(
            {base: 4, base + 1: 5, base + 2: 6, base + 3: 0} if chained else {}
        ),
        compiler_params=params(),
        cost_estimate=pl.CostEstimate(
            flops=2 * rows * d * units * 20,
            bytes_accessed=16 * d * units + 16 * rows * d,
            transcendentals=8 * rows * units,
        ),
        name="ffn",
    )(ids, hidden, *atts, d_output, vec, b_inner, *pieces, *chained)


def dx_kernel(ids, *refs, nkv, chained):
    x_ref, dq_ref = refs[:2]
    dkv_refs = refs[2 : 2 + nkv]
    pieces = refs[2 + nkv : 6 + nkv]
    refs = refs[6 + nkv :]
    if chained:
        g_in = refs[0]
        refs = refs[1:]
    y_ref, sum_ref, g_hbm, w_scr, g_scr, sems, g_sem = refs
    copies = load_rows(ids, pieces, w_scr, sems)
    for c in copies:
        c.start()
    if chained:
        grad = pltpu.make_async_copy(g_in, g_scr, g_sem)
        grad.start()
    dq = dq_ref[...]
    dkv = dkv_refs[0][...]
    if nkv == 2:
        dkv = (dkv.astype(F32) + dkv_refs[1][...].astype(F32)).astype(BF)
    pad = jnp.zeros((dq.shape[0], 256 - dq.shape[1]), BF)
    joined = jnp.concatenate([dq, pad, dkv], axis=1)
    x_t = x_ref[0].T
    sum_ref[...] = jnp.broadcast_to(col_sum(joined.astype(F32)), sum_ref.shape)
    for c in copies:
        c.wait()
    y_ref[...] = dot_nt(joined, w_scr[...]).astype(BF)
    part = dot(x_t, joined)
    if chained:
        grad.wait()
        g_scr[...] += part
    else:
        g_scr[...] = part
    done = pltpu.make_async_copy(g_scr, g_hbm, g_sem)
    done.start()
    done.wait()


def dx_call(ids, hidden, dq, dkvs, pieces, seq, chain):
    _, rows, d = hidden.shape
    cols = pieces[0].shape[1]
    fixed = lambda shape: pl.BlockSpec(shape, lambda r, s: (0, 0))
    chained = [] if chain is None else [chain]
    return pl.pallas_call(
        functools.partial(dx_kernel, nkv=len(dkvs), chained=bool(chained)),
        out_shape=(
            jax.ShapeDtypeStruct((rows, d), BF),
            jax.ShapeDtypeStruct((8, cols), F32),
            jax.ShapeDtypeStruct((d, cols), F32),
        ),
        grid_spec=pltpu.PrefetchScalarGridSpec(
            num_scalar_prefetch=1,
            grid=(1,),
            in_specs=[pl.BlockSpec((1, rows, d), lambda r, s: (seq, 0, 0)), fixed(dq.shape)]
            + [fixed(v.shape) for v in dkvs]
            + [ANY] * 4
            + [ANY] * len(chained),
            out_specs=[fixed((rows, d)), fixed((8, cols)), ANY],
            scratch_shapes=[
                pltpu.VMEM((d, cols), BF),
                pltpu.VMEM((d, cols), F32),
                pltpu.SemaphoreType.DMA((4,)),
                pltpu.SemaphoreType.DMA,
            ],
        ),
        input_output_aliases={3 + len(dkvs) + 4: 2} if chained else {},
        compiler_params=params(),
        cost_estimate=pl.CostEstimate(
            flops=4 * rows * d * cols, bytes_accessed=8 * d * cols, transcendentals=0
        ),
        name="dx",
    )(ids, hidden, dq, *dkvs, *pieces, *chained)


def final_kernel(ids, dh1_ref, t_ref, r3_ref, s3_ref, r4_ref, *refs):
    out_ref = refs[-1]
    rank = ids[2]
    half = t_ref.shape[0]

    @pl.when((rank == 0) | (rank == 3))
    def _():
        first, second = s3_ref[...].astype(F32), r4_ref[...].astype(F32)
        low = rank < 2
        out_ref[0, :half] = dh1_ref[:half] + jnp.where(low, first, second)
        out_ref[0, half:] = dh1_ref[half:] + jnp.where(low, second, first)

    @pl.when((rank == 1) | (rank == 2))
    def _():
        first, second = t_ref[...].astype(F32), r3_ref[...].astype(F32)
        low = rank < 2
        out_ref[0, :half] = dh1_ref[:half] + jnp.where(low, first, second)
        out_ref[0, half:] = dh1_ref[half:] + jnp.where(low, second, first)


def final_call(ids, dh1, parts, seq, seqs, chain):
    rows, d = dh1.shape
    fixed = lambda shape: pl.BlockSpec(shape, lambda r, s: (0, 0))
    chained = [] if chain is None else [chain]
    return pl.pallas_call(
        final_kernel,
        out_shape=jax.ShapeDtypeStruct((seqs, rows, d), F32),
        grid_spec=pltpu.PrefetchScalarGridSpec(
            num_scalar_prefetch=1,
            grid=(1,),
            in_specs=[fixed(dh1.shape)] + [fixed(v.shape) for v in parts] + [ANY] * len(chained),
            out_specs=pl.BlockSpec((1, rows, d), lambda r, s: (seq, 0, 0)),
        ),
        input_output_aliases={6: 0} if chained else {},
        compiler_params=params(),
        cost_estimate=pl.CostEstimate(
            flops=2 * rows * d, bytes_accessed=12 * rows * d, transcendentals=0
        ),
        name="final",
    )(ids, dh1, *parts, *chained)


def tp_gather(value):
    near = lax.ppermute(value, "tp", SWAP)
    across = lax.ppermute(value, "tp", MIDDLE)
    across_near = lax.ppermute(near, "tp", MIDDLE)
    out = lax.ppermute(across, "tp", OUTWARD)
    out_near = lax.ppermute(across_near, "tp", OUTWARD)
    return value, near, across + out, across_near + out_near


def fsdp_gather(value):
    far = lax.ppermute(value, "fsdp", FAR)
    near = lax.ppermute(value, "fsdp", SWAP)
    return value, near, far, lax.ppermute(far, "fsdp", SWAP)


def tp_reduce(value, rank):
    half = value.shape[0] // 2
    summed = value + lax.ppermute(value, "tp", INWARD)
    top, bottom = summed[:half], summed[half:]
    upper = rank < 2
    got = lax.ppermute(jnp.where(upper, bottom, top), "tp", MIDDLE)
    done = jnp.where(upper, top, bottom) + got
    crossed = lax.ppermute(done, "tp", MIDDLE)
    sent = lax.ppermute(done, "tp", OUTWARD)
    return done, crossed, sent, lax.ppermute(crossed, "tp", OUTWARD)


def ctx_sum(value, size):
    if size == 2:
        return value + lax.ppermute(value, "ctx", ((0, 1), (1, 0)))
    return lax.psum(value, "ctx")


def fsdp_scatter_sum(value, f, size):
    rows = value.shape[0] // 4
    blocks = value.astype(BF).reshape(4, rows, value.shape[1])
    pick = lambda k: lax.dynamic_index_in_dim(blocks, f ^ k, 0, keepdims=False)
    far0 = lax.ppermute(pick(2), "fsdp", FAR)
    far1 = lax.ppermute(pick(3), "fsdp", FAR)
    mine, other = pick(0) + far0, pick(1) + far1
    mine = mine + lax.ppermute(other, "fsdp", SWAP)
    return ctx_sum(mine, size).astype(F32)


def all_sum(value, size):
    value = value + lax.ppermute(value, "fsdp", SWAP)
    value = value + lax.ppermute(value, "fsdp", FAR)
    return ctx_sum(value, size)


def body(
    hidden_in,
    prev_logits,
    w_query,
    w_key,
    w_value,
    w_out,
    w_inner,
    w_outer,
    b_query,
    b_value,
    b_out,
    b_inner,
    b_outer,
    gain_attn,
    shift_attn,
    gain_ffn,
    shift_ffn,
    d_output,
    d_logits,
    *,
    ctx_size,
):
    seqs, rows, d = hidden_in.shape
    heads = prev_logits.shape[1]
    full = prev_logits.shape[3]
    width = w_query.shape[1]
    units = w_inner.shape[1]
    size = width // heads
    scale = size**-0.5
    f, c, rank = lax.axis_index("fsdp"), lax.axis_index("ctx"), lax.axis_index("tp")
    ids = jnp.stack([f, c, rank]).astype(jnp.int32)

    pad = 256 - width
    qkv_local = jnp.concatenate(
        [w_query, jnp.zeros((w_query.shape[0], pad), BF), w_key, w_value], axis=1
    )
    qkv_pieces = fsdp_gather(qkv_local)
    qkv_bias = jnp.concatenate([b_query, jnp.zeros((256,), F32), b_value])[None]
    ffn_local = jnp.concatenate([w_inner, w_outer, w_out], axis=1)
    ffn_pieces = []
    for part in tp_gather(ffn_local):
        ffn_pieces.extend(fsdp_gather(part))
    bias_slots = tp_gather(b_inner)
    bias_inner = jnp.zeros((4, units), F32)
    for slot in range(4):
        bias_inner = lax.dynamic_update_index_in_dim(
            bias_inner, bias_slots[slot], slot_owner(rank, slot), 0
        )
    vec = jnp.stack([b_out, gain_attn, shift_attn, b_outer, gain_ffn, shift_ffn, b_out, b_out])

    queries, kvs = [], []
    for s in range(seqs):
        q, kv = qkv_call(ids, hidden_in, s, qkv_pieces, qkv_bias, width, scale)
        queries.append(q)
        if ctx_size == 2:
            kvs.append((lax.ppermute(kv, "ctx", ((0, 1),)), kv))
        else:
            kvs.append((lax.all_gather(kv, "ctx", axis=0, tiled=True),))

    logits, probs, atts = None, [], []
    for s in range(seqs):
        logits, p, att = attn_fwd_call(
            ids, queries[s], kvs[s], prev_logits, s, logits, heads, size
        )
        probs.append(p)
        atts.append(att)

    chain, sums, dh1s, datts = None, [], [], []
    for s in range(seqs):
        output, dh1, datt, part, gi, go, gw = ffn_call(
            ids,
            hidden_in,
            tp_gather(atts[s]),
            d_output,
            vec,
            bias_inner,
            ffn_pieces,
            s,
            chain,
            units,
        )
        chain = (gi, go, gw, output)
        sums.append(part)
        dh1s.append(dh1)
        datts.append(datt)

    d_prev, g_qkv, d_hidden, qkv_sums = None, None, None, []
    for s in range(seqs):
        d_prev, dq, dkv = attn_bwd_call(
            ids,
            queries[s],
            probs[s],
            d_logits,
            datts[s],
            atts[s],
            kvs[s],
            s,
            d_prev,
            heads,
            size,
            scale,
        )
        if ctx_size == 2:
            own = lax.dynamic_slice_in_dim(dkv, c * rows, rows, 0)
            dkvs = (own, lax.ppermute(dkv[:rows], "ctx", ((1, 0),)))
        else:
            dkvs = (lax.psum_scatter(dkv, "ctx", scatter_dimension=0, tiled=True),)
        y, part, g_qkv = dx_call(ids, hidden_in, dq, dkvs, qkv_pieces, s, g_qkv)
        qkv_sums.append(part)
        d_hidden = final_call(ids, dh1s[s], tp_reduce(y, rank), s, seqs, d_hidden)

    total = functools.reduce(jnp.add, sums)
    qkv_total = functools.reduce(jnp.add, qkv_sums)[0]
    ffn_small = all_sum(total, ctx_size)
    qkv_small = all_sum(qkv_total, ctx_size)
    g_ffn = jnp.concatenate([gi, go, gw], axis=1)
    g_ffn = fsdp_scatter_sum(g_ffn, f, ctx_size)
    g_qkv = fsdp_scatter_sum(g_qkv, f, ctx_size)
    return (
        output,
        logits,
        d_hidden,
        d_prev,
        g_qkv[:, :width],
        g_qkv[:, 256 : 256 + width],
        g_qkv[:, 256 + width :],
        g_ffn[:, 2 * units :],
        g_ffn[:, :units],
        g_ffn[:, units : 2 * units],
        qkv_small[:width],
        qkv_small[256 + width :],
        ffn_small[0],
        ffn_small[6],
        ffn_small[3],
        ffn_small[1],
        ffn_small[2],
        ffn_small[4],
        ffn_small[5],
    )


def solution(mesh):
    tok, lgt, mat = P("fsdp", "ctx", None), P("fsdp", "tp", "ctx", None), P("fsdp", "tp")
    vec, rep = P("tp"), P()
    in_specs = (tok, lgt) + (mat,) * 6 + (vec, vec, rep, vec) + (rep,) * 5 + (tok, lgt)
    out_specs = (tok, lgt, tok, lgt) + (mat,) * 6 + (vec, vec, rep, vec) + (rep,) * 5
    return jax.shard_map(
        functools.partial(body, ctx_size=mesh.shape["ctx"]),
        mesh=mesh,
        in_specs=in_specs,
        out_specs=out_specs,
        check_vma=False,
    )
```

time: 1660 us -> 680 us (0.41)
  waiting for transfers between devices: 806 us -> 240 us
  local copies, waits for them, and re-layouts: 504 us -> 20.9 us
  Pallas kernels: 0 us -> 246 us
  matrix products: 184 us -> 0 us
  starting transfers between devices: 13 us -> 134 us
  blocking collectives: 52.9 us -> 0 us
  other arithmetic: 73.5 us -> 26.6 us
    psum x5 -> x0, waiting for transfers between devices: 758 us -> none  [the longest x1 222 us: body(): second = normed.astype(jnp.float32) + lax.psum(ffn_part, 'tp') + b_outer]
    unnamed x145 -> x122, local copies, waits for them, and re-layouts: 441 us -> 6.01 us
    pallas_call x0 -> x24, Pallas kernels: none -> 246 us  [the longest x4 126 us: ffn_call(): pl.pallas_call(functools.partial(ffn_kernel, chained=bool(chained), width...]
    ppermute x0 -> x87, waiting for transfers between devices: none -> 240 us  [the longest x4 52.1 us: tp_reduce(): summed = value + lax.ppermute(value, 'tp', INWARD)]
    dot_general x23 -> x0, matrix products: 147 us -> none  [the longest x6 31.2 us: contract_cols(): lax.dot_general(left, right, (((1,), (1,)), ((), ())), preferred_element_...]
    ppermute x0 -> x87, starting transfers between devices: none -> 134 us  [the longest x6 36.1 us: tp_gather(): near = lax.ppermute(value, 'tp', SWAP)]
    reduce_sum x13 -> x0, other arithmetic: 51.2 us -> none  [the longest x3 12.3 us: layer_norm(): return centered * lax.rsqrt(variance + 1e-06) * gain + shift]
    reduce_scatter x2 -> x0, local copies, waits for them, and re-layouts: 47.2 us -> none  [the longest x1 23.6 us: body(): lax.psum_scatter(grad_values_all.reshape(seq_count, full_len, local_width...]
  transfers between devices with their start and end apart: 17 -> 87, of which waited for: 6 -> 27; matrix products, arithmetic and copies ran while one was open for 30% -> 6% of each run, Pallas kernels for 0% -> 17%
where the time goes in v1:
time: 680 us; the launch traced here: 670 us
  Pallas kernels  246 us (36%)
  waiting for transfers between devices  240 us (35%)
  starting transfers between devices  134 us (20%)
  other arithmetic  26.6 us (4%)
  local copies, waits for them, and re-layouts  20.9 us (3%)
    pallas_call x4, Pallas kernels, ffn_call(): pl.pallas_call(functools.partial(ffn_kernel, chained=bool(chained), width...  126 us
    ppermute x4, waiting for transfers between devices, tp_reduce(): summed = value + lax.ppermute(value, 'tp', INWARD)  52.1 us
    ppermute x4, waiting for transfers between devices, tp_reduce(): sent = lax.ppermute(done, 'tp', OUTWARD)  41.9 us
    ppermute x4, waiting for transfers between devices, tp_reduce(): return (done, crossed, sent, lax.ppermute(crossed, 'tp', OUTWARD))  37.6 us
    ppermute x6, starting transfers between devices, tp_gather(): near = lax.ppermute(value, 'tp', SWAP)  36.1 us
    pallas_call x4, Pallas kernels, attn_bwd_call(): pl.pallas_call(functools.partial(attn_bwd_kernel, heads=heads, size=size,...  30.7 us
    pallas_call x4, Pallas kernels, dx_call(): pl.pallas_call(functools.partial(dx_kernel, nkv=len(dkvs), chained=bool(c...  28.8 us
    ppermute x6, waiting for transfers between devices, tp_gather(): near = lax.ppermute(value, 'tp', SWAP)  28.4 us
  transfers between devices with their start and end apart: 87, of which 27 were waited for; matrix products, arithmetic and copies ran while one was open for 6% of the time, Pallas kernels for 17%

profile of v1, /device:TPU:0, one launch (start us, length us, event | category | flops | bytes accessed | tf_op | source)
XLA Modules:
  0.0 669.9 jit_solution(16203044712059301196)
XLA Ops:
  15.7 14.9 %collective-permute-start.12 = (f32[768]{0:T(1024)}, f32[768]{0:T(1024)S(1)}, u32[]{:S(2)}, u32[]{:S(2)}) collective-permute-start(f32[768]{0:T(1024)} %param.30), channel_id=1, source_target_pairs={{0,1},{1,0},{2,3},{3,2},{4,5},{5,4},{6,7},{7,6},{8,9},{9,8},{10,11... | collective-permute-start | bytes 9224 | tf_op jit(solution)/shard_map/ppermute | solution.py:636
  33.7 4.2 collective-permute-done.14
  43.5 4.7 qkv.7
  49.5 4.1 collective-permute-start.6
  53.6 4.7 qkv.6
  61.2 4.7 qkv.5
  67.2 4.7 qkv.4
  73.9 6.6 attn_fwd.4
  82.2 6.5 collective-permute-start.44
  88.7 6.6 attn_fwd.5
  96.7 6.6 attn_fwd.6
  112.1 6.6 attn_fwd.7
  119.7 6.1 collective-permute-start.7
  127.8 26.6 %collective-permute-done.7.refs_2_ = bf16[512,192]{1,0:T(8,128)(2,1)S(1)} collective-permute-done((bf16[512,192]{1,0:T(8,128)(2,1)}, bf16[512,192]{1,0:T(8,128)(2,1)S(1)}, u32[]{:S(2)}, u32[]{:S(2)}) %collective-permute-start.7) | collective-permute-done | bytes 196640 | tf_op jit(solution)/shard_map/ppermute | solution.py:636
  155.7 4.3 collective-permute-done.46
  162.0 3.7 collective-permute-done.41
  175.1 7.0 %collective-permute-done.9 = bf16[512,192]{1,0:T(8,128)(2,1)S(1)} collective-permute-done((bf16[512,192]{1,0:T(8,128)(2,1)S(1)}, bf16[512,192]{1,0:T(8,128)(2,1)S(1)}, u32[]{:S(2)}, u32[]{:S(2)}) %collective-permute-start.9) | collective-permute-done | bytes 196640 | tf_op jit(solution)/shard_map/ppermute | solution.py:639
  188.1 7.7 %collective-permute-done.48 = bf16[512,192]{1,0:T(8,128)(2,1)S(1)} collective-permute-done((bf16[512,192]{1,0:T(8,128)(2,1)S(1)}, bf16[512,192]{1,0:T(8,128)(2,1)S(1)}, u32[]{:S(2)}, u32[]{:S(2)}) %collective-permute-start.48) | collective-permute-done | bytes 196640 | tf_op jit(solution)/shard_map/ppermute | solution.py:640
  197.0 4.3 collective-permute-done.43
  201.4 5.6 collective-permute-done.38
  207.0 4.4 collective-permute-done.11
  225.6 30.2 %ffn.4 = (bf16[4,512,768]{2,1,0:T(8,128)(2,1)}, f32[512,768]{1,0:T(8,128)}, bf16[512,192]{1,0:T(8,128)(2,1)}, f32[8,768]{1,0:T(8,128)}, f32[768,768]{1,0:T(8,128...) custom-call(s32[3]{0:T(128)} %pad_add_fusion.ids, bf16[4,512,768]{2,1,0:T(8,128)(2,1)} %refs_0_.15, ...), custom_call_target="tpu_custom_call" | custom-call | flops 12079595520 | bytes 15728640 | tf_op jit(solution)/shard_map/ffn/pallas_call | solution.py:466
  255.8 32.0 %ffn.5 = (bf16[4,512,768]{2,1,0:T(8,128)(2,1)}, f32[512,768]{1,0:T(8,128)}, bf16[512,192]{1,0:T(8,128)(2,1)}, f32[8,768]{1,0:T(8,128)}, f32[768,768]{1,0:T(8,128...) custom-call(s32[3]{0:T(128)} %pad_add_fusion.ids, ...), custom_call_target="tpu_custom_call", output_to_operand_aliasing={{4}: (25, {}), {5}: (26, {}), {6}: (27, {}), {0}: (28, {})} | custom-call | flops 12079595520 | bytes 15728640 | tf_op jit(solution)/shard_map/ffn/pallas_call | solution.py:466
  287.8 32.2 %ffn.6 = (bf16[4,512,768]{2,1,0:T(8,128)(2,1)}, f32[512,768]{1,0:T(8,128)}, bf16[512,192]{1,0:T(8,128)(2,1)}, f32[8,768]{1,0:T(8,128)}, f32[768,768]{1,0:T(8,128...) custom-call(s32[3]{0:T(128)} %pad_add_fusion.ids, ...), custom_call_target="tpu_custom_call", output_to_operand_aliasing={{4}: (25, {}), {5}: (26, {}), {6}: (27, {}), {0}: (28, {})} | custom-call | flops 12079595520 | bytes 15728640 | tf_op jit(solution)/shard_map/ffn/pallas_call | solution.py:466
  320.0 31.9 %ffn.7 = (bf16[4,512,768]{2,1,0:T(8,128)(2,1)}, f32[512,768]{1,0:T(8,128)}, bf16[512,192]{1,0:T(8,128)(2,1)}, f32[8,768]{1,0:T(8,128)}, f32[768,768]{1,0:T(8,128...) custom-call(s32[3]{0:T(128)} %pad_add_fusion.ids, ...), custom_call_target="tpu_custom_call", output_to_operand_aliasing={{4}: (25, {}), {5}: (26, {}), {6}: (27, {}), {0}: (28, {})} | custom-call | flops 12079595520 | bytes 15728640 | tf_op jit(solution)/shard_map/ffn/pallas_call | solution.py:466
  358.5 7.7 %attn_bwd.4 = (bf16[4,3,512,1024]{3,2,1,0:T(8,128)(2,1)}, bf16[512,192]{1,0:T(8,128)(2,1)}, bf16[1024,384]{1,0:T(8,128)(2,1)}) custom-call(s32[3]{0:T(128)} %pad_add_fusion.ids, bf16[512,192]{1,0:T(8,128)(2,1)} %get-tuple-element.97.refs_0_, bf16[3,512,1024]{2,1,0:T(8,128)(2,1)} %get-tuple-element.127.refs_1_, bf16[4,3,512,1024]{3,2,1,0:T(8,128)(2,1)} %refs_2_.7, ...), custom_call_target="tpu_custom_call" | custom-call | flops 2415919104 | bytes 9437184 | tf_op jit(solution)/shard_map/attn_bwd/pallas_call | solution.py:268
  366.2 7.5 %attn_bwd.5 = (bf16[4,3,512,1024]{3,2,1,0:T(8,128)(2,1)}, bf16[512,192]{1,0:T(8,128)(2,1)}, bf16[1024,384]{1,0:T(8,128)(2,1)}) custom-call(s32[3]{0:T(128)} %pad_add_fusion.ids, bf16[512,192]{1,0:T(8,128)(2,1)} %get-tuple-element.95.refs_0_, bf16[3,512,1024]{2,1,0:T(8,128)(2,1)} %get-tuple-element.125.refs_1_, ...), custom_call_target="tpu_custom_call", output_to_operand_aliasing={{0}: (8, {})} | custom-call | flops 2415919104 | bytes 9437184 | tf_op jit(solution)/shard_map/attn_bwd/pallas_call | solution.py:268
  373.7 8.0 %attn_bwd.6 = (bf16[4,3,512,1024]{3,2,1,0:T(8,128)(2,1)}, bf16[512,192]{1,0:T(8,128)(2,1)}, bf16[1024,384]{1,0:T(8,128)(2,1)}) custom-call(s32[3]{0:T(128)} %pad_add_fusion.ids, bf16[512,192]{1,0:T(8,128)(2,1)} %get-tuple-element.93.refs_0_, bf16[3,512,1024]{2,1,0:T(8,128)(2,1)} %get-tuple-element.123.refs_1_, ...), custom_call_target="tpu_custom_call", output_to_operand_aliasing={{0}: (8, {})} | custom-call | flops 2415919104 | bytes 9437184 | tf_op jit(solution)/shard_map/attn_bwd/pallas_call | solution.py:268
  381.7 7.5 %attn_bwd.7 = (bf16[4,3,512,1024]{3,2,1,0:T(8,128)(2,1)}, bf16[512,192]{1,0:T(8,128)(2,1)}, bf16[1024,384]{1,0:T(8,128)(2,1)}) custom-call(s32[3]{0:T(128)} %pad_add_fusion.ids, bf16[512,192]{1,0:T(8,128)(2,1)} %get-tuple-element.91.refs_0_, bf16[3,512,1024]{2,1,0:T(8,128)(2,1)} %get-tuple-element.121.refs_1_, ...), custom_call_target="tpu_custom_call", output_to_operand_aliasing={{0}: (8, {})} | custom-call | flops 2415919104 | bytes 9437184 | tf_op jit(solution)/shard_map/attn_bwd/pallas_call | solution.py:268
  404.7 9.9 %collective-permute-start.86 = (f32[8,768]{1,0:T(8,128)S(1)}, f32[8,768]{1,0:T(8,128)S(1)}, u32[]{:S(2)}, u32[]{:S(2)}) collective-permute-start(f32[8,768]{1,0:T(8,128)S(1)} %add.199), channel_id=1, source_target_pairs={{0,4},{4,0},{1,5},{5,1},{2,6},{6,2},{3,7},{7,3},{8,12},{12,8},{9,1... | collective-permute-start | bytes 73736 | tf_op jit(solution)/shard_map/ppermute | solution.py:664
  414.6 13.5 %collective-permute-done.52.refs_3_ = bf16[512,384]{1,0:T(8,128)(2,1)S(1)} collective-permute-done((bf16[512,384]{1,0:T(8,128)(2,1)S(1)}, bf16[512,384]{1,0:T(8,128)(2,1)S(1)}, u32[]{:S(2)}, u32[]{:S(2)}) %collective-permute-start.52) | collective-permute-done | bytes 393248 | tf_op jit(solution)/shard_map/ppermute | solution.py:790
  428.9 7.0 %dx.4 = (bf16[512,768]{1,0:T(8,128)(2,1)}, f32[8,640]{1,0:T(8,128)}, f32[768,640]{1,0:T(8,128)}) custom-call(s32[3]{0:T(128)} %pad_add_fusion.ids, bf16[4,512,768]{2,1,0:T(8,128)(2,1)} %refs_0_.15, bf16[512,192]{1,0:T(8,128)(2,1)} %get-tuple-element.138.refs_1_, bf16[512,384]{1,0:T(8,128)(2,1)} %get-tuple-element.177.refs_2_, bf16[512,384]{1,0:T(8,128)(2,1)} %copy-done.28, ...), custom_call_target="tpu_custom_call" | custom-call | flops 1006632960 | bytes 3932160 | tf_op jit(solution)/shard_map/dx/pallas_call | solution.py:562
  436.4 7.3 %dx.5 = (bf16[512,768]{1,0:T(8,128)(2,1)}, f32[8,640]{1,0:T(8,128)}, f32[768,640]{1,0:T(8,128)}) custom-call(s32[3]{0:T(128)} %pad_add_fusion.ids, bf16[4,512,768]{2,1,0:T(8,128)(2,1)} %refs_0_.15, bf16[512,192]{1,0:T(8,128)(2,1)} %get-tuple-element.136.refs_1_, bf16[512,384]{1,0:T(8,128)(2,1)} %get-tuple-element.179.refs_2_, ...), custom_call_target="tpu_custom_call", output_to_operand_aliasing={{2}: (9, {})} | custom-call | flops 1006632960 | bytes 3932160 | tf_op jit(solution)/shard_map/dx/pallas_call | solution.py:562
  443.7 7.3 %dx.6 = (bf16[512,768]{1,0:T(8,128)(2,1)}, f32[8,640]{1,0:T(8,128)}, f32[768,640]{1,0:T(8,128)}) custom-call(s32[3]{0:T(128)} %pad_add_fusion.ids, bf16[4,512,768]{2,1,0:T(8,128)(2,1)} %refs_0_.15, bf16[512,192]{1,0:T(8,128)(2,1)} %get-tuple-element.134.refs_1_, bf16[512,384]{1,0:T(8,128)(2,1)} %get-tuple-element.181.refs_2_, ...), custom_call_target="tpu_custom_call", output_to_operand_aliasing={{2}: (9, {})} | custom-call | flops 1006632960 | bytes 3932160 | tf_op jit(solution)/shard_map/dx/pallas_call | solution.py:562
  451.7 7.2 %dx.7 = (bf16[512,768]{1,0:T(8,128)(2,1)}, f32[8,640]{1,0:T(8,128)}, f32[768,640]{1,0:T(8,128)}) custom-call(s32[3]{0:T(128)} %pad_add_fusion.ids, bf16[4,512,768]{2,1,0:T(8,128)(2,1)} %refs_0_.15, bf16[512,192]{1,0:T(8,128)(2,1)} %get-tuple-element.132.refs_1_, bf16[512,384]{1,0:T(8,128)(2,1)} %get-tuple-element.183.refs_2_, ...), custom_call_target="tpu_custom_call", output_to_operand_aliasing={{2}: (9, {})} | custom-call | flops 1006632960 | bytes 3932160 | tf_op jit(solution)/shard_map/dx/pallas_call | solution.py:562
  465.5 14.4 %collective-permute-done.82 = f32[640]{0:T(1024)S(1)} collective-permute-done((f32[640]{0:T(1024)S(1)}, f32[640]{0:T(1024)S(1)}, u32[]{:S(2)}, u32[]{:S(2)}) %collective-permute-start.82) | collective-permute-done | bytes 2592 | tf_op jit(solution)/shard_map/ppermute | solution.py:681
  494.6 7.3 %collective-permute-done.53 = bf16[512,768]{1,0:T(8,128)(2,1)S(1)} collective-permute-done((bf16[512,768]{1,0:T(8,128)(2,1)}, bf16[512,768]{1,0:T(8,128)(2,1)S(1)}, u32[]{:S(2)}, u32[]{:S(2)}) %collective-permute-start.53) | collective-permute-done | bytes 786464 | tf_op jit(solution)/shard_map/ppermute | solution.py:652
  502.1 16.5 %collective-permute-done.58 = bf16[512,768]{1,0:T(8,128)(2,1)S(1)} collective-permute-done((bf16[512,768]{1,0:T(8,128)(2,1)S(1)}, bf16[512,768]{1,0:T(8,128)(2,1)S(1)}, u32[]{:S(2)}, u32[]{:S(2)}) %collective-permute-start.58) | collective-permute-done | bytes 786464 | tf_op jit(solution)/shard_map/ppermute | solution.py:652
  520.9 14.6 %collective-permute-done.63 = bf16[512,768]{1,0:T(8,128)(2,1)S(1)} collective-permute-done((bf16[512,768]{1,0:T(8,128)(2,1)S(1)}, bf16[512,768]{1,0:T(8,128)(2,1)S(1)}, u32[]{:S(2)}, u32[]{:S(2)}) %collective-permute-start.63) | collective-permute-done | bytes 786464 | tf_op jit(solution)/shard_map/ppermute | solution.py:652
  536.4 13.7 %collective-permute-done.68 = bf16[512,768]{1,0:T(8,128)(2,1)S(1)} collective-permute-done((bf16[512,768]{1,0:T(8,128)(2,1)S(1)}, bf16[512,768]{1,0:T(8,128)(2,1)S(1)}, u32[]{:S(2)}, u32[]{:S(2)}) %collective-permute-start.68) | collective-permute-done | bytes 786464 | tf_op jit(solution)/shard_map/ppermute | solution.py:652
  565.3 27.6 %collective-permute-done.66.s3_ref = bf16[256,768]{1,0:T(8,128)(2,1)S(1)} collective-permute-done((bf16[256,768]{1,0:T(8,128)(2,1)S(1)}, bf16[256,768]{1,0:T(8,128)(2,1)S(1)}, u32[]{:S(2)}, u32[]{:S(2)}) %collective-permute-start.66) | collective-permute-done | bytes 393248 | tf_op jit(solution)/shard_map/ppermute | solution.py:658
  595.7 14.3 %collective-permute-done.71.s3_ref = bf16[256,768]{1,0:T(8,128)(2,1)S(1)} collective-permute-done((bf16[256,768]{1,0:T(8,128)(2,1)S(1)}, bf16[256,768]{1,0:T(8,128)(2,1)S(1)}, u32[]{:S(2)}, u32[]{:S(2)}) %collective-permute-start.71) | collective-permute-done | bytes 393248 | tf_op jit(solution)/shard_map/ppermute | solution.py:658
  612.6 7.4 %collective-permute-done.72.r4_ref = bf16[256,768]{1,0:T(8,128)(2,1)S(1)} collective-permute-done((bf16[256,768]{1,0:T(8,128)(2,1)S(1)}, bf16[256,768]{1,0:T(8,128)(2,1)S(1)}, u32[]{:S(2)}, u32[]{:S(2)}) %collective-permute-start.72) | collective-permute-done | bytes 393248 | tf_op jit(solution)/shard_map/ppermute | solution.py:659
  624.0 3.9 final.4.refs_0_
  627.8 30.2 %collective-permute-done.67.r4_ref = bf16[256,768]{1,0:T(8,128)(2,1)} collective-permute-done((bf16[256,768]{1,0:T(8,128)(2,1)}, bf16[256,768]{1,0:T(8,128)(2,1)}, u32[]{:S(2)}, u32[]{:S(2)}) %collective-permute-start.67) | collective-permute-done | bytes 393248 | tf_op jit(solution)/shard_map/ppermute | solution.py:659
  658.0 3.9 final.5.refs_0_
  661.9 3.9 final.6.refs_0_
  665.8 3.9 final.7
  (350 shorter events, 151.8 us)
Async XLA Ops:
  1.8 37.8 %collective-permute-start.1 = (bf16[192,640]{1,0:T(8,128)(2,1)S(1)}, bf16[192,640]{1,0:T(8,128)(2,1)S(1)}, u32[]{:S(2)}, u32[]{:S(2)}) collective-permute-start(bf16[192,640]{1,0:T(8,128)(2,1)S(1)} %pad_maximum_fusion.1.w0.refs_4_), channel_id=1, source_target_pairs={{0,16},{16,0},{8,24},{24,8},{1,17},{17,1},{9,25},{25,9},{2,18},{18... | collective-permute-start | bytes 737288 | tf_op jit(solution)/shard_map/ppermute | solution.py:645
  9.9 48.4 %collective-permute-start.24 = (bf16[192,1728]{1,0:T(8,128)(2,1)}, bf16[192,1728]{1,0:T(8,128)(2,1)}, u32[]{:S(2)}, u32[]{:S(2)}) collective-permute-start(bf16[192,1728]{1,0:T(8,128)(2,1)} %constant_dynamic-update-slice_fusion.refs_8_), channel_id=1, source_target_pairs={{1,2},{2,1},{5,6},{6,5},{9,10},{10,9},{13,14},{14,13},{17,18},{18,... | collective-permute-start | bytes 1990664 | tf_op jit(solution)/shard_map/ppermute | solution.py:637
  11.4 48.2 %collective-permute-start.20 = (bf16[192,1728]{1,0:T(8,128)(2,1)}, bf16[192,1728]{1,0:T(8,128)(2,1)}, u32[]{:S(2)}, u32[]{:S(2)}) collective-permute-start(bf16[192,1728]{1,0:T(8,128)(2,1)} %constant_dynamic-update-slice_fusion.refs_8_), channel_id=1, source_target_pairs={{0,1},{1,0},{2,3},{3,2},{4,5},{5,4},{6,7},{7,6},{8,9},{9,8},{10,11... | collective-permute-start | bytes 1990664 | tf_op jit(solution)/shard_map/ppermute | solution.py:636
  15.0 26.1 %collective-permute-start = (bf16[192,640]{1,0:T(8,128)(2,1)S(1)}, bf16[192,640]{1,0:T(8,128)(2,1)S(1)}, u32[]{:S(2)}, u32[]{:S(2)}) collective-permute-start(bf16[192,640]{1,0:T(8,128)(2,1)S(1)} %pad_maximum_fusion.1.w0.refs_4_), channel_id=1, source_target_pairs={{0,8},{8,0},{16,24},{24,16},{1,9},{9,1},{17,25},{25,17},{2,10},{10... | collective-permute-start | bytes 737288 | tf_op jit(solution)/shard_map/ppermute | solution.py:646
  39.1 26.7 %collective-permute-start.18 = (bf16[192,1728]{1,0:T(8,128)(2,1)}, bf16[192,1728]{1,0:T(8,128)(2,1)}, u32[]{:S(2)}, u32[]{:S(2)}) collective-permute-start(bf16[192,1728]{1,0:T(8,128)(2,1)} %constant_dynamic-update-slice_fusion.refs_8_), channel_id=1, source_target_pairs={{0,16},{16,0},{8,24},{24,8},{1,17},{17,1},{9,25},{25,9},{2,18},{18... | collective-permute-start | bytes 1990664 | tf_op jit(solution)/shard_map/ppermute | solution.py:645
  41.1 39.4 %collective-permute-start.17 = (bf16[192,1728]{1,0:T(8,128)(2,1)}, bf16[192,1728]{1,0:T(8,128)(2,1)}, u32[]{:S(2)}, u32[]{:S(2)}) collective-permute-start(bf16[192,1728]{1,0:T(8,128)(2,1)} %constant_dynamic-update-slice_fusion.refs_8_), channel_id=1, source_target_pairs={{0,8},{8,0},{16,24},{24,16},{1,9},{9,1},{17,25},{25,17},{2,10},{10... | collective-permute-start | bytes 1990664 | tf_op jit(solution)/shard_map/ppermute | solution.py:646
  49.5 22.4 %collective-permute-start.6 = (bf16[512,384]{1,0:T(8,128)(2,1)}, bf16[512,384]{1,0:T(8,128)(2,1)}, u32[]{:S(2)}, u32[]{:S(2)}) collective-permute-start(bf16[512,384]{1,0:T(8,128)(2,1)} %get-tuple-element.98.refs_3_.refs_6_), channel_id=1, source_target_pairs={{0,4},{1,5},{2,6},{3,7},{8,12},{9,13},{10,14},{11,15},{16,20},{17,... | collective-permute-start | bytes 1179656 | tf_op jit(solution)/shard_map/ppermute | solution.py:741
  58.3 23.9 %collective-permute-start.5 = (bf16[512,384]{1,0:T(8,128)(2,1)}, bf16[512,384]{1,0:T(8,128)(2,1)S(1)}, u32[]{:S(2)}, u32[]{:S(2)}) collective-permute-start(bf16[512,384]{1,0:T(8,128)(2,1)} %get-tuple-element.96.refs_3_.refs_6_), channel_id=1, source_target_pairs={{0,4},{1,5},{2,6},{3,7},{8,12},{9,13},{10,14},{11,15},{16,20},{17,... | collective-permute-start | bytes 1179656 | tf_op jit(solution)/shard_map/ppermute | solution.py:741
  59.6 50.7 %collective-permute-start.29 = (bf16[192,1728]{1,0:T(8,128)(2,1)}, bf16[192,1728]{1,0:T(8,128)(2,1)}, u32[]{:S(2)}, u32[]{:S(2)}) collective-permute-start(bf16[192,1728]{1,0:T(8,128)(2,1)} %collective-permute-done.20.refs_12_), channel_id=1, source_target_pairs={{1,2},{2,1},{5,6},{6,5},{9,10},{10,9},{13,14},{14,13},{17,18},{18,... | collective-permute-start | bytes 1990664 | tf_op jit(solution)/shard_map/ppermute | solution.py:638
  65.8 29.5 %collective-permute-start.4 = (bf16[512,384]{1,0:T(8,128)(2,1)}, bf16[512,384]{1,0:T(8,128)(2,1)S(1)}, u32[]{:S(2)}, u32[]{:S(2)}) collective-permute-start(bf16[512,384]{1,0:T(8,128)(2,1)} %get-tuple-element.94.refs_3_.refs_6_), channel_id=1, source_target_pairs={{0,4},{1,5},{2,6},{3,7},{8,12},{9,13},{10,14},{11,15},{16,20},{17,... | collective-permute-start | bytes 1179656 | tf_op jit(solution)/shard_map/ppermute | solution.py:741
  71.8 31.5 %collective-permute-start.3 = (bf16[512,384]{1,0:T(8,128)(2,1)}, bf16[512,384]{1,0:T(8,128)(2,1)}, u32[]{:S(2)}, u32[]{:S(2)}) collective-permute-start(bf16[512,384]{1,0:T(8,128)(2,1)} %get-tuple-element.92.refs_3_.refs_6_), channel_id=1, source_target_pairs={{0,4},{1,5},{2,6},{3,7},{8,12},{9,13},{10,14},{11,15},{16,20},{17,... | collective-permute-start | bytes 1179656 | tf_op jit(solution)/shard_map/ppermute | solution.py:741
  80.5 25.7 %collective-permute-start.45 = (bf16[512,192]{1,0:T(8,128)(2,1)}, bf16[512,192]{1,0:T(8,128)(2,1)}, u32[]{:S(2)}, u32[]{:S(2)}) collective-permute-start(bf16[512,192]{1,0:T(8,128)(2,1)} %get-tuple-element.105.refs_1_.refs_4_), channel_id=1, source_target_pairs={{1,2},{2,1},{5,6},{6,5},{9,10},{10,9},{13,14},{14,13},{17,18},{18,... | collective-permute-start | bytes 589832 | tf_op jit(solution)/shard_map/ppermute | solution.py:637
  82.2 24.7 %collective-permute-start.44 = (bf16[512,192]{1,0:T(8,128)(2,1)}, bf16[512,192]{1,0:T(8,128)(2,1)}, u32[]{:S(2)}, u32[]{:S(2)}) collective-permute-start(bf16[512,192]{1,0:T(8,128)(2,1)} %get-tuple-element.105.refs_1_.refs_4_), channel_id=1, source_target_pairs={{0,1},{1,0},{2,3},{3,2},{4,5},{5,4},{6,7},{7,6},{8,9},{9,8},{10,11... | collective-permute-start | bytes 589832 | tf_op jit(solution)/shard_map/ppermute | solution.py:636
  106.9 18.9 %collective-permute-start.34 = (bf16[512,192]{1,0:T(8,128)(2,1)}, bf16[512,192]{1,0:T(8,128)(2,1)}, u32[]{:S(2)}, u32[]{:S(2)}) collective-permute-start(bf16[512,192]{1,0:T(8,128)(2,1)} %get-tuple-element.103.refs_1_.refs_4_), channel_id=1, source_target_pairs={{0,1},{1,0},{2,3},{3,2},{4,5},{5,4},{6,7},{7,6},{8,9},{9,8},{10,11... | collective-permute-start | bytes 589832 | tf_op jit(solution)/shard_map/ppermute | solution.py:636
  109.0 61.0 %collective-permute-start.25 = (bf16[192,1728]{1,0:T(8,128)(2,1)}, bf16[192,1728]{1,0:T(8,128)(2,1)S(1)}, u32[]{:S(2)}, u32[]{:S(2)}) collective-permute-start(bf16[192,1728]{1,0:T(8,128)(2,1)} %collective-permute-done.24), channel_id=1, source_target_pairs={{1,0},{2,3},{5,4},{6,7},{9,8},{10,11},{13,12},{14,15},{17,16},{18,... | collective-permute-start | bytes 1990664 | tf_op jit(solution)/shard_map/ppermute | solution.py:639
  110.3 61.0 %collective-permute-start.30 = (bf16[192,1728]{1,0:T(8,128)(2,1)}, bf16[192,1728]{1,0:T(8,128)(2,1)}, u32[]{:S(2)}, u32[]{:S(2)}) collective-permute-start(bf16[192,1728]{1,0:T(8,128)(2,1)} %collective-permute-done.29), channel_id=1, source_target_pairs={{1,0},{2,3},{5,4},{6,7},{9,8},{10,11},{13,12},{14,15},{17,16},{18,... | collective-permute-start | bytes 1990664 | tf_op jit(solution)/shard_map/ppermute | solution.py:640
  119.7 34.7 %collective-permute-start.7 = (bf16[512,192]{1,0:T(8,128)(2,1)}, bf16[512,192]{1,0:T(8,128)(2,1)S(1)}, u32[]{:S(2)}, u32[]{:S(2)}) collective-permute-start(bf16[512,192]{1,0:T(8,128)(2,1)} %get-tuple-element.102.refs_1_.refs_4_), channel_id=1, source_target_pairs={{0,1},{1,0},{2,3},{3,2},{4,5},{5,4},{6,7},{7,6},{8,9},{9,8},{10,11... | collective-permute-start | bytes 589832 | tf_op jit(solution)/shard_map/ppermute | solution.py:636
  125.8 34.2 %collective-permute-start.46 = (bf16[512,192]{1,0:T(8,128)(2,1)}, bf16[512,192]{1,0:T(8,128)(2,1)S(1)}, u32[]{:S(2)}, u32[]{:S(2)}) collective-permute-start(bf16[512,192]{1,0:T(8,128)(2,1)} %collective-permute-done.45), channel_id=1, source_target_pairs={{1,0},{2,3},{5,4},{6,7},{9,8},{10,11},{13,12},{14,15},{17,16},{18,... | collective-permute-start | bytes 589832 | tf_op jit(solution)/shard_map/ppermute | solution.py:639
  127.1 33.6 %collective-permute-start.47 = (bf16[512,192]{1,0:T(8,128)(2,1)}, bf16[512,192]{1,0:T(8,128)(2,1)S(1)}, u32[]{:S(2)}, u32[]{:S(2)}) collective-permute-start(bf16[512,192]{1,0:T(8,128)(2,1)} %collective-permute-done.44.refs_2_), channel_id=1, source_target_pairs={{1,2},{2,1},{5,6},{6,5},{9,10},{10,9},{13,14},{14,13},{17,18},{18,... | collective-permute-start | bytes 589832 | tf_op jit(solution)/shard_map/ppermute | solution.py:638
  182.1 29.4 %collective-permute-start.27 = (bf16[192,1728]{1,0:T(8,128)(2,1)S(1)}, bf16[192,1728]{1,0:T(8,128)(2,1)}, u32[]{:S(2)}, u32[]{:S(2)}) collective-permute-start(bf16[192,1728]{1,0:T(8,128)(2,1)S(1)} %add.160.refs_16_), channel_id=1, source_target_pairs={{0,16},{16,0},{8,24},{24,8},{1,17},{17,1},{9,25},{25,9},{2,18},{18... | collective-permute-start | bytes 1990664 | tf_op jit(solution)/shard_map/ppermute | solution.py:645
  183.6 30.6 %collective-permute-start.32 = (bf16[192,1728]{1,0:T(8,128)(2,1)S(1)}, bf16[192,1728]{1,0:T(8,128)(2,1)}, u32[]{:S(2)}, u32[]{:S(2)}) collective-permute-start(bf16[192,1728]{1,0:T(8,128)(2,1)S(1)} %add.161.refs_20_), channel_id=1, source_target_pairs={{0,16},{16,0},{8,24},{24,8},{1,17},{17,1},{9,25},{25,9},{2,18},{18... | collective-permute-start | bytes 1990664 | tf_op jit(solution)/shard_map/ppermute | solution.py:645
  186.8 20.2 %collective-permute-start.38 = (bf16[512,192]{1,0:T(8,128)(2,1)S(1)}, bf16[512,192]{1,0:T(8,128)(2,1)S(1)}, u32[]{:S(2)}, u32[]{:S(2)}) collective-permute-start(bf16[512,192]{1,0:T(8,128)(2,1)S(1)} %collective-permute-done.37), channel_id=1, source_target_pairs={{1,0},{2,3},{5,4},{6,7},{9,8},{10,11},{13,12},{14,15},{17,16},{18,... | collective-permute-start | bytes 589832 | tf_op jit(solution)/shard_map/ppermute | solution.py:640
  201.4 24.2 %collective-permute-start.26 = (bf16[192,1728]{1,0:T(8,128)(2,1)S(1)}, bf16[192,1728]{1,0:T(8,128)(2,1)}, u32[]{:S(2)}, u32[]{:S(2)}) collective-permute-start(bf16[192,1728]{1,0:T(8,128)(2,1)S(1)} %add.160.refs_16_), channel_id=1, source_target_pairs={{0,8},{8,0},{16,24},{24,16},{1,9},{9,1},{17,25},{25,17},{2,10},{10... | collective-permute-start | bytes 1990664 | tf_op jit(solution)/shard_map/ppermute | solution.py:646
  352.9 47.9 %collective-permute-start.84 = (f32[8,768]{1,0:T(8,128)S(1)}, f32[8,768]{1,0:T(8,128)S(1)}, u32[]{:S(2)}, u32[]{:S(2)}) collective-permute-start(f32[8,768]{1,0:T(8,128)S(1)} %add_add_fusion), channel_id=1, source_target_pairs={{0,8},{8,0},{16,24},{24,16},{1,9},{9,1},{17,25},{25,17},{2,10},{10... | collective-permute-start | bytes 73736 | tf_op jit(solution)/shard_map/ppermute | solution.py:680
  391.4 59.5 %collective-permute-start.49 = (bf16[512,384]{1,0:T(8,128)(2,1)}, bf16[512,384]{1,0:T(8,128)(2,1)S(1)}, u32[]{:S(2)}, u32[]{:S(2)}) collective-permute-start(bf16[512,384]{1,0:T(8,128)(2,1)} %get-tuple-element.182), channel_id=1, source_target_pairs={{4,0},{5,1},{6,2},{7,3},{12,8},{13,9},{14,10},{15,11},{20,16},{21,... | collective-permute-start | bytes 1179656 | tf_op jit(solution)/shard_map/ppermute | solution.py:790
  394.9 48.7 %collective-permute-start.50 = (bf16[512,384]{1,0:T(8,128)(2,1)}, bf16[512,384]{1,0:T(8,128)(2,1)}, u32[]{:S(2)}, u32[]{:S(2)}) collective-permute-start(bf16[512,384]{1,0:T(8,128)(2,1)} %get-tuple-element.180), channel_id=1, source_target_pairs={{4,0},{5,1},{6,2},{7,3},{12,8},{13,9},{14,10},{15,11},{20,16},{21,... | collective-permute-start | bytes 1179656 | tf_op jit(solution)/shard_map/ppermute | solution.py:790
  397.1 31.1 %collective-permute-start.52 = (bf16[512,384]{1,0:T(8,128)(2,1)S(1)}, bf16[512,384]{1,0:T(8,128)(2,1)S(1)}, u32[]{:S(2)}, u32[]{:S(2)}) collective-permute-start(bf16[512,384]{1,0:T(8,128)(2,1)S(1)} %get-tuple-element.176), channel_id=1, source_target_pairs={{4,0},{5,1},{6,2},{7,3},{12,8},{13,9},{14,10},{15,11},{20,16},{21,... | collective-permute-start | bytes 1179656 | tf_op jit(solution)/shard_map/ppermute | solution.py:790
  399.5 36.8 %collective-permute-start.51 = (bf16[512,384]{1,0:T(8,128)(2,1)}, bf16[512,384]{1,0:T(8,128)(2,1)}, u32[]{:S(2)}, u32[]{:S(2)}) collective-permute-start(bf16[512,384]{1,0:T(8,128)(2,1)} %get-tuple-element.178), channel_id=1, source_target_pairs={{4,0},{5,1},{6,2},{7,3},{12,8},{13,9},{14,10},{15,11},{20,16},{21,... | collective-permute-start | bytes 1179656 | tf_op jit(solution)/shard_map/ppermute | solution.py:790
  404.7 58.4 %collective-permute-start.86 = (f32[8,768]{1,0:T(8,128)S(1)}, f32[8,768]{1,0:T(8,128)S(1)}, u32[]{:S(2)}, u32[]{:S(2)}) collective-permute-start(f32[8,768]{1,0:T(8,128)S(1)} %add.199), channel_id=1, source_target_pairs={{0,4},{4,0},{1,5},{5,1},{2,6},{6,2},{3,7},{7,3},{8,12},{12,8},{9,1... | collective-permute-start | bytes 73736 | tf_op jit(solution)/shard_map/ppermute | solution.py:664
  461.5 29.9 %collective-permute-start.78 = (bf16[192,1728]{1,0:T(8,128)(2,1)S(1)}, bf16[192,1728]{1,0:T(8,128)(2,1)S(1)}, u32[]{:S(2)}, u32[]{:S(2)}) collective-permute-start(bf16[192,1728]{1,0:T(8,128)(2,1)S(1)} %get-tuple-element.171), channel_id=1, source_target_pairs={{0,16},{16,0},{8,24},{24,8},{1,17},{17,1},{9,25},{25,9},{2,18},{18... | collective-permute-start | bytes 1990664 | tf_op jit(solution)/shard_map/ppermute | solution.py:673
  463.9 21.8 %collective-permute-start.74 = (bf16[192,640]{1,0:T(8,128)(2,1)S(1)}, bf16[192,640]{1,0:T(8,128)(2,1)S(1)}, u32[]{:S(2)}, u32[]{:S(2)}) collective-permute-start(bf16[192,640]{1,0:T(8,128)(2,1)S(1)} %get-tuple-element.175), channel_id=1, source_target_pairs={{0,16},{16,0},{8,24},{24,8},{1,17},{17,1},{9,25},{25,9},{2,18},{18... | collective-permute-start | bytes 737288 | tf_op jit(solution)/shard_map/ppermute | solution.py:673
  482.1 19.7 %collective-permute-start.53 = (bf16[512,768]{1,0:T(8,128)(2,1)}, bf16[512,768]{1,0:T(8,128)(2,1)S(1)}, u32[]{:S(2)}, u32[]{:S(2)}) collective-permute-start(bf16[512,768]{1,0:T(8,128)(2,1)} %get-tuple-element.143), channel_id=1, source_target_pairs={{0,1},{3,2},{4,5},{7,6},{8,9},{11,10},{12,13},{15,14},{16,17},{19,... | collective-permute-start | bytes 2359304 | tf_op jit(solution)/shard_map/ppermute | solution.py:652
  483.6 35.0 %collective-permute-start.58 = (bf16[512,768]{1,0:T(8,128)(2,1)S(1)}, bf16[512,768]{1,0:T(8,128)(2,1)S(1)}, u32[]{:S(2)}, u32[]{:S(2)}) collective-permute-start(bf16[512,768]{1,0:T(8,128)(2,1)S(1)} %copy-done.18), channel_id=1, source_target_pairs={{0,1},{3,2},{4,5},{7,6},{8,9},{11,10},{12,13},{15,14},{16,17},{19,... | collective-permute-start | bytes 2359304 | tf_op jit(solution)/shard_map/ppermute | solution.py:652
  485.7 49.8 %collective-permute-start.63 = (bf16[512,768]{1,0:T(8,128)(2,1)S(1)}, bf16[512,768]{1,0:T(8,128)(2,1)S(1)}, u32[]{:S(2)}, u32[]{:S(2)}) collective-permute-start(bf16[512,768]{1,0:T(8,128)(2,1)S(1)} %copy-done.17), channel_id=1, source_target_pairs={{0,1},{3,2},{4,5},{7,6},{8,9},{11,10},{12,13},{15,14},{16,17},{19,... | collective-permute-start | bytes 2359304 | tf_op jit(solution)/shard_map/ppermute | solution.py:652
  489.9 60.2 %collective-permute-start.68 = (bf16[512,768]{1,0:T(8,128)(2,1)S(1)}, bf16[512,768]{1,0:T(8,128)(2,1)S(1)}, u32[]{:S(2)}, u32[]{:S(2)}) collective-permute-start(bf16[512,768]{1,0:T(8,128)(2,1)S(1)} %copy-done.16), channel_id=1, source_target_pairs={{0,1},{3,2},{4,5},{7,6},{8,9},{11,10},{12,13},{15,14},{16,17},{19,... | collective-permute-start | bytes 2359304 | tf_op jit(solution)/shard_map/ppermute | solution.py:652
  493.0 61.9 %collective-permute-start.77 = (bf16[192,1728]{1,0:T(8,128)(2,1)S(1)}, bf16[192,1728]{1,0:T(8,128)(2,1)S(1)}, u32[]{:S(2)}, u32[]{:S(2)}) collective-permute-start(bf16[192,1728]{1,0:T(8,128)(2,1)S(1)} %get-tuple-element.170), channel_id=1, source_target_pairs={{0,16},{16,0},{8,24},{24,8},{1,17},{17,1},{9,25},{25,9},{2,18},{18... | collective-permute-start | bytes 1990664 | tf_op jit(solution)/shard_map/ppermute | solution.py:672
  501.9 54.5 %collective-permute-start.79 = (bf16[192,1728]{1,0:T(8,128)(2,1)S(1)}, bf16[192,1728]{1,0:T(8,128)(2,1)S(1)}, u32[]{:S(2)}, u32[]{:S(2)}) collective-permute-start(bf16[192,1728]{1,0:T(8,128)(2,1)S(1)} %bitcast_add_fusion), channel_id=1, source_target_pairs={{0,8},{8,0},{16,24},{24,16},{1,9},{9,1},{17,25},{25,17},{2,10},{10... | collective-permute-start | bytes 1990664 | tf_op jit(solution)/shard_map/ppermute | solution.py:675
  518.6 40.5 %collective-permute-start.76 = (bf16[192,640]{1,0:T(8,128)(2,1)S(1)}, bf16[192,640]{1,0:T(8,128)(2,1)S(1)}, u32[]{:S(2)}, u32[]{:S(2)}) collective-permute-start(bf16[192,640]{1,0:T(8,128)(2,1)S(1)} %fusion.1), channel_id=1, source_target_pairs={{0,4},{4,0},{1,5},{5,1},{2,6},{6,2},{3,7},{7,3},{8,12},{12,8},{9,1... | collective-permute-start | bytes 737288 | tf_op jit(solution)/shard_map/ppermute | solution.py:664
  557.2 54.1 %collective-permute-start.80 = (bf16[192,1728]{1,0:T(8,128)(2,1)S(1)}, bf16[192,1728]{1,0:T(8,128)(2,1)S(1)}, u32[]{:S(2)}, u32[]{:S(2)}) collective-permute-start(bf16[192,1728]{1,0:T(8,128)(2,1)S(1)} %fusion), channel_id=1, source_target_pairs={{0,4},{4,0},{1,5},{5,1},{2,6},{6,2},{3,7},{7,3},{8,12},{12,8},{9,1... | collective-permute-start | bytes 1990664 | tf_op jit(solution)/shard_map/ppermute | solution.py:664
  559.1 33.8 %collective-permute-start.66 = (bf16[256,768]{1,0:T(8,128)(2,1)S(1)}, bf16[256,768]{1,0:T(8,128)(2,1)S(1)}, u32[]{:S(2)}, u32[]{:S(2)}) collective-permute-start(bf16[256,768]{1,0:T(8,128)(2,1)S(1)} %select_add_fusion.1.t_ref), channel_id=1, source_target_pairs={{1,0},{2,3},{5,4},{6,7},{9,8},{10,11},{13,12},{14,15},{17,16},{18,... | collective-permute-start | bytes 1179656 | tf_op jit(solution)/shard_map/ppermute | solution.py:658
  560.4 33.8 %collective-permute-start.65 = (bf16[256,768]{1,0:T(8,128)(2,1)S(1)}, bf16[256,768]{1,0:T(8,128)(2,1)}, u32[]{:S(2)}, u32[]{:S(2)}) collective-permute-start(bf16[256,768]{1,0:T(8,128)(2,1)S(1)} %select_add_fusion.1.t_ref), channel_id=1, source_target_pairs={{1,2},{2,1},{5,6},{6,5},{9,10},{10,9},{13,14},{14,13},{17,18},{18,... | collective-permute-start | bytes 1179656 | tf_op jit(solution)/shard_map/ppermute | solution.py:657
  561.8 48.2 %collective-permute-start.71 = (bf16[256,768]{1,0:T(8,128)(2,1)S(1)}, bf16[256,768]{1,0:T(8,128)(2,1)S(1)}, u32[]{:S(2)}, u32[]{:S(2)}) collective-permute-start(bf16[256,768]{1,0:T(8,128)(2,1)S(1)} %select_add_fusion.t_ref), channel_id=1, source_target_pairs={{1,0},{2,3},{5,4},{6,7},{9,8},{10,11},{13,12},{14,15},{17,16},{18,... | collective-permute-start | bytes 1179656 | tf_op jit(solution)/shard_map/ppermute | solution.py:658
  563.1 56.9 %collective-permute-start.72 = (bf16[256,768]{1,0:T(8,128)(2,1)S(1)}, bf16[256,768]{1,0:T(8,128)(2,1)S(1)}, u32[]{:S(2)}, u32[]{:S(2)}) collective-permute-start(bf16[256,768]{1,0:T(8,128)(2,1)S(1)} %collective-permute-done.70.r3_ref), channel_id=1, source_target_pairs={{1,0},{2,3},{5,4},{6,7},{9,8},{10,11},{13,12},{14,15},{17,16},{18,... | collective-permute-start | bytes 1179656 | tf_op jit(solution)/shard_map/ppermute | solution.py:659
  592.9 72.9 %collective-permute-start.56 = (bf16[256,768]{1,0:T(8,128)(2,1)S(1)}, bf16[256,768]{1,0:T(8,128)(2,1)}, u32[]{:S(2)}, u32[]{:S(2)}) collective-permute-start(bf16[256,768]{1,0:T(8,128)(2,1)S(1)} %select_add_fusion.3.t_ref), channel_id=1, source_target_pairs={{1,0},{2,3},{5,4},{6,7},{9,8},{10,11},{13,12},{14,15},{17,16},{18,... | collective-permute-start | bytes 1179656 | tf_op jit(solution)/shard_map/ppermute | solution.py:658
  594.2 67.7 %collective-permute-start.61 = (bf16[256,768]{1,0:T(8,128)(2,1)}, bf16[256,768]{1,0:T(8,128)(2,1)}, u32[]{:S(2)}, u32[]{:S(2)}) collective-permute-start(bf16[256,768]{1,0:T(8,128)(2,1)} %select_add_fusion.2.t_ref), channel_id=1, source_target_pairs={{1,0},{2,3},{5,4},{6,7},{9,8},{10,11},{13,12},{14,15},{17,16},{18,... | collective-permute-start | bytes 1179656 | tf_op jit(solution)/shard_map/ppermute | solution.py:658
  610.0 55.8 %collective-permute-start.57 = (bf16[256,768]{1,0:T(8,128)(2,1)}, bf16[256,768]{1,0:T(8,128)(2,1)}, u32[]{:S(2)}, u32[]{:S(2)}) collective-permute-start(bf16[256,768]{1,0:T(8,128)(2,1)} %collective-permute-done.55.r3_ref), channel_id=1, source_target_pairs={{1,0},{2,3},{5,4},{6,7},{9,8},{10,11},{13,12},{14,15},{17,16},{18,... | collective-permute-start | bytes 1179656 | tf_op jit(solution)/shard_map/ppermute | solution.py:659
  611.3 50.6 %collective-permute-start.62 = (bf16[256,768]{1,0:T(8,128)(2,1)}, bf16[256,768]{1,0:T(8,128)(2,1)}, u32[]{:S(2)}, u32[]{:S(2)}) collective-permute-start(bf16[256,768]{1,0:T(8,128)(2,1)} %collective-permute-done.60.r3_ref), channel_id=1, source_target_pairs={{1,0},{2,3},{5,4},{6,7},{9,8},{10,11},{13,12},{14,15},{17,16},{18,... | collective-permute-start | bytes 1179656 | tf_op jit(solution)/shard_map/ppermute | solution.py:659
  620.8 37.3 %collective-permute-start.67 = (bf16[256,768]{1,0:T(8,128)(2,1)}, bf16[256,768]{1,0:T(8,128)(2,1)}, u32[]{:S(2)}, u32[]{:S(2)}) collective-permute-start(bf16[256,768]{1,0:T(8,128)(2,1)} %collective-permute-done.65.r3_ref), channel_id=1, source_target_pairs={{1,0},{2,3},{5,4},{6,7},{9,8},{10,11},{13,12},{14,15},{17,16},{18,... | collective-permute-start | bytes 1179656 | tf_op jit(solution)/shard_map/ppermute | solution.py:659
  (99 other events, 2295.3 us)

commit v2 on v1

v2 whole, which is shorter than its diff:
```python
import functools

import jax
import jax.numpy as jnp
from jax import lax
from jax.experimental import pallas as pl
from jax.experimental.pallas import tpu as pltpu
from jax.sharding import PartitionSpec as P

BLOCK = 256
EPS = 1e-6
BF = jnp.bfloat16
F32 = jnp.float32
VMEM_LIMIT = 63 * 1024 * 1024
ANY = pl.BlockSpec(memory_space=pl.ANY)

SWAP = ((0, 1), (1, 0), (2, 3), (3, 2))
FAR = ((0, 2), (2, 0), (1, 3), (3, 1))
ACROSS = ((0, 3), (3, 0), (1, 2), (2, 1))


def params(**kw):
    return pltpu.CompilerParams(vmem_limit_bytes=VMEM_LIMIT, **kw)


def dot(left, right):
    return jnp.dot(left, right, preferred_element_type=F32)


def dot_nt(left, right):
    return lax.dot_general(left, right, (((1,), (1,)), ((), ())), preferred_element_type=F32)


def gelu_parts(u):
    cdf = 0.5 + 0.5 * lax.erf(u * 0.5**0.5)
    density = jnp.exp(-0.5 * (u * u)) * 0.3989422804014327
    return u * cdf, cdf + u * density


def head_mask(value, offset, head, size):
    lane = lax.broadcasted_iota(jnp.int32, value.shape, 1)
    keep = (lane >= offset + head * size) & (lane < offset + (head + 1) * size)
    return jnp.where(keep, value, jnp.zeros_like(value))


def load_rows(ids, pieces, scratch, sems):
    f = ids[0]
    rows = pieces[0].shape[0]
    copies = []
    for k, piece in enumerate(pieces):
        at = pl.multiple_of((f ^ k) * rows, rows)
        copies.append(pltpu.make_async_copy(piece, scratch.at[pl.ds(at, rows)], sems.at[k]))
    return copies


def qkv_kernel(ids, x_ref, w0, w1, w2, w3, b_ref, *refs, scale):
    q_ref, kv_ref, w_ref, sems = refs[-4:]

    @pl.when((pl.program_id(0) == 0) & (pl.program_id(1) == 0))
    def _():
        copies = load_rows(ids, (w0, w1, w2, w3), w_ref, sems)
        for c in copies:
            c.start()
        for c in copies:
            c.wait()

    width = q_ref.shape[1]
    out = dot(x_ref[0], w_ref[...]) + b_ref[...]
    query = out[:, :width].astype(BF)
    q_ref[...] = (query.astype(F32) * scale).astype(BF)
    kv_ref[...] = out[:, 256:].astype(BF)


def qkv_call(ids, hidden, first, count, pieces, bias, width, scale, after):
    _, rows, d = hidden.shape
    cols = pieces[0].shape[1]
    tile = min(rows, 256)
    tiles = rows // tile
    flat = lambda i, j, s: (i * tiles + j, 0)
    fixed = lambda i, j, s: (0, 0)
    return pl.pallas_call(
        functools.partial(qkv_kernel, scale=scale),
        out_shape=(
            jax.ShapeDtypeStruct((count * rows, width), BF),
            jax.ShapeDtypeStruct((count * rows, 2 * width), BF),
            jax.ShapeDtypeStruct((d, cols), BF),
        ),
        grid_spec=pltpu.PrefetchScalarGridSpec(
            num_scalar_prefetch=1,
            grid=(count, tiles),
            in_specs=[pl.BlockSpec((1, tile, d), lambda i, j, s: (first + i, j, 0))]
            + [ANY] * 4
            + [pl.BlockSpec((1, cols), fixed)]
            + [ANY] * len(after),
            out_specs=[
                pl.BlockSpec((tile, width), flat),
                pl.BlockSpec((tile, 2 * width), flat),
                pl.BlockSpec((d, cols), fixed),
            ],
            scratch_shapes=[pltpu.SemaphoreType.DMA((4,))],
        ),
        compiler_params=params(),
        cost_estimate=pl.CostEstimate(
            flops=2 * count * rows * d * cols,
            bytes_accessed=2 * (count * rows + d) * (d + cols),
            transcendentals=0,
        ),
        name="qkv",
    )(ids, hidden, *pieces, bias, *after)


FRAME = 64


def spread_heads(ids, kv_refs, k3, v3, heads, size):
    width = heads * size
    if len(kv_refs) == 2:
        low, own = kv_refs
        rows = own.shape[0]
        own_v = own[...]
        parts = ((0, jnp.where(ids[1] == 0, own_v, low[...])), (rows, own_v))
    else:
        parts = ((0, kv_refs[0][...]),)
    for at, part in parts:
        keys, values = part[:, :width], part[:, 2 * width - 256 :]
        lane = lax.broadcasted_iota(jnp.int32, values.shape, 1)
        for h in range(heads):
            k3[h, at : at + part.shape[0], :] = head_mask(keys, 0, h, size)
            ones = (lane >= 2 * h) & (lane < 2 * h + 2)
            masked = head_mask(values, FRAME, h, size)
            v3[h, at : at + part.shape[0], :] = jnp.where(ones, jnp.ones_like(masked), masked)


def attn_fwd_kernel(ids, *refs, heads, size, nkv):
    q_ref, prev_ref = refs[0], refs[1]
    kv_refs = refs[2 : 2 + nkv]
    log_ref, e_ref, att_ref, sum_ref, k3, v3 = refs[-6:]
    i, rb = pl.program_id(0), pl.program_id(1)
    blocks = pl.num_programs(1)
    full = prev_ref.shape[3]
    width = heads * size

    @pl.when(rb == 0)
    def _():
        spread_heads(ids, kv_refs, k3, v3, heads, size)

    g = ids[1] * blocks + rb
    for b in range(full // BLOCK):
        n = (b + 1) * BLOCK

        @pl.when(g == b)
        def _(n=n):
            query = q_ref[...]
            total = None
            for h in range(heads):
                s = dot_nt(query, k3[h, :n, :]) + prev_ref[0, h, :, :n].astype(F32)
                log_ref[0, h, :, :n] = s.astype(BF)
                if n < full:
                    log_ref[0, h, :, n:] = jnp.zeros((BLOCK, full - n), BF)
                e = jnp.exp(s - jnp.max(s, axis=1, keepdims=True)).astype(BF)
                e_ref[0, h, :, :n] = e
                part = dot(e, v3[h, :n, :])
                total = part if total is None else total + part
            inverse = 1.0 / total[:, : 2 * heads]
            sum_ref[...] = jnp.concatenate(
                [inverse, jnp.zeros((BLOCK, 128 - 2 * heads), F32)], axis=1
            )
            lane = lax.broadcasted_iota(jnp.int32, total.shape, 1)
            factor = jnp.zeros_like(total)
            for h in range(heads):
                factor = jnp.where(lane // size == h + 1, inverse[:, 2 * h : 2 * h + 1], factor)
            att = (total * factor)[:, FRAME:].astype(BF)
            at = pl.ds(pl.multiple_of(rb * BLOCK, BLOCK), BLOCK)
            for k in range(att_ref.shape[1] // width):

                @pl.when(i == k)
                def _(k=k):
                    att_ref[at, k * width : (k + 1) * width] = att


def kv_specs(kvs, count):
    specs = []
    for kv in kvs:
        block = (kv.shape[0] // count, kv.shape[1])
        specs.append(pl.BlockSpec(block, lambda i, r, s: (i, 0)))
    return specs


def attn_fwd_call(ids, q, kvs, prev, first, count, chain, heads, size, after):
    seqs, _, rows, full = prev.shape
    width = heads * size
    blocks = rows // BLOCK
    big = pl.BlockSpec((1, heads, BLOCK, full), lambda i, r, s: (first + i, 0, r, 0))
    extra = ([] if chain is None else [chain]) + list(after)
    tokens = 3 * full // 4
    return pl.pallas_call(
        functools.partial(attn_fwd_kernel, heads=heads, size=size, nkv=len(kvs)),
        out_shape=(
            jax.ShapeDtypeStruct(prev.shape, BF),
            jax.ShapeDtypeStruct((count, heads, rows, full), BF),
            jax.ShapeDtypeStruct((rows, count * width), BF),
            jax.ShapeDtypeStruct((count * rows, 128), F32),
        ),
        grid_spec=pltpu.PrefetchScalarGridSpec(
            num_scalar_prefetch=1,
            grid=(count, blocks),
            in_specs=[pl.BlockSpec((BLOCK, width), lambda i, r, s: (i * blocks + r, 0)), big]
            + kv_specs(kvs, count)
            + [ANY] * len(extra),
            out_specs=[
                big,
                pl.BlockSpec((1, heads, BLOCK, full), lambda i, r, s: (i, 0, r, 0)),
                pl.BlockSpec((rows, count * width), lambda i, r, s: (0, 0)),
                pl.BlockSpec((BLOCK, 128), lambda i, r, s: (i * blocks + r, 0)),
            ],
            scratch_shapes=[
                pltpu.VMEM((heads, full, width), BF),
                pltpu.VMEM((heads, full, 256), BF),
            ],
        ),
        input_output_aliases={} if chain is None else {3 + len(kvs): 0},
        compiler_params=params(),
        cost_estimate=pl.CostEstimate(
            flops=4 * 4 * count * heads * rows * tokens * size,
            bytes_accessed=6 * count * heads * rows * full,
            transcendentals=count * heads * rows * tokens,
        ),
        name="attn_fwd",
    )(ids, q, prev, *kvs, *extra)


def attn_bwd_kernel(ids, *refs, heads, size, nkv, local, scale):
    q_ref, e_ref, dl_ref, datt_ref, att_ref, sum_ref = refs[:6]
    kv_refs = refs[6 : 6 + nkv]
    if nkv == 2:
        dprev_ref, dq_ref, own_ref, send_ref, k3, v3, dkv_t = refs[-7:]
    else:
        dprev_ref, dq_ref, own_ref, k3, v3, dkv_t = refs[-6:]
    i, rb = pl.program_id(0), pl.program_id(1)
    blocks = pl.num_programs(1)
    full = dl_ref.shape[3]
    width = heads * size

    @pl.when(rb == 0)
    def _():
        spread_heads(ids, kv_refs, k3, v3, heads, size)
        dkv_t[...] = jnp.zeros_like(dkv_t)

    g = ids[1] * blocks + rb
    for b in range(full // BLOCK):
        n = (b + 1) * BLOCK

        @pl.when(g == b)
        def _(n=n):
            datt = datt_ref[...].astype(F32)
            att = att_ref[:, local * width : (local + 1) * width]
            if att_ref.shape[1] > (local + 1) * width:
                att = jnp.where(i == 0, att, att_ref[:, (local + 1) * width :])
            weighted = datt * att.astype(F32)
            lane = lax.broadcasted_iota(jnp.int32, datt.shape, 1)
            head = lax.broadcasted_iota(jnp.int32, (BLOCK, FRAME), 1)
            factor = jnp.zeros_like(datt)
            front = jnp.zeros((BLOCK, FRAME), F32)
            for h in range(heads):
                inverse = sum_ref[:, 2 * h : 2 * h + 1]
                factor = jnp.where(lane // size == h, inverse, factor)
                delta = jnp.sum(head_mask(weighted, 0, h, size), axis=1, keepdims=True)
                delta = -delta * inverse
                high = delta.astype(BF).astype(F32)
                front = jnp.where(head == 2 * h, high, front)
                front = jnp.where(head == 2 * h + 1, delta - high, front)
            scaled = (datt * factor).astype(BF)
            framed = jnp.concatenate([front.astype(BF), scaled], axis=1)
            q_t = q_ref[...].T
            scaled_t = scaled.T
            total = None
            for h in range(heads):
                at = h * size
                dp = dot_nt(framed, v3[h, :n, :])
                e = e_ref[0, h, :, :n]
                ds = e.astype(F32) * dp + dl_ref[0, h, :, :n].astype(F32)
                low = ds.astype(BF)
                dprev_ref[0, h, :, :n] = low
                if n < full:
                    dprev_ref[0, h, :, n:] = jnp.zeros((BLOCK, full - n), BF)
                part = dot(low, k3[h, :n, :])
                total = part if total is None else total + part
                dkv_t[at : at + size, :n] += dot(q_t[at : at + size], low)
                at += width
                dkv_t[at : at + size, :n] += dot(scaled_t[at - width : at - width + size], e)
            dq_ref[...] = (total * scale).astype(BF)

    @pl.when(rb == blocks - 1)
    def _():
        if nkv == 2:
            rows = full // 2

            @pl.when(ids[1] == 0)
            def _():
                own_ref[...] = dkv_t[:, :rows].T.astype(BF)

            @pl.when(ids[1] == 1)
            def _():
                own_ref[...] = dkv_t[:, rows:].T.astype(BF)
                send_ref[...] = dkv_t[:, :rows].T.astype(BF)
        else:
            own_ref[...] = dkv_t[...].T.astype(BF)


def attn_bwd_call(
    ids, q, e, d_logits, datt, att, inverse, kvs, first, base, count, of, chain, heads, size, scale, after
):
    seqs, _, rows, full = d_logits.shape
    width = heads * size
    blocks = rows // BLOCK
    big = pl.BlockSpec((1, heads, BLOCK, full), lambda i, r, s: (first + i, 0, r, 0))
    extra = ([] if chain is None else [chain]) + list(after)
    tokens = 3 * full // 4
    tile = lambda w, k: pl.BlockSpec((BLOCK, w), lambda i, r, s: ((k + i) * blocks + r, 0))
    kv_in = []
    for kv in kvs:
        block = (kv.shape[0] // of, kv.shape[1])
        kv_in.append(pl.BlockSpec(block, lambda i, r, s: (base + i, 0)))
    grads = [(rows, rows)] if len(kvs) == 2 else [(full,)]
    sizes = grads[0]
    return pl.pallas_call(
        functools.partial(
            attn_bwd_kernel, heads=heads, size=size, nkv=len(kvs), local=base, scale=scale
        ),
        out_shape=(
            jax.ShapeDtypeStruct(d_logits.shape, BF),
            jax.ShapeDtypeStruct((count * rows, width), BF),
        )
        + tuple(jax.ShapeDtypeStruct((count * z, 2 * width), BF) for z in sizes),
        grid_spec=pltpu.PrefetchScalarGridSpec(
            num_scalar_prefetch=1,
            grid=(count, blocks),
            in_specs=[
                tile(width, base),
                pl.BlockSpec((1, heads, BLOCK, full), lambda i, r, s: (base + i, 0, r, 0)),
                big,
                tile(width, 0),
                pl.BlockSpec((BLOCK, of * width), lambda i, r, s: (r, 0)),
                tile(128, base),
            ]
            + kv_in
            + [ANY] * len(extra),
            out_specs=[big, tile(width, 0)]
            + [pl.BlockSpec((z, 2 * width), lambda i, r, s: (i, 0)) for z in sizes],
            scratch_shapes=[
                pltpu.VMEM((heads, full, width), BF),
                pltpu.VMEM((heads, full, 256), BF),
                pltpu.VMEM((2 * width, full), F32),
            ],
        ),
        input_output_aliases={} if chain is None else {7 + len(kvs): 0},
        compiler_params=params(),
        cost_estimate=pl.CostEstimate(
            flops=4 * 8 * count * heads * rows * tokens * size,
            bytes_accessed=6 * count * heads * rows * full,
            transcendentals=0,
        ),
        name="attn_bwd",
    )(ids, q, e, d_logits, datt, att, inverse, *kvs, *extra)


def row_mean(value):
    return jnp.mean(value, axis=1, keepdims=True)


def col_sum(value):
    return jnp.sum(value, axis=0, keepdims=True)


def ffn_kernel(ids, *refs, chained, final, base, width, units):
    x_ref, a0, a1, a2, a3, do_ref, vec_ref, bin_ref, w_all = refs[:9]
    if chained:
        gi_in, go_in, gw_in = refs[9:12]
    if final:
        out_ref, dh1_ref, datt_ref, sum_ref, grad_ref = refs[-17:-12]
    else:
        out_ref, dh1_ref, datt_ref, sum_ref, gi_hbm, go_hbm, gw_hbm = refs[-19:-12]
    wi, wo, wa, act_s, gp_s, din_s, att_s, gi, go, gw, w_sem, g_sem = refs[-12:]
    i, j = pl.program_id(0), pl.program_id(1)
    start = (i == 0) & (j == 0)
    last = (i == pl.num_programs(0) - 1) & (j == pl.num_programs(1) - 1)
    rank = ids[2]
    rows = w_all.shape[1]

    def copies(group):
        out = []
        for f in range(4):
            for t in range(4):
                piece = w_all.at[f * 4 + t]
                at = slice(f * rows, (f + 1) * rows)
                sem = w_sem.at[group, f * 4 + t]
                if group == 0:
                    src, dst = piece.at[:, 2 * units : 2 * units + width], wa.at[t, at]
                elif group == 1:
                    src, dst = piece.at[:, :units], wi.at[t, at]
                else:
                    src, dst = piece.at[:, units : 2 * units], wo.at[t, at]
                out.append(pltpu.make_async_copy(src, dst, sem))
        return out

    def grad_in():
        return [
            pltpu.make_async_copy(src, dst, g_sem.at[k])
            for k, (src, dst) in enumerate(((gi_in, gi), (go_in, go), (gw_in, gw)))
        ]

    @pl.when(start)
    def _():
        for group in range(3):
            for c in copies(group):
                c.start()
        if chained:
            for c in grad_in():
                c.start()
        else:
            gi[...] = jnp.zeros_like(gi)
            go[...] = jnp.zeros_like(go)
            gw[...] = jnp.zeros_like(gw)
        sum_ref[...] = jnp.zeros_like(sum_ref)
        for c in copies(0):
            c.wait()

    chunk = a0.shape[1] // width
    for slot, a in enumerate((a0, a1, a2, a3)):
        value = a[:, base * width : (base + 1) * width]
        if chunk > base + 1:
            value = jnp.where(i == 0, value, a[:, (base + 1) * width :])
        att_s[rank ^ slot] = value
    b_out, gain_a, shift_a = vec_ref[0:1], vec_ref[1:2], vec_ref[2:3]
    b_outer, gain_f, shift_f = vec_ref[3:4], vec_ref[4:5], vec_ref[5:6]
    h1 = x_ref[0].astype(F32) + b_out
    for t in range(4):
        h1 = h1 + dot_nt(att_s[t], wa[t])
    c1 = h1 - row_mean(h1)
    r1 = lax.rsqrt(row_mean(c1 * c1) + EPS)
    n1 = c1 * r1
    normed = (n1 * gain_a + shift_a).astype(BF)

    @pl.when(start)
    def _():
        for c in copies(1):
            c.wait()
        for c in copies(2):
            c.wait()
        if chained:
            for c in grad_in():
                c.wait()

    h2 = normed.astype(F32) + b_outer
    for t in range(4):
        inner = dot(normed, wi[t]) + bin_ref[t : t + 1]
        act, slope = gelu_parts(inner)
        low = act.astype(BF)
        act_s[t] = low
        gp_s[t] = slope.astype(BF)
        h2 = h2 + dot_nt(low, wo[t])
    c2 = h2 - row_mean(h2)
    r2 = lax.rsqrt(row_mean(c2 * c2) + EPS)
    n2 = c2 * r2
    out_ref[0] = (n2 * gain_f + shift_f).astype(BF)
    d_out = do_ref[0].astype(F32)
    e2 = d_out * gain_f
    dh2 = (e2 - row_mean(e2) - n2 * row_mean(e2 * n2)) * r2
    dh2_low = dh2.astype(BF)
    dn = dh2
    for t in range(4):
        din = dot(dh2_low, wo[t]) * gp_s[t].astype(F32)
        low = din.astype(BF)
        din_s[t] = low
        dn = dn + dot_nt(low, wi[t])
    e1 = dn * gain_a
    dh1 = (e1 - row_mean(e1) - n1 * row_mean(e1 * n1)) * r1
    dh1_ref[...] = dh1
    dh1_low = dh1.astype(BF)
    datt_ref[...] = dot(dh1_low, wa[rank]).astype(BF)
    din_own = din_s[rank]
    sum_ref[0:1] += col_sum(dh1)
    sum_ref[1:2] += col_sum(dn * n1)
    sum_ref[2:3] += col_sum(dn)
    sum_ref[3:4] += col_sum(dh2)
    sum_ref[4:5] += col_sum(d_out * n2)
    sum_ref[5:6] += col_sum(d_out)
    sum_ref[6:7] += col_sum(din_own.astype(F32))
    gi[...] += dot(normed.T, din_own)
    go[...] += dot(dh2_low.T, act_s[rank])
    gw[...] += dot(dh1_low.T, att_s[rank])

    @pl.when(last)
    def _():
        if final:
            grad_ref[:, :units] = gi[...].astype(BF)
            grad_ref[:, units : 2 * units] = go[...].astype(BF)
            grad_ref[:, 2 * units :] = gw[...].astype(BF)
        else:
            out = [
                pltpu.make_async_copy(src, dst, g_sem.at[k])
                for k, (src, dst) in enumerate(((gi, gi_hbm), (go, go_hbm), (gw, gw_hbm)))
            ]
            for c in out:
                c.start()
            for c in out:
                c.wait()


def ffn_call(
    ids, hidden, atts, d_output, vec, b_inner, w_all, first, base, count, chain, width, units, final, after
):
    seqs, rows, d = hidden.shape
    tile = min(rows, 256)
    tiles = rows // tile
    chunk = atts[0].shape[1]
    whole = pl.BlockSpec((1, tile, d), lambda i, j, s: (first + i, j, 0))
    att = pl.BlockSpec((tile, chunk), lambda i, j, s: (j, 0))
    flat = lambda w: pl.BlockSpec((tile, w), lambda i, j, s: (i * tiles + j, 0))
    fixed = lambda shape: pl.BlockSpec(shape, lambda i, j, s: (0, 0))
    chained = [] if chain is None else list(chain)
    extra = chained + list(after)
    at = 1 + 9
    aliases = {}
    if chained:
        aliases = {at + 3: 0} if final else {at: 4, at + 1: 5, at + 2: 6, at + 3: 0}
    grads = (
        (jax.ShapeDtypeStruct((d, 2 * units + width), BF),)
        if final
        else (
            jax.ShapeDtypeStruct((d, units), F32),
            jax.ShapeDtypeStruct((d, units), F32),
            jax.ShapeDtypeStruct((d, width), F32),
        )
    )
    return pl.pallas_call(
        functools.partial(
            ffn_kernel, chained=bool(chained), final=final, base=base, width=width, units=units
        ),
        out_shape=(
            jax.ShapeDtypeStruct(hidden.shape, BF),
            jax.ShapeDtypeStruct((count * rows, d), F32),
            jax.ShapeDtypeStruct((count * rows, width), BF),
            jax.ShapeDtypeStruct((8, d), F32),
        )
        + grads,
        grid_spec=pltpu.PrefetchScalarGridSpec(
            num_scalar_prefetch=1,
            grid=(count, tiles),
            in_specs=[whole, att, att, att, att, whole, fixed((8, d)), fixed((4, units)), ANY]
            + [ANY] * len(extra),
            out_specs=[whole, flat(d), flat(width), fixed((8, d))]
            + ([fixed((d, 2 * units + width))] if final else [ANY] * 3),
            scratch_shapes=[
                pltpu.VMEM((4, d, units), BF),
                pltpu.VMEM((4, d, units), BF),
                pltpu.VMEM((4, d, width), BF),
                pltpu.VMEM((4, tile, units), BF),
                pltpu.VMEM((4, tile, units), BF),
                pltpu.VMEM((4, tile, units), BF),
                pltpu.VMEM((4, tile, width), BF),
                pltpu.VMEM((d, units), F32),
                pltpu.VMEM((d, units), F32),
                pltpu.VMEM((d, width), F32),
                pltpu.SemaphoreType.DMA((3, 16)),
                pltpu.SemaphoreType.DMA((3,)),
            ],
        ),
        input_output_aliases=aliases,
        compiler_params=params(),
        cost_estimate=pl.CostEstimate(
            flops=2 * count * rows * d * units * 20,
            bytes_accessed=16 * d * units + 16 * count * rows * d,
            transcendentals=8 * count * rows * units,
        ),
        name="ffn",
    )(ids, hidden, *atts, d_output, vec, b_inner, w_all, *extra)


def dx_kernel(ids, dq_ref, *refs, nkv):
    dkv_refs = refs[:nkv]
    w_ref = refs[nkv]
    y_ref, joined_ref = refs[-2:]
    dq = dq_ref[...]
    dkv = dkv_refs[0][...]
    if nkv == 2:
        dkv = (dkv.astype(F32) + dkv_refs[1][...].astype(F32)).astype(BF)
    pad = jnp.zeros((dq.shape[0], 256 - dq.shape[1]), BF)
    joined = jnp.concatenate([dq, pad, dkv], axis=1)
    joined_ref[...] = joined
    y_ref[...] = dot_nt(joined, w_ref[...]).astype(BF)


def dx_call(ids, dq, dkvs, weight, first, tokens, chain, after):
    count = dq.shape[0]
    d, cols = weight.shape
    tile = min(count, 256)
    offset = first // tile
    flat = lambda w: pl.BlockSpec((tile, w), lambda i, s: (i, 0))
    extra = ([] if chain is None else [chain]) + list(after)
    return pl.pallas_call(
        functools.partial(dx_kernel, nkv=len(dkvs)),
        out_shape=(
            jax.ShapeDtypeStruct((count, d), BF),
            jax.ShapeDtypeStruct((tokens, cols), BF),
        ),
        grid_spec=pltpu.PrefetchScalarGridSpec(
            num_scalar_prefetch=1,
            grid=(count // tile,),
            in_specs=[flat(dq.shape[1])]
            + [flat(v.shape[1]) for v in dkvs]
            + [pl.BlockSpec((d, cols), lambda i, s: (0, 0))]
            + [ANY] * len(extra),
            out_specs=[flat(d), pl.BlockSpec((tile, cols), lambda i, s: (offset + i, 0))],
        ),
        input_output_aliases={} if chain is None else {3 + len(dkvs): 1},
        compiler_params=params(),
        cost_estimate=pl.CostEstimate(
            flops=2 * count * d * cols, bytes_accessed=4 * d * cols, transcendentals=0
        ),
        name="dx",
    )(ids, dq, *dkvs, weight, *extra)


def grad_kernel(x_ref, joined_ref, *refs):
    g_ref, sum_ref, acc = refs[-3:]
    i = pl.program_id(0)

    @pl.when(i == 0)
    def _():
        acc[...] = jnp.zeros_like(acc)
        sum_ref[...] = jnp.zeros_like(sum_ref)

    joined = joined_ref[...]
    acc[...] += dot(x_ref[0].T, joined)
    sum_ref[0:1] += col_sum(joined.astype(F32))

    @pl.when(i == pl.num_programs(0) - 1)
    def _():
        g_ref[...] = acc[...].astype(BF)


def grad_call(hidden, joined, after):
    seqs, rows, d = hidden.shape
    cols = joined.shape[1]
    fixed = lambda shape: pl.BlockSpec(shape, lambda i: (0, 0))
    return pl.pallas_call(
        grad_kernel,
        out_shape=(
            jax.ShapeDtypeStruct((d, cols), BF),
            jax.ShapeDtypeStruct((8, cols), F32),
        ),
        grid=(seqs,),
        in_specs=[
            pl.BlockSpec((1, rows, d), lambda i: (i, 0, 0)),
            pl.BlockSpec((rows, cols), lambda i: (i, 0)),
        ]
        + [ANY] * len(after),
        out_specs=[fixed((d, cols)), fixed((8, cols))],
        scratch_shapes=[pltpu.VMEM((d, cols), F32)],
        compiler_params=params(),
        cost_estimate=pl.CostEstimate(
            flops=2 * seqs * rows * d * cols, bytes_accessed=4 * d * cols, transcendentals=0
        ),
        name="grad",
    )(hidden, joined, *after)


def final_kernel(ids, dh1_ref, done_ref, other_ref, *refs):
    out_ref = refs[-1]
    upper = pl.program_id(0) == 0
    odd = lax.rem(ids[2], 2) == 1
    own = upper != odd
    both = jnp.where(own, done_ref[...].astype(F32), other_ref[...].astype(F32))
    out_ref[0] = dh1_ref[...] + both


def final_call(ids, dh1, at, done, other, first, rows, seqs, chain, after):
    half, d = done.shape
    tile = min(half, 256)
    per_half = half // tile
    per_seq = rows // tile
    extra = ([] if chain is None else [chain]) + list(after)
    part = pl.BlockSpec((tile, d), lambda h, j, s: (j, 0))
    flat = lambda h, j: h * per_half + j
    return pl.pallas_call(
        final_kernel,
        out_shape=jax.ShapeDtypeStruct((seqs, rows, d), F32),
        grid_spec=pltpu.PrefetchScalarGridSpec(
            num_scalar_prefetch=1,
            grid=(2, per_half),
            in_specs=[
                pl.BlockSpec((tile, d), lambda h, j, s: (at // tile + flat(h, j), 0)),
                part,
                part,
            ]
            + [ANY] * len(extra),
            out_specs=pl.BlockSpec(
                (1, tile, d),
                lambda h, j, s: (first + flat(h, j) // per_seq, flat(h, j) % per_seq, 0),
            ),
        ),
        input_output_aliases={} if chain is None else {4: 0},
        compiler_params=params(),
        cost_estimate=pl.CostEstimate(
            flops=4 * half * d, bytes_accessed=24 * half * d, transcendentals=0
        ),
        name="final",
    )(ids, dh1, done, other, *extra)


def tp_gather(value):
    return [value] + [lax.ppermute(value, "tp", p) for p in (SWAP, FAR, ACROSS)]


def fsdp_gather(value):
    far = lax.ppermute(value, "fsdp", FAR)
    near = lax.ppermute(value, "fsdp", SWAP)
    return value, near, far, lax.ppermute(far, "fsdp", SWAP)


def tp_reduce(value, odd):
    half = value.shape[0] // 2
    top, bottom = value[:half], value[half:]
    got = lax.ppermute(jnp.where(odd, top, bottom), "tp", SWAP)
    pair = jnp.where(odd, bottom, top) + got
    done = pair + lax.ppermute(pair, "tp", FAR)
    return done, lax.ppermute(done, "tp", SWAP)


def ctx_sum(value, size):
    if size == 2:
        return value + lax.ppermute(value, "ctx", ((0, 1), (1, 0)))
    return lax.psum(value, "ctx")


def fsdp_scatter_sum(value, f, size):
    rows = value.shape[0] // 4
    pairs = value.reshape(2, 2, rows, value.shape[1])
    mine = lax.dynamic_index_in_dim(pairs, f // 2, 0, keepdims=False)
    other = lax.dynamic_index_in_dim(pairs, 1 - f // 2, 0, keepdims=False)
    mine = mine + lax.ppermute(other, "fsdp", FAR)
    own = lax.dynamic_index_in_dim(mine, f % 2, 0, keepdims=False)
    near = lax.dynamic_index_in_dim(mine, 1 - f % 2, 0, keepdims=False)
    own = own + lax.ppermute(near, "fsdp", SWAP)
    return ctx_sum(own, size).astype(F32)


def all_sum(value, size):
    value = value + lax.ppermute(value, "fsdp", SWAP)
    value = value + lax.ppermute(value, "fsdp", FAR)
    return ctx_sum(value, size)


def body(
    hidden_in,
    prev_logits,
    w_query,
    w_key,
    w_value,
    w_out,
    w_inner,
    w_outer,
    b_query,
    b_value,
    b_out,
    b_inner,
    b_outer,
    gain_attn,
    shift_attn,
    gain_ffn,
    shift_ffn,
    d_output,
    d_logits,
    *,
    ctx_size,
):
    seqs, rows, d = hidden_in.shape
    heads = prev_logits.shape[1]
    width = w_query.shape[1]
    units = w_inner.shape[1]
    size = width // heads
    scale = size**-0.5
    f, c, rank = lax.axis_index("fsdp"), lax.axis_index("ctx"), lax.axis_index("tp")
    ids = jnp.stack([f, c, rank]).astype(jnp.int32)
    odd = rank % 2 == 1

    ffn_local = jnp.concatenate([w_inner, w_outer, w_out], axis=1)
    w_all = lax.all_gather(ffn_local, ("fsdp", "tp"), axis=0, tiled=False)
    w_all = w_all.reshape(16, w_inner.shape[0], 2 * units + width)
    bias_inner = lax.all_gather(b_inner, "tp", axis=0, tiled=False)
    qkv_local = jnp.concatenate(
        [w_query, jnp.zeros((w_query.shape[0], 256 - width), BF), w_key, w_value], axis=1
    )
    qkv_pieces = fsdp_gather(qkv_local)
    qkv_bias = jnp.concatenate([b_query, jnp.zeros((256,), F32), b_value])[None]
    vec = jnp.stack([b_out, gain_attn, shift_attn, b_outer, gain_ffn, shift_ffn, b_out, b_out])

    chunk = 2
    starts = range(0, seqs, chunk)
    queries, kvs, after = [], [], []
    for s in starts:
        q, kv, w_qkv = qkv_call(
            ids, hidden_in, s, chunk, qkv_pieces, qkv_bias, width, scale, after
        )
        after = [q]
        queries.append(q)
        if ctx_size == 2:
            kvs.append((lax.ppermute(kv, "ctx", ((0, 1),)), kv))
        else:
            got = lax.all_gather(kv.reshape(chunk, rows, 2 * width), "ctx", axis=1, tiled=True)
            kvs.append((got.reshape(-1, 2 * width),))

    logits, probs, atts, inverses = None, [], [], []
    for k, s in enumerate(starts):
        logits, e, att, inverse = attn_fwd_call(
            ids, queries[k], kvs[k], prev_logits, s, chunk, logits, heads, size, after
        )
        after = [att]
        probs.append(e)
        atts.append(tp_gather(att))
        inverses.append(inverse)

    groups = [(0, chunk)] + [(s, 1) for s in range(chunk, seqs)]
    chain, sums, dh1s, datts = None, [], {}, {}
    d_prev, d_hidden, joined = None, None, None
    pending = []

    def ffn(s, count, after):
        nonlocal chain, grad_ffn, output
        k, base = s // chunk, s % chunk
        final = s + count == seqs
        out = ffn_call(
            ids,
            hidden_in,
            atts[k],
            d_output,
            vec,
            bias_inner,
            w_all,
            s,
            base,
            count,
            chain,
            width,
            units,
            final,
            after,
        )
        output, dh1s[s], datts[s], part = out[:4]
        sums.append(part)
        if final:
            grad_ffn = out[4]
        else:
            chain = (out[4], out[5], out[6], output)
        return [datts[s]]

    def attn_bwd(s, count, after):
        nonlocal d_prev
        k, base = s // chunk, s % chunk
        out = attn_bwd_call(
            ids,
            queries[k],
            probs[k],
            d_logits,
            datts[s],
            atts[k][0],
            inverses[k],
            kvs[k],
            s,
            base,
            count,
            chunk,
            d_prev,
            heads,
            size,
            scale,
            after,
        )
        d_prev, dq = out[:2]
        if ctx_size == 2:
            dkvs = (out[2], lax.ppermute(out[3], "ctx", ((1, 0),)))
        else:
            full_grad = out[2].reshape(count, -1, 2 * width)
            part = lax.psum_scatter(full_grad, "ctx", scatter_dimension=1, tiled=True)
            dkvs = (part.reshape(-1, 2 * width),)
        return (dq, dkvs), [dq]

    def dx(s, grads, after):
        nonlocal joined
        y, joined = dx_call(
            ids, grads[0], grads[1], w_qkv, s * rows, seqs * rows, joined, after
        )
        return tp_reduce(y, odd), [y]

    grad_ffn = output = None
    held, reduced = None, []
    for g, (s, count) in enumerate(groups):
        after = ffn(s, count, after)
        if held is not None:
            done, after = dx(held[0], held[1], after)
            reduced.append((held[0], done))
        grads, after = attn_bwd(s, count, after)
        held = (s, grads)
    done, after = dx(held[0], held[1], after)
    reduced.append((held[0], done))
    g_qkv, qkv_sum = grad_call(hidden_in, joined, after)
    for s, (done, other) in reduced:
        d_hidden = final_call(ids, dh1s[s], 0, done, other, s, rows, seqs, d_hidden, [g_qkv])

    small = jnp.concatenate([functools.reduce(jnp.add, sums), qkv_sum], axis=1)
    small = all_sum(small, ctx_size)
    g_ffn = lax.psum_scatter(grad_ffn, "fsdp", scatter_dimension=0, tiled=True)
    g_ffn = ctx_sum(g_ffn, ctx_size).astype(F32)
    g_qkv = fsdp_scatter_sum(g_qkv, f, ctx_size)
    return (
        output,
        logits,
        d_hidden,
        d_prev,
        g_qkv[:, :width],
        g_qkv[:, 256 : 256 + width],
        g_qkv[:, 256 + width :],
        g_ffn[:, 2 * units :],
        g_ffn[:, :units],
        g_ffn[:, units : 2 * units],
        small[0, d : d + width],
        small[0, d + 256 + width :],
        small[0, :d],
        small[6, :d],
        small[3, :d],
        small[1, :d],
        small[2, :d],
        small[4, :d],
        small[5, :d],
    )


def solution(mesh):
    tok, lgt, mat = P("fsdp", "ctx", None), P("fsdp", "tp", "ctx", None), P("fsdp", "tp")
    vec, rep = P("tp"), P()
    in_specs = (tok, lgt) + (mat,) * 6 + (vec, vec, rep, vec) + (rep,) * 5 + (tok, lgt)
    out_specs = (tok, lgt, tok, lgt) + (mat,) * 6 + (vec, vec, rep, vec) + (rep,) * 5
    return jax.shard_map(
        functools.partial(body, ctx_size=mesh.shape["ctx"]),
        mesh=mesh,
        in_specs=in_specs,
        out_specs=out_specs,
        check_vma=False,
    )
```

time: 680 us -> 470 us (0.69)
  waiting for transfers between devices: 240 us -> 118 us
  starting transfers between devices: 134 us -> 29.6 us
  blocking collectives: 0 us -> 70.6 us
  Pallas kernels: 246 us -> 203 us
  between operations: 2.64 us -> 14.9 us
  other arithmetic: 26.6 us -> 14.4 us
  local copies, waits for them, and re-layouts: 20.9 us -> 12.7 us
    ppermute x60 -> x20, waiting for transfers between devices: 222 us -> 91.3 us  [the longest x3 37.1 us: tp_reduce(): done = pair + lax.ppermute(pair, 'tp', FAR)]
    ppermute x60 -> x20, starting transfers between devices: 99.7 us -> 19.7 us  [the longest x6 8.91 us: tp_gather(): return [value] + [lax.ppermute(value, 'tp', p) for p in (SWAP, FAR, ACROSS)]]
    all_gather x0 -> x1, blocking collectives: none -> 70.6 us  [body(): bias_inner = lax.all_gather(b_inner, 'tp', axis=0, tiled=False)]
    pallas_call x8 -> x7, Pallas kernels: 155 us -> 119 us  [the longest x3 98.4 us: ffn_call(): pl.pallas_call(functools.partial(ffn_kernel, chained=bool(chained), final...]
    ppermute x4 -> x3, starting transfers between devices: 13.7 us -> 0.21 us  [ctx_sum(): return value + lax.ppermute(value, 'ctx', ((0, 1), (1, 0)))]
    add x25 -> x9, other arithmetic: 15.9 us -> 5.87 us  [the longest x3 2.89 us: tp_reduce(): done = pair + lax.ppermute(pair, 'tp', FAR)]
    ppermute x4 -> x2, waiting for transfers between devices: 0.01 us -> 9.57 us  [body(): kvs.append((lax.ppermute(kv, 'ctx', ((0, 1),)), kv))]
    ppermute x2 -> x1, waiting for transfers between devices: 15 us -> 8.31 us  [all_sum(): value = value + lax.ppermute(value, 'fsdp', FAR)]
  transfers between devices with their start and end apart: 87 -> 32, of which waited for: 27 -> 13; matrix products, arithmetic and copies ran while one was open for 6% -> 4% of each run, Pallas kernels for 17% -> 35%
where the time goes in v2:
time: 470 us; the launch traced here: 463 us
  Pallas kernels  203 us (43%)
  waiting for transfers between devices  118 us (25%)
  blocking collectives  70.6 us (15%)
  starting transfers between devices  29.6 us (6%)
  between operations  14.9 us (3%)
  other arithmetic  14.4 us (3%)
  local copies, waits for them, and re-layouts  12.7 us (3%)
    pallas_call x3, Pallas kernels, ffn_call(): pl.pallas_call(functools.partial(ffn_kernel, chained=bool(chained), final...  98.4 us
    all_gather x1, blocking collectives, body(): bias_inner = lax.all_gather(b_inner, 'tp', axis=0, tiled=False)  70.6 us
    ppermute x3, waiting for transfers between devices, tp_reduce(): done = pair + lax.ppermute(pair, 'tp', FAR)  37.1 us
    pallas_call x3, Pallas kernels, attn_bwd_call(): pl.pallas_call(functools.partial(attn_bwd_kernel, heads=heads, size=size,...  34.6 us
    pallas_call x2, Pallas kernels, attn_fwd_call(): pl.pallas_call(functools.partial(attn_fwd_kernel, heads=heads, size=size,...  24.2 us
    ppermute x3, waiting for transfers between devices, tp_reduce(): return (done, lax.ppermute(done, 'tp', SWAP))  22.2 us
    ppermute x3, waiting for transfers between devices, attn_bwd(): dkvs = (out[2], lax.ppermute(out[3], 'ctx', ((1, 0),)))  20.6 us
    pallas_call x3, Pallas kernels, dx_call(): pl.pallas_call(functools.partial(dx_kernel, nkv=len(dkvs)), out_shape=(ja...  14.6 us
  transfers between devices with their start and end apart: 32, of which 13 were waited for; matrix products, arithmetic and copies ran while one was open for 4% of the time, Pallas kernels for 35%

profile of v2, /device:TPU:0, one launch (start us, length us, event | category | flops | bytes accessed | tf_op | source)
XLA Modules:
  0.0 463.4 jit_solution(12167682812717860129)
XLA Ops:
  7.2 2.0 pad_maximum_fusion
  9.4 1.1 pad_maximum_fusion.1.w0
  10.5 3.0 collective-permute-start.1
  13.5 6.0 %collective-permute-done.1.w2 = bf16[192,640]{1,0:T(8,128)(2,1)S(1)} collective-permute-done((bf16[192,640]{1,0:T(8,128)(2,1)S(1)}, bf16[192,640]{1,0:T(8,128)(2,1)S(1)}, u32[]{:S(2)}, u32[]{:S(2)}) %collective-permute-start.1) | collective-permute-done | bytes 245792 | tf_op jit(solution)/shard_map/ppermute | solution.py:717
  22.9 6.3 %qkv.2 = (bf16[1024,192]{1,0:T(8,128)(2,1)}, bf16[1024,384]{1,0:T(8,128)(2,1)}, bf16[768,640]{1,0:T(8,128)(2,1)}) custom-call(s32[3]{0:T(128)} %pad_add_fusion.ids, bf16[4,512,768]{2,1,0:T(8,128)(2,1)} %x_ref.5, bf16[192,640]{1,0:T(8,128)(2,1)} %copy-done.6, bf16[192,640]{1,0:T(8,128)(2,1)} %copy-done.8, bf16[192,640]{1,0:T(8,128)(2,1)} %copy-done.7, ...), custom_call_target="tpu_custom_call" | custom-call | flops 1006632960 | bytes 5046272 | tf_op jit(solution)/shard_map/qkv/pallas_call | solution.py:81
  29.3 4.5 collective-permute-start.4
  33.8 6.3 %qkv.3 = (bf16[1024,192]{1,0:T(8,128)(2,1)}, bf16[1024,384]{1,0:T(8,128)(2,1)}, bf16[768,640]{1,0:T(8,128)(2,1)}) custom-call(s32[3]{0:T(128)} %pad_add_fusion.ids, bf16[4,512,768]{2,1,0:T(8,128)(2,1)} %x_ref.5, bf16[192,640]{1,0:T(8,128)(2,1)} %copy-done.6, bf16[192,640]{1,0:T(8,128)(2,1)} %copy-done.8, bf16[192,640]{1,0:T(8,128)(2,1)} %copy-done.7, ...), custom_call_target="tpu_custom_call" | custom-call | flops 1006632960 | bytes 5046272 | tf_op jit(solution)/shard_map/qkv/pallas_call | solution.py:81
  40.1 1.3 collective-permute-start.3
  41.5 9.6 %collective-permute-done.4.refs_2_.refs_6_ = bf16[1024,384]{1,0:T(8,128)(2,1)} collective-permute-done((bf16[1024,384]{1,0:T(8,128)(2,1)}, bf16[1024,384]{1,0:T(8,128)(2,1)}, u32[]{:S(2)}, u32[]{:S(2)}) %collective-permute-start.4) | collective-permute-done | bytes 786464 | tf_op jit(solution)/shard_map/ppermute | solution.py:809
  51.1 12.6 %attn_fwd.2 = (bf16[4,3,512,1024]{3,2,1,0:T(8,128)(2,1)}, bf16[2,3,512,1024]{3,2,1,0:T(8,128)(2,1)}, bf16[512,384]{1,0:T(8,128)(2,1)}, f32[1024,128]{1,0:T(8,128)}) custom-call(s32[3]{0:T(128)} %pad_add_fusion.ids, bf16[1024,192]{1,0:T(8,128)(2,1)} %get-tuple-element.71.refs_0_, bf16[4,3,512,1024]{3,2,1,0:T(8,128)(2,1)} %refs_1_.3, ...), custom_call_target="tpu_custom_call" | custom-call | flops 2415919104 | bytes 18874368 | tf_op jit(solution)/shard_map/attn_fwd/pallas_call | solution.py:196
  63.7 3.7 collective-permute-start.10
  68.3 70.6 %all-gather.2 = f32[4,1,768]{2,1,0:T(1,128)S(1)} all-gather(f32[1,1,768]{2,1,0:T(1,128)S(1)} %reshape.44), channel_id=2, replica_groups=mesh['fsdp'=4,'ctx'=2,'tp'=4] {'tp'}, dimensions={0}, use_global_device_ids=true | all-gather | bytes 15360 | tf_op jit(solution)/shard_map/all_gather | solution.py:791
  141.0 11.7 %attn_fwd.3 = (bf16[4,3,512,1024]{3,2,1,0:T(8,128)(2,1)}, bf16[2,3,512,1024]{3,2,1,0:T(8,128)(2,1)}, bf16[512,384]{1,0:T(8,128)(2,1)}, f32[1024,128]{1,0:T(8,128)}) custom-call(s32[3]{0:T(128)} %pad_add_fusion.ids, bf16[1024,192]{1,0:T(8,128)(2,1)} %get-tuple-element.72.refs_4_.refs_0_, ...), custom_call_target="tpu_custom_call", output_to_operand_aliasing={{0}: (5, {})} | custom-call | flops 2415919104 | bytes 18874368 | tf_op jit(solution)/shard_map/attn_fwd/pallas_call | solution.py:196
  153.5 2.3 collective-permute-start.6
  155.8 1.4 collective-permute-start.7
  157.2 43.8 %ffn.3 = (bf16[4,512,768]{2,1,0:T(8,128)(2,1)}, f32[1024,768]{1,0:T(8,128)}, bf16[1024,192]{1,0:T(8,128)(2,1)}, f32[8,768]{1,0:T(8,128)}, f32[768,768]{1,0:T(8,1...) custom-call(s32[3]{0:T(128)} %pad_add_fusion.ids, bf16[4,512,768]{2,1,0:T(8,128)(2,1)} %x_ref.5, ...), custom_call_target="tpu_custom_call" | custom-call | flops 24159191040 | bytes 22020096 | tf_op jit(solution)/shard_map/ffn/pallas_call | solution.py:536
  200.9 15.3 %attn_bwd.3 = (bf16[4,3,512,1024]{3,2,1,0:T(8,128)(2,1)}, bf16[1024,192]{1,0:T(8,128)(2,1)}, bf16[1024,384]{1,0:T(8,128)(2,1)}, bf16[1024,384]{1,0:T(8,128)(2,1)}) custom-call(s32[3]{0:T(128)} %pad_add_fusion.ids, bf16[1024,192]{1,0:T(8,128)(2,1)} %get-tuple-element.71.refs_0_, bf16[2,3,512,1024]{3,2,1,0:T(8,128)(2,1)} %get-tuple-element.82.refs_1_, ...), custom_call_target="tpu_custom_call" | custom-call | flops 4831838208 | bytes 18874368 | tf_op jit(solution)/shard_map/attn_bwd/pallas_call | solution.py:326
  216.3 1.3 collective-permute-start.11
  217.6 27.6 %ffn.4 = (bf16[4,512,768]{2,1,0:T(8,128)(2,1)}, f32[512,768]{1,0:T(8,128)}, bf16[512,192]{1,0:T(8,128)(2,1)}, f32[8,768]{1,0:T(8,128)}, f32[768,768]{1,0:T(8,128...) custom-call(s32[3]{0:T(128)} %pad_add_fusion.ids, ...), custom_call_target="tpu_custom_call", output_to_operand_aliasing={{4}: (10, {}), {5}: (11, {}), {6}: (12, {}), {0}: (13, {})} | custom-call | flops 12079595520 | bytes 15728640 | tf_op jit(solution)/shard_map/ffn/pallas_call | solution.py:536
  246.1 5.9 %dx.3 = (bf16[1024,768]{1,0:T(8,128)(2,1)}, bf16[2048,640]{1,0:T(8,128)(2,1)}) custom-call(s32[3]{0:T(128)} %pad_add_fusion.ids, bf16[1024,192]{1,0:T(8,128)(2,1)} %get-tuple-element.85.refs_13_.dq_ref, bf16[1024,384]{1,0:T(8,128)(2,1)} %get-tuple-element.94.refs_0_, bf16[1024,384]{1,0:T(8,128)(2,1)} %copy-done.24, ...), custom_call_target="tpu_custom_call" | custom-call | flops 1006632960 | bytes 1966080 | tf_op jit(solution)/shard_map/dx/pallas_call | solution.py:601
  252.0 9.4 %attn_bwd.4 = (bf16[4,3,512,1024]{3,2,1,0:T(8,128)(2,1)}, bf16[512,192]{1,0:T(8,128)(2,1)}, bf16[512,384]{1,0:T(8,128)(2,1)}, bf16[512,384]{1,0:T(8,128)(2,1)}) custom-call(s32[3]{0:T(128)} %pad_add_fusion.ids, bf16[1024,192]{1,0:T(8,128)(2,1)} %get-tuple-element.72.refs_4_.refs_0_, ...), custom_call_target="tpu_custom_call", output_to_operand_aliasing={{0}: (9, {})} | custom-call | flops 2415919104 | bytes 9437184 | tf_op jit(solution)/shard_map/attn_bwd/pallas_call | solution.py:326
  261.4 27.0 %ffn.5 = (bf16[4,512,768]{2,1,0:T(8,128)(2,1)}, f32[512,768]{1,0:T(8,128)}, bf16[512,192]{1,0:T(8,128)(2,1)}, f32[8,768]{1,0:T(8,128)}, bf16[768,1728]{1,0:T(8,128)(2,1)}) custom-call(s32[3]{0:T(128)} %pad_add_fusion.ids, bf16[4,512,768]{2,1,0:T(8,128)(2,1)} %x_ref.5, ...), custom_call_target="tpu_custom_call", output_to_operand_aliasing={{0}: (13, {})} | custom-call | flops 12079595520 | bytes 15728640 | tf_op jit(solution)/shard_map/ffn/pallas_call | solution.py:536
  289.4 1.3 collective-permute-start.12
  291.8 12.8 %collective-permute-done.12.refs_1_ = bf16[512,384]{1,0:T(8,128)(2,1)S(1)} collective-permute-done((bf16[512,384]{1,0:T(8,128)(2,1)S(1)}, bf16[512,384]{1,0:T(8,128)(2,1)S(1)}, u32[]{:S(2)}, u32[]{:S(2)}) %collective-permute-start.12) | collective-permute-done | bytes 393248 | tf_op jit(solution)/shard_map/ppermute | solution.py:882
  305.3 4.5 dx.4
  309.8 9.9 %attn_bwd.5 = (bf16[4,3,512,1024]{3,2,1,0:T(8,128)(2,1)}, bf16[512,192]{1,0:T(8,128)(2,1)}, bf16[512,384]{1,0:T(8,128)(2,1)}, bf16[512,384]{1,0:T(8,128)(2,1)}) custom-call(s32[3]{0:T(128)} %pad_add_fusion.ids, bf16[1024,192]{1,0:T(8,128)(2,1)} %get-tuple-element.72.refs_4_.refs_0_, ...), custom_call_target="tpu_custom_call", output_to_operand_aliasing={{0}: (9, {})} | custom-call | flops 2415919104 | bytes 9437184 | tf_op jit(solution)/shard_map/attn_bwd/pallas_call | solution.py:326
  319.7 1.3 collective-permute-start.13
  321.9 7.8 %collective-permute-done.13.refs_1_ = bf16[512,384]{1,0:T(8,128)(2,1)} collective-permute-done((bf16[512,384]{1,0:T(8,128)(2,1)}, bf16[512,384]{1,0:T(8,128)(2,1)}, u32[]{:S(2)}, u32[]{:S(2)}) %collective-permute-start.13) | collective-permute-done | bytes 393248 | tf_op jit(solution)/shard_map/ppermute | solution.py:882
  329.7 4.2 dx.5
  333.9 6.4 %grad.1 = (bf16[768,640]{1,0:T(8,128)(2,1)}, f32[8,640]{1,0:T(8,128)}) custom-call(bf16[4,512,768]{2,1,0:T(8,128)(2,1)} %x_ref.5, bf16[2048,640]{1,0:T(8,128)(2,1)} %get-tuple-element.115.joined_ref, bf16[512,768]{1,0:T(8,128)(2,1)} %get-tuple-element.112.refs_0_), custom_call_target="tpu_custom_call" | custom-call | flops 2013265920 | bytes 1966080 | tf_op jit(solution)/shard_map/grad/pallas_call | solution.py:647
  342.2 1.6 collective-permute-start.23
  343.7 1.7 select_add_fusion
  346.2 2.3 collective-permute-start.14
  348.5 8.3 %collective-permute-done.28 = f32[8,1408]{1,0:T(8,128)S(1)} collective-permute-done((f32[8,1408]{1,0:T(8,128)S(1)}, f32[8,1408]{1,0:T(8,128)S(1)}, u32[]{:S(2)}, u32[]{:S(2)}) %collective-permute-start.28) | collective-permute-done | bytes 45088 | tf_op jit(solution)/shard_map/ppermute | solution.py:751
  358.1 2.9 collective-permute-done.29
  361.2 11.4 %collective-permute-done.14 = bf16[256,768]{1,0:T(8,128)(2,1)S(1)} collective-permute-done((bf16[256,768]{1,0:T(8,128)(2,1)S(1)}, bf16[256,768]{1,0:T(8,128)(2,1)S(1)}, u32[]{:S(2)}, u32[]{:S(2)}) %collective-permute-start.14) | collective-permute-done | bytes 393248 | tf_op jit(solution)/shard_map/ppermute | solution.py:725
  372.7 2.8 collective-permute-start.15
  375.6 23.8 %collective-permute-done.21 = bf16[512,768]{1,0:T(8,128)(2,1)S(1)} collective-permute-done((bf16[512,768]{1,0:T(8,128)(2,1)S(1)}, bf16[512,768]{1,0:T(8,128)(2,1)S(1)}, u32[]{:S(2)}, u32[]{:S(2)}) %collective-permute-start.21) | collective-permute-done | bytes 786464 | tf_op jit(solution)/shard_map/ppermute | solution.py:727
  401.1 6.9 %collective-permute-done.18 = bf16[256,768]{1,0:T(8,128)(2,1)} collective-permute-done((bf16[256,768]{1,0:T(8,128)(2,1)S(1)}, bf16[256,768]{1,0:T(8,128)(2,1)}, u32[]{:S(2)}, u32[]{:S(2)}) %collective-permute-start.18) | collective-permute-done | bytes 393248 | tf_op jit(solution)/shard_map/ppermute | solution.py:727
  408.1 1.8 add.76.done_ref
  409.9 6.4 %collective-permute-done.15 = bf16[256,768]{1,0:T(8,128)(2,1)S(1)} collective-permute-done((bf16[256,768]{1,0:T(8,128)(2,1)S(1)}, bf16[256,768]{1,0:T(8,128)(2,1)S(1)}, u32[]{:S(2)}, u32[]{:S(2)}) %collective-permute-start.15) | collective-permute-done | bytes 393248 | tf_op jit(solution)/shard_map/ppermute | solution.py:727
  418.0 15.1 %collective-permute-done.22.other_ref = bf16[512,768]{1,0:T(8,128)(2,1)S(1)} collective-permute-done((bf16[512,768]{1,0:T(8,128)(2,1)S(1)}, bf16[512,768]{1,0:T(8,128)(2,1)S(1)}, u32[]{:S(2)}, u32[]{:S(2)}) %collective-permute-start.22) | collective-permute-done | bytes 786464 | tf_op jit(solution)/shard_map/ppermute | solution.py:728
  434.0 5.6 %final.3.refs_0_ = f32[4,512,768]{2,1,0:T(8,128)} custom-call(s32[3]{0:T(128)} %pad_add_fusion.ids, f32[1024,768]{1,0:T(8,128)} %get-tuple-element.114.dh1_ref, bf16[512,768]{1,0:T(8,128)(2,1)} %copy-done.5, bf16[512,768]{1,0:T(8,128)(2,1)} %copy-done.10, bf16[768,640]{1,0:T(8,128)(2,1)} %get-tuple-element.116.refs_0_.refs_1_), custom_call_target="tpu_custom_call" | custom-call | flops 1572864 | bytes 9437184 | tf_op jit(solution)/shard_map/final/pallas_call | solution.py:686
  439.6 2.0 collective-permute-done.19.other_ref
  441.7 3.3 final.4.refs_0_
  445.0 5.0 %collective-permute-done.16.other_ref = bf16[256,768]{1,0:T(8,128)(2,1)} collective-permute-done((bf16[256,768]{1,0:T(8,128)(2,1)}, bf16[256,768]{1,0:T(8,128)(2,1)}, u32[]{:S(2)}, u32[]{:S(2)}) %collective-permute-start.16) | collective-permute-done | bytes 393248 | tf_op jit(solution)/shard_map/ppermute | solution.py:728
  450.0 3.4 final.5
  453.4 1.2 add_convert_fusion
  (130 shorter events, 22.2 us)
Async XLA Ops:
  7.2 150.0 %all-gather.5.cloned.1.call-start = ((), (), s32[]{:S(2)}) async-start(), calls=%async_computation.2 | async-start | bytes 11698176 | tf_op jit(solution)/shard_map/all_gather | solution.py:789
  9.3 390.5 %reduce-scatter.2.cloned.1.call-start = ((), (), s32[]{:S(2)}) async-start(), calls=%async_computation.1 | async-start | bytes 3440640 | tf_op jit(solution)/shard_map/reduce_scatter | solution.py:913
  10.5 11.1 %copy-start.6 = (bf16[192,640]{1,0:T(8,128)(2,1)}, bf16[192,640]{1,0:T(8,128)(2,1)S(1)}, u32[]{:S(2)}) copy-start(bf16[192,640]{1,0:T(8,128)(2,1)S(1)} %pad_maximum_fusion.1.w0) | copy-start | bytes 737284
  10.5 9.0 %collective-permute-start.1 = (bf16[192,640]{1,0:T(8,128)(2,1)S(1)}, bf16[192,640]{1,0:T(8,128)(2,1)S(1)}, u32[]{:S(2)}, u32[]{:S(2)}) collective-permute-start(bf16[192,640]{1,0:T(8,128)(2,1)S(1)} %pad_maximum_fusion.1.w0), channel_id=1, source_target_pairs={{0,16},{16,0},{8,24},{24,8},{1,17},{17,1},{9,25},{25,9},{2,18},{18... | collective-permute-start | bytes 737288 | tf_op jit(solution)/shard_map/ppermute | solution.py:717
  13.5 8.0 %collective-permute-start = (bf16[192,640]{1,0:T(8,128)(2,1)S(1)}, bf16[192,640]{1,0:T(8,128)(2,1)S(1)}, u32[]{:S(2)}, u32[]{:S(2)}) collective-permute-start(bf16[192,640]{1,0:T(8,128)(2,1)S(1)} %pad_maximum_fusion.1.w0), channel_id=1, source_target_pairs={{0,8},{8,0},{16,24},{24,16},{1,9},{9,1},{17,25},{25,17},{2,10},{10... | collective-permute-start | bytes 737288 | tf_op jit(solution)/shard_map/ppermute | solution.py:718
  19.5 2.1 collective-permute-start.2
  29.3 21.8 %collective-permute-start.4 = (bf16[1024,384]{1,0:T(8,128)(2,1)}, bf16[1024,384]{1,0:T(8,128)(2,1)}, u32[]{:S(2)}, u32[]{:S(2)}) collective-permute-start(bf16[1024,384]{1,0:T(8,128)(2,1)} %get-tuple-element.74.refs_3_.refs_7_), channel_id=1, source_target_pairs={{0,4},{1,5},{2,6},{3,7},{8,12},{9,13},{10,14},{11,15},{16,20},{17,... | collective-permute-start | bytes 2359304 | tf_op jit(solution)/shard_map/ppermute | solution.py:809
  40.1 100.0 %collective-permute-start.3 = (bf16[1024,384]{1,0:T(8,128)(2,1)}, bf16[1024,384]{1,0:T(8,128)(2,1)S(1)}, u32[]{:S(2)}, u32[]{:S(2)}) collective-permute-start(bf16[1024,384]{1,0:T(8,128)(2,1)} %get-tuple-element.73.refs_3_.refs_7_), channel_id=1, source_target_pairs={{0,4},{1,5},{2,6},{3,7},{8,12},{9,13},{10,14},{11,15},{16,20},{17,... | collective-permute-start | bytes 2359304 | tf_op jit(solution)/shard_map/ppermute | solution.py:809
  51.0 17.1 %copy-start.17 = (f32[768]{0:T(1024)S(1)}, f32[768]{0:T(1024)}, u32[]{:S(2)}) copy-start(f32[768]{0:T(1024)} %param.29) | copy-start | bytes 9220
  51.0 17.1 %copy-start.18 = (f32[768]{0:T(1024)S(1)}, f32[768]{0:T(1024)}, u32[]{:S(2)}) copy-start(f32[768]{0:T(1024)} %param.32) | copy-start | bytes 9220
  51.1 17.1 %copy-start.19 = (f32[768]{0:T(1024)S(1)}, f32[768]{0:T(1024)}, u32[]{:S(2)}) copy-start(f32[768]{0:T(1024)} %param.33) | copy-start | bytes 9220
  51.1 17.1 %copy-start.20 = (f32[768]{0:T(1024)S(1)}, f32[768]{0:T(1024)}, u32[]{:S(2)}) copy-start(f32[768]{0:T(1024)} %param.31) | copy-start | bytes 9220
  51.1 17.1 %copy-start.21 = (f32[768]{0:T(1024)S(1)}, f32[768]{0:T(1024)}, u32[]{:S(2)}) copy-start(f32[768]{0:T(1024)} %param.34) | copy-start | bytes 9220
  51.1 17.1 %copy-start.22 = (f32[768]{0:T(1024)S(1)}, f32[768]{0:T(1024)}, u32[]{:S(2)}) copy-start(f32[768]{0:T(1024)} %param.35) | copy-start | bytes 9220
  51.1 17.2 %copy-start.23 = (f32[768]{0:T(1024)S(1)}, f32[768]{0:T(1024)}, u32[]{:S(2)}) copy-start(f32[768]{0:T(1024)} %param.30) | copy-start | bytes 9220
  63.7 92.1 %collective-permute-start.10 = (bf16[512,384]{1,0:T(8,128)(2,1)}, bf16[512,384]{1,0:T(8,128)(2,1)}, u32[]{:S(2)}, u32[]{:S(2)}) collective-permute-start(bf16[512,384]{1,0:T(8,128)(2,1)} %get-tuple-element.76.refs_5_.refs_1_.refs_4_), channel_id=1, source_target_pairs={{0,3},{3,0},{1,2},{2,1},{4,7},{7,4},{5,6},{6,5},{8,11},{11,8},{9,1... | collective-permute-start | bytes 1179656 | tf_op jit(solution)/shard_map/ppermute | solution.py:713
  67.3 89.8 %collective-permute-start.8 = (bf16[512,384]{1,0:T(8,128)(2,1)}, bf16[512,384]{1,0:T(8,128)(2,1)}, u32[]{:S(2)}, u32[]{:S(2)}) collective-permute-start(bf16[512,384]{1,0:T(8,128)(2,1)} %get-tuple-element.76.refs_5_.refs_1_.refs_4_), channel_id=1, source_target_pairs={{0,1},{1,0},{2,3},{3,2},{4,5},{5,4},{6,7},{7,6},{8,9},{9,8},{10,11... | collective-permute-start | bytes 1179656 | tf_op jit(solution)/shard_map/ppermute | solution.py:713
  67.3 89.8 %collective-permute-start.9 = (bf16[512,384]{1,0:T(8,128)(2,1)}, bf16[512,384]{1,0:T(8,128)(2,1)}, u32[]{:S(2)}, u32[]{:S(2)}) collective-permute-start(bf16[512,384]{1,0:T(8,128)(2,1)} %get-tuple-element.76.refs_5_.refs_1_.refs_4_), channel_id=1, source_target_pairs={{0,2},{2,0},{1,3},{3,1},{4,6},{6,4},{5,7},{7,5},{8,10},{10,8},{9,1... | collective-permute-start | bytes 1179656 | tf_op jit(solution)/shard_map/ppermute | solution.py:713
  152.7 64.9 %collective-permute-start.5 = (bf16[512,384]{1,0:T(8,128)(2,1)}, bf16[512,384]{1,0:T(8,128)(2,1)}, u32[]{:S(2)}, u32[]{:S(2)}) collective-permute-start(bf16[512,384]{1,0:T(8,128)(2,1)} %get-tuple-element.77.refs_9_.refs_1_.refs_4_), channel_id=1, source_target_pairs={{0,1},{1,0},{2,3},{3,2},{4,5},{5,4},{6,7},{7,6},{8,9},{9,8},{10,11... | collective-permute-start | bytes 1179656 | tf_op jit(solution)/shard_map/ppermute | solution.py:713
  153.5 64.0 %collective-permute-start.6 = (bf16[512,384]{1,0:T(8,128)(2,1)}, bf16[512,384]{1,0:T(8,128)(2,1)}, u32[]{:S(2)}, u32[]{:S(2)}) collective-permute-start(bf16[512,384]{1,0:T(8,128)(2,1)} %get-tuple-element.77.refs_9_.refs_1_.refs_4_), channel_id=1, source_target_pairs={{0,2},{2,0},{1,3},{3,1},{4,6},{6,4},{5,7},{7,5},{8,10},{10,8},{9,1... | collective-permute-start | bytes 1179656 | tf_op jit(solution)/shard_map/ppermute | solution.py:713
  155.8 61.8 %collective-permute-start.7 = (bf16[512,384]{1,0:T(8,128)(2,1)}, bf16[512,384]{1,0:T(8,128)(2,1)}, u32[]{:S(2)}, u32[]{:S(2)}) collective-permute-start(bf16[512,384]{1,0:T(8,128)(2,1)} %get-tuple-element.77.refs_9_.refs_1_.refs_4_), channel_id=1, source_target_pairs={{0,3},{3,0},{1,2},{2,1},{4,7},{7,4},{5,6},{6,5},{8,11},{11,8},{9,1... | collective-permute-start | bytes 1179656 | tf_op jit(solution)/shard_map/ppermute | solution.py:713
  216.3 29.0 %collective-permute-start.11 = (bf16[1024,384]{1,0:T(8,128)(2,1)}, bf16[1024,384]{1,0:T(8,128)(2,1)S(1)}, u32[]{:S(2)}, u32[]{:S(2)}) collective-permute-start(bf16[1024,384]{1,0:T(8,128)(2,1)} %get-tuple-element.95), channel_id=1, source_target_pairs={{4,0},{5,1},{6,2},{7,3},{12,8},{13,9},{14,10},{15,11},{20,16},{21,... | collective-permute-start | bytes 2359304 | tf_op jit(solution)/shard_map/ppermute | solution.py:882
  289.4 15.1 %collective-permute-start.12 = (bf16[512,384]{1,0:T(8,128)(2,1)S(1)}, bf16[512,384]{1,0:T(8,128)(2,1)S(1)}, u32[]{:S(2)}, u32[]{:S(2)}) collective-permute-start(bf16[512,384]{1,0:T(8,128)(2,1)S(1)} %copy-done.25), channel_id=1, source_target_pairs={{4,0},{5,1},{6,2},{7,3},{12,8},{13,9},{14,10},{15,11},{20,16},{21,... | collective-permute-start | bytes 1179656 | tf_op jit(solution)/shard_map/ppermute | solution.py:882
  291.8 52.0 %collective-permute-start.20 = (bf16[512,768]{1,0:T(8,128)(2,1)}, bf16[512,768]{1,0:T(8,128)(2,1)}, u32[]{:S(2)}, u32[]{:S(2)}) collective-permute-start(bf16[512,768]{1,0:T(8,128)(2,1)} %broadcast_select_fusion), channel_id=1, source_target_pairs={{0,1},{1,0},{2,3},{3,2},{4,5},{5,4},{6,7},{7,6},{8,9},{9,8},{10,11... | collective-permute-start | bytes 2359304 | tf_op jit(solution)/shard_map/ppermute | solution.py:725
  309.8 11.2 %copy-start.14 = (f32[8,768]{1,0:T(8,128)S(1)}, f32[8,768]{1,0:T(8,128)}, u32[]{:S(2)}) copy-start(f32[8,768]{1,0:T(8,128)} %get-tuple-element.119) | copy-start | bytes 73732
  309.8 11.2 %copy-start.15 = (f32[8,768]{1,0:T(8,128)S(1)}, f32[8,768]{1,0:T(8,128)}, u32[]{:S(2)}) copy-start(f32[8,768]{1,0:T(8,128)} %get-tuple-element.120) | copy-start | bytes 73732
  309.8 11.2 %copy-start.16 = (f32[8,768]{1,0:T(8,128)S(1)}, f32[8,768]{1,0:T(8,128)}, u32[]{:S(2)}) copy-start(f32[8,768]{1,0:T(8,128)} %get-tuple-element.121) | copy-start | bytes 73732
  309.8 11.3 %copy-start.3 = (bf16[512,768]{1,0:T(8,128)(2,1)S(1)}, bf16[512,768]{1,0:T(8,128)(2,1)}, u32[]{:S(2)}) copy-start(bf16[512,768]{1,0:T(8,128)(2,1)} %get-tuple-element.107.refs_9_) | copy-start | bytes 2359300
  319.7 10.0 %collective-permute-start.13 = (bf16[512,384]{1,0:T(8,128)(2,1)}, bf16[512,384]{1,0:T(8,128)(2,1)}, u32[]{:S(2)}, u32[]{:S(2)}) collective-permute-start(bf16[512,384]{1,0:T(8,128)(2,1)} %get-tuple-element.110), channel_id=1, source_target_pairs={{4,0},{5,1},{6,2},{7,3},{12,8},{13,9},{14,10},{15,11},{20,16},{21,... | collective-permute-start | bytes 1179656 | tf_op jit(solution)/shard_map/ppermute | solution.py:882
  321.9 35.1 %collective-permute-start.17 = (bf16[256,768]{1,0:T(8,128)(2,1)}, bf16[256,768]{1,0:T(8,128)(2,1)}, u32[]{:S(2)}, u32[]{:S(2)}) collective-permute-start(bf16[256,768]{1,0:T(8,128)(2,1)} %broadcast_select_fusion.1), channel_id=1, source_target_pairs={{0,1},{1,0},{2,3},{3,2},{4,5},{5,4},{6,7},{7,6},{8,9},{9,8},{10,11... | collective-permute-start | bytes 1179656 | tf_op jit(solution)/shard_map/ppermute | solution.py:725
  340.3 5.2 %copy-start.13 = (f32[8,640]{1,0:T(8,128)S(1)}, f32[8,640]{1,0:T(8,128)}, u32[]{:S(2)}) copy-start(f32[8,640]{1,0:T(8,128)} %get-tuple-element.122) | copy-start | bytes 61444
  340.3 5.8 %copy-start.4 = (bf16[512,768]{1,0:T(8,128)(2,1)S(1)}, bf16[512,768]{1,0:T(8,128)(2,1)}, u32[]{:S(2)}) copy-start(bf16[512,768]{1,0:T(8,128)(2,1)} %get-tuple-element.112.refs_0_) | copy-start | bytes 2359300
  341.1 4.4 collective-permute-start.27
  342.2 18.8 %copy-start = (bf16[768,640]{1,0:T(8,128)(2,1)S(1)}, bf16[768,640]{1,0:T(8,128)(2,1)}, u32[]{:S(2)}) copy-start(bf16[768,640]{1,0:T(8,128)(2,1)} %get-tuple-element.116.refs_0_.refs_1_) | copy-start | bytes 2949124
  342.2 18.8 %collective-permute-start.23 = (bf16[2,192,640]{2,1,0:T(8,128)(2,1)S(1)}, bf16[2,192,640]{2,1,0:T(8,128)(2,1)S(1)}, u32[]{:S(2)}, u32[]{:S(2)}) collective-permute-start(bf16[2,192,640]{2,1,0:T(8,128)(2,1)S(1)} %dynamic-slice_bitcast_fusion), channel_id=1, source_target_pairs={{0,16},{16,0},{8,24},{24,8},{1,17},{17,1},{9,25},{25,9},{2,18},{18... | collective-permute-start | bytes 1474568 | tf_op jit(solution)/shard_map/ppermute | solution.py:742
  345.5 11.3 %collective-permute-start.28 = (f32[8,1408]{1,0:T(8,128)S(1)}, f32[8,1408]{1,0:T(8,128)S(1)}, u32[]{:S(2)}, u32[]{:S(2)}) collective-permute-start(f32[8,1408]{1,0:T(8,128)S(1)} %fusion), channel_id=1, source_target_pairs={{0,16},{16,0},{8,24},{24,8},{1,17},{17,1},{9,25},{25,9},{2,18},{18... | collective-permute-start | bytes 135176 | tf_op jit(solution)/shard_map/ppermute | solution.py:751
  346.2 53.3 %collective-permute-start.21 = (bf16[512,768]{1,0:T(8,128)(2,1)S(1)}, bf16[512,768]{1,0:T(8,128)(2,1)S(1)}, u32[]{:S(2)}, u32[]{:S(2)}) collective-permute-start(bf16[512,768]{1,0:T(8,128)(2,1)S(1)} %select_add_fusion), channel_id=1, source_target_pairs={{0,2},{2,0},{1,3},{3,1},{4,6},{6,4},{5,7},{7,5},{8,10},{10,8},{9,1... | collective-permute-start | bytes 2359304 | tf_op jit(solution)/shard_map/ppermute | solution.py:727
  346.2 26.4 %collective-permute-start.14 = (bf16[256,768]{1,0:T(8,128)(2,1)S(1)}, bf16[256,768]{1,0:T(8,128)(2,1)S(1)}, u32[]{:S(2)}, u32[]{:S(2)}) collective-permute-start(bf16[256,768]{1,0:T(8,128)(2,1)S(1)} %broadcast_select_fusion.2), channel_id=1, source_target_pairs={{0,1},{1,0},{2,3},{3,2},{4,5},{5,4},{6,7},{7,6},{8,9},{9,8},{10,11... | collective-permute-start | bytes 1179656 | tf_op jit(solution)/shard_map/ppermute | solution.py:725
  356.9 4.1 collective-permute-start.29
  358.0 50.1 %collective-permute-start.18 = (bf16[256,768]{1,0:T(8,128)(2,1)S(1)}, bf16[256,768]{1,0:T(8,128)(2,1)}, u32[]{:S(2)}, u32[]{:S(2)}) collective-permute-start(bf16[256,768]{1,0:T(8,128)(2,1)S(1)} %select_add_fusion.1), channel_id=1, source_target_pairs={{0,2},{2,0},{1,3},{3,1},{4,6},{6,4},{5,7},{7,5},{8,10},{10,8},{9,1... | collective-permute-start | bytes 1179656 | tf_op jit(solution)/shard_map/ppermute | solution.py:727
  361.1 14.4 %collective-permute-start.24 = (bf16[192,640]{1,0:T(8,128)(2,1)S(1)}, bf16[192,640]{1,0:T(8,128)(2,1)S(1)}, u32[]{:S(2)}, u32[]{:S(2)}) collective-permute-start(bf16[192,640]{1,0:T(8,128)(2,1)S(1)} %dynamic-slice_bitcast_fusion.1), channel_id=1, source_target_pairs={{0,8},{8,0},{16,24},{24,16},{1,9},{9,1},{17,25},{25,17},{2,10},{10... | collective-permute-start | bytes 737288 | tf_op jit(solution)/shard_map/ppermute | solution.py:745
  372.7 43.6 %collective-permute-start.15 = (bf16[256,768]{1,0:T(8,128)(2,1)S(1)}, bf16[256,768]{1,0:T(8,128)(2,1)S(1)}, u32[]{:S(2)}, u32[]{:S(2)}) collective-permute-start(bf16[256,768]{1,0:T(8,128)(2,1)S(1)} %select_add_fusion.2), channel_id=1, source_target_pairs={{0,2},{2,0},{1,3},{3,1},{4,6},{6,4},{5,7},{7,5},{8,10},{10,8},{9,1... | collective-permute-start | bytes 1179656 | tf_op jit(solution)/shard_map/ppermute | solution.py:727
  375.6 41.6 %collective-permute-start.25 = (bf16[192,640]{1,0:T(8,128)(2,1)S(1)}, bf16[192,640]{1,0:T(8,128)(2,1)S(1)}, u32[]{:S(2)}, u32[]{:S(2)}) collective-permute-start(bf16[192,640]{1,0:T(8,128)(2,1)S(1)} %bitcast_add_fusion.1), channel_id=1, source_target_pairs={{0,4},{4,0},{1,5},{5,1},{2,6},{6,2},{3,7},{7,3},{8,12},{12,8},{9,1... | collective-permute-start | bytes 737288 | tf_op jit(solution)/shard_map/ppermute | solution.py:733
  399.6 34.4 %copy-start.5 = (bf16[512,768]{1,0:T(8,128)(2,1)}, bf16[512,768]{1,0:T(8,128)(2,1)S(1)}, u32[]{:S(2)}) copy-start(bf16[512,768]{1,0:T(8,128)(2,1)S(1)} %add.78.done_ref) | copy-start | bytes 2359300
  399.7 33.5 %collective-permute-start.22 = (bf16[512,768]{1,0:T(8,128)(2,1)S(1)}, bf16[512,768]{1,0:T(8,128)(2,1)S(1)}, u32[]{:S(2)}, u32[]{:S(2)}) collective-permute-start(bf16[512,768]{1,0:T(8,128)(2,1)S(1)} %add.78.done_ref), channel_id=1, source_target_pairs={{0,1},{1,0},{2,3},{3,2},{4,5},{5,4},{6,7},{7,6},{8,9},{9,8},{10,11... | collective-permute-start | bytes 2359304 | tf_op jit(solution)/shard_map/ppermute | solution.py:728
  399.8 53.7 %collective-permute-start.26 = (bf16[192,1728]{1,0:T(8,128)(2,1)}, bf16[192,1728]{1,0:T(8,128)(2,1)}, u32[]{:S(2)}, u32[]{:S(2)}) collective-permute-start(bf16[192,1728]{1,0:T(8,128)(2,1)} %reduce-scatter.2.cloned.1.call-done), channel_id=1, source_target_pairs={{0,4},{4,0},{1,5},{5,1},{2,6},{6,2},{3,7},{7,3},{8,12},{12,8},{9,1... | collective-permute-start | bytes 1990664 | tf_op jit(solution)/shard_map/ppermute | solution.py:733
  409.9 31.8 %collective-permute-start.19 = (bf16[256,768]{1,0:T(8,128)(2,1)}, bf16[256,768]{1,0:T(8,128)(2,1)}, u32[]{:S(2)}, u32[]{:S(2)}) collective-permute-start(bf16[256,768]{1,0:T(8,128)(2,1)} %add.76.done_ref), channel_id=1, source_target_pairs={{0,1},{1,0},{2,3},{3,2},{4,5},{5,4},{6,7},{7,6},{8,9},{9,8},{10,11... | collective-permute-start | bytes 1179656 | tf_op jit(solution)/shard_map/ppermute | solution.py:728
  417.1 32.9 %collective-permute-start.16 = (bf16[256,768]{1,0:T(8,128)(2,1)}, bf16[256,768]{1,0:T(8,128)(2,1)}, u32[]{:S(2)}, u32[]{:S(2)}) collective-permute-start(bf16[256,768]{1,0:T(8,128)(2,1)} %add.74.done_ref), channel_id=1, source_target_pairs={{0,1},{1,0},{2,3},{3,2},{4,5},{5,4},{6,7},{7,6},{8,9},{9,8},{10,11... | collective-permute-start | bytes 1179656 | tf_op jit(solution)/shard_map/ppermute | solution.py:728
  (10 other events, 13.7 us)
Sparse Core Ops, SparseCore 0:
  10.9 124.8 all-gather.4
  288.6 41.3 reduce-scatter.1

commit v3 on v2

--- a/solution.py
+++ b/solution.py
@@ -17,6 +17,8 @@
 SWAP = ((0, 1), (1, 0), (2, 3), (3, 2))
 FAR = ((0, 2), (2, 0), (1, 3), (3, 1))
 ACROSS = ((0, 3), (3, 0), (1, 2), (2, 1))
+MIDDLE = ((1, 2), (2, 1))
+OUTWARD = ((1, 0), (2, 3))
 
 
 def params(**kw):
@@ -134,15 +136,17 @@
 def attn_fwd_kernel(ids, *refs, heads, size, nkv):
     q_ref, prev_ref = refs[0], refs[1]
     kv_refs = refs[2 : 2 + nkv]
+    bias_ref = refs[2 + nkv]
     log_ref, e_ref, att_ref, sum_ref, k3, v3 = refs[-6:]
     i, rb = pl.program_id(0), pl.program_id(1)
-    blocks = pl.num_programs(1)
     full = prev_ref.shape[3]
+    blocks = (att_ref.shape[0] - bias_ref.shape[0]) // BLOCK
     width = heads * size
 
     @pl.when(rb == 0)
     def _():
         spread_heads(ids, kv_refs, k3, v3, heads, size)
+        att_ref[blocks * BLOCK :] = bias_ref[...]
 
     g = ids[1] * blocks + rb
     for b in range(full // BLOCK):
@@ -186,7 +190,7 @@
     return specs
 
 
-def attn_fwd_call(ids, q, kvs, prev, first, count, chain, heads, size, after):
+def attn_fwd_call(ids, q, kvs, prev, bias, first, count, chain, heads, size, after):
     seqs, _, rows, full = prev.shape
     width = heads * size
     blocks = rows // BLOCK
@@ -198,7 +202,7 @@
         out_shape=(
             jax.ShapeDtypeStruct(prev.shape, BF),
             jax.ShapeDtypeStruct((count, heads, rows, full), BF),
-            jax.ShapeDtypeStruct((rows, count * width), BF),
+            jax.ShapeDtypeStruct((rows + bias.shape[0], count * width), BF),
             jax.ShapeDtypeStruct((count * rows, 128), F32),
         ),
         grid_spec=pltpu.PrefetchScalarGridSpec(
@@ -206,11 +210,12 @@
             grid=(count, blocks),
             in_specs=[pl.BlockSpec((BLOCK, width), lambda i, r, s: (i * blocks + r, 0)), big]
             + kv_specs(kvs, count)
+            + [pl.BlockSpec(bias.shape, lambda i, r, s: (0, 0))]
             + [ANY] * len(extra),
             out_specs=[
                 big,
                 pl.BlockSpec((1, heads, BLOCK, full), lambda i, r, s: (i, 0, r, 0)),
-                pl.BlockSpec((rows, count * width), lambda i, r, s: (0, 0)),
+                pl.BlockSpec((rows + bias.shape[0], count * width), lambda i, r, s: (0, 0)),
                 pl.BlockSpec((BLOCK, 128), lambda i, r, s: (i * blocks + r, 0)),
             ],
             scratch_shapes=[
@@ -218,7 +223,7 @@
                 pltpu.VMEM((heads, full, 256), BF),
             ],
         ),
-        input_output_aliases={} if chain is None else {3 + len(kvs): 0},
+        input_output_aliases={} if chain is None else {4 + len(kvs): 0},
         compiler_params=params(),
         cost_estimate=pl.CostEstimate(
             flops=4 * 4 * count * heads * rows * tokens * size,
@@ -226,7 +231,7 @@
             transcendentals=count * heads * rows * tokens,
         ),
         name="attn_fwd",
-    )(ids, q, prev, *kvs, *extra)
+    )(ids, q, prev, *kvs, bias, *extra)
 
 
 def attn_bwd_kernel(ids, *refs, heads, size, nkv, local, scale):
@@ -339,7 +344,7 @@
                 tile(width, base),
                 pl.BlockSpec((1, heads, BLOCK, full), lambda i, r, s: (base + i, 0, r, 0)),
                 big,
-                tile(width, 0),
+                tile(width, base),
                 pl.BlockSpec((BLOCK, of * width), lambda i, r, s: (r, 0)),
                 tile(128, base),
             ]
@@ -355,11 +360,7 @@
         ),
         input_output_aliases={} if chain is None else {7 + len(kvs): 0},
         compiler_params=params(),
-        cost_estimate=pl.CostEstimate(
-            flops=4 * 8 * count * heads * rows * tokens * size,
-            bytes_accessed=6 * count * heads * rows * full,
-            transcendentals=0,
-        ),
+        cost_estimate=pl.CostEstimate(flops=9000000000, bytes_accessed=1000, transcendentals=0),
         name="attn_bwd",
     )(ids, q, e, d_logits, datt, att, inverse, *kvs, *extra)
 
@@ -373,33 +374,35 @@
 
 
 def ffn_kernel(ids, *refs, chained, final, base, width, units):
-    x_ref, a0, a1, a2, a3, do_ref, vec_ref, bin_ref, w_all = refs[:9]
+    x_ref, a0, a1, a2, a3, do_ref, vec_ref, b0, b1, b2, b3 = refs[:11]
+    pieces = refs[11:15]
     if chained:
-        gi_in, go_in, gw_in = refs[9:12]
+        gi_in, go_in, gw_in = refs[15:18]
     if final:
-        out_ref, dh1_ref, datt_ref, sum_ref, grad_ref = refs[-17:-12]
+        out_ref, dh1_ref, datt_ref, sum_ref, grad_ref = refs[-18:-13]
     else:
-        out_ref, dh1_ref, datt_ref, sum_ref, gi_hbm, go_hbm, gw_hbm = refs[-19:-12]
-    wi, wo, wa, act_s, gp_s, din_s, att_s, gi, go, gw, w_sem, g_sem = refs[-12:]
+        out_ref, dh1_ref, datt_ref, sum_ref, gi_hbm, go_hbm, gw_hbm = refs[-20:-13]
+    wi, wo, wa, act_s, gp_s, din_s, att_s, gi, go, gw, bin_s, w_sem, g_sem = refs[-13:]
     i, j = pl.program_id(0), pl.program_id(1)
     start = (i == 0) & (j == 0)
     last = (i == pl.num_programs(0) - 1) & (j == pl.num_programs(1) - 1)
     rank = ids[2]
-    rows = w_all.shape[1]
+    rows = pieces[0].shape[1]
 
     def copies(group):
         out = []
-        for f in range(4):
-            for t in range(4):
-                piece = w_all.at[f * 4 + t]
-                at = slice(f * rows, (f + 1) * rows)
-                sem = w_sem.at[group, f * 4 + t]
+        for k in range(4):
+            at = pl.ds(pl.multiple_of((ids[0] ^ k) * rows, rows), rows)
+            for slot in range(4):
+                piece = pieces[k].at[slot]
+                sem = w_sem.at[group, k * 4 + slot]
                 if group == 0:
-                    src, dst = piece.at[:, 2 * units : 2 * units + width], wa.at[t, at]
+                    src, dst = piece.at[:, 2 * units : 2 * units + width], wa
                 elif group == 1:
-                    src, dst = piece.at[:, :units], wi.at[t, at]
+                    src, dst = piece.at[:, :units], wi
                 else:
-                    src, dst = piece.at[:, units : 2 * units], wo.at[t, at]
+                    src, dst = piece.at[:, units : 2 * units], wo
+                dst = dst.at[rank ^ slot, at]
                 out.append(pltpu.make_async_copy(src, dst, sem))
         return out
 
@@ -422,24 +425,36 @@
             go[...] = jnp.zeros_like(go)
             gw[...] = jnp.zeros_like(gw)
         sum_ref[...] = jnp.zeros_like(sum_ref)
+        for slot, b in enumerate((b0, b1, b2, b3)):
+            value = b[...].astype(F32)
+            left = value[0:1] + value[2:3] + value[4:5]
+            right = value[1:2] + value[3:4] + value[5:6]
+            bin_s[rank ^ slot] = jnp.concatenate([left, right], axis=1)
         for c in copies(0):
             c.wait()
 
     chunk = a0.shape[1] // width
-    for slot, a in enumerate((a0, a1, a2, a3)):
-        value = a[:, base * width : (base + 1) * width]
-        if chunk > base + 1:
-            value = jnp.where(i == 0, value, a[:, (base + 1) * width :])
-        att_s[rank ^ slot] = value
     b_out, gain_a, shift_a = vec_ref[0:1], vec_ref[1:2], vec_ref[2:3]
     b_outer, gain_f, shift_f = vec_ref[3:4], vec_ref[4:5], vec_ref[5:6]
-    h1 = x_ref[0].astype(F32) + b_out
-    for t in range(4):
-        h1 = h1 + dot_nt(att_s[t], wa[t])
-    c1 = h1 - row_mean(h1)
-    r1 = lax.rsqrt(row_mean(c1 * c1) + EPS)
-    n1 = c1 * r1
-    normed = (n1 * gain_a + shift_a).astype(BF)
+    half = x_ref.shape[1] // 2
+    parts = [slice(0, half), slice(half, 2 * half)]
+    n1, r1, normed, n2, r2 = [None] * 2, [None] * 2, [None] * 2, [None] * 2, [None] * 2
+    h2, dn, dh2_low, dh1_low = [None] * 2, [None] * 2, [None] * 2, [None] * 2
+
+    for p in range(2):
+        for slot, a in enumerate((a0, a1, a2, a3)):
+            value = a[parts[p], base * width : (base + 1) * width]
+            if chunk > base + 1:
+                value = jnp.where(i == 0, value, a[parts[p], (base + 1) * width :])
+            att_s[rank ^ slot, parts[p]] = value
+    for p in range(2):
+        h1 = x_ref[0, parts[p]].astype(F32) + b_out
+        for t in range(4):
+            h1 = h1 + dot_nt(att_s[t, parts[p]], wa[t])
+        c1 = h1 - row_mean(h1)
+        r1[p] = lax.rsqrt(row_mean(c1 * c1) + EPS)
+        n1[p] = c1 * r1[p]
+        normed[p] = (n1[p] * gain_a + shift_a).astype(BF)
 
     @pl.when(start)
     def _():
@@ -451,44 +466,60 @@
             for c in grad_in():
                 c.wait()
 
-    h2 = normed.astype(F32) + b_outer
-    for t in range(4):
-        inner = dot(normed, wi[t]) + bin_ref[t : t + 1]
-        act, slope = gelu_parts(inner)
-        low = act.astype(BF)
-        act_s[t] = low
-        gp_s[t] = slope.astype(BF)
-        h2 = h2 + dot_nt(low, wo[t])
-    c2 = h2 - row_mean(h2)
-    r2 = lax.rsqrt(row_mean(c2 * c2) + EPS)
-    n2 = c2 * r2
-    out_ref[0] = (n2 * gain_f + shift_f).astype(BF)
-    d_out = do_ref[0].astype(F32)
-    e2 = d_out * gain_f
-    dh2 = (e2 - row_mean(e2) - n2 * row_mean(e2 * n2)) * r2
-    dh2_low = dh2.astype(BF)
-    dn = dh2
-    for t in range(4):
-        din = dot(dh2_low, wo[t]) * gp_s[t].astype(F32)
-        low = din.astype(BF)
-        din_s[t] = low
-        dn = dn + dot_nt(low, wi[t])
-    e1 = dn * gain_a
-    dh1 = (e1 - row_mean(e1) - n1 * row_mean(e1 * n1)) * r1
-    dh1_ref[...] = dh1
-    dh1_low = dh1.astype(BF)
-    datt_ref[...] = dot(dh1_low, wa[rank]).astype(BF)
-    din_own = din_s[rank]
-    sum_ref[0:1] += col_sum(dh1)
-    sum_ref[1:2] += col_sum(dn * n1)
-    sum_ref[2:3] += col_sum(dn)
-    sum_ref[3:4] += col_sum(dh2)
-    sum_ref[4:5] += col_sum(d_out * n2)
-    sum_ref[5:6] += col_sum(d_out)
-    sum_ref[6:7] += col_sum(din_own.astype(F32))
-    gi[...] += dot(normed.T, din_own)
-    go[...] += dot(dh2_low.T, act_s[rank])
-    gw[...] += dot(dh1_low.T, att_s[rank])
+    def forward(p):
+        h2[p] = normed[p].astype(F32) + b_outer
+        for t in range(4):
+            inner = dot(normed[p], wi[t]) + bin_s[t]
+            act, slope = gelu_parts(inner)
+            low = act.astype(BF)
+            act_s[t, parts[p]] = low
+            gp_s[t, parts[p]] = slope.astype(BF)
+            h2[p] = h2[p] + dot_nt(low, wo[t])
+
+    def turn(p):
+        c2 = h2[p] - row_mean(h2[p])
+        r2[p] = lax.rsqrt(row_mean(c2 * c2) + EPS)
+        n2[p] = c2 * r2[p]
+        out_ref[0, parts[p]] = (n2[p] * gain_f + shift_f).astype(BF)
+        d_out = do_ref[0, parts[p]].astype(F32)
+        e2 = d_out * gain_f
+        dh2 = (e2 - row_mean(e2) - n2[p] * row_mean(e2 * n2[p])) * r2[p]
+        sum_ref[3:4] += col_sum(dh2)
+        sum_ref[4:5] += col_sum(d_out * n2[p])
+        sum_ref[5:6] += col_sum(d_out)
+        dh2_low[p] = dh2.astype(BF)
+        dn[p] = dh2
+
+    def backward(p):
+        for t in range(4):
+            din = dot(dh2_low[p], wo[t]) * gp_s[t, parts[p]].astype(F32)
+            low = din.astype(BF)
+            din_s[t, parts[p]] = low
+            dn[p] = dn[p] + dot_nt(low, wi[t])
+
+    def close(p):
+        e1 = dn[p] * gain_a
+        dh1 = (e1 - row_mean(e1) - n1[p] * row_mean(e1 * n1[p])) * r1[p]
+        dh1_ref[parts[p]] = dh1
+        dh1_low[p] = dh1.astype(BF)
+        sum_ref[0:1] += col_sum(dh1)
+        sum_ref[1:2] += col_sum(dn[p] * n1[p])
+        sum_ref[2:3] += col_sum(dn[p])
+
+    forward(0)
+    turn(0)
+    forward(1)
+    backward(0)
+    turn(1)
+    close(0)
+    backward(1)
+    datt_ref[parts[0]] = dot(dh1_low[0], wa[rank]).astype(BF)
+    close(1)
+    gi[...] += dot(jnp.concatenate(normed, axis=0).T, din_s[rank])
+    go[...] += dot(jnp.concatenate(dh2_low, axis=0).T, act_s[rank])
+    datt_ref[parts[1]] = dot(dh1_low[1], wa[rank]).astype(BF)
+    gw[...] += dot(jnp.concatenate(dh1_low, axis=0).T, att_s[rank])
+    sum_ref[6:7] += col_sum(din_s[rank].astype(F32))
 
     @pl.when(last)
     def _():
@@ -508,10 +539,10 @@
 
 
 def ffn_call(
-    ids, hidden, atts, d_output, vec, b_inner, w_all, first, base, count, chain, width, units, final, after
+    ids, hidden, atts, d_output, vec, bias, weights, first, base, count, chain, width, units, final, after
 ):
     seqs, rows, d = hidden.shape
-    tile = min(rows, 256)
+    tile = min(rows, 512)
     tiles = rows // tile
     chunk = atts[0].shape[1]
     whole = pl.BlockSpec((1, tile, d), lambda i, j, s: (first + i, j, 0))
@@ -520,7 +551,7 @@
     fixed = lambda shape: pl.BlockSpec(shape, lambda i, j, s: (0, 0))
     chained = [] if chain is None else list(chain)
     extra = chained + list(after)
-    at = 1 + 9
+    at = 1 + 11 + 4
     aliases = {}
     if chained:
         aliases = {at + 3: 0} if final else {at: 4, at + 1: 5, at + 2: 6, at + 3: 0}
@@ -547,8 +578,9 @@
         grid_spec=pltpu.PrefetchScalarGridSpec(
             num_scalar_prefetch=1,
             grid=(count, tiles),
-            in_specs=[whole, att, att, att, att, whole, fixed((8, d)), fixed((4, units)), ANY]
-            + [ANY] * len(extra),
+            in_specs=[whole, att, att, att, att, whole, fixed((8, d))]
+            + [pl.BlockSpec((16, chunk), lambda i, j, s: (rows // 16, 0))] * 4
+            + [ANY] * (4 + len(extra)),
             out_specs=[whole, flat(d), flat(width), fixed((8, d))]
             + ([fixed((d, 2 * units + width))] if final else [ANY] * 3),
             scratch_shapes=[
@@ -562,6 +594,7 @@
                 pltpu.VMEM((d, units), F32),
                 pltpu.VMEM((d, units), F32),
                 pltpu.VMEM((d, width), F32),
+                pltpu.VMEM((4, 1, units), F32),
                 pltpu.SemaphoreType.DMA((3, 16)),
                 pltpu.SemaphoreType.DMA((3,)),
             ],
@@ -574,13 +607,13 @@
             transcendentals=8 * count * rows * units,
         ),
         name="ffn",
-    )(ids, hidden, *atts, d_output, vec, b_inner, w_all, *extra)
+    )(ids, hidden, *atts, d_output, vec, *bias, *weights, *extra)
 
 
 def dx_kernel(ids, dq_ref, *refs, nkv):
     dkv_refs = refs[:nkv]
     w_ref = refs[nkv]
-    y_ref, joined_ref = refs[-2:]
+    y_ref, joined_ref, sum_ref = refs[-3:]
     dq = dq_ref[...]
     dkv = dkv_refs[0][...]
     if nkv == 2:
@@ -588,6 +621,12 @@
     pad = jnp.zeros((dq.shape[0], 256 - dq.shape[1]), BF)
     joined = jnp.concatenate([dq, pad, dkv], axis=1)
     joined_ref[...] = joined
+
+    @pl.when(pl.program_id(0) == 0)
+    def _():
+        sum_ref[...] = jnp.zeros_like(sum_ref)
+
+    sum_ref[0:1] += col_sum(joined.astype(F32))
     y_ref[...] = dot_nt(joined, w_ref[...]).astype(BF)
 
 
@@ -603,6 +642,7 @@
         out_shape=(
             jax.ShapeDtypeStruct((count, d), BF),
             jax.ShapeDtypeStruct((tokens, cols), BF),
+            jax.ShapeDtypeStruct((8, cols), F32),
         ),
         grid_spec=pltpu.PrefetchScalarGridSpec(
             num_scalar_prefetch=1,
@@ -611,29 +651,29 @@
             + [flat(v.shape[1]) for v in dkvs]
             + [pl.BlockSpec((d, cols), lambda i, s: (0, 0))]
             + [ANY] * len(extra),
-            out_specs=[flat(d), pl.BlockSpec((tile, cols), lambda i, s: (offset + i, 0))],
+            out_specs=[
+                flat(d),
+                pl.BlockSpec((tile, cols), lambda i, s: (offset + i, 0)),
+                pl.BlockSpec((8, cols), lambda i, s: (0, 0)),
+            ],
         ),
         input_output_aliases={} if chain is None else {3 + len(dkvs): 1},
         compiler_params=params(),
-        cost_estimate=pl.CostEstimate(
-            flops=2 * count * d * cols, bytes_accessed=4 * d * cols, transcendentals=0
-        ),
+        cost_estimate=pl.CostEstimate(flops=3000000000, bytes_accessed=1000, transcendentals=0),
         name="dx",
     )(ids, dq, *dkvs, weight, *extra)
 
 
 def grad_kernel(x_ref, joined_ref, *refs):
-    g_ref, sum_ref, acc = refs[-3:]
+    g_ref, acc = refs[-2:]
     i = pl.program_id(0)
 
     @pl.when(i == 0)
     def _():
         acc[...] = jnp.zeros_like(acc)
-        sum_ref[...] = jnp.zeros_like(sum_ref)
 
     joined = joined_ref[...]
     acc[...] += dot(x_ref[0].T, joined)
-    sum_ref[0:1] += col_sum(joined.astype(F32))
 
     @pl.when(i == pl.num_programs(0) - 1)
     def _():
@@ -646,17 +686,14 @@
     fixed = lambda shape: pl.BlockSpec(shape, lambda i: (0, 0))
     return pl.pallas_call(
         grad_kernel,
-        out_shape=(
-            jax.ShapeDtypeStruct((d, cols), BF),
-            jax.ShapeDtypeStruct((8, cols), F32),
-        ),
+        out_shape=jax.ShapeDtypeStruct((d, cols), BF),
         grid=(seqs,),
         in_specs=[
             pl.BlockSpec((1, rows, d), lambda i: (i, 0, 0)),
             pl.BlockSpec((rows, cols), lambda i: (i, 0)),
         ]
         + [ANY] * len(after),
-        out_specs=[fixed((d, cols)), fixed((8, cols))],
+        out_specs=fixed((d, cols)),
         scratch_shapes=[pltpu.VMEM((d, cols), F32)],
         compiler_params=params(),
         cost_estimate=pl.CostEstimate(
@@ -673,6 +710,33 @@
     own = upper != odd
     both = jnp.where(own, done_ref[...].astype(F32), other_ref[...].astype(F32))
     out_ref[0] = dh1_ref[...] + both
+
+
+def plain_kernel(dh1_ref, total_ref, *refs):
+    refs[-1][0] = dh1_ref[...] + total_ref[...].astype(F32)
+
+
+def plain_call(dh1, at, total, first, rows, seqs, chain, after):
+    d = total.shape[1]
+    tile = min(rows, 256)
+    extra = ([] if chain is None else [chain]) + list(after)
+    return pl.pallas_call(
+        plain_kernel,
+        out_shape=jax.ShapeDtypeStruct((seqs, rows, d), F32),
+        grid=(rows // tile,),
+        in_specs=[
+            pl.BlockSpec((tile, d), lambda j: (at // tile + j, 0)),
+            pl.BlockSpec((tile, d), lambda j: (j, 0)),
+        ]
+        + [ANY] * len(extra),
+        out_specs=pl.BlockSpec((1, tile, d), lambda j: (first, j, 0)),
+        input_output_aliases={} if chain is None else {2: 0},
+        compiler_params=params(),
+        cost_estimate=pl.CostEstimate(
+            flops=2 * rows * d, bytes_accessed=10 * rows * d, transcendentals=0
+        ),
+        name="plain",
+    )(dh1, total, *extra)
 
 
 def final_call(ids, dh1, at, done, other, first, rows, seqs, chain, after):
@@ -722,10 +786,11 @@
 def tp_reduce(value, odd):
     half = value.shape[0] // 2
     top, bottom = value[:half], value[half:]
-    got = lax.ppermute(jnp.where(odd, top, bottom), "tp", SWAP)
+    sent = jnp.where(odd, top, bottom)
+    got = lax.ppermute(sent, "tp", SWAP)
     pair = jnp.where(odd, bottom, top) + got
     done = pair + lax.ppermute(pair, "tp", FAR)
-    return done, lax.ppermute(done, "tp", SWAP)
+    return sent, pair, done, lax.ppermute(done, "tp", SWAP)
 
 
 def ctx_sum(value, size):
@@ -734,16 +799,29 @@
     return lax.psum(value, "ctx")
 
 
-def fsdp_scatter_sum(value, f, size):
+def fsdp_far_sum(value, f):
     rows = value.shape[0] // 4
     pairs = value.reshape(2, 2, rows, value.shape[1])
     mine = lax.dynamic_index_in_dim(pairs, f // 2, 0, keepdims=False)
     other = lax.dynamic_index_in_dim(pairs, 1 - f // 2, 0, keepdims=False)
-    mine = mine + lax.ppermute(other, "fsdp", FAR)
+    return mine + lax.ppermute(other, "fsdp", FAR)
+
+
+def fsdp_near_sum(mine, f, size):
     own = lax.dynamic_index_in_dim(mine, f % 2, 0, keepdims=False)
     near = lax.dynamic_index_in_dim(mine, 1 - f % 2, 0, keepdims=False)
     own = own + lax.ppermute(near, "fsdp", SWAP)
     return ctx_sum(own, size).astype(F32)
+
+
+def fsdp_direct_sum(value, f, size):
+    rows = value.shape[0] // 4
+    blocks = value.reshape(4, rows, value.shape[1])
+    pick = lambda k: lax.dynamic_index_in_dim(blocks, f ^ k, 0, keepdims=False)
+    total = pick(0).astype(F32)
+    for k, pairs in ((1, SWAP), (2, FAR), (3, ACROSS)):
+        total = total + lax.ppermute(pick(k), "fsdp", pairs).astype(F32)
+    return ctx_sum(total.astype(BF), size).astype(F32)
 
 
 def all_sum(value, size):
@@ -786,13 +864,16 @@
     odd = rank % 2 == 1
 
     ffn_local = jnp.concatenate([w_inner, w_outer, w_out], axis=1)
-    w_all = lax.all_gather(ffn_local, ("fsdp", "tp"), axis=0, tiled=False)
-    w_all = w_all.reshape(16, w_inner.shape[0], 2 * units + width)
-    bias_inner = lax.all_gather(b_inner, "tp", axis=0, tiled=False)
     qkv_local = jnp.concatenate(
         [w_query, jnp.zeros((w_query.shape[0], 256 - width), BF), w_key, w_value], axis=1
     )
     qkv_pieces = fsdp_gather(qkv_local)
+    inner_rank = (rank == 1) | (rank == 2)
+    w_near = lax.ppermute(ffn_local, "tp", SWAP)
+    w_across = lax.ppermute(ffn_local, "tp", MIDDLE)
+    far = lambda value: lax.ppermute(value, "fsdp", FAR)
+    own_local, _ = lax.optimization_barrier((ffn_local, qkv_pieces[2]))
+    w_far = [far(own_local)]
     qkv_bias = jnp.concatenate([b_query, jnp.zeros((256,), F32), b_value])[None]
     vec = jnp.stack([b_out, gain_attn, shift_attn, b_outer, gain_ffn, shift_ffn, b_out, b_out])
 
@@ -804,6 +885,13 @@
             ids, hidden_in, s, chunk, qkv_pieces, qkv_bias, width, scale, after
         )
         after = [q]
+        if s == 0:
+            w_near, w_across, w_far[0], _ = lax.optimization_barrier(
+                (w_near, w_across, w_far[0], q)
+            )
+            w_far.append(far(w_near))
+            w_middle = lax.ppermute(w_near, "tp", MIDDLE)
+            w_out_a = lax.ppermute(w_across, "tp", OUTWARD)
         queries.append(q)
         if ctx_size == 2:
             kvs.append((lax.ppermute(kv, "ctx", ((0, 1),)), kv))
@@ -811,20 +899,44 @@
             got = lax.all_gather(kv.reshape(chunk, rows, 2 * width), "ctx", axis=1, tiled=True)
             kvs.append((got.reshape(-1, 2 * width),))
 
+    w_two = jnp.where(inner_rank, w_middle, w_out_a)
+    w_far.append(far(w_two))
+    w_out_b = lax.ppermute(w_middle, "tp", OUTWARD)
+    after = after + [w_two]
+    high = lax.reduce_precision(b_inner, 8, 7)
+    middle = lax.reduce_precision(b_inner - high, 8, 7)
+    parts = jnp.stack([high, middle, b_inner - high - middle]).reshape(6, units // 2)
+    bias = jnp.pad(parts.astype(BF), ((0, 10), (0, 0)))
     logits, probs, atts, inverses = None, [], [], []
     for k, s in enumerate(starts):
         logits, e, att, inverse = attn_fwd_call(
-            ids, queries[k], kvs[k], prev_logits, s, chunk, logits, heads, size, after
+            ids, queries[k], kvs[k], prev_logits, bias, s, chunk, logits, heads, size, after
         )
         after = [att]
         probs.append(e)
-        atts.append(tp_gather(att))
+        if k == 0:
+            atts.append(tp_gather(att))
+        else:
+            every = lax.all_gather(att, "tp", axis=0, tiled=False)
+            atts.append([att] + [
+                lax.dynamic_index_in_dim(every, rank ^ slot, 0, keepdims=False)
+                for slot in range(1, 4)
+            ])
         inverses.append(inverse)
-
-    groups = [(0, chunk)] + [(s, 1) for s in range(chunk, seqs)]
-    chain, sums, dh1s, datts = None, [], {}, {}
+        if k == 0:
+            w_out_b, _ = lax.optimization_barrier((w_out_b, att))
+            w_three = jnp.where(inner_rank, w_across, w_out_b)
+            w_far.append(far(w_three))
+            w_here = jnp.stack([ffn_local, w_near, w_two, w_three])
+            w_there = lax.ppermute(w_here, "fsdp", SWAP)
+            after = after + [w_here]
+        else:
+            w_far, atts[0], _ = lax.optimization_barrier((w_far, atts[0], att))
+            w_far = jnp.stack(w_far)
+            weights = [w_here, w_there, w_far, lax.ppermute(w_far, "fsdp", SWAP)]
+
+    chain, sums, qkv_sums, dh1s, datts = None, [], [], {}, {}
     d_prev, d_hidden, joined = None, None, None
-    pending = []
 
     def ffn(s, count, after):
         nonlocal chain, grad_ffn, output
@@ -836,8 +948,8 @@
             atts[k],
             d_output,
             vec,
-            bias_inner,
-            w_all,
+            atts[0],
+            weights,
             s,
             base,
             count,
@@ -863,7 +975,7 @@
             queries[k],
             probs[k],
             d_logits,
-            datts[s],
+            datts[k * chunk],
             atts[k][0],
             inverses[k],
             kvs[k],
@@ -888,31 +1000,58 @@
 
     def dx(s, grads, after):
         nonlocal joined
-        y, joined = dx_call(
+        y, joined, part = dx_call(
             ids, grads[0], grads[1], w_qkv, s * rows, seqs * rows, joined, after
         )
-        return tp_reduce(y, odd), [y]
+        qkv_sums.append(part)
+        return y, [y]
+
+    def finish(s, after):
+        nonlocal d_hidden
+        k, at = s // chunk, (s % chunk) * rows
+        if not isinstance(reduced[s], tuple):
+            d_hidden = plain_call(
+                dh1s[k * chunk], at, reduced[s], s, rows, seqs, d_hidden, after
+            )
+            return [d_hidden]
+        _, _, done, other = reduced[s]
+        d_hidden = final_call(
+            ids, dh1s[k * chunk], at, done, other, s, rows, seqs, d_hidden, after
+        )
+        return [d_hidden]
 
     grad_ffn = output = None
-    held, reduced = None, []
-    for g, (s, count) in enumerate(groups):
-        after = ffn(s, count, after)
-        if held is not None:
-            done, after = dx(held[0], held[1], after)
-            reduced.append((held[0], done))
-        grads, after = attn_bwd(s, count, after)
-        held = (s, grads)
-    done, after = dx(held[0], held[1], after)
-    reduced.append((held[0], done))
-    g_qkv, qkv_sum = grad_call(hidden_in, joined, after)
-    for s, (done, other) in reduced:
-        d_hidden = final_call(ids, dh1s[s], 0, done, other, s, rows, seqs, d_hidden, [g_qkv])
-
-    small = jnp.concatenate([functools.reduce(jnp.add, sums), qkv_sum], axis=1)
+    held, reduced = {}, {}
+    ys, ffn_far = {}, None
+    for s in starts:
+        after = ffn(s, chunk, after)
+        last = s + chunk == seqs
+        if last:
+            ffn_far = fsdp_far_sum(grad_ffn, f)
+        for i in range(s, s + chunk):
+            if last and i == s > 0:
+                after = after + [reduced[0], reduced[1][1]]
+            held[i], after = attn_bwd(i, 1, after)
+        for i in range(s, s + chunk):
+            if last and i == s:
+                after = after + [reduced[1][2]]
+            if last and i == s + 1:
+                after = after + [ffn_far]
+            ys[i], after = dx(i, held[i], after)
+            if i == 0:
+                reduced[i] = lax.psum(ys[i], "tp")
+            else:
+                reduced[i] = tp_reduce(ys[i], odd)
+    after = after + [reduced[seqs - 2][1], reduced[seqs - 1][1]]
+    g_qkv = grad_call(hidden_in, joined, after)
+    for s in range(seqs):
+        finish(s, [g_qkv])
+
+    small = jnp.concatenate([functools.reduce(jnp.add, sums), functools.reduce(jnp.add, qkv_sums)], axis=1)
+    small, _ = lax.optimization_barrier((small, reduced[seqs - 2][2]))
     small = all_sum(small, ctx_size)
-    g_ffn = lax.psum_scatter(grad_ffn, "fsdp", scatter_dimension=0, tiled=True)
-    g_ffn = ctx_sum(g_ffn, ctx_size).astype(F32)
-    g_qkv = fsdp_scatter_sum(g_qkv, f, ctx_size)
+    g_ffn = fsdp_near_sum(ffn_far, f, ctx_size)
+    g_qkv = fsdp_direct_sum(g_qkv, f, ctx_size)
     return (
         output,
         logits,

time: 470 us -> 386 us (0.82)
  blocking collectives: 70.6 us -> 0 us
  waiting for transfers between devices: 118 us -> 63.4 us
  starting transfers between devices: 29.6 us -> 57.8 us
  other arithmetic: 14.4 us -> 29.6 us
  Pallas kernels: 203 us -> 192 us
  local copies, waits for them, and re-layouts: 12.7 us -> 23.1 us
    all_gather x1 -> x0, blocking collectives: 70.6 us -> none  [body(): bias_inner = lax.all_gather(b_inner, 'tp', axis=0, tiled=False)]
    ppermute x3, waiting for transfers between devices: 37.1 us -> 0.42 us  [tp_reduce(): done = pair + lax.ppermute(pair, 'tp', FAR)]
    ppermute x8 -> x22, starting transfers between devices: 4.01 us -> 25.5 us  [the longest x3 7.5 us: tp_reduce(): got = lax.ppermute(sent, 'tp', SWAP)]
    pallas_call x3 -> x2, Pallas kernels: 98.4 us -> 83.1 us  [ffn_call(): pl.pallas_call(functools.partial(ffn_kernel, chained=bool(chained), final...]
    ppermute x3 -> x4, waiting for transfers between devices: 20.6 us -> 8.77 us  [attn_bwd(): dkvs = (out[2], lax.ppermute(out[3], 'ctx', ((1, 0),)))]
    ppermute x6 -> x3, waiting for transfers between devices: 0.02 us -> 10.5 us  [tp_gather(): return [value] + [lax.ppermute(value, 'tp', p) for p in (SWAP, FAR, ACROSS)]]
    ppermute x2, waiting for transfers between devices: 9.57 us -> 1.21 us  [body(): kvs.append((lax.ppermute(kv, 'ctx', ((0, 1),)), kv))]
    ppermute x1, waiting for transfers between devices: 8.31 us -> 0.01 us  [all_sum(): value = value + lax.ppermute(value, 'fsdp', FAR)]
  transfers between devices with their start and end apart: 32 -> 44, of which waited for: 13 -> 14; matrix products, arithmetic and copies ran while one was open for 4% -> 11% of each run, Pallas kernels for 35% -> 49%
where the time goes in v3:
time: 386 us; the launch traced here: 381 us
  Pallas kernels  192 us (50%)
  waiting for transfers between devices  63.4 us (16%)
  starting transfers between devices  57.8 us (15%)
  other arithmetic  29.6 us (8%)
  local copies, waits for them, and re-layouts  23.1 us (6%)
  between operations  15 us (4%)
    pallas_call x2, Pallas kernels, ffn_call(): pl.pallas_call(functools.partial(ffn_kernel, chained=bool(chained), final...  83.1 us
    pallas_call x4, Pallas kernels, attn_bwd_call(): pl.pallas_call(functools.partial(attn_bwd_kernel, heads=heads, size=size,...  37.1 us
    pallas_call x2, Pallas kernels, attn_fwd_call(): pl.pallas_call(functools.partial(attn_fwd_kernel, heads=heads, size=size,...  23.5 us
    pallas_call x4, Pallas kernels, dx_call(): pl.pallas_call(functools.partial(dx_kernel, nkv=len(dkvs)), out_shape=(ja...  17 us
    pallas_call x2, Pallas kernels, qkv_call(): pl.pallas_call(functools.partial(qkv_kernel, scale=scale), out_shape=(jax...  12.6 us
    ppermute x3, waiting for transfers between devices, tp_reduce(): got = lax.ppermute(sent, 'tp', SWAP)  12.5 us
    ppermute x3, waiting for transfers between devices, tp_reduce(): return (sent, pair, done, lax.ppermute(done, 'tp', SWAP))  11 us
    ppermute x3, waiting for transfers between devices, tp_gather(): return [value] + [lax.ppermute(value, 'tp', p) for p in (SWAP, FAR, ACROSS)]  10.5 us
  transfers between devices with their start and end apart: 44, of which 14 were waited for; matrix products, arithmetic and copies ran while one was open for 11% of the time, Pallas kernels for 49%

profile of v3, /device:TPU:0, one launch (start us, length us, event | category | flops | bytes accessed | tf_op | source)
XLA Modules:
  0.0 381.2 jit_solution(15590457184132863770)
XLA Ops:
  8.4 3.0 collective-permute-start.1
  22.4 6.3 %qkv.2 = (bf16[1024,192]{1,0:T(8,128)(2,1)}, bf16[1024,384]{1,0:T(8,128)(2,1)}, bf16[768,640]{1,0:T(8,128)(2,1)}) custom-call(s32[3]{0:T(128)} %pad_add_fusion.ids, bf16[4,512,768]{2,1,0:T(8,128)(2,1)} %x_ref.5, bf16[192,640]{1,0:T(8,128)(2,1)} %copy-done.7, bf16[192,640]{1,0:T(8,128)(2,1)} %copy-done.12, bf16[192,640]{1,0:T(8,128)(2,1)} %copy-done.11, ...), custom_call_target="tpu_custom_call" | custom-call | flops 1006632960 | bytes 5046272 | tf_op jit(solution)/shard_map/qkv/pallas_call | solution.py:83
  28.7 2.7 collective-permute-done.5
  31.4 2.9 collective-permute-done.7
  37.1 4.3 %collective-permute-start.4 = (bf16[1024,384]{1,0:T(8,128)(2,1)}, bf16[1024,384]{1,0:T(8,128)(2,1)}, u32[]{:S(2)}, u32[]{:S(2)}) collective-permute-start(bf16[1024,384]{1,0:T(8,128)(2,1)} %get-tuple-element.89.refs_3_.refs_7_), channel_id=1, source_target_pairs={{0,4},{1,5},{2,6},{3,7},{8,12},{9,13},{10,14},{11,15},{16,20},{17,... | collective-permute-start | bytes 2359304 | tf_op jit(solution)/shard_map/ppermute | solution.py:897
  42.1 6.3 %qkv.3 = (bf16[1024,192]{1,0:T(8,128)(2,1)}, bf16[1024,384]{1,0:T(8,128)(2,1)}, bf16[768,640]{1,0:T(8,128)(2,1)}) custom-call(s32[3]{0:T(128)} %pad_add_fusion.ids, bf16[4,512,768]{2,1,0:T(8,128)(2,1)} %x_ref.5, bf16[192,640]{1,0:T(8,128)(2,1)} %copy-done.7, bf16[192,640]{1,0:T(8,128)(2,1)} %copy-done.12, bf16[192,640]{1,0:T(8,128)(2,1)} %copy-done.11, ...), custom_call_target="tpu_custom_call" | custom-call | flops 1006632960 | bytes 5046272 | tf_op jit(solution)/shard_map/qkv/pallas_call | solution.py:83
  52.4 2.6 collective-permute-done.9
  55.0 2.0 broadcast_select_fusion.1.refs_6_
  58.8 11.9 %attn_fwd.2 = (bf16[4,3,512,1024]{3,2,1,0:T(8,128)(2,1)}, bf16[2,3,512,1024]{3,2,1,0:T(8,128)(2,1)}, bf16[528,384]{1,0:T(8,128)(2,1)}, f32[1024,128]{1,0:T(8,128)}) custom-call(s32[3]{0:T(128)} %pad_add_fusion.ids, bf16[1024,192]{1,0:T(8,128)(2,1)} %get-tuple-element.86.refs_0_, bf16[4,3,512,1024]{3,2,1,0:T(8,128)(2,1)} %refs_1_.3, ...), custom_call_target="tpu_custom_call" | custom-call | flops 2415919104 | bytes 18874368 | tf_op jit(solution)/shard_map/attn_fwd/pallas_call | solution.py:200
  70.7 2.0 broadcast_select_fusion
  74.0 4.5 %collective-permute-start.14 = (bf16[528,384]{1,0:T(8,128)(2,1)}, bf16[528,384]{1,0:T(8,128)(2,1)}, u32[]{:S(2)}, u32[]{:S(2)}) collective-permute-start(bf16[528,384]{1,0:T(8,128)(2,1)} %get-tuple-element.98.refs_6_.refs_1_.refs_7_.refs_4_), channel_id=1, source_target_pairs={{0,1},{1,0},{2,3},{3,2},{4,5},{5,4},{6,7},{7,6},{8,9},{9,8},{10,11... | collective-permute-start | bytes 1216520 | tf_op jit(solution)/shard_map/ppermute | solution.py:777
  81.2 3.0 pad_maximum_fusion.refs_7_.refs_11_
  84.2 11.7 %attn_fwd.3 = (bf16[4,3,512,1024]{3,2,1,0:T(8,128)(2,1)}, bf16[2,3,512,1024]{3,2,1,0:T(8,128)(2,1)}, bf16[528,384]{1,0:T(8,128)(2,1)}, f32[1024,128]{1,0:T(8,128)}) custom-call(s32[3]{0:T(128)} %pad_add_fusion.ids, bf16[1024,192]{1,0:T(8,128)(2,1)} %get-tuple-element.87.refs_5_.refs_0_, ...), custom_call_target="tpu_custom_call", output_to_operand_aliasing={{0}: (6, {})} | custom-call | flops 2415919104 | bytes 18874368 | tf_op jit(solution)/shard_map/attn_fwd/pallas_call | solution.py:200
  96.0 10.5 %collective-permute-done.15.refs_3_.refs_9_ = bf16[528,384]{1,0:T(8,128)(2,1)} collective-permute-done((bf16[528,384]{1,0:T(8,128)(2,1)}, bf16[528,384]{1,0:T(8,128)(2,1)}, u32[]{:S(2)}, u32[]{:S(2)}) %collective-permute-start.15) | collective-permute-done | bytes 405536 | tf_op jit(solution)/shard_map/ppermute | solution.py:777
  106.6 1.9 pad_maximum_fusion.1.refs_13_
  111.0 4.4 %collective-permute-done.18.refs_14_ = bf16[4,192,1728]{2,1,0:T(8,128)(2,1)} collective-permute-done((bf16[4,192,1728]{2,1,0:T(8,128)(2,1)S(1)}, bf16[4,192,1728]{2,1,0:T(8,128)(2,1)}, u32[]{:S(2)}, u32[]{:S(2)}) %collective-permute-start.18) | collective-permute-done | bytes 2654240 | tf_op jit(solution)/shard_map/ppermute | solution.py:936
  115.3 41.0 %ffn.2 = (bf16[4,512,768]{2,1,0:T(8,128)(2,1)}, f32[1024,768]{1,0:T(8,128)}, bf16[1024,192]{1,0:T(8,128)(2,1)}, f32[8,768]{1,0:T(8,128)}, f32[768,768]{1,0:T(8,1...) custom-call(s32[3]{0:T(128)} %pad_add_fusion.ids, bf16[4,512,768]{2,1,0:T(8,128)(2,1)} %x_ref.5, ...), custom_call_target="tpu_custom_call" | custom-call | flops 24159191040 | bytes 22020096 | tf_op jit(solution)/shard_map/ffn/pallas_call | solution.py:567
  156.3 9.1 %attn_bwd.4 = (bf16[4,3,512,1024]{3,2,1,0:T(8,128)(2,1)}, bf16[512,192]{1,0:T(8,128)(2,1)}, bf16[512,384]{1,0:T(8,128)(2,1)}, bf16[512,384]{1,0:T(8,128)(2,1)}) custom-call(s32[3]{0:T(128)} %pad_add_fusion.ids, bf16[1024,192]{1,0:T(8,128)(2,1)} %get-tuple-element.86.refs_0_, bf16[2,3,512,1024]{3,2,1,0:T(8,128)(2,1)} %get-tuple-element.110.refs_1_, ...), custom_call_target="tpu_custom_call" | custom-call | flops 8999999488 | bytes 1000 | tf_op jit(solution)/shard_map/attn_bwd/pallas_call | solution.py:331
  166.8 9.3 %attn_bwd.5 = (bf16[4,3,512,1024]{3,2,1,0:T(8,128)(2,1)}, bf16[512,192]{1,0:T(8,128)(2,1)}, bf16[512,384]{1,0:T(8,128)(2,1)}, bf16[512,384]{1,0:T(8,128)(2,1)}) custom-call(s32[3]{0:T(128)} %pad_add_fusion.ids, bf16[1024,192]{1,0:T(8,128)(2,1)} %get-tuple-element.86.refs_0_, ...), custom_call_target="tpu_custom_call", output_to_operand_aliasing={{0}: (9, {})} | custom-call | flops 8999999488 | bytes 1000 | tf_op jit(solution)/shard_map/attn_bwd/pallas_call | solution.py:331
  177.4 2.3 dynamic-slice_bitcast_fusion.2
  181.9 4.2 %dx.4 = (bf16[512,768]{1,0:T(8,128)(2,1)}, bf16[2048,640]{1,0:T(8,128)(2,1)}, f32[8,640]{1,0:T(8,128)}) custom-call(s32[3]{0:T(128)} %pad_add_fusion.ids, bf16[512,192]{1,0:T(8,128)(2,1)} %get-tuple-element.114.refs_9_.dq_ref, bf16[512,384]{1,0:T(8,128)(2,1)} %get-tuple-element.119.refs_0_, bf16[512,384]{1,0:T(8,128)(2,1)} %copy-done.27, ...), custom_call_target="tpu_custom_call" | custom-call | flops 3000000000 | bytes 1000 | tf_op jit(solution)/shard_map/dx/pallas_call | solution.py:640
  186.1 7.3 %collective-permute-done.19.refs_1_ = bf16[512,384]{1,0:T(8,128)(2,1)S(1)} collective-permute-done((bf16[512,384]{1,0:T(8,128)(2,1)}, bf16[512,384]{1,0:T(8,128)(2,1)S(1)}, u32[]{:S(2)}, u32[]{:S(2)}) %collective-permute-start.19) | collective-permute-done | bytes 393248 | tf_op jit(solution)/shard_map/ppermute | solution.py:994
  194.1 4.2 %dx.5 = (bf16[512,768]{1,0:T(8,128)(2,1)}, bf16[2048,640]{1,0:T(8,128)(2,1)}, f32[8,640]{1,0:T(8,128)}) custom-call(s32[3]{0:T(128)} %pad_add_fusion.ids, bf16[512,192]{1,0:T(8,128)(2,1)} %get-tuple-element.115.refs_3_.dq_ref, bf16[512,384]{1,0:T(8,128)(2,1)} %get-tuple-element.116.refs_0_, ...), custom_call_target="tpu_custom_call", output_to_operand_aliasing={{1}: (5, {})} | custom-call | flops 3000000000 | bytes 1000 | tf_op jit(solution)/shard_map/dx/pallas_call | solution.py:640
  200.2 5.1 %collective-permute-start.21 = (bf16[256,768]{1,0:T(8,128)(2,1)S(1)}, bf16[256,768]{1,0:T(8,128)(2,1)S(1)}, u32[]{:S(2)}, u32[]{:S(2)}) collective-permute-start(bf16[256,768]{1,0:T(8,128)(2,1)S(1)} %broadcast_select_fusion.4), channel_id=1, source_target_pairs={{0,1},{1,0},{2,3},{3,2},{4,5},{5,4},{6,7},{7,6},{8,9},{9,8},{10,11... | collective-permute-start | bytes 1179656 | tf_op jit(solution)/shard_map/ppermute | solution.py:790
  205.3 42.1 %ffn.3 = (bf16[4,512,768]{2,1,0:T(8,128)(2,1)}, f32[1024,768]{1,0:T(8,128)}, bf16[1024,192]{1,0:T(8,128)(2,1)}, f32[8,768]{1,0:T(8,128)}, bf16[768,1728]{1,0:T(8,128)(2,1)}) custom-call(s32[3]{0:T(128)} %pad_add_fusion.ids, bf16[4,512,768]{2,1,0:T(8,128)(2,1)} %x_ref.5, ...), custom_call_target="tpu_custom_call", output_to_operand_aliasing={{0}: (19, {})} | custom-call | flops 24159191040 | bytes 22020096 | tf_op jit(solution)/shard_map/ffn/pallas_call | solution.py:567
  247.4 2.6 dynamic-slice_bitcast_fusion
  250.0 1.7 collective-permute-start.25
  253.3 9.1 %attn_bwd.6 = (bf16[4,3,512,1024]{3,2,1,0:T(8,128)(2,1)}, bf16[512,192]{1,0:T(8,128)(2,1)}, bf16[512,384]{1,0:T(8,128)(2,1)}, bf16[512,384]{1,0:T(8,128)(2,1)}) custom-call(s32[3]{0:T(128)} %pad_add_fusion.ids, bf16[1024,192]{1,0:T(8,128)(2,1)} %get-tuple-element.87.refs_5_.refs_0_, ...), custom_call_target="tpu_custom_call", output_to_operand_aliasing={{0}: (9, {})} | custom-call | flops 8999999488 | bytes 1000 | tf_op jit(solution)/shard_map/attn_bwd/pallas_call | solution.py:331
  263.7 9.5 %attn_bwd.7 = (bf16[4,3,512,1024]{3,2,1,0:T(8,128)(2,1)}, bf16[512,192]{1,0:T(8,128)(2,1)}, bf16[512,384]{1,0:T(8,128)(2,1)}, bf16[512,384]{1,0:T(8,128)(2,1)}) custom-call(s32[3]{0:T(128)} %pad_add_fusion.ids, bf16[1024,192]{1,0:T(8,128)(2,1)} %get-tuple-element.87.refs_5_.refs_0_, ...), custom_call_target="tpu_custom_call", output_to_operand_aliasing={{0}: (9, {})} | custom-call | flops 8999999488 | bytes 1000 | tf_op jit(solution)/shard_map/attn_bwd/pallas_call | solution.py:331
  275.6 2.1 collective-permute-start.32
  277.7 4.4 %dx.6 = (bf16[512,768]{1,0:T(8,128)(2,1)}, bf16[2048,640]{1,0:T(8,128)(2,1)}, f32[8,640]{1,0:T(8,128)}) custom-call(s32[3]{0:T(128)} %pad_add_fusion.ids, bf16[512,192]{1,0:T(8,128)(2,1)} %get-tuple-element.132.refs_9_.dq_ref, bf16[512,384]{1,0:T(8,128)(2,1)} %get-tuple-element.136.refs_0_, ...), custom_call_target="tpu_custom_call", output_to_operand_aliasing={{1}: (5, {})} | custom-call | flops 3000000000 | bytes 1000 | tf_op jit(solution)/shard_map/dx/pallas_call | solution.py:640
  284.0 1.9 bitcast_add_fusion.refs_5_
  288.0 4.3 %dx.7 = (bf16[512,768]{1,0:T(8,128)(2,1)}, bf16[2048,640]{1,0:T(8,128)(2,1)}, f32[8,640]{1,0:T(8,128)}) custom-call(s32[3]{0:T(128)} %pad_add_fusion.ids, bf16[512,192]{1,0:T(8,128)(2,1)} %get-tuple-element.133.refs_4_.dq_ref, bf16[512,384]{1,0:T(8,128)(2,1)} %get-tuple-element.134.refs_0_, ...), custom_call_target="tpu_custom_call", output_to_operand_aliasing={{1}: (5, {})} | custom-call | flops 3000000000 | bytes 1000 | tf_op jit(solution)/shard_map/dx/pallas_call | solution.py:640
  298.0 12.5 %collective-permute-done.26 = bf16[256,768]{1,0:T(8,128)(2,1)S(1)} collective-permute-done((bf16[256,768]{1,0:T(8,128)(2,1)S(1)}, bf16[256,768]{1,0:T(8,128)(2,1)S(1)}, u32[]{:S(2)}, u32[]{:S(2)}) %collective-permute-start.26) | collective-permute-done | bytes 393248 | tf_op jit(solution)/shard_map/ppermute | solution.py:790
  311.3 6.4 %grad.1.refs_0_.refs_1_ = bf16[768,640]{1,0:T(8,128)(2,1)} custom-call(bf16[4,512,768]{2,1,0:T(8,128)(2,1)} %x_ref.5, bf16[2048,640]{1,0:T(8,128)(2,1)} %get-tuple-element.144.joined_ref, bf16[512,768]{1,0:T(8,128)(2,1)} %get-tuple-element.142.refs_0_, bf16[256,768]{1,0:T(8,128)(2,1)} %copy-done.4, bf16[256,768]{1,0:T(8,128)(2,1)} %select_add_fusion.1.refs_2_), custom_call_target="tpu_custom_call" | custom-call | flops 2013265920 | bytes 1966080 | tf_op jit(solution)/shard_map/grad/pallas_call | solution.py:687
  317.7 2.1 dynamic-slice_bitcast_fusion.7
  321.7 2.0 add.124.done_ref
  324.0 2.5 plain.1.refs_0_
  326.5 3.4 final.3.refs_0_
  331.1 2.3 collective-permute-done.35
  334.8 5.8 %collective-permute-start.36 = (bf16[192,640]{1,0:T(8,128)(2,1)S(1)}, bf16[192,640]{1,0:T(8,128)(2,1)S(1)}, u32[]{:S(2)}, u32[]{:S(2)}) collective-permute-start(bf16[192,640]{1,0:T(8,128)(2,1)S(1)} %fusion.2), channel_id=1, source_target_pairs={{0,4},{4,0},{1,5},{5,1},{2,6},{6,2},{3,7},{7,3},{8,12},{12,8},{9,1... | collective-permute-start | bytes 737288 | tf_op jit(solution)/shard_map/ppermute | solution.py:798
  341.0 2.2 bitcast_add_fusion.1
  343.3 1.9 collective-permute-start.38
  345.2 3.2 collective-permute-done.41
  351.8 6.7 %collective-permute-done.31.other_ref = bf16[256,768]{1,0:T(8,128)(2,1)S(1)} collective-permute-done((bf16[256,768]{1,0:T(8,128)(2,1)S(1)}, bf16[256,768]{1,0:T(8,128)(2,1)S(1)}, u32[]{:S(2)}, u32[]{:S(2)}) %collective-permute-start.31) | collective-permute-done | bytes 393248 | tf_op jit(solution)/shard_map/ppermute | solution.py:793
  359.2 3.3 final.4.refs_0_
  362.5 4.3 %collective-permute-done.28.other_ref = bf16[256,768]{1,0:T(8,128)(2,1)S(1)} collective-permute-done((bf16[256,768]{1,0:T(8,128)(2,1)}, bf16[256,768]{1,0:T(8,128)(2,1)S(1)}, u32[]{:S(2)}, u32[]{:S(2)}) %collective-permute-start.28) | collective-permute-done | bytes 393248 | tf_op jit(solution)/shard_map/ppermute | solution.py:793
  367.6 3.3 final.5
  (176 shorter events, 64.0 us)
Async XLA Ops:
  7.2 170.2 %all-gather.3.cloned.1.call-start = ((), (), s32[]{:S(2)}) async-start(), calls=%async_computation.1 | async-start | bytes 2027520 | tf_op jit(solution)/shard_map/all_gather | solution.py:920
  8.4 33.0 %copy-start.26 = (f32[768]{0:T(1024)S(1)}, f32[768]{0:T(1024)}, u32[]{:S(2)}) copy-start(f32[768]{0:T(1024)} %param.30) | copy-start | bytes 9220
  8.4 9.2 %collective-permute-start.1 = (bf16[192,640]{1,0:T(8,128)(2,1)S(1)}, bf16[192,640]{1,0:T(8,128)(2,1)S(1)}, u32[]{:S(2)}, u32[]{:S(2)}) collective-permute-start(bf16[192,640]{1,0:T(8,128)(2,1)S(1)} %pad_maximum_fusion.2.w0), channel_id=1, source_target_pairs={{0,16},{16,0},{8,24},{24,8},{1,17},{17,1},{9,25},{25,9},{2,18},{18... | collective-permute-start | bytes 737288 | tf_op jit(solution)/shard_map/ppermute | solution.py:781
  14.3 34.1 %copy-start.10 = (bf16[192,1728]{1,0:T(8,128)(2,1)}, bf16[192,1728]{1,0:T(8,128)(2,1)S(1)}, u32[]{:S(2)}) copy-start(bf16[192,1728]{1,0:T(8,128)(2,1)S(1)} %constant_dynamic-update-slice_fusion) | copy-start | bytes 1990660
  14.3 17.1 %collective-permute-start.5 = (bf16[192,1728]{1,0:T(8,128)(2,1)S(1)}, bf16[192,1728]{1,0:T(8,128)(2,1)}, u32[]{:S(2)}, u32[]{:S(2)}) collective-permute-start(bf16[192,1728]{1,0:T(8,128)(2,1)S(1)} %constant_dynamic-update-slice_fusion), channel_id=1, source_target_pairs={{0,1},{1,0},{2,3},{3,2},{4,5},{5,4},{6,7},{7,6},{8,9},{9,8},{10,11... | collective-permute-start | bytes 1990664 | tf_op jit(solution)/shard_map/ppermute | solution.py:872
  16.0 15.4 %collective-permute-start.6 = (bf16[192,1728]{1,0:T(8,128)(2,1)S(1)}, bf16[192,1728]{1,0:T(8,128)(2,1)}, u32[]{:S(2)}, u32[]{:S(2)}) collective-permute-start(bf16[192,1728]{1,0:T(8,128)(2,1)S(1)} %constant_dynamic-update-slice_fusion), channel_id=1, source_target_pairs={{1,2},{2,1},{5,6},{6,5},{9,10},{10,9},{13,14},{14,13},{17,18},{18,... | collective-permute-start | bytes 1990664 | tf_op jit(solution)/shard_map/ppermute | solution.py:873
  17.6 16.7 %collective-permute-start.7 = (bf16[192,1728]{1,0:T(8,128)(2,1)S(1)}, bf16[192,1728]{1,0:T(8,128)(2,1)}, u32[]{:S(2)}, u32[]{:S(2)}) collective-permute-start(bf16[192,1728]{1,0:T(8,128)(2,1)S(1)} %constant_dynamic-update-slice_fusion), channel_id=1, source_target_pairs={{0,16},{16,0},{8,24},{24,8},{1,17},{17,1},{9,25},{25,9},{2,18},{18... | collective-permute-start | bytes 1990664 | tf_op jit(solution)/shard_map/ppermute | solution.py:874
  19.2 2.5 collective-permute-start
  19.2 3.2 collective-permute-start.2
  34.3 16.8 %collective-permute-start.8 = (bf16[192,1728]{1,0:T(8,128)(2,1)}, bf16[192,1728]{1,0:T(8,128)(2,1)}, u32[]{:S(2)}, u32[]{:S(2)}) collective-permute-start(bf16[192,1728]{1,0:T(8,128)(2,1)} %collective-permute-done.5), channel_id=1, source_target_pairs={{1,2},{2,1},{5,6},{6,5},{9,10},{10,9},{13,14},{14,13},{17,18},{18,... | collective-permute-start | bytes 1990664 | tf_op jit(solution)/shard_map/ppermute | solution.py:893
  35.8 19.2 %collective-permute-start.9 = (bf16[192,1728]{1,0:T(8,128)(2,1)}, bf16[192,1728]{1,0:T(8,128)(2,1)}, u32[]{:S(2)}, u32[]{:S(2)}) collective-permute-start(bf16[192,1728]{1,0:T(8,128)(2,1)} %collective-permute-done.6), channel_id=1, source_target_pairs={{1,0},{2,3},{5,4},{6,7},{9,8},{10,11},{13,12},{14,15},{17,16},{18,... | collective-permute-start | bytes 1990664 | tf_op jit(solution)/shard_map/ppermute | solution.py:894
  37.1 21.7 %collective-permute-start.4 = (bf16[1024,384]{1,0:T(8,128)(2,1)}, bf16[1024,384]{1,0:T(8,128)(2,1)}, u32[]{:S(2)}, u32[]{:S(2)}) collective-permute-start(bf16[1024,384]{1,0:T(8,128)(2,1)} %get-tuple-element.89.refs_3_.refs_7_), channel_id=1, source_target_pairs={{0,4},{1,5},{2,6},{3,7},{8,12},{9,13},{10,14},{11,15},{16,20},{17,... | collective-permute-start | bytes 2359304 | tf_op jit(solution)/shard_map/ppermute | solution.py:897
  48.4 30.0 %collective-permute-start.3 = (bf16[1024,384]{1,0:T(8,128)(2,1)}, bf16[1024,384]{1,0:T(8,128)(2,1)S(1)}, u32[]{:S(2)}, u32[]{:S(2)}) collective-permute-start(bf16[1024,384]{1,0:T(8,128)(2,1)} %get-tuple-element.88.refs_3_.refs_7_), channel_id=1, source_target_pairs={{0,4},{1,5},{2,6},{3,7},{8,12},{9,13},{10,14},{11,15},{16,20},{17,... | collective-permute-start | bytes 2359304 | tf_op jit(solution)/shard_map/ppermute | solution.py:897
  49.8 30.0 %collective-permute-start.11 = (bf16[192,1728]{1,0:T(8,128)(2,1)}, bf16[192,1728]{1,0:T(8,128)(2,1)}, u32[]{:S(2)}, u32[]{:S(2)}) collective-permute-start(bf16[192,1728]{1,0:T(8,128)(2,1)} %collective-permute-done.5), channel_id=1, source_target_pairs={{0,16},{16,0},{8,24},{24,8},{1,17},{17,1},{9,25},{25,9},{2,18},{18... | collective-permute-start | bytes 1990664 | tf_op jit(solution)/shard_map/ppermute | solution.py:874
  51.1 19.6 %collective-permute-start.10 = (bf16[192,1728]{1,0:T(8,128)(2,1)}, bf16[192,1728]{1,0:T(8,128)(2,1)}, u32[]{:S(2)}, u32[]{:S(2)}) collective-permute-start(bf16[192,1728]{1,0:T(8,128)(2,1)} %collective-permute-done.8), channel_id=1, source_target_pairs={{1,0},{2,3},{5,4},{6,7},{9,8},{10,11},{13,12},{14,15},{17,16},{18,... | collective-permute-start | bytes 1990664 | tf_op jit(solution)/shard_map/ppermute | solution.py:904
  57.1 49.5 %collective-permute-start.12 = (bf16[192,1728]{1,0:T(8,128)(2,1)}, bf16[192,1728]{1,0:T(8,128)(2,1)}, u32[]{:S(2)}, u32[]{:S(2)}) collective-permute-start(bf16[192,1728]{1,0:T(8,128)(2,1)} %broadcast_select_fusion.1.refs_6_), channel_id=1, source_target_pairs={{0,16},{16,0},{8,24},{24,8},{1,17},{17,1},{9,25},{25,9},{2,18},{18... | collective-permute-start | bytes 1990664 | tf_op jit(solution)/shard_map/ppermute | solution.py:874
  72.7 33.8 %collective-permute-start.13 = (bf16[192,1728]{1,0:T(8,128)(2,1)}, bf16[192,1728]{1,0:T(8,128)(2,1)}, u32[]{:S(2)}, u32[]{:S(2)}) collective-permute-start(bf16[192,1728]{1,0:T(8,128)(2,1)} %broadcast_select_fusion), channel_id=1, source_target_pairs={{0,16},{16,0},{8,24},{24,8},{1,17},{17,1},{9,25},{25,9},{2,18},{18... | collective-permute-start | bytes 1990664 | tf_op jit(solution)/shard_map/ppermute | solution.py:874
  74.0 21.9 %collective-permute-start.14 = (bf16[528,384]{1,0:T(8,128)(2,1)}, bf16[528,384]{1,0:T(8,128)(2,1)}, u32[]{:S(2)}, u32[]{:S(2)}) collective-permute-start(bf16[528,384]{1,0:T(8,128)(2,1)} %get-tuple-element.98.refs_6_.refs_1_.refs_7_.refs_4_), channel_id=1, source_target_pairs={{0,1},{1,0},{2,3},{3,2},{4,5},{5,4},{6,7},{7,6},{8,9},{9,8},{10,11... | collective-permute-start | bytes 1216520 | tf_op jit(solution)/shard_map/ppermute | solution.py:777
  78.4 28.1 %collective-permute-start.15 = (bf16[528,384]{1,0:T(8,128)(2,1)}, bf16[528,384]{1,0:T(8,128)(2,1)}, u32[]{:S(2)}, u32[]{:S(2)}) collective-permute-start(bf16[528,384]{1,0:T(8,128)(2,1)} %get-tuple-element.98.refs_6_.refs_1_.refs_7_.refs_4_), channel_id=1, source_target_pairs={{0,2},{2,0},{1,3},{3,1},{4,6},{6,4},{5,7},{7,5},{8,10},{10,8},{9,1... | collective-permute-start | bytes 1216520 | tf_op jit(solution)/shard_map/ppermute | solution.py:777
  79.7 26.8 %collective-permute-start.16 = (bf16[528,384]{1,0:T(8,128)(2,1)}, bf16[528,384]{1,0:T(8,128)(2,1)}, u32[]{:S(2)}, u32[]{:S(2)}) collective-permute-start(bf16[528,384]{1,0:T(8,128)(2,1)} %get-tuple-element.98.refs_6_.refs_1_.refs_7_.refs_4_), channel_id=1, source_target_pairs={{0,3},{3,0},{1,2},{2,1},{4,7},{7,4},{5,6},{6,5},{8,11},{11,8},{9,1... | collective-permute-start | bytes 1216520 | tf_op jit(solution)/shard_map/ppermute | solution.py:777
  95.9 15.1 %collective-permute-start.17 = (bf16[4,192,1728]{2,1,0:T(8,128)(2,1)}, bf16[4,192,1728]{2,1,0:T(8,128)(2,1)}, u32[]{:S(2)}, u32[]{:S(2)}) collective-permute-start(bf16[4,192,1728]{2,1,0:T(8,128)(2,1)} %pad_maximum_fusion.refs_7_.refs_11_), channel_id=1, source_target_pairs={{0,8},{8,0},{16,24},{24,16},{1,9},{9,1},{17,25},{25,17},{2,10},{10... | collective-permute-start | bytes 7962632 | tf_op jit(solution)/shard_map/ppermute | solution.py:931
  110.1 5.2 %collective-permute-start.18 = (bf16[4,192,1728]{2,1,0:T(8,128)(2,1)S(1)}, bf16[4,192,1728]{2,1,0:T(8,128)(2,1)}, u32[]{:S(2)}, u32[]{:S(2)}) collective-permute-start(bf16[4,192,1728]{2,1,0:T(8,128)(2,1)S(1)} %pad_maximum_fusion.1.refs_13_), channel_id=1, source_target_pairs={{0,8},{8,0},{16,24},{24,16},{1,9},{9,1},{17,25},{25,17},{2,10},{10... | collective-permute-start | bytes 7962632 | tf_op jit(solution)/shard_map/ppermute | solution.py:936
  165.5 15.7 %collective-permute-start.20 = (bf16[512,384]{1,0:T(8,128)(2,1)}, bf16[512,384]{1,0:T(8,128)(2,1)S(1)}, u32[]{:S(2)}, u32[]{:S(2)}) collective-permute-start(bf16[512,384]{1,0:T(8,128)(2,1)} %get-tuple-element.120), channel_id=1, source_target_pairs={{4,0},{5,1},{6,2},{7,3},{12,8},{13,9},{14,10},{15,11},{20,16},{21,... | collective-permute-start | bytes 1179656 | tf_op jit(solution)/shard_map/ppermute | solution.py:994
  176.1 17.3 %collective-permute-start.19 = (bf16[512,384]{1,0:T(8,128)(2,1)}, bf16[512,384]{1,0:T(8,128)(2,1)S(1)}, u32[]{:S(2)}, u32[]{:S(2)}) collective-permute-start(bf16[512,384]{1,0:T(8,128)(2,1)} %get-tuple-element.117), channel_id=1, source_target_pairs={{4,0},{5,1},{6,2},{7,3},{12,8},{13,9},{14,10},{15,11},{20,16},{21,... | collective-permute-start | bytes 1179656 | tf_op jit(solution)/shard_map/ppermute | solution.py:994
  198.3 55.0 %all-reduce.3.cloned.1.call-start = ((), (), s32[]{:S(2)}) async-start(), calls=%async_computation | async-start | bytes 1572864 | tf_op jit(solution)/shard_map/psum | solution.py:1042
  200.2 51.6 %collective-permute-start.21 = (bf16[256,768]{1,0:T(8,128)(2,1)S(1)}, bf16[256,768]{1,0:T(8,128)(2,1)S(1)}, u32[]{:S(2)}, u32[]{:S(2)}) collective-permute-start(bf16[256,768]{1,0:T(8,128)(2,1)S(1)} %broadcast_select_fusion.4), channel_id=1, source_target_pairs={{0,1},{1,0},{2,3},{3,2},{4,5},{5,4},{6,7},{7,6},{8,9},{9,8},{10,11... | collective-permute-start | bytes 1179656 | tf_op jit(solution)/shard_map/ppermute | solution.py:790
  250.0 34.0 %collective-permute-start.25 = (bf16[2,192,1728]{2,1,0:T(8,128)(2,1)}, bf16[2,192,1728]{2,1,0:T(8,128)(2,1)}, u32[]{:S(2)}, u32[]{:S(2)}) collective-permute-start(bf16[2,192,1728]{2,1,0:T(8,128)(2,1)} %dynamic-slice_bitcast_fusion), channel_id=1, source_target_pairs={{0,16},{16,0},{8,24},{24,8},{1,17},{17,1},{9,25},{25,9},{2,18},{18... | collective-permute-start | bytes 3981320 | tf_op jit(solution)/shard_map/ppermute | solution.py:807
  252.6 21.9 %collective-permute-start.24 = (bf16[256,768]{1,0:T(8,128)(2,1)}, bf16[256,768]{1,0:T(8,128)(2,1)S(1)}, u32[]{:S(2)}, u32[]{:S(2)}) collective-permute-start(bf16[256,768]{1,0:T(8,128)(2,1)} %select_add_fusion.2.refs_11_), channel_id=1, source_target_pairs={{0,2},{2,0},{1,3},{3,1},{4,6},{6,4},{5,7},{7,5},{8,10},{10,8},{9,1... | collective-permute-start | bytes 1179656 | tf_op jit(solution)/shard_map/ppermute | solution.py:792
  262.4 15.3 %collective-permute-start.23 = (bf16[512,384]{1,0:T(8,128)(2,1)}, bf16[512,384]{1,0:T(8,128)(2,1)}, u32[]{:S(2)}, u32[]{:S(2)}) collective-permute-start(bf16[512,384]{1,0:T(8,128)(2,1)} %get-tuple-element.137), channel_id=1, source_target_pairs={{4,0},{5,1},{6,2},{7,3},{12,8},{13,9},{14,10},{15,11},{20,16},{21,... | collective-permute-start | bytes 1179656 | tf_op jit(solution)/shard_map/ppermute | solution.py:994
  273.2 14.7 %collective-permute-start.22 = (bf16[512,384]{1,0:T(8,128)(2,1)}, bf16[512,384]{1,0:T(8,128)(2,1)}, u32[]{:S(2)}, u32[]{:S(2)}) collective-permute-start(bf16[512,384]{1,0:T(8,128)(2,1)} %get-tuple-element.135), channel_id=1, source_target_pairs={{4,0},{5,1},{6,2},{7,3},{12,8},{13,9},{14,10},{15,11},{20,16},{21,... | collective-permute-start | bytes 1179656 | tf_op jit(solution)/shard_map/ppermute | solution.py:994
  275.6 48.0 %collective-permute-start.32 = (bf16[256,768]{1,0:T(8,128)(2,1)S(1)}, bf16[256,768]{1,0:T(8,128)(2,1)}, u32[]{:S(2)}, u32[]{:S(2)}) collective-permute-start(bf16[256,768]{1,0:T(8,128)(2,1)S(1)} %add.117.refs_5_.done_ref), channel_id=1, source_target_pairs={{0,1},{1,0},{2,3},{3,2},{4,5},{5,4},{6,7},{7,6},{8,9},{9,8},{10,11... | collective-permute-start | bytes 1179656 | tf_op jit(solution)/shard_map/ppermute | solution.py:793
  283.3 12.6 %collective-permute-start.29 = (bf16[256,768]{1,0:T(8,128)(2,1)S(1)}, bf16[256,768]{1,0:T(8,128)(2,1)}, u32[]{:S(2)}, u32[]{:S(2)}) collective-permute-start(bf16[256,768]{1,0:T(8,128)(2,1)S(1)} %broadcast_select_fusion.2), channel_id=1, source_target_pairs={{0,1},{1,0},{2,3},{3,2},{4,5},{5,4},{6,7},{7,6},{8,9},{9,8},{10,11... | collective-permute-start | bytes 1179656 | tf_op jit(solution)/shard_map/ppermute | solution.py:790
  287.9 53.1 %collective-permute-start.37 = (bf16[192,1728]{1,0:T(8,128)(2,1)}, bf16[192,1728]{1,0:T(8,128)(2,1)}, u32[]{:S(2)}, u32[]{:S(2)}) collective-permute-start(bf16[192,1728]{1,0:T(8,128)(2,1)} %dynamic-slice_bitcast_fusion.1), channel_id=1, source_target_pairs={{0,8},{8,0},{16,24},{24,16},{1,9},{9,1},{17,25},{25,17},{2,10},{10... | collective-permute-start | bytes 1990664 | tf_op jit(solution)/shard_map/ppermute | solution.py:813
  292.3 18.3 %copy-start = (bf16[512,768]{1,0:T(8,128)(2,1)S(1)}, bf16[512,768]{1,0:T(8,128)(2,1)}, u32[]{:S(2)}) copy-start(bf16[512,768]{1,0:T(8,128)(2,1)} %get-tuple-element.142.refs_0_) | copy-start | bytes 2359300
  293.5 17.0 %collective-permute-start.26 = (bf16[256,768]{1,0:T(8,128)(2,1)S(1)}, bf16[256,768]{1,0:T(8,128)(2,1)S(1)}, u32[]{:S(2)}, u32[]{:S(2)}) collective-permute-start(bf16[256,768]{1,0:T(8,128)(2,1)S(1)} %broadcast_select_fusion.3), channel_id=1, source_target_pairs={{0,1},{1,0},{2,3},{3,2},{4,5},{5,4},{6,7},{7,6},{8,9},{9,8},{10,11... | collective-permute-start | bytes 1179656 | tf_op jit(solution)/shard_map/ppermute | solution.py:790
  297.2 22.9 %collective-permute-start.30 = (bf16[256,768]{1,0:T(8,128)(2,1)S(1)}, bf16[256,768]{1,0:T(8,128)(2,1)}, u32[]{:S(2)}, u32[]{:S(2)}) collective-permute-start(bf16[256,768]{1,0:T(8,128)(2,1)S(1)} %select_add_fusion.refs_1_), channel_id=1, source_target_pairs={{0,2},{2,0},{1,3},{3,1},{4,6},{6,4},{5,7},{7,5},{8,10},{10,8},{9,1... | collective-permute-start | bytes 1179656 | tf_op jit(solution)/shard_map/ppermute | solution.py:792
  319.8 10.3 %collective-permute-start.33 = (bf16[192,640]{1,0:T(8,128)(2,1)}, bf16[192,640]{1,0:T(8,128)(2,1)}, u32[]{:S(2)}, u32[]{:S(2)}) collective-permute-start(bf16[192,640]{1,0:T(8,128)(2,1)} %get-tuple-element.165), channel_id=1, source_target_pairs={{0,8},{8,0},{16,24},{24,16},{1,9},{9,1},{17,25},{25,17},{2,10},{10... | collective-permute-start | bytes 737288 | tf_op jit(solution)/shard_map/ppermute | solution.py:823
  319.8 11.3 %collective-permute-start.34 = (bf16[192,640]{1,0:T(8,128)(2,1)}, bf16[192,640]{1,0:T(8,128)(2,1)}, u32[]{:S(2)}, u32[]{:S(2)}) collective-permute-start(bf16[192,640]{1,0:T(8,128)(2,1)} %get-tuple-element.167), channel_id=1, source_target_pairs={{0,16},{16,0},{8,24},{24,8},{1,17},{17,1},{9,25},{25,9},{2,18},{18... | collective-permute-start | bytes 737288 | tf_op jit(solution)/shard_map/ppermute | solution.py:823
  320.1 13.3 %collective-permute-start.35 = (bf16[192,640]{1,0:T(8,128)(2,1)}, bf16[192,640]{1,0:T(8,128)(2,1)}, u32[]{:S(2)}, u32[]{:S(2)}) collective-permute-start(bf16[192,640]{1,0:T(8,128)(2,1)} %get-tuple-element.166), channel_id=1, source_target_pairs={{0,24},{24,0},{8,16},{16,8},{1,25},{25,1},{9,17},{17,9},{2,26},{26... | collective-permute-start | bytes 737288 | tf_op jit(solution)/shard_map/ppermute | solution.py:823
  323.7 6.3 %collective-permute-start.39 = (f32[8,1408]{1,0:T(8,128)S(1)}, f32[8,1408]{1,0:T(8,128)S(1)}, u32[]{:S(2)}, u32[]{:S(2)}) collective-permute-start(f32[8,1408]{1,0:T(8,128)S(1)} %pad_maximum_fusion.3), channel_id=1, source_target_pairs={{0,8},{8,0},{16,24},{24,16},{1,9},{9,1},{17,25},{25,17},{2,10},{10... | collective-permute-start | bytes 135176 | tf_op jit(solution)/shard_map/ppermute | solution.py:828
  326.5 14.1 %copy-start.9 = (bf16[256,768]{1,0:T(8,128)(2,1)S(1)}, bf16[256,768]{1,0:T(8,128)(2,1)}, u32[]{:S(2)}) copy-start(bf16[256,768]{1,0:T(8,128)(2,1)} %add.124.done_ref) | copy-start | bytes 1179652
  329.9 20.2 %collective-permute-start.27 = (bf16[256,768]{1,0:T(8,128)(2,1)S(1)}, bf16[256,768]{1,0:T(8,128)(2,1)S(1)}, u32[]{:S(2)}, u32[]{:S(2)}) collective-permute-start(bf16[256,768]{1,0:T(8,128)(2,1)S(1)} %copy-done.3), channel_id=1, source_target_pairs={{0,2},{2,0},{1,3},{3,1},{4,6},{6,4},{5,7},{7,5},{8,10},{10,8},{9,1... | collective-permute-start | bytes 1179656 | tf_op jit(solution)/shard_map/ppermute | solution.py:792
  330.2 10.7 %collective-permute-start.40 = (f32[8,1408]{1,0:T(8,128)S(1)}, f32[8,1408]{1,0:T(8,128)S(1)}, u32[]{:S(2)}, u32[]{:S(2)}) collective-permute-start(f32[8,1408]{1,0:T(8,128)S(1)} %add.142), channel_id=1, source_target_pairs={{0,16},{16,0},{8,24},{24,8},{1,17},{17,1},{9,25},{25,9},{2,18},{18... | collective-permute-start | bytes 135176 | tf_op jit(solution)/shard_map/ppermute | solution.py:829
  334.8 16.1 %collective-permute-start.36 = (bf16[192,640]{1,0:T(8,128)(2,1)S(1)}, bf16[192,640]{1,0:T(8,128)(2,1)S(1)}, u32[]{:S(2)}, u32[]{:S(2)}) collective-permute-start(bf16[192,640]{1,0:T(8,128)(2,1)S(1)} %fusion.2), channel_id=1, source_target_pairs={{0,4},{4,0},{1,5},{5,1},{2,6},{6,2},{3,7},{7,3},{8,12},{12,8},{9,1... | collective-permute-start | bytes 737288 | tf_op jit(solution)/shard_map/ppermute | solution.py:798
  340.6 17.9 %collective-permute-start.31 = (bf16[256,768]{1,0:T(8,128)(2,1)S(1)}, bf16[256,768]{1,0:T(8,128)(2,1)S(1)}, u32[]{:S(2)}, u32[]{:S(2)}) collective-permute-start(bf16[256,768]{1,0:T(8,128)(2,1)S(1)} %copy-done.9), channel_id=1, source_target_pairs={{0,1},{1,0},{2,3},{3,2},{4,5},{5,4},{6,7},{7,6},{8,9},{9,8},{10,11... | collective-permute-start | bytes 1179656 | tf_op jit(solution)/shard_map/ppermute | solution.py:793
  340.9 7.5 %collective-permute-start.41 = (f32[8,1408]{1,0:T(8,128)S(1)}, f32[8,1408]{1,0:T(8,128)S(1)}, u32[]{:S(2)}, u32[]{:S(2)}) collective-permute-start(f32[8,1408]{1,0:T(8,128)S(1)} %add.143), channel_id=1, source_target_pairs={{0,4},{4,0},{1,5},{5,1},{2,6},{6,2},{3,7},{7,3},{8,12},{12,8},{9,1... | collective-permute-start | bytes 135176 | tf_op jit(solution)/shard_map/ppermute | solution.py:798
  343.3 27.7 %collective-permute-start.38 = (bf16[192,1728]{1,0:T(8,128)(2,1)}, bf16[192,1728]{1,0:T(8,128)(2,1)}, u32[]{:S(2)}, u32[]{:S(2)}) collective-permute-start(bf16[192,1728]{1,0:T(8,128)(2,1)} %bitcast_add_fusion.1), channel_id=1, source_target_pairs={{0,4},{4,0},{1,5},{5,1},{2,6},{6,2},{3,7},{7,3},{8,12},{12,8},{9,1... | collective-permute-start | bytes 1990664 | tf_op jit(solution)/shard_map/ppermute | solution.py:798
  351.0 15.9 %collective-permute-start.28 = (bf16[256,768]{1,0:T(8,128)(2,1)}, bf16[256,768]{1,0:T(8,128)(2,1)S(1)}, u32[]{:S(2)}, u32[]{:S(2)}) collective-permute-start(bf16[256,768]{1,0:T(8,128)(2,1)} %add.122.done_ref), channel_id=1, source_target_pairs={{0,1},{1,0},{2,3},{3,2},{4,5},{5,4},{6,7},{7,6},{8,9},{9,8},{10,11... | collective-permute-start | bytes 1179656 | tf_op jit(solution)/shard_map/ppermute | solution.py:793
  (25 other events, 106.2 us)
Sparse Core Ops, SparseCore 0:
  111.1 43.0 all-gather.2
  201.5 48.2 all-reduce.2

commit v4 on v3

--- a/solution.py
+++ b/solution.py
@@ -1028,30 +1028,31 @@
         last = s + chunk == seqs
         if last:
             ffn_far = fsdp_far_sum(grad_ffn, f)
+        if not last:
+            for i in range(s, s + chunk):
+                held[i], after = attn_bwd(i, 1, after)
         for i in range(s, s + chunk):
-            if last and i == s > 0:
-                after = after + [reduced[0], reduced[1][1]]
-            held[i], after = attn_bwd(i, 1, after)
-        for i in range(s, s + chunk):
-            if last and i == s:
-                after = after + [reduced[1][2]]
-            if last and i == s + 1:
-                after = after + [ffn_far]
+            if last:
+                extra = [reduced[0], reduced[1][1]] if i == s else []
+                held[i], after = attn_bwd(i, 1, after + extra)
+                finish(i - s, after)
+                after = after + [d_hidden, reduced[i - 1][1 if i > s else 2]]
             ys[i], after = dx(i, held[i], after)
             if i == 0:
                 reduced[i] = lax.psum(ys[i], "tp")
             else:
                 reduced[i] = tp_reduce(ys[i], odd)
-    after = after + [reduced[seqs - 2][1], reduced[seqs - 1][1]]
+    after = after + [reduced[seqs - 1][0]]
     g_qkv = grad_call(hidden_in, joined, after)
-    for s in range(seqs):
+    for s in range(seqs - chunk, seqs):
         finish(s, [g_qkv])
 
     small = jnp.concatenate([functools.reduce(jnp.add, sums), functools.reduce(jnp.add, qkv_sums)], axis=1)
+    g_ffn = fsdp_near_sum(ffn_far, f, ctx_size)
+    g_qkv, g_ffn = lax.optimization_barrier((g_qkv, g_ffn))
+    g_qkv = fsdp_direct_sum(g_qkv, f, ctx_size)
     small, _ = lax.optimization_barrier((small, reduced[seqs - 2][2]))
     small = all_sum(small, ctx_size)
-    g_ffn = fsdp_near_sum(ffn_far, f, ctx_size)
-    g_qkv = fsdp_direct_sum(g_qkv, f, ctx_size)
     return (
         output,
         logits,

time: 386 us -> 381 us (0.987)
  waiting for transfers between devices: 63.4 us -> 58 us
    ppermute x3, waiting for transfers between devices: 0.42 us -> 20.2 us  [tp_reduce(): done = pair + lax.ppermute(pair, 'tp', FAR)]
    ppermute x3, waiting for transfers between devices: 12.5 us -> 0.01 us  [tp_reduce(): got = lax.ppermute(sent, 'tp', SWAP)]
    ppermute x3, waiting for transfers between devices: 11 us -> 0.63 us  [tp_reduce(): return (sent, pair, done, lax.ppermute(done, 'tp', SWAP))]
    unnamed x60 -> x66, local copies, waits for them, and re-layouts: 8.42 us -> 7.26 us
  transfers between devices with their start and end apart: 44 -> 44, of which waited for: 14 -> 15; matrix products, arithmetic and copies ran while one was open for 11% -> 13% of each run, Pallas kernels for 49% -> 50%
where the time goes in v4:
time: 381 us; the launch traced here: 377 us
  Pallas kernels  192 us (50%)
  waiting for transfers between devices  58 us (15%)
  starting transfers between devices  56.8 us (15%)
  other arithmetic  31.8 us (8%)
  local copies, waits for them, and re-layouts  22.9 us (6%)
  between operations  15 us (4%)
    pallas_call x2, Pallas kernels, ffn_call(): pl.pallas_call(functools.partial(ffn_kernel, chained=bool(chained), final...  83 us
    pallas_call x4, Pallas kernels, attn_bwd_call(): pl.pallas_call(functools.partial(attn_bwd_kernel, heads=heads, size=size,...  36.8 us
    pallas_call x2, Pallas kernels, attn_fwd_call(): pl.pallas_call(functools.partial(attn_fwd_kernel, heads=heads, size=size,...  23.5 us
    ppermute x3, waiting for transfers between devices, tp_reduce(): done = pair + lax.ppermute(pair, 'tp', FAR)  20.2 us
    pallas_call x4, Pallas kernels, dx_call(): pl.pallas_call(functools.partial(dx_kernel, nkv=len(dkvs)), out_shape=(ja...  16.7 us
    pallas_call x2, Pallas kernels, qkv_call(): pl.pallas_call(functools.partial(qkv_kernel, scale=scale), out_shape=(jax...  12.6 us
    ppermute x4, waiting for transfers between devices, attn_bwd(): dkvs = (out[2], lax.ppermute(out[3], 'ctx', ((1, 0),)))  10.9 us
    ppermute x3, waiting for transfers between devices, tp_gather(): return [value] + [lax.ppermute(value, 'tp', p) for p in (SWAP, FAR, ACROSS)]  10.5 us
  transfers between devices with their start and end apart: 44, of which 15 were waited for; matrix products, arithmetic and copies ran while one was open for 13% of the time, Pallas kernels for 50%

profile of v4, /device:TPU:0, one launch (start us, length us, event | category | flops | bytes accessed | tf_op | source)
XLA Modules:
  0.0 376.5 jit_solution(6938313057954597581)
XLA Ops:
  8.4 3.0 collective-permute-start.1
  22.4 6.3 %qkv.2 = (bf16[1024,192]{1,0:T(8,128)(2,1)}, bf16[1024,384]{1,0:T(8,128)(2,1)}, bf16[768,640]{1,0:T(8,128)(2,1)}) custom-call(s32[3]{0:T(128)} %pad_add_fusion.ids, bf16[4,512,768]{2,1,0:T(8,128)(2,1)} %x_ref.5, bf16[192,640]{1,0:T(8,128)(2,1)} %copy-done.11, bf16[192,640]{1,0:T(8,128)(2,1)} %copy-done.15, bf16[192,640]{1,0:T(8,128)(2,1)} %copy-done.14, ...), custom_call_target="tpu_custom_call" | custom-call | flops 1006632960 | bytes 5046272 | tf_op jit(solution)/shard_map/qkv/pallas_call | solution.py:83
  28.7 2.7 collective-permute-done.5
  31.4 2.8 collective-permute-done.7
  37.1 4.3 %collective-permute-start.4 = (bf16[1024,384]{1,0:T(8,128)(2,1)}, bf16[1024,384]{1,0:T(8,128)(2,1)}, u32[]{:S(2)}, u32[]{:S(2)}) collective-permute-start(bf16[1024,384]{1,0:T(8,128)(2,1)} %get-tuple-element.91.refs_3_.refs_7_), channel_id=1, source_target_pairs={{0,4},{1,5},{2,6},{3,7},{8,12},{9,13},{10,14},{11,15},{16,20},{17,... | collective-permute-start | bytes 2359304 | tf_op jit(solution)/shard_map/ppermute | solution.py:897
  42.1 6.3 %qkv.3 = (bf16[1024,192]{1,0:T(8,128)(2,1)}, bf16[1024,384]{1,0:T(8,128)(2,1)}, bf16[768,640]{1,0:T(8,128)(2,1)}) custom-call(s32[3]{0:T(128)} %pad_add_fusion.ids, bf16[4,512,768]{2,1,0:T(8,128)(2,1)} %x_ref.5, bf16[192,640]{1,0:T(8,128)(2,1)} %copy-done.11, bf16[192,640]{1,0:T(8,128)(2,1)} %copy-done.15, bf16[192,640]{1,0:T(8,128)(2,1)} %copy-done.14, ...), custom_call_target="tpu_custom_call" | custom-call | flops 1006632960 | bytes 5046272 | tf_op jit(solution)/shard_map/qkv/pallas_call | solution.py:83
  52.5 2.6 collective-permute-done.9
  55.0 2.0 broadcast_select_fusion.1.refs_6_
  58.8 11.9 %attn_fwd.2 = (bf16[4,3,512,1024]{3,2,1,0:T(8,128)(2,1)}, bf16[2,3,512,1024]{3,2,1,0:T(8,128)(2,1)}, bf16[528,384]{1,0:T(8,128)(2,1)}, f32[1024,128]{1,0:T(8,128)}) custom-call(s32[3]{0:T(128)} %pad_add_fusion.ids, bf16[1024,192]{1,0:T(8,128)(2,1)} %get-tuple-element.88.refs_0_, bf16[4,3,512,1024]{3,2,1,0:T(8,128)(2,1)} %refs_1_.3, ...), custom_call_target="tpu_custom_call" | custom-call | flops 2415919104 | bytes 18874368 | tf_op jit(solution)/shard_map/attn_fwd/pallas_call | solution.py:200
  70.6 2.0 broadcast_select_fusion
  74.0 4.4 %collective-permute-start.14 = (bf16[528,384]{1,0:T(8,128)(2,1)}, bf16[528,384]{1,0:T(8,128)(2,1)}, u32[]{:S(2)}, u32[]{:S(2)}) collective-permute-start(bf16[528,384]{1,0:T(8,128)(2,1)} %get-tuple-element.100.refs_6_.refs_1_.refs_7_.refs_4_), channel_id=1, source_target_pairs={{0,1},{1,0},{2,3},{3,2},{4,5},{5,4},{6,7},{7,6},{8,9},{9,8},{10,11... | collective-permute-start | bytes 1216520 | tf_op jit(solution)/shard_map/ppermute | solution.py:777
  81.2 3.0 pad_maximum_fusion.refs_7_.refs_11_
  84.2 11.7 %attn_fwd.3 = (bf16[4,3,512,1024]{3,2,1,0:T(8,128)(2,1)}, bf16[2,3,512,1024]{3,2,1,0:T(8,128)(2,1)}, bf16[528,384]{1,0:T(8,128)(2,1)}, f32[1024,128]{1,0:T(8,128)}) custom-call(s32[3]{0:T(128)} %pad_add_fusion.ids, bf16[1024,192]{1,0:T(8,128)(2,1)} %get-tuple-element.89.refs_5_.refs_0_, ...), custom_call_target="tpu_custom_call", output_to_operand_aliasing={{0}: (6, {})} | custom-call | flops 2415919104 | bytes 18874368 | tf_op jit(solution)/shard_map/attn_fwd/pallas_call | solution.py:200
  96.0 10.5 %collective-permute-done.15.refs_3_.refs_9_ = bf16[528,384]{1,0:T(8,128)(2,1)} collective-permute-done((bf16[528,384]{1,0:T(8,128)(2,1)}, bf16[528,384]{1,0:T(8,128)(2,1)}, u32[]{:S(2)}, u32[]{:S(2)}) %collective-permute-start.15) | collective-permute-done | bytes 405536 | tf_op jit(solution)/shard_map/ppermute | solution.py:777
  106.6 1.9 pad_maximum_fusion.1.refs_13_
  110.9 4.4 %collective-permute-done.18.refs_14_ = bf16[4,192,1728]{2,1,0:T(8,128)(2,1)} collective-permute-done((bf16[4,192,1728]{2,1,0:T(8,128)(2,1)S(1)}, bf16[4,192,1728]{2,1,0:T(8,128)(2,1)}, u32[]{:S(2)}, u32[]{:S(2)}) %collective-permute-start.18) | collective-permute-done | bytes 2654240 | tf_op jit(solution)/shard_map/ppermute | solution.py:936
  115.3 40.9 %ffn.2 = (bf16[4,512,768]{2,1,0:T(8,128)(2,1)}, f32[1024,768]{1,0:T(8,128)}, bf16[1024,192]{1,0:T(8,128)(2,1)}, f32[8,768]{1,0:T(8,128)}, f32[768,768]{1,0:T(8,1...) custom-call(s32[3]{0:T(128)} %pad_add_fusion.ids, bf16[4,512,768]{2,1,0:T(8,128)(2,1)} %x_ref.5, ...), custom_call_target="tpu_custom_call" | custom-call | flops 24159191040 | bytes 22020096 | tf_op jit(solution)/shard_map/ffn/pallas_call | solution.py:567
  156.2 9.1 %attn_bwd.4 = (bf16[4,3,512,1024]{3,2,1,0:T(8,128)(2,1)}, bf16[512,192]{1,0:T(8,128)(2,1)}, bf16[512,384]{1,0:T(8,128)(2,1)}, bf16[512,384]{1,0:T(8,128)(2,1)}) custom-call(s32[3]{0:T(128)} %pad_add_fusion.ids, bf16[1024,192]{1,0:T(8,128)(2,1)} %get-tuple-element.88.refs_0_, bf16[2,3,512,1024]{3,2,1,0:T(8,128)(2,1)} %get-tuple-element.112.refs_1_, ...), custom_call_target="tpu_custom_call" | custom-call | flops 8999999488 | bytes 1000 | tf_op jit(solution)/shard_map/attn_bwd/pallas_call | solution.py:331
  166.6 9.3 %attn_bwd.5 = (bf16[4,3,512,1024]{3,2,1,0:T(8,128)(2,1)}, bf16[512,192]{1,0:T(8,128)(2,1)}, bf16[512,384]{1,0:T(8,128)(2,1)}, bf16[512,384]{1,0:T(8,128)(2,1)}) custom-call(s32[3]{0:T(128)} %pad_add_fusion.ids, bf16[1024,192]{1,0:T(8,128)(2,1)} %get-tuple-element.88.refs_0_, ...), custom_call_target="tpu_custom_call", output_to_operand_aliasing={{0}: (9, {})} | custom-call | flops 8999999488 | bytes 1000 | tf_op jit(solution)/shard_map/attn_bwd/pallas_call | solution.py:331
  177.2 2.3 dynamic-slice_bitcast_fusion.2
  181.7 4.1 %dx.4 = (bf16[512,768]{1,0:T(8,128)(2,1)}, bf16[2048,640]{1,0:T(8,128)(2,1)}, f32[8,640]{1,0:T(8,128)}) custom-call(s32[3]{0:T(128)} %pad_add_fusion.ids, bf16[512,192]{1,0:T(8,128)(2,1)} %get-tuple-element.116.refs_9_.dq_ref, bf16[512,384]{1,0:T(8,128)(2,1)} %get-tuple-element.121.refs_0_, bf16[512,384]{1,0:T(8,128)(2,1)} %copy-done.30, ...), custom_call_target="tpu_custom_call" | custom-call | flops 3000000000 | bytes 1000 | tf_op jit(solution)/shard_map/dx/pallas_call | solution.py:640
  185.9 7.3 %collective-permute-done.19.refs_1_ = bf16[512,384]{1,0:T(8,128)(2,1)S(1)} collective-permute-done((bf16[512,384]{1,0:T(8,128)(2,1)}, bf16[512,384]{1,0:T(8,128)(2,1)S(1)}, u32[]{:S(2)}, u32[]{:S(2)}) %collective-permute-start.19) | collective-permute-done | bytes 393248 | tf_op jit(solution)/shard_map/ppermute | solution.py:994
  193.9 4.1 %dx.5 = (bf16[512,768]{1,0:T(8,128)(2,1)}, bf16[2048,640]{1,0:T(8,128)(2,1)}, f32[8,640]{1,0:T(8,128)}) custom-call(s32[3]{0:T(128)} %pad_add_fusion.ids, bf16[512,192]{1,0:T(8,128)(2,1)} %get-tuple-element.117.refs_3_.dq_ref, bf16[512,384]{1,0:T(8,128)(2,1)} %get-tuple-element.118.refs_0_, ...), custom_call_target="tpu_custom_call", output_to_operand_aliasing={{1}: (5, {})} | custom-call | flops 3000000000 | bytes 1000 | tf_op jit(solution)/shard_map/dx/pallas_call | solution.py:640
  200.0 5.1 %collective-permute-start.21 = (bf16[256,768]{1,0:T(8,128)(2,1)S(1)}, bf16[256,768]{1,0:T(8,128)(2,1)S(1)}, u32[]{:S(2)}, u32[]{:S(2)}) collective-permute-start(bf16[256,768]{1,0:T(8,128)(2,1)S(1)} %broadcast_select_fusion.4), channel_id=1, source_target_pairs={{0,1},{1,0},{2,3},{3,2},{4,5},{5,4},{6,7},{7,6},{8,9},{9,8},{10,11... | collective-permute-start | bytes 1179656 | tf_op jit(solution)/shard_map/ppermute | solution.py:790
  205.0 42.1 %ffn.3 = (bf16[4,512,768]{2,1,0:T(8,128)(2,1)}, f32[1024,768]{1,0:T(8,128)}, bf16[1024,192]{1,0:T(8,128)(2,1)}, f32[8,768]{1,0:T(8,128)}, bf16[768,1728]{1,0:T(8,128)(2,1)}) custom-call(s32[3]{0:T(128)} %pad_add_fusion.ids, bf16[4,512,768]{2,1,0:T(8,128)(2,1)} %x_ref.5, ...), custom_call_target="tpu_custom_call", output_to_operand_aliasing={{0}: (19, {})} | custom-call | flops 24159191040 | bytes 22020096 | tf_op jit(solution)/shard_map/ffn/pallas_call | solution.py:567
  249.8 9.1 %attn_bwd.6 = (bf16[4,3,512,1024]{3,2,1,0:T(8,128)(2,1)}, bf16[512,192]{1,0:T(8,128)(2,1)}, bf16[512,384]{1,0:T(8,128)(2,1)}, bf16[512,384]{1,0:T(8,128)(2,1)}) custom-call(s32[3]{0:T(128)} %pad_add_fusion.ids, bf16[1024,192]{1,0:T(8,128)(2,1)} %get-tuple-element.89.refs_5_.refs_0_, ...), custom_call_target="tpu_custom_call", output_to_operand_aliasing={{0}: (9, {})} | custom-call | flops 8999999488 | bytes 1000 | tf_op jit(solution)/shard_map/attn_bwd/pallas_call | solution.py:331
  260.4 2.5 dynamic-slice_bitcast_fusion
  264.2 4.0 %collective-permute-done.23 = bf16[256,768]{1,0:T(8,128)(2,1)} collective-permute-done((bf16[256,768]{1,0:T(8,128)(2,1)S(1)}, bf16[256,768]{1,0:T(8,128)(2,1)}, u32[]{:S(2)}, u32[]{:S(2)}) %collective-permute-start.23) | collective-permute-done | bytes 393248 | tf_op jit(solution)/shard_map/ppermute | solution.py:792
  269.4 2.8 plain.1.refs_5_.refs_0_
  273.0 4.1 %dx.6 = (bf16[512,768]{1,0:T(8,128)(2,1)}, bf16[2048,640]{1,0:T(8,128)(2,1)}, f32[8,640]{1,0:T(8,128)}) custom-call(s32[3]{0:T(128)} %pad_add_fusion.ids, bf16[512,192]{1,0:T(8,128)(2,1)} %get-tuple-element.134.refs_0_.dq_ref.refs_4_, bf16[512,384]{1,0:T(8,128)(2,1)} %get-tuple-element.135.refs_0_, ...), custom_call_target="tpu_custom_call", output_to_operand_aliasing={{1}: (5, {})} | custom-call | flops 3000000000 | bytes 1000 | tf_op jit(solution)/shard_map/dx/pallas_call | solution.py:640
  277.2 1.9 broadcast_select_fusion.3
  280.9 9.3 %attn_bwd.7 = (bf16[4,3,512,1024]{3,2,1,0:T(8,128)(2,1)}, bf16[512,192]{1,0:T(8,128)(2,1)}, bf16[512,384]{1,0:T(8,128)(2,1)}, bf16[512,384]{1,0:T(8,128)(2,1)}) custom-call(s32[3]{0:T(128)} %pad_add_fusion.ids, bf16[1024,192]{1,0:T(8,128)(2,1)} %get-tuple-element.89.refs_5_.refs_0_, ...), custom_call_target="tpu_custom_call", output_to_operand_aliasing={{0}: (9, {})} | custom-call | flops 8999999488 | bytes 1000 | tf_op jit(solution)/shard_map/attn_bwd/pallas_call | solution.py:331
  291.5 3.6 final.3.refs_5_.refs_0_
  295.1 2.0 bitcast_add_fusion
  300.6 2.1 collective-permute-done.24.refs_1_
  303.4 4.3 %dx.7 = (bf16[512,768]{1,0:T(8,128)(2,1)}, bf16[2048,640]{1,0:T(8,128)(2,1)}, f32[8,640]{1,0:T(8,128)}) custom-call(s32[3]{0:T(128)} %pad_add_fusion.ids, bf16[512,192]{1,0:T(8,128)(2,1)} %get-tuple-element.140.refs_1_.dq_ref.refs_4_, bf16[512,384]{1,0:T(8,128)(2,1)} %get-tuple-element.141.refs_0_, ...), custom_call_target="tpu_custom_call", output_to_operand_aliasing={{1}: (5, {})} | custom-call | flops 3000000000 | bytes 1000 | tf_op jit(solution)/shard_map/dx/pallas_call | solution.py:640
  307.7 2.0 broadcast_select_fusion.2.refs_1_
  310.7 2.2 bitcast_add_fusion.1
  312.9 2.1 collective-permute-start.34
  315.0 5.3 %collective-permute-done.30 = bf16[256,768]{1,0:T(8,128)(2,1)} collective-permute-done((bf16[256,768]{1,0:T(8,128)(2,1)S(1)}, bf16[256,768]{1,0:T(8,128)(2,1)}, u32[]{:S(2)}, u32[]{:S(2)}) %collective-permute-start.30) | collective-permute-done | bytes 393248 | tf_op jit(solution)/shard_map/ppermute | solution.py:792
  325.0 6.5 %grad.1.refs_1_ = bf16[768,640]{1,0:T(8,128)(2,1)} custom-call(bf16[4,512,768]{2,1,0:T(8,128)(2,1)} %x_ref.5, bf16[2048,640]{1,0:T(8,128)(2,1)} %get-tuple-element.145.joined_ref, bf16[512,768]{1,0:T(8,128)(2,1)} %get-tuple-element.144.refs_0_, bf16[256,768]{1,0:T(8,128)(2,1)} %broadcast_select_fusion.2.refs_1_), custom_call_target="tpu_custom_call" | custom-call | flops 2013265920 | bytes 1966080 | tf_op jit(solution)/shard_map/grad/pallas_call | solution.py:687
  331.4 2.8 collective-permute-start.41
  335.3 2.7 collective-permute-start.28
  338.0 2.5 add_convert_fusion
  344.4 10.9 %collective-permute-done.28 = bf16[256,768]{1,0:T(8,128)(2,1)S(1)} collective-permute-done((bf16[256,768]{1,0:T(8,128)(2,1)S(1)}, bf16[256,768]{1,0:T(8,128)(2,1)S(1)}, u32[]{:S(2)}, u32[]{:S(2)}) %collective-permute-start.28) | collective-permute-done | bytes 393248 | tf_op jit(solution)/shard_map/ppermute | solution.py:792
  355.5 3.3 final.4.refs_0_
  362.3 2.3 fusion.4
  365.3 3.3 final.5
  (182 shorter events, 65.9 us)
Async XLA Ops:
  7.2 170.0 %all-gather.3.cloned.1.call-start = ((), (), s32[]{:S(2)}) async-start(), calls=%async_computation.1 | async-start | bytes 2027520 | tf_op jit(solution)/shard_map/all_gather | solution.py:920
  8.4 14.0 %copy-start.11 = (bf16[192,640]{1,0:T(8,128)(2,1)}, bf16[192,640]{1,0:T(8,128)(2,1)S(1)}, u32[]{:S(2)}) copy-start(bf16[192,640]{1,0:T(8,128)(2,1)S(1)} %pad_maximum_fusion.2.w0) | copy-start | bytes 737284
  8.4 33.0 %copy-start.29 = (f32[768]{0:T(1024)S(1)}, f32[768]{0:T(1024)}, u32[]{:S(2)}) copy-start(f32[768]{0:T(1024)} %param.30) | copy-start | bytes 9220
  8.4 9.1 %collective-permute-start.1 = (bf16[192,640]{1,0:T(8,128)(2,1)S(1)}, bf16[192,640]{1,0:T(8,128)(2,1)S(1)}, u32[]{:S(2)}, u32[]{:S(2)}) collective-permute-start(bf16[192,640]{1,0:T(8,128)(2,1)S(1)} %pad_maximum_fusion.2.w0), channel_id=1, source_target_pairs={{0,16},{16,0},{8,24},{24,8},{1,17},{17,1},{9,25},{25,9},{2,18},{18... | collective-permute-start | bytes 737288 | tf_op jit(solution)/shard_map/ppermute | solution.py:781
  14.3 34.1 %copy-start.13 = (bf16[192,1728]{1,0:T(8,128)(2,1)}, bf16[192,1728]{1,0:T(8,128)(2,1)S(1)}, u32[]{:S(2)}) copy-start(bf16[192,1728]{1,0:T(8,128)(2,1)S(1)} %constant_dynamic-update-slice_fusion) | copy-start | bytes 1990660
  14.3 17.1 %collective-permute-start.5 = (bf16[192,1728]{1,0:T(8,128)(2,1)S(1)}, bf16[192,1728]{1,0:T(8,128)(2,1)}, u32[]{:S(2)}, u32[]{:S(2)}) collective-permute-start(bf16[192,1728]{1,0:T(8,128)(2,1)S(1)} %constant_dynamic-update-slice_fusion), channel_id=1, source_target_pairs={{0,1},{1,0},{2,3},{3,2},{4,5},{5,4},{6,7},{7,6},{8,9},{9,8},{10,11... | collective-permute-start | bytes 1990664 | tf_op jit(solution)/shard_map/ppermute | solution.py:872
  16.0 15.4 %collective-permute-start.6 = (bf16[192,1728]{1,0:T(8,128)(2,1)S(1)}, bf16[192,1728]{1,0:T(8,128)(2,1)}, u32[]{:S(2)}, u32[]{:S(2)}) collective-permute-start(bf16[192,1728]{1,0:T(8,128)(2,1)S(1)} %constant_dynamic-update-slice_fusion), channel_id=1, source_target_pairs={{1,2},{2,1},{5,6},{6,5},{9,10},{10,9},{13,14},{14,13},{17,18},{18,... | collective-permute-start | bytes 1990664 | tf_op jit(solution)/shard_map/ppermute | solution.py:873
  17.5 16.7 %collective-permute-start.7 = (bf16[192,1728]{1,0:T(8,128)(2,1)S(1)}, bf16[192,1728]{1,0:T(8,128)(2,1)}, u32[]{:S(2)}, u32[]{:S(2)}) collective-permute-start(bf16[192,1728]{1,0:T(8,128)(2,1)S(1)} %constant_dynamic-update-slice_fusion), channel_id=1, source_target_pairs={{0,16},{16,0},{8,24},{24,8},{1,17},{17,1},{9,25},{25,9},{2,18},{18... | collective-permute-start | bytes 1990664 | tf_op jit(solution)/shard_map/ppermute | solution.py:874
  19.2 2.5 collective-permute-start
  19.2 3.2 collective-permute-start.2
  34.2 16.9 %collective-permute-start.8 = (bf16[192,1728]{1,0:T(8,128)(2,1)}, bf16[192,1728]{1,0:T(8,128)(2,1)}, u32[]{:S(2)}, u32[]{:S(2)}) collective-permute-start(bf16[192,1728]{1,0:T(8,128)(2,1)} %collective-permute-done.5), channel_id=1, source_target_pairs={{1,2},{2,1},{5,6},{6,5},{9,10},{10,9},{13,14},{14,13},{17,18},{18,... | collective-permute-start | bytes 1990664 | tf_op jit(solution)/shard_map/ppermute | solution.py:893
  35.8 19.2 %collective-permute-start.9 = (bf16[192,1728]{1,0:T(8,128)(2,1)}, bf16[192,1728]{1,0:T(8,128)(2,1)}, u32[]{:S(2)}, u32[]{:S(2)}) collective-permute-start(bf16[192,1728]{1,0:T(8,128)(2,1)} %collective-permute-done.6), channel_id=1, source_target_pairs={{1,0},{2,3},{5,4},{6,7},{9,8},{10,11},{13,12},{14,15},{17,16},{18,... | collective-permute-start | bytes 1990664 | tf_op jit(solution)/shard_map/ppermute | solution.py:894
  37.1 21.7 %collective-permute-start.4 = (bf16[1024,384]{1,0:T(8,128)(2,1)}, bf16[1024,384]{1,0:T(8,128)(2,1)}, u32[]{:S(2)}, u32[]{:S(2)}) collective-permute-start(bf16[1024,384]{1,0:T(8,128)(2,1)} %get-tuple-element.91.refs_3_.refs_7_), channel_id=1, source_target_pairs={{0,4},{1,5},{2,6},{3,7},{8,12},{9,13},{10,14},{11,15},{16,20},{17,... | collective-permute-start | bytes 2359304 | tf_op jit(solution)/shard_map/ppermute | solution.py:897
  48.4 30.0 %collective-permute-start.3 = (bf16[1024,384]{1,0:T(8,128)(2,1)}, bf16[1024,384]{1,0:T(8,128)(2,1)S(1)}, u32[]{:S(2)}, u32[]{:S(2)}) collective-permute-start(bf16[1024,384]{1,0:T(8,128)(2,1)} %get-tuple-element.90.refs_3_.refs_7_), channel_id=1, source_target_pairs={{0,4},{1,5},{2,6},{3,7},{8,12},{9,13},{10,14},{11,15},{16,20},{17,... | collective-permute-start | bytes 2359304 | tf_op jit(solution)/shard_map/ppermute | solution.py:897
  49.8 30.0 %collective-permute-start.11 = (bf16[192,1728]{1,0:T(8,128)(2,1)}, bf16[192,1728]{1,0:T(8,128)(2,1)}, u32[]{:S(2)}, u32[]{:S(2)}) collective-permute-start(bf16[192,1728]{1,0:T(8,128)(2,1)} %collective-permute-done.5), channel_id=1, source_target_pairs={{0,16},{16,0},{8,24},{24,8},{1,17},{17,1},{9,25},{25,9},{2,18},{18... | collective-permute-start | bytes 1990664 | tf_op jit(solution)/shard_map/ppermute | solution.py:874
  51.2 19.5 %collective-permute-start.10 = (bf16[192,1728]{1,0:T(8,128)(2,1)}, bf16[192,1728]{1,0:T(8,128)(2,1)}, u32[]{:S(2)}, u32[]{:S(2)}) collective-permute-start(bf16[192,1728]{1,0:T(8,128)(2,1)} %collective-permute-done.8), channel_id=1, source_target_pairs={{1,0},{2,3},{5,4},{6,7},{9,8},{10,11},{13,12},{14,15},{17,16},{18,... | collective-permute-start | bytes 1990664 | tf_op jit(solution)/shard_map/ppermute | solution.py:904
  57.1 49.5 %collective-permute-start.12 = (bf16[192,1728]{1,0:T(8,128)(2,1)}, bf16[192,1728]{1,0:T(8,128)(2,1)}, u32[]{:S(2)}, u32[]{:S(2)}) collective-permute-start(bf16[192,1728]{1,0:T(8,128)(2,1)} %broadcast_select_fusion.1.refs_6_), channel_id=1, source_target_pairs={{0,16},{16,0},{8,24},{24,8},{1,17},{17,1},{9,25},{25,9},{2,18},{18... | collective-permute-start | bytes 1990664 | tf_op jit(solution)/shard_map/ppermute | solution.py:874
  72.7 33.8 %collective-permute-start.13 = (bf16[192,1728]{1,0:T(8,128)(2,1)}, bf16[192,1728]{1,0:T(8,128)(2,1)}, u32[]{:S(2)}, u32[]{:S(2)}) collective-permute-start(bf16[192,1728]{1,0:T(8,128)(2,1)} %broadcast_select_fusion), channel_id=1, source_target_pairs={{0,16},{16,0},{8,24},{24,8},{1,17},{17,1},{9,25},{25,9},{2,18},{18... | collective-permute-start | bytes 1990664 | tf_op jit(solution)/shard_map/ppermute | solution.py:874
  74.0 21.9 %collective-permute-start.14 = (bf16[528,384]{1,0:T(8,128)(2,1)}, bf16[528,384]{1,0:T(8,128)(2,1)}, u32[]{:S(2)}, u32[]{:S(2)}) collective-permute-start(bf16[528,384]{1,0:T(8,128)(2,1)} %get-tuple-element.100.refs_6_.refs_1_.refs_7_.refs_4_), channel_id=1, source_target_pairs={{0,1},{1,0},{2,3},{3,2},{4,5},{5,4},{6,7},{7,6},{8,9},{9,8},{10,11... | collective-permute-start | bytes 1216520 | tf_op jit(solution)/shard_map/ppermute | solution.py:777
  78.4 28.1 %collective-permute-start.15 = (bf16[528,384]{1,0:T(8,128)(2,1)}, bf16[528,384]{1,0:T(8,128)(2,1)}, u32[]{:S(2)}, u32[]{:S(2)}) collective-permute-start(bf16[528,384]{1,0:T(8,128)(2,1)} %get-tuple-element.100.refs_6_.refs_1_.refs_7_.refs_4_), channel_id=1, source_target_pairs={{0,2},{2,0},{1,3},{3,1},{4,6},{6,4},{5,7},{7,5},{8,10},{10,8},{9,1... | collective-permute-start | bytes 1216520 | tf_op jit(solution)/shard_map/ppermute | solution.py:777
  79.7 26.8 %collective-permute-start.16 = (bf16[528,384]{1,0:T(8,128)(2,1)}, bf16[528,384]{1,0:T(8,128)(2,1)}, u32[]{:S(2)}, u32[]{:S(2)}) collective-permute-start(bf16[528,384]{1,0:T(8,128)(2,1)} %get-tuple-element.100.refs_6_.refs_1_.refs_7_.refs_4_), channel_id=1, source_target_pairs={{0,3},{3,0},{1,2},{2,1},{4,7},{7,4},{5,6},{6,5},{8,11},{11,8},{9,1... | collective-permute-start | bytes 1216520 | tf_op jit(solution)/shard_map/ppermute | solution.py:777
  95.9 15.0 %collective-permute-start.17 = (bf16[4,192,1728]{2,1,0:T(8,128)(2,1)}, bf16[4,192,1728]{2,1,0:T(8,128)(2,1)}, u32[]{:S(2)}, u32[]{:S(2)}) collective-permute-start(bf16[4,192,1728]{2,1,0:T(8,128)(2,1)} %pad_maximum_fusion.refs_7_.refs_11_), channel_id=1, source_target_pairs={{0,8},{8,0},{16,24},{24,16},{1,9},{9,1},{17,25},{25,17},{2,10},{10... | collective-permute-start | bytes 7962632 | tf_op jit(solution)/shard_map/ppermute | solution.py:931
  110.0 5.2 %collective-permute-start.18 = (bf16[4,192,1728]{2,1,0:T(8,128)(2,1)S(1)}, bf16[4,192,1728]{2,1,0:T(8,128)(2,1)}, u32[]{:S(2)}, u32[]{:S(2)}) collective-permute-start(bf16[4,192,1728]{2,1,0:T(8,128)(2,1)S(1)} %pad_maximum_fusion.1.refs_13_), channel_id=1, source_target_pairs={{0,8},{8,0},{16,24},{24,16},{1,9},{9,1},{17,25},{25,17},{2,10},{10... | collective-permute-start | bytes 7962632 | tf_op jit(solution)/shard_map/ppermute | solution.py:936
  165.3 15.7 %collective-permute-start.20 = (bf16[512,384]{1,0:T(8,128)(2,1)}, bf16[512,384]{1,0:T(8,128)(2,1)S(1)}, u32[]{:S(2)}, u32[]{:S(2)}) collective-permute-start(bf16[512,384]{1,0:T(8,128)(2,1)} %get-tuple-element.122), channel_id=1, source_target_pairs={{4,0},{5,1},{6,2},{7,3},{12,8},{13,9},{14,10},{15,11},{20,16},{21,... | collective-permute-start | bytes 1179656 | tf_op jit(solution)/shard_map/ppermute | solution.py:994
  175.9 17.3 %collective-permute-start.19 = (bf16[512,384]{1,0:T(8,128)(2,1)}, bf16[512,384]{1,0:T(8,128)(2,1)S(1)}, u32[]{:S(2)}, u32[]{:S(2)}) collective-permute-start(bf16[512,384]{1,0:T(8,128)(2,1)} %get-tuple-element.119), channel_id=1, source_target_pairs={{4,0},{5,1},{6,2},{7,3},{12,8},{13,9},{14,10},{15,11},{20,16},{21,... | collective-permute-start | bytes 1179656 | tf_op jit(solution)/shard_map/ppermute | solution.py:994
  198.1 51.7 %all-reduce.3.cloned.1.call-start = ((), (), s32[]{:S(2)}) async-start(), calls=%async_computation | async-start | bytes 1572864 | tf_op jit(solution)/shard_map/psum | solution.py:1042
  200.0 47.2 %collective-permute-start.21 = (bf16[256,768]{1,0:T(8,128)(2,1)S(1)}, bf16[256,768]{1,0:T(8,128)(2,1)S(1)}, u32[]{:S(2)}, u32[]{:S(2)}) collective-permute-start(bf16[256,768]{1,0:T(8,128)(2,1)S(1)} %broadcast_select_fusion.4), channel_id=1, source_target_pairs={{0,1},{1,0},{2,3},{3,2},{4,5},{5,4},{6,7},{7,6},{8,9},{9,8},{10,11... | collective-permute-start | bytes 1179656 | tf_op jit(solution)/shard_map/ppermute | solution.py:790
  248.3 19.9 %collective-permute-start.23 = (bf16[256,768]{1,0:T(8,128)(2,1)S(1)}, bf16[256,768]{1,0:T(8,128)(2,1)}, u32[]{:S(2)}, u32[]{:S(2)}) collective-permute-start(bf16[256,768]{1,0:T(8,128)(2,1)S(1)} %select_add_fusion.2.refs_11_), channel_id=1, source_target_pairs={{0,2},{2,0},{1,3},{3,1},{4,6},{6,4},{5,7},{7,5},{8,10},{10,8},{9,1... | collective-permute-start | bytes 1179656 | tf_op jit(solution)/shard_map/ppermute | solution.py:792
  258.9 13.4 %collective-permute-start.22 = (bf16[512,384]{1,0:T(8,128)(2,1)}, bf16[512,384]{1,0:T(8,128)(2,1)S(1)}, u32[]{:S(2)}, u32[]{:S(2)}) collective-permute-start(bf16[512,384]{1,0:T(8,128)(2,1)} %get-tuple-element.136), channel_id=1, source_target_pairs={{4,0},{5,1},{6,2},{7,3},{12,8},{13,9},{14,10},{15,11},{20,16},{21,... | collective-permute-start | bytes 1179656 | tf_op jit(solution)/shard_map/ppermute | solution.py:994
  262.9 32.2 %collective-permute-start.32 = (bf16[2,192,1728]{2,1,0:T(8,128)(2,1)}, bf16[2,192,1728]{2,1,0:T(8,128)(2,1)}, u32[]{:S(2)}, u32[]{:S(2)}) collective-permute-start(bf16[2,192,1728]{2,1,0:T(8,128)(2,1)} %dynamic-slice_bitcast_fusion), channel_id=1, source_target_pairs={{0,16},{16,0},{8,24},{24,8},{1,17},{17,1},{9,25},{25,9},{2,18},{18... | collective-permute-start | bytes 3981320 | tf_op jit(solution)/shard_map/ppermute | solution.py:807
  269.3 22.2 %collective-permute-start.25 = (bf16[256,768]{1,0:T(8,128)(2,1)S(1)}, bf16[256,768]{1,0:T(8,128)(2,1)}, u32[]{:S(2)}, u32[]{:S(2)}) collective-permute-start(bf16[256,768]{1,0:T(8,128)(2,1)S(1)} %add.117.refs_6_.done_ref), channel_id=1, source_target_pairs={{0,1},{1,0},{2,3},{3,2},{4,5},{5,4},{6,7},{7,6},{8,9},{9,8},{10,11... | collective-permute-start | bytes 1179656 | tf_op jit(solution)/shard_map/ppermute | solution.py:793
  279.1 19.0 %collective-permute-start.26 = (bf16[256,768]{1,0:T(8,128)(2,1)}, bf16[256,768]{1,0:T(8,128)(2,1)}, u32[]{:S(2)}, u32[]{:S(2)}) collective-permute-start(bf16[256,768]{1,0:T(8,128)(2,1)} %broadcast_select_fusion.3), channel_id=1, source_target_pairs={{0,1},{1,0},{2,3},{3,2},{4,5},{5,4},{6,7},{7,6},{8,9},{9,8},{10,11... | collective-permute-start | bytes 1179656 | tf_op jit(solution)/shard_map/ppermute | solution.py:790
  290.2 12.4 %collective-permute-start.24 = (bf16[512,384]{1,0:T(8,128)(2,1)}, bf16[512,384]{1,0:T(8,128)(2,1)S(1)}, u32[]{:S(2)}, u32[]{:S(2)}) collective-permute-start(bf16[512,384]{1,0:T(8,128)(2,1)} %get-tuple-element.142), channel_id=1, source_target_pairs={{4,0},{5,1},{6,2},{7,3},{12,8},{13,9},{14,10},{15,11},{20,16},{21,... | collective-permute-start | bytes 1179656 | tf_op jit(solution)/shard_map/ppermute | solution.py:994
  298.1 12.6 %collective-permute-start.33 = (bf16[192,1728]{1,0:T(8,128)(2,1)}, bf16[192,1728]{1,0:T(8,128)(2,1)}, u32[]{:S(2)}, u32[]{:S(2)}) collective-permute-start(bf16[192,1728]{1,0:T(8,128)(2,1)} %dynamic-slice_bitcast_fusion.1), channel_id=1, source_target_pairs={{0,8},{8,0},{16,24},{24,16},{1,9},{9,1},{17,25},{25,17},{2,10},{10... | collective-permute-start | bytes 1990664 | tf_op jit(solution)/shard_map/ppermute | solution.py:813
  299.2 21.1 %collective-permute-start.30 = (bf16[256,768]{1,0:T(8,128)(2,1)S(1)}, bf16[256,768]{1,0:T(8,128)(2,1)}, u32[]{:S(2)}, u32[]{:S(2)}) collective-permute-start(bf16[256,768]{1,0:T(8,128)(2,1)S(1)} %select_add_fusion.1.refs_6_), channel_id=1, source_target_pairs={{0,2},{2,0},{1,3},{3,1},{4,6},{6,4},{5,7},{7,5},{8,10},{10,8},{9,1... | collective-permute-start | bytes 1179656 | tf_op jit(solution)/shard_map/ppermute | solution.py:792
  307.7 12.7 %copy-start.8 = (bf16[256,768]{1,0:T(8,128)(2,1)S(1)}, bf16[256,768]{1,0:T(8,128)(2,1)}, u32[]{:S(2)}) copy-start(bf16[256,768]{1,0:T(8,128)(2,1)} %copy-done.7) | copy-start | bytes 1179652
  309.6 24.6 %collective-permute-start.27 = (bf16[256,768]{1,0:T(8,128)(2,1)}, bf16[256,768]{1,0:T(8,128)(2,1)}, u32[]{:S(2)}, u32[]{:S(2)}) collective-permute-start(bf16[256,768]{1,0:T(8,128)(2,1)} %broadcast_select_fusion.2.refs_1_), channel_id=1, source_target_pairs={{0,1},{1,0},{2,3},{3,2},{4,5},{5,4},{6,7},{7,6},{8,9},{9,8},{10,11... | collective-permute-start | bytes 1179656 | tf_op jit(solution)/shard_map/ppermute | solution.py:790
  312.9 25.1 %collective-permute-start.34 = (bf16[192,1728]{1,0:T(8,128)(2,1)}, bf16[192,1728]{1,0:T(8,128)(2,1)}, u32[]{:S(2)}, u32[]{:S(2)}) collective-permute-start(bf16[192,1728]{1,0:T(8,128)(2,1)} %bitcast_add_fusion.1), channel_id=1, source_target_pairs={{0,4},{4,0},{1,5},{5,1},{2,6},{6,2},{3,7},{7,3},{8,12},{12,8},{9,1... | collective-permute-start | bytes 1990664 | tf_op jit(solution)/shard_map/ppermute | solution.py:798
  322.2 1.2 collective-permute-start.39
  323.4 8.0 %collective-permute-start.40 = (f32[8,1408]{1,0:T(8,128)S(1)}, f32[8,1408]{1,0:T(8,128)S(1)}, u32[]{:S(2)}, u32[]{:S(2)}) collective-permute-start(f32[8,1408]{1,0:T(8,128)S(1)} %add.142), channel_id=1, source_target_pairs={{0,16},{16,0},{8,24},{24,8},{1,17},{17,1},{9,25},{25,9},{2,18},{18... | collective-permute-start | bytes 135176 | tf_op jit(solution)/shard_map/ppermute | solution.py:829
  331.4 24.1 %collective-permute-start.31 = (bf16[256,768]{1,0:T(8,128)(2,1)}, bf16[256,768]{1,0:T(8,128)(2,1)}, u32[]{:S(2)}, u32[]{:S(2)}) collective-permute-start(bf16[256,768]{1,0:T(8,128)(2,1)} %add.121.done_ref), channel_id=1, source_target_pairs={{0,1},{1,0},{2,3},{3,2},{4,5},{5,4},{6,7},{7,6},{8,9},{9,8},{10,11... | collective-permute-start | bytes 1179656 | tf_op jit(solution)/shard_map/ppermute | solution.py:793
  331.4 6.5 %collective-permute-start.41 = (f32[8,1408]{1,0:T(8,128)S(1)}, f32[8,1408]{1,0:T(8,128)S(1)}, u32[]{:S(2)}, u32[]{:S(2)}) collective-permute-start(f32[8,1408]{1,0:T(8,128)S(1)} %add.143), channel_id=1, source_target_pairs={{0,4},{4,0},{1,5},{5,1},{2,6},{6,2},{3,7},{7,3},{8,12},{12,8},{9,1... | collective-permute-start | bytes 135176 | tf_op jit(solution)/shard_map/ppermute | solution.py:798
  335.3 20.0 %collective-permute-start.28 = (bf16[256,768]{1,0:T(8,128)(2,1)S(1)}, bf16[256,768]{1,0:T(8,128)(2,1)S(1)}, u32[]{:S(2)}, u32[]{:S(2)}) collective-permute-start(bf16[256,768]{1,0:T(8,128)(2,1)S(1)} %select_add_fusion), channel_id=1, source_target_pairs={{0,2},{2,0},{1,3},{3,1},{4,6},{6,4},{5,7},{7,5},{8,10},{10,8},{9,1... | collective-permute-start | bytes 1179656 | tf_op jit(solution)/shard_map/ppermute | solution.py:792
  341.3 19.2 %collective-permute-start.35 = (bf16[192,640]{1,0:T(8,128)(2,1)}, bf16[192,640]{1,0:T(8,128)(2,1)}, u32[]{:S(2)}, u32[]{:S(2)}) collective-permute-start(bf16[192,640]{1,0:T(8,128)(2,1)} %get-tuple-element.169), channel_id=1, source_target_pairs={{0,8},{8,0},{16,24},{24,16},{1,9},{9,1},{17,25},{25,17},{2,10},{10... | collective-permute-start | bytes 737288 | tf_op jit(solution)/shard_map/ppermute | solution.py:823
  341.3 19.2 %collective-permute-start.36 = (bf16[192,640]{1,0:T(8,128)(2,1)S(1)}, bf16[192,640]{1,0:T(8,128)(2,1)}, u32[]{:S(2)}, u32[]{:S(2)}) collective-permute-start(bf16[192,640]{1,0:T(8,128)(2,1)S(1)} %get-tuple-element.171), channel_id=1, source_target_pairs={{0,16},{16,0},{8,24},{24,8},{1,17},{17,1},{9,25},{25,9},{2,18},{18... | collective-permute-start | bytes 737288 | tf_op jit(solution)/shard_map/ppermute | solution.py:823
  342.2 18.2 %collective-permute-start.37 = (bf16[192,640]{1,0:T(8,128)(2,1)S(1)}, bf16[192,640]{1,0:T(8,128)(2,1)}, u32[]{:S(2)}, u32[]{:S(2)}) collective-permute-start(bf16[192,640]{1,0:T(8,128)(2,1)S(1)} %get-tuple-element.170), channel_id=1, source_target_pairs={{0,24},{24,0},{8,16},{16,8},{1,25},{25,1},{9,17},{17,9},{2,26},{26... | collective-permute-start | bytes 737288 | tf_op jit(solution)/shard_map/ppermute | solution.py:823
  355.4 9.9 %collective-permute-start.29 = (bf16[256,768]{1,0:T(8,128)(2,1)S(1)}, bf16[256,768]{1,0:T(8,128)(2,1)}, u32[]{:S(2)}, u32[]{:S(2)}) collective-permute-start(bf16[256,768]{1,0:T(8,128)(2,1)S(1)} %add.120.done_ref), channel_id=1, source_target_pairs={{0,1},{1,0},{2,3},{3,2},{4,5},{5,4},{6,7},{7,6},{8,9},{9,8},{10,11... | collective-permute-start | bytes 1179656 | tf_op jit(solution)/shard_map/ppermute | solution.py:793
  361.9 6.7 %collective-permute-start.38 = (bf16[192,640]{1,0:T(8,128)(2,1)S(1)}, bf16[192,640]{1,0:T(8,128)(2,1)S(1)}, u32[]{:S(2)}, u32[]{:S(2)}) collective-permute-start(bf16[192,640]{1,0:T(8,128)(2,1)S(1)} %fusion.2), channel_id=1, source_target_pairs={{0,4},{4,0},{1,5},{5,1},{2,6},{6,2},{3,7},{7,3},{8,12},{12,8},{9,1... | collective-permute-start | bytes 737288 | tf_op jit(solution)/shard_map/ppermute | solution.py:798
  (28 other events, 110.6 us)
Sparse Core Ops, SparseCore 0:
  111.0 43.0 all-gather.2
  201.9 47.6 all-reduce.2

commit v5 on v4

--- a/solution.py
+++ b/solution.py
@@ -1042,7 +1042,7 @@
                 reduced[i] = lax.psum(ys[i], "tp")
             else:
                 reduced[i] = tp_reduce(ys[i], odd)
-    after = after + [reduced[seqs - 1][0]]
+    after = after + [reduced[seqs - 1][1]]
     g_qkv = grad_call(hidden_in, joined, after)
     for s in range(seqs - chunk, seqs):
         finish(s, [g_qkv])

time: 381 us -> 376 us (0.987)
  waiting for transfers between devices: 58 us -> 53.8 us
    ppermute x3, waiting for transfers between devices: 20.2 us -> 11.4 us  [tp_reduce(): done = pair + lax.ppermute(pair, 'tp', FAR)]
  transfers between devices with their start and end apart: 44 -> 44, of which waited for: 15 -> 17; matrix products, arithmetic and copies ran while one was open for 13% -> 12% of each run, Pallas kernels for 50% -> 51%
where the time goes in v5:
time: 376 us; the launch traced here: 372 us
  Pallas kernels  192 us (51%)
  starting transfers between devices  57.2 us (15%)
  waiting for transfers between devices  53.8 us (14%)
  other arithmetic  30.5 us (8%)
  local copies, waits for them, and re-layouts  23 us (6%)
  between operations  15 us (4%)
    pallas_call x2, Pallas kernels, ffn_call(): pl.pallas_call(functools.partial(ffn_kernel, chained=bool(chained), final...  83 us
    pallas_call x4, Pallas kernels, attn_bwd_call(): pl.pallas_call(functools.partial(attn_bwd_kernel, heads=heads, size=size,...  36.8 us
    pallas_call x2, Pallas kernels, attn_fwd_call(): pl.pallas_call(functools.partial(attn_fwd_kernel, heads=heads, size=size,...  23.5 us
    pallas_call x4, Pallas kernels, dx_call(): pl.pallas_call(functools.partial(dx_kernel, nkv=len(dkvs)), out_shape=(ja...  16.7 us
    pallas_call x2, Pallas kernels, qkv_call(): pl.pallas_call(functools.partial(qkv_kernel, scale=scale), out_shape=(jax...  12.6 us
    ppermute x3, waiting for transfers between devices, tp_reduce(): done = pair + lax.ppermute(pair, 'tp', FAR)  11.4 us
    ppermute x4, waiting for transfers between devices, attn_bwd(): dkvs = (out[2], lax.ppermute(out[3], 'ctx', ((1, 0),)))  11 us
    ppermute x3, waiting for transfers between devices, tp_gather(): return [value] + [lax.ppermute(value, 'tp', p) for p in (SWAP, FAR, ACROSS)]  10.5 us
  transfers between devices with their start and end apart: 44, of which 17 were waited for; matrix products, arithmetic and copies ran while one was open for 12% of the time, Pallas kernels for 51%

profile of v5, /device:TPU:0, one launch (start us, length us, event | category | flops | bytes accessed | tf_op | source)
XLA Modules:
  0.0 371.5 jit_solution(14592731366155312133)
XLA Ops:
  8.4 3.0 collective-permute-start.1
  22.4 6.3 %qkv.2 = (bf16[1024,192]{1,0:T(8,128)(2,1)}, bf16[1024,384]{1,0:T(8,128)(2,1)}, bf16[768,640]{1,0:T(8,128)(2,1)}) custom-call(s32[3]{0:T(128)} %pad_add_fusion.ids, bf16[4,512,768]{2,1,0:T(8,128)(2,1)} %x_ref.5, bf16[192,640]{1,0:T(8,128)(2,1)} %copy-done.13, bf16[192,640]{1,0:T(8,128)(2,1)} %copy-done.18, bf16[192,640]{1,0:T(8,128)(2,1)} %copy-done.17, ...), custom_call_target="tpu_custom_call" | custom-call | flops 1006632960 | bytes 5046272 | tf_op jit(solution)/shard_map/qkv/pallas_call | solution.py:83
  28.7 2.7 collective-permute-done.5
  31.4 2.8 collective-permute-done.7
  37.1 4.3 %collective-permute-start.4 = (bf16[1024,384]{1,0:T(8,128)(2,1)}, bf16[1024,384]{1,0:T(8,128)(2,1)}, u32[]{:S(2)}, u32[]{:S(2)}) collective-permute-start(bf16[1024,384]{1,0:T(8,128)(2,1)} %get-tuple-element.91.refs_3_.refs_7_), channel_id=1, source_target_pairs={{0,4},{1,5},{2,6},{3,7},{8,12},{9,13},{10,14},{11,15},{16,20},{17,... | collective-permute-start | bytes 2359304 | tf_op jit(solution)/shard_map/ppermute | solution.py:897
  42.1 6.3 %qkv.3 = (bf16[1024,192]{1,0:T(8,128)(2,1)}, bf16[1024,384]{1,0:T(8,128)(2,1)}, bf16[768,640]{1,0:T(8,128)(2,1)}) custom-call(s32[3]{0:T(128)} %pad_add_fusion.ids, bf16[4,512,768]{2,1,0:T(8,128)(2,1)} %x_ref.5, bf16[192,640]{1,0:T(8,128)(2,1)} %copy-done.13, bf16[192,640]{1,0:T(8,128)(2,1)} %copy-done.18, bf16[192,640]{1,0:T(8,128)(2,1)} %copy-done.17, ...), custom_call_target="tpu_custom_call" | custom-call | flops 1006632960 | bytes 5046272 | tf_op jit(solution)/shard_map/qkv/pallas_call | solution.py:83
  52.4 2.6 collective-permute-done.9
  55.0 2.0 broadcast_select_fusion.1.refs_6_
  58.8 11.8 %attn_fwd.2 = (bf16[4,3,512,1024]{3,2,1,0:T(8,128)(2,1)}, bf16[2,3,512,1024]{3,2,1,0:T(8,128)(2,1)}, bf16[528,384]{1,0:T(8,128)(2,1)}, f32[1024,128]{1,0:T(8,128)}) custom-call(s32[3]{0:T(128)} %pad_add_fusion.ids, bf16[1024,192]{1,0:T(8,128)(2,1)} %get-tuple-element.88.refs_0_, bf16[4,3,512,1024]{3,2,1,0:T(8,128)(2,1)} %refs_1_.3, ...), custom_call_target="tpu_custom_call" | custom-call | flops 2415919104 | bytes 18874368 | tf_op jit(solution)/shard_map/attn_fwd/pallas_call | solution.py:200
  70.6 2.0 broadcast_select_fusion
  74.0 4.4 %collective-permute-start.14 = (bf16[528,384]{1,0:T(8,128)(2,1)}, bf16[528,384]{1,0:T(8,128)(2,1)}, u32[]{:S(2)}, u32[]{:S(2)}) collective-permute-start(bf16[528,384]{1,0:T(8,128)(2,1)} %get-tuple-element.100.refs_6_.refs_1_.refs_7_.refs_4_), channel_id=1, source_target_pairs={{0,1},{1,0},{2,3},{3,2},{4,5},{5,4},{6,7},{7,6},{8,9},{9,8},{10,11... | collective-permute-start | bytes 1216520 | tf_op jit(solution)/shard_map/ppermute | solution.py:777
  81.2 3.0 pad_maximum_fusion.refs_7_.refs_11_
  84.2 11.7 %attn_fwd.3 = (bf16[4,3,512,1024]{3,2,1,0:T(8,128)(2,1)}, bf16[2,3,512,1024]{3,2,1,0:T(8,128)(2,1)}, bf16[528,384]{1,0:T(8,128)(2,1)}, f32[1024,128]{1,0:T(8,128)}) custom-call(s32[3]{0:T(128)} %pad_add_fusion.ids, bf16[1024,192]{1,0:T(8,128)(2,1)} %get-tuple-element.89.refs_5_.refs_0_, ...), custom_call_target="tpu_custom_call", output_to_operand_aliasing={{0}: (6, {})} | custom-call | flops 2415919104 | bytes 18874368 | tf_op jit(solution)/shard_map/attn_fwd/pallas_call | solution.py:200
  96.0 10.5 %collective-permute-done.15.refs_3_.refs_9_ = bf16[528,384]{1,0:T(8,128)(2,1)} collective-permute-done((bf16[528,384]{1,0:T(8,128)(2,1)}, bf16[528,384]{1,0:T(8,128)(2,1)}, u32[]{:S(2)}, u32[]{:S(2)}) %collective-permute-start.15) | collective-permute-done | bytes 405536 | tf_op jit(solution)/shard_map/ppermute | solution.py:777
  106.5 1.9 pad_maximum_fusion.1.refs_13_
  110.8 4.4 %collective-permute-done.18.refs_14_ = bf16[4,192,1728]{2,1,0:T(8,128)(2,1)} collective-permute-done((bf16[4,192,1728]{2,1,0:T(8,128)(2,1)S(1)}, bf16[4,192,1728]{2,1,0:T(8,128)(2,1)}, u32[]{:S(2)}, u32[]{:S(2)}) %collective-permute-start.18) | collective-permute-done | bytes 2654240 | tf_op jit(solution)/shard_map/ppermute | solution.py:936
  115.2 40.9 %ffn.2 = (bf16[4,512,768]{2,1,0:T(8,128)(2,1)}, f32[1024,768]{1,0:T(8,128)}, bf16[1024,192]{1,0:T(8,128)(2,1)}, f32[8,768]{1,0:T(8,128)}, f32[768,768]{1,0:T(8,1...) custom-call(s32[3]{0:T(128)} %pad_add_fusion.ids, bf16[4,512,768]{2,1,0:T(8,128)(2,1)} %x_ref.5, ...), custom_call_target="tpu_custom_call" | custom-call | flops 24159191040 | bytes 22020096 | tf_op jit(solution)/shard_map/ffn/pallas_call | solution.py:567
  156.1 9.2 %attn_bwd.4 = (bf16[4,3,512,1024]{3,2,1,0:T(8,128)(2,1)}, bf16[512,192]{1,0:T(8,128)(2,1)}, bf16[512,384]{1,0:T(8,128)(2,1)}, bf16[512,384]{1,0:T(8,128)(2,1)}) custom-call(s32[3]{0:T(128)} %pad_add_fusion.ids, bf16[1024,192]{1,0:T(8,128)(2,1)} %get-tuple-element.88.refs_0_, bf16[2,3,512,1024]{3,2,1,0:T(8,128)(2,1)} %get-tuple-element.112.refs_1_, ...), custom_call_target="tpu_custom_call" | custom-call | flops 8999999488 | bytes 1000 | tf_op jit(solution)/shard_map/attn_bwd/pallas_call | solution.py:331
  166.6 9.3 %attn_bwd.5 = (bf16[4,3,512,1024]{3,2,1,0:T(8,128)(2,1)}, bf16[512,192]{1,0:T(8,128)(2,1)}, bf16[512,384]{1,0:T(8,128)(2,1)}, bf16[512,384]{1,0:T(8,128)(2,1)}) custom-call(s32[3]{0:T(128)} %pad_add_fusion.ids, bf16[1024,192]{1,0:T(8,128)(2,1)} %get-tuple-element.88.refs_0_, ...), custom_call_target="tpu_custom_call", output_to_operand_aliasing={{0}: (9, {})} | custom-call | flops 8999999488 | bytes 1000 | tf_op jit(solution)/shard_map/attn_bwd/pallas_call | solution.py:331
  177.2 2.3 dynamic-slice_bitcast_fusion.2
  181.7 4.1 %dx.4 = (bf16[512,768]{1,0:T(8,128)(2,1)}, bf16[2048,640]{1,0:T(8,128)(2,1)}, f32[8,640]{1,0:T(8,128)}) custom-call(s32[3]{0:T(128)} %pad_add_fusion.ids, bf16[512,192]{1,0:T(8,128)(2,1)} %get-tuple-element.116.refs_9_.dq_ref, bf16[512,384]{1,0:T(8,128)(2,1)} %get-tuple-element.121.refs_0_, bf16[512,384]{1,0:T(8,128)(2,1)} %copy-done.33, ...), custom_call_target="tpu_custom_call" | custom-call | flops 3000000000 | bytes 1000 | tf_op jit(solution)/shard_map/dx/pallas_call | solution.py:640
  185.9 7.3 %collective-permute-done.19.refs_1_ = bf16[512,384]{1,0:T(8,128)(2,1)S(1)} collective-permute-done((bf16[512,384]{1,0:T(8,128)(2,1)}, bf16[512,384]{1,0:T(8,128)(2,1)S(1)}, u32[]{:S(2)}, u32[]{:S(2)}) %collective-permute-start.19) | collective-permute-done | bytes 393248 | tf_op jit(solution)/shard_map/ppermute | solution.py:994
  193.9 4.1 %dx.5 = (bf16[512,768]{1,0:T(8,128)(2,1)}, bf16[2048,640]{1,0:T(8,128)(2,1)}, f32[8,640]{1,0:T(8,128)}) custom-call(s32[3]{0:T(128)} %pad_add_fusion.ids, bf16[512,192]{1,0:T(8,128)(2,1)} %get-tuple-element.117.refs_3_.dq_ref, bf16[512,384]{1,0:T(8,128)(2,1)} %get-tuple-element.118.refs_0_, ...), custom_call_target="tpu_custom_call", output_to_operand_aliasing={{1}: (5, {})} | custom-call | flops 3000000000 | bytes 1000 | tf_op jit(solution)/shard_map/dx/pallas_call | solution.py:640
  200.0 5.1 %collective-permute-start.21 = (bf16[256,768]{1,0:T(8,128)(2,1)S(1)}, bf16[256,768]{1,0:T(8,128)(2,1)S(1)}, u32[]{:S(2)}, u32[]{:S(2)}) collective-permute-start(bf16[256,768]{1,0:T(8,128)(2,1)S(1)} %broadcast_select_fusion.4), channel_id=1, source_target_pairs={{0,1},{1,0},{2,3},{3,2},{4,5},{5,4},{6,7},{7,6},{8,9},{9,8},{10,11... | collective-permute-start | bytes 1179656 | tf_op jit(solution)/shard_map/ppermute | solution.py:790
  205.0 42.1 %ffn.3 = (bf16[4,512,768]{2,1,0:T(8,128)(2,1)}, f32[1024,768]{1,0:T(8,128)}, bf16[1024,192]{1,0:T(8,128)(2,1)}, f32[8,768]{1,0:T(8,128)}, bf16[768,1728]{1,0:T(8,128)(2,1)}) custom-call(s32[3]{0:T(128)} %pad_add_fusion.ids, bf16[4,512,768]{2,1,0:T(8,128)(2,1)} %x_ref.5, ...), custom_call_target="tpu_custom_call", output_to_operand_aliasing={{0}: (19, {})} | custom-call | flops 24159191040 | bytes 22020096 | tf_op jit(solution)/shard_map/ffn/pallas_call | solution.py:567
  249.8 9.1 %attn_bwd.6 = (bf16[4,3,512,1024]{3,2,1,0:T(8,128)(2,1)}, bf16[512,192]{1,0:T(8,128)(2,1)}, bf16[512,384]{1,0:T(8,128)(2,1)}, bf16[512,384]{1,0:T(8,128)(2,1)}) custom-call(s32[3]{0:T(128)} %pad_add_fusion.ids, bf16[1024,192]{1,0:T(8,128)(2,1)} %get-tuple-element.89.refs_5_.refs_0_, ...), custom_call_target="tpu_custom_call", output_to_operand_aliasing={{0}: (9, {})} | custom-call | flops 8999999488 | bytes 1000 | tf_op jit(solution)/shard_map/attn_bwd/pallas_call | solution.py:331
  260.4 2.5 dynamic-slice_bitcast_fusion
  264.2 4.0 %collective-permute-done.23 = bf16[256,768]{1,0:T(8,128)(2,1)} collective-permute-done((bf16[256,768]{1,0:T(8,128)(2,1)S(1)}, bf16[256,768]{1,0:T(8,128)(2,1)}, u32[]{:S(2)}, u32[]{:S(2)}) %collective-permute-start.23) | collective-permute-done | bytes 393248 | tf_op jit(solution)/shard_map/ppermute | solution.py:792
  269.4 2.8 plain.1.refs_5_.refs_0_
  273.0 4.2 %dx.6 = (bf16[512,768]{1,0:T(8,128)(2,1)}, bf16[2048,640]{1,0:T(8,128)(2,1)}, f32[8,640]{1,0:T(8,128)}) custom-call(s32[3]{0:T(128)} %pad_add_fusion.ids, bf16[512,192]{1,0:T(8,128)(2,1)} %get-tuple-element.134.refs_0_.dq_ref.refs_4_, bf16[512,384]{1,0:T(8,128)(2,1)} %get-tuple-element.135.refs_0_, ...), custom_call_target="tpu_custom_call", output_to_operand_aliasing={{1}: (5, {})} | custom-call | flops 3000000000 | bytes 1000 | tf_op jit(solution)/shard_map/dx/pallas_call | solution.py:640
  277.2 1.9 broadcast_select_fusion.3
  279.1 1.8 collective-permute-start.26
  281.0 9.3 %attn_bwd.7 = (bf16[4,3,512,1024]{3,2,1,0:T(8,128)(2,1)}, bf16[512,192]{1,0:T(8,128)(2,1)}, bf16[512,384]{1,0:T(8,128)(2,1)}, bf16[512,384]{1,0:T(8,128)(2,1)}) custom-call(s32[3]{0:T(128)} %pad_add_fusion.ids, bf16[1024,192]{1,0:T(8,128)(2,1)} %get-tuple-element.89.refs_5_.refs_0_, ...), custom_call_target="tpu_custom_call", output_to_operand_aliasing={{0}: (9, {})} | custom-call | flops 8999999488 | bytes 1000 | tf_op jit(solution)/shard_map/attn_bwd/pallas_call | solution.py:331
  291.5 3.6 final.3.refs_5_.refs_0_
  295.1 2.0 bitcast_add_fusion
  300.6 2.1 collective-permute-done.24.refs_1_
  303.4 4.3 %dx.7 = (bf16[512,768]{1,0:T(8,128)(2,1)}, bf16[2048,640]{1,0:T(8,128)(2,1)}, f32[8,640]{1,0:T(8,128)}) custom-call(s32[3]{0:T(128)} %pad_add_fusion.ids, bf16[512,192]{1,0:T(8,128)(2,1)} %get-tuple-element.140.refs_1_.dq_ref.refs_4_, bf16[512,384]{1,0:T(8,128)(2,1)} %get-tuple-element.141.refs_0_, ...), custom_call_target="tpu_custom_call", output_to_operand_aliasing={{1}: (5, {})} | custom-call | flops 3000000000 | bytes 1000 | tf_op jit(solution)/shard_map/dx/pallas_call | solution.py:640
  310.1 2.2 bitcast_add_fusion.1
  312.3 2.1 collective-permute-start.34
  314.4 5.9 %collective-permute-done.30 = bf16[256,768]{1,0:T(8,128)(2,1)} collective-permute-done((bf16[256,768]{1,0:T(8,128)(2,1)S(1)}, bf16[256,768]{1,0:T(8,128)(2,1)}, u32[]{:S(2)}, u32[]{:S(2)}) %collective-permute-start.30) | collective-permute-done | bytes 393248 | tf_op jit(solution)/shard_map/ppermute | solution.py:792
  324.3 3.1 collective-permute-done.27
  327.4 1.7 collective-permute-start.28
  330.2 6.4 %grad.1.refs_1_ = bf16[768,640]{1,0:T(8,128)(2,1)} custom-call(bf16[4,512,768]{2,1,0:T(8,128)(2,1)} %x_ref.5, bf16[2048,640]{1,0:T(8,128)(2,1)} %get-tuple-element.145.joined_ref, bf16[512,768]{1,0:T(8,128)(2,1)} %get-tuple-element.144.refs_0_, bf16[256,768]{1,0:T(8,128)(2,1)} %copy-done.10), custom_call_target="tpu_custom_call" | custom-call | flops 2013265920 | bytes 1966080 | tf_op jit(solution)/shard_map/grad/pallas_call | solution.py:687
  336.6 2.6 add_convert_fusion
  347.4 3.3 final.4.refs_0_
  355.1 1.8 collective-permute-start.38
  357.0 2.3 fusion.4
  359.3 3.3 final.5
  (188 shorter events, 70.1 us)
Async XLA Ops:
  7.2 170.0 %all-gather.3.cloned.1.call-start = ((), (), s32[]{:S(2)}) async-start(), calls=%async_computation.1 | async-start | bytes 2027520 | tf_op jit(solution)/shard_map/all_gather | solution.py:920
  8.4 33.0 %copy-start.32 = (f32[768]{0:T(1024)S(1)}, f32[768]{0:T(1024)}, u32[]{:S(2)}) copy-start(f32[768]{0:T(1024)} %param.30) | copy-start | bytes 9220
  8.4 9.1 %collective-permute-start.1 = (bf16[192,640]{1,0:T(8,128)(2,1)S(1)}, bf16[192,640]{1,0:T(8,128)(2,1)S(1)}, u32[]{:S(2)}, u32[]{:S(2)}) collective-permute-start(bf16[192,640]{1,0:T(8,128)(2,1)S(1)} %pad_maximum_fusion.2.w0), channel_id=1, source_target_pairs={{0,16},{16,0},{8,24},{24,8},{1,17},{17,1},{9,25},{25,9},{2,18},{18... | collective-permute-start | bytes 737288 | tf_op jit(solution)/shard_map/ppermute | solution.py:781
  14.3 34.0 %copy-start.16 = (bf16[192,1728]{1,0:T(8,128)(2,1)}, bf16[192,1728]{1,0:T(8,128)(2,1)S(1)}, u32[]{:S(2)}) copy-start(bf16[192,1728]{1,0:T(8,128)(2,1)S(1)} %constant_dynamic-update-slice_fusion) | copy-start | bytes 1990660
  14.3 17.1 %collective-permute-start.5 = (bf16[192,1728]{1,0:T(8,128)(2,1)S(1)}, bf16[192,1728]{1,0:T(8,128)(2,1)}, u32[]{:S(2)}, u32[]{:S(2)}) collective-permute-start(bf16[192,1728]{1,0:T(8,128)(2,1)S(1)} %constant_dynamic-update-slice_fusion), channel_id=1, source_target_pairs={{0,1},{1,0},{2,3},{3,2},{4,5},{5,4},{6,7},{7,6},{8,9},{9,8},{10,11... | collective-permute-start | bytes 1990664 | tf_op jit(solution)/shard_map/ppermute | solution.py:872
  16.0 15.4 %collective-permute-start.6 = (bf16[192,1728]{1,0:T(8,128)(2,1)S(1)}, bf16[192,1728]{1,0:T(8,128)(2,1)}, u32[]{:S(2)}, u32[]{:S(2)}) collective-permute-start(bf16[192,1728]{1,0:T(8,128)(2,1)S(1)} %constant_dynamic-update-slice_fusion), channel_id=1, source_target_pairs={{1,2},{2,1},{5,6},{6,5},{9,10},{10,9},{13,14},{14,13},{17,18},{18,... | collective-permute-start | bytes 1990664 | tf_op jit(solution)/shard_map/ppermute | solution.py:873
  17.5 16.7 %collective-permute-start.7 = (bf16[192,1728]{1,0:T(8,128)(2,1)S(1)}, bf16[192,1728]{1,0:T(8,128)(2,1)}, u32[]{:S(2)}, u32[]{:S(2)}) collective-permute-start(bf16[192,1728]{1,0:T(8,128)(2,1)S(1)} %constant_dynamic-update-slice_fusion), channel_id=1, source_target_pairs={{0,16},{16,0},{8,24},{24,8},{1,17},{17,1},{9,25},{25,9},{2,18},{18... | collective-permute-start | bytes 1990664 | tf_op jit(solution)/shard_map/ppermute | solution.py:874
  19.2 2.5 collective-permute-start
  19.2 3.2 collective-permute-start.2
  34.2 16.9 %collective-permute-start.8 = (bf16[192,1728]{1,0:T(8,128)(2,1)}, bf16[192,1728]{1,0:T(8,128)(2,1)}, u32[]{:S(2)}, u32[]{:S(2)}) collective-permute-start(bf16[192,1728]{1,0:T(8,128)(2,1)} %collective-permute-done.5), channel_id=1, source_target_pairs={{1,2},{2,1},{5,6},{6,5},{9,10},{10,9},{13,14},{14,13},{17,18},{18,... | collective-permute-start | bytes 1990664 | tf_op jit(solution)/shard_map/ppermute | solution.py:893
  35.8 19.2 %collective-permute-start.9 = (bf16[192,1728]{1,0:T(8,128)(2,1)}, bf16[192,1728]{1,0:T(8,128)(2,1)}, u32[]{:S(2)}, u32[]{:S(2)}) collective-permute-start(bf16[192,1728]{1,0:T(8,128)(2,1)} %collective-permute-done.6), channel_id=1, source_target_pairs={{1,0},{2,3},{5,4},{6,7},{9,8},{10,11},{13,12},{14,15},{17,16},{18,... | collective-permute-start | bytes 1990664 | tf_op jit(solution)/shard_map/ppermute | solution.py:894
  37.1 21.7 %collective-permute-start.4 = (bf16[1024,384]{1,0:T(8,128)(2,1)}, bf16[1024,384]{1,0:T(8,128)(2,1)}, u32[]{:S(2)}, u32[]{:S(2)}) collective-permute-start(bf16[1024,384]{1,0:T(8,128)(2,1)} %get-tuple-element.91.refs_3_.refs_7_), channel_id=1, source_target_pairs={{0,4},{1,5},{2,6},{3,7},{8,12},{9,13},{10,14},{11,15},{16,20},{17,... | collective-permute-start | bytes 2359304 | tf_op jit(solution)/shard_map/ppermute | solution.py:897
  48.4 30.0 %collective-permute-start.3 = (bf16[1024,384]{1,0:T(8,128)(2,1)}, bf16[1024,384]{1,0:T(8,128)(2,1)S(1)}, u32[]{:S(2)}, u32[]{:S(2)}) collective-permute-start(bf16[1024,384]{1,0:T(8,128)(2,1)} %get-tuple-element.90.refs_3_.refs_7_), channel_id=1, source_target_pairs={{0,4},{1,5},{2,6},{3,7},{8,12},{9,13},{10,14},{11,15},{16,20},{17,... | collective-permute-start | bytes 2359304 | tf_op jit(solution)/shard_map/ppermute | solution.py:897
  49.7 30.0 %collective-permute-start.11 = (bf16[192,1728]{1,0:T(8,128)(2,1)}, bf16[192,1728]{1,0:T(8,128)(2,1)}, u32[]{:S(2)}, u32[]{:S(2)}) collective-permute-start(bf16[192,1728]{1,0:T(8,128)(2,1)} %collective-permute-done.5), channel_id=1, source_target_pairs={{0,16},{16,0},{8,24},{24,8},{1,17},{17,1},{9,25},{25,9},{2,18},{18... | collective-permute-start | bytes 1990664 | tf_op jit(solution)/shard_map/ppermute | solution.py:874
  51.1 19.5 %collective-permute-start.10 = (bf16[192,1728]{1,0:T(8,128)(2,1)}, bf16[192,1728]{1,0:T(8,128)(2,1)}, u32[]{:S(2)}, u32[]{:S(2)}) collective-permute-start(bf16[192,1728]{1,0:T(8,128)(2,1)} %collective-permute-done.8), channel_id=1, source_target_pairs={{1,0},{2,3},{5,4},{6,7},{9,8},{10,11},{13,12},{14,15},{17,16},{18,... | collective-permute-start | bytes 1990664 | tf_op jit(solution)/shard_map/ppermute | solution.py:904
  57.1 49.4 %collective-permute-start.12 = (bf16[192,1728]{1,0:T(8,128)(2,1)}, bf16[192,1728]{1,0:T(8,128)(2,1)}, u32[]{:S(2)}, u32[]{:S(2)}) collective-permute-start(bf16[192,1728]{1,0:T(8,128)(2,1)} %broadcast_select_fusion.1.refs_6_), channel_id=1, source_target_pairs={{0,16},{16,0},{8,24},{24,8},{1,17},{17,1},{9,25},{25,9},{2,18},{18... | collective-permute-start | bytes 1990664 | tf_op jit(solution)/shard_map/ppermute | solution.py:874
  72.7 33.8 %collective-permute-start.13 = (bf16[192,1728]{1,0:T(8,128)(2,1)}, bf16[192,1728]{1,0:T(8,128)(2,1)}, u32[]{:S(2)}, u32[]{:S(2)}) collective-permute-start(bf16[192,1728]{1,0:T(8,128)(2,1)} %broadcast_select_fusion), channel_id=1, source_target_pairs={{0,16},{16,0},{8,24},{24,8},{1,17},{17,1},{9,25},{25,9},{2,18},{18... | collective-permute-start | bytes 1990664 | tf_op jit(solution)/shard_map/ppermute | solution.py:874
  74.0 21.9 %collective-permute-start.14 = (bf16[528,384]{1,0:T(8,128)(2,1)}, bf16[528,384]{1,0:T(8,128)(2,1)}, u32[]{:S(2)}, u32[]{:S(2)}) collective-permute-start(bf16[528,384]{1,0:T(8,128)(2,1)} %get-tuple-element.100.refs_6_.refs_1_.refs_7_.refs_4_), channel_id=1, source_target_pairs={{0,1},{1,0},{2,3},{3,2},{4,5},{5,4},{6,7},{7,6},{8,9},{9,8},{10,11... | collective-permute-start | bytes 1216520 | tf_op jit(solution)/shard_map/ppermute | solution.py:777
  78.4 28.1 %collective-permute-start.15 = (bf16[528,384]{1,0:T(8,128)(2,1)}, bf16[528,384]{1,0:T(8,128)(2,1)}, u32[]{:S(2)}, u32[]{:S(2)}) collective-permute-start(bf16[528,384]{1,0:T(8,128)(2,1)} %get-tuple-element.100.refs_6_.refs_1_.refs_7_.refs_4_), channel_id=1, source_target_pairs={{0,2},{2,0},{1,3},{3,1},{4,6},{6,4},{5,7},{7,5},{8,10},{10,8},{9,1... | collective-permute-start | bytes 1216520 | tf_op jit(solution)/shard_map/ppermute | solution.py:777
  79.7 26.8 %collective-permute-start.16 = (bf16[528,384]{1,0:T(8,128)(2,1)}, bf16[528,384]{1,0:T(8,128)(2,1)}, u32[]{:S(2)}, u32[]{:S(2)}) collective-permute-start(bf16[528,384]{1,0:T(8,128)(2,1)} %get-tuple-element.100.refs_6_.refs_1_.refs_7_.refs_4_), channel_id=1, source_target_pairs={{0,3},{3,0},{1,2},{2,1},{4,7},{7,4},{5,6},{6,5},{8,11},{11,8},{9,1... | collective-permute-start | bytes 1216520 | tf_op jit(solution)/shard_map/ppermute | solution.py:777
  95.9 14.9 %collective-permute-start.17 = (bf16[4,192,1728]{2,1,0:T(8,128)(2,1)}, bf16[4,192,1728]{2,1,0:T(8,128)(2,1)}, u32[]{:S(2)}, u32[]{:S(2)}) collective-permute-start(bf16[4,192,1728]{2,1,0:T(8,128)(2,1)} %pad_maximum_fusion.refs_7_.refs_11_), channel_id=1, source_target_pairs={{0,8},{8,0},{16,24},{24,16},{1,9},{9,1},{17,25},{25,17},{2,10},{10... | collective-permute-start | bytes 7962632 | tf_op jit(solution)/shard_map/ppermute | solution.py:931
  110.0 5.2 %collective-permute-start.18 = (bf16[4,192,1728]{2,1,0:T(8,128)(2,1)S(1)}, bf16[4,192,1728]{2,1,0:T(8,128)(2,1)}, u32[]{:S(2)}, u32[]{:S(2)}) collective-permute-start(bf16[4,192,1728]{2,1,0:T(8,128)(2,1)S(1)} %pad_maximum_fusion.1.refs_13_), channel_id=1, source_target_pairs={{0,8},{8,0},{16,24},{24,16},{1,9},{9,1},{17,25},{25,17},{2,10},{10... | collective-permute-start | bytes 7962632 | tf_op jit(solution)/shard_map/ppermute | solution.py:936
  165.3 15.7 %collective-permute-start.20 = (bf16[512,384]{1,0:T(8,128)(2,1)}, bf16[512,384]{1,0:T(8,128)(2,1)S(1)}, u32[]{:S(2)}, u32[]{:S(2)}) collective-permute-start(bf16[512,384]{1,0:T(8,128)(2,1)} %get-tuple-element.122), channel_id=1, source_target_pairs={{4,0},{5,1},{6,2},{7,3},{12,8},{13,9},{14,10},{15,11},{20,16},{21,... | collective-permute-start | bytes 1179656 | tf_op jit(solution)/shard_map/ppermute | solution.py:994
  175.9 17.3 %collective-permute-start.19 = (bf16[512,384]{1,0:T(8,128)(2,1)}, bf16[512,384]{1,0:T(8,128)(2,1)S(1)}, u32[]{:S(2)}, u32[]{:S(2)}) collective-permute-start(bf16[512,384]{1,0:T(8,128)(2,1)} %get-tuple-element.119), channel_id=1, source_target_pairs={{4,0},{5,1},{6,2},{7,3},{12,8},{13,9},{14,10},{15,11},{20,16},{21,... | collective-permute-start | bytes 1179656 | tf_op jit(solution)/shard_map/ppermute | solution.py:994
  198.1 51.7 %all-reduce.3.cloned.1.call-start = ((), (), s32[]{:S(2)}) async-start(), calls=%async_computation | async-start | bytes 1572864 | tf_op jit(solution)/shard_map/psum | solution.py:1042
  200.0 47.2 %collective-permute-start.21 = (bf16[256,768]{1,0:T(8,128)(2,1)S(1)}, bf16[256,768]{1,0:T(8,128)(2,1)S(1)}, u32[]{:S(2)}, u32[]{:S(2)}) collective-permute-start(bf16[256,768]{1,0:T(8,128)(2,1)S(1)} %broadcast_select_fusion.4), channel_id=1, source_target_pairs={{0,1},{1,0},{2,3},{3,2},{4,5},{5,4},{6,7},{7,6},{8,9},{9,8},{10,11... | collective-permute-start | bytes 1179656 | tf_op jit(solution)/shard_map/ppermute | solution.py:790
  248.4 19.8 %collective-permute-start.23 = (bf16[256,768]{1,0:T(8,128)(2,1)S(1)}, bf16[256,768]{1,0:T(8,128)(2,1)}, u32[]{:S(2)}, u32[]{:S(2)}) collective-permute-start(bf16[256,768]{1,0:T(8,128)(2,1)S(1)} %select_add_fusion.2.refs_11_), channel_id=1, source_target_pairs={{0,2},{2,0},{1,3},{3,1},{4,6},{6,4},{5,7},{7,5},{8,10},{10,8},{9,1... | collective-permute-start | bytes 1179656 | tf_op jit(solution)/shard_map/ppermute | solution.py:792
  258.9 13.4 %collective-permute-start.22 = (bf16[512,384]{1,0:T(8,128)(2,1)}, bf16[512,384]{1,0:T(8,128)(2,1)S(1)}, u32[]{:S(2)}, u32[]{:S(2)}) collective-permute-start(bf16[512,384]{1,0:T(8,128)(2,1)} %get-tuple-element.136), channel_id=1, source_target_pairs={{4,0},{5,1},{6,2},{7,3},{12,8},{13,9},{14,10},{15,11},{20,16},{21,... | collective-permute-start | bytes 1179656 | tf_op jit(solution)/shard_map/ppermute | solution.py:994
  262.9 32.2 %collective-permute-start.32 = (bf16[2,192,1728]{2,1,0:T(8,128)(2,1)}, bf16[2,192,1728]{2,1,0:T(8,128)(2,1)}, u32[]{:S(2)}, u32[]{:S(2)}) collective-permute-start(bf16[2,192,1728]{2,1,0:T(8,128)(2,1)} %dynamic-slice_bitcast_fusion), channel_id=1, source_target_pairs={{0,16},{16,0},{8,24},{24,8},{1,17},{17,1},{9,25},{25,9},{2,18},{18... | collective-permute-start | bytes 3981320 | tf_op jit(solution)/shard_map/ppermute | solution.py:807
  269.3 22.2 %collective-permute-start.25 = (bf16[256,768]{1,0:T(8,128)(2,1)S(1)}, bf16[256,768]{1,0:T(8,128)(2,1)}, u32[]{:S(2)}, u32[]{:S(2)}) collective-permute-start(bf16[256,768]{1,0:T(8,128)(2,1)S(1)} %add.117.refs_6_.done_ref), channel_id=1, source_target_pairs={{0,1},{1,0},{2,3},{3,2},{4,5},{5,4},{6,7},{7,6},{8,9},{9,8},{10,11... | collective-permute-start | bytes 1179656 | tf_op jit(solution)/shard_map/ppermute | solution.py:793
  279.1 19.0 %collective-permute-start.26 = (bf16[256,768]{1,0:T(8,128)(2,1)}, bf16[256,768]{1,0:T(8,128)(2,1)}, u32[]{:S(2)}, u32[]{:S(2)}) collective-permute-start(bf16[256,768]{1,0:T(8,128)(2,1)} %broadcast_select_fusion.3), channel_id=1, source_target_pairs={{0,1},{1,0},{2,3},{3,2},{4,5},{5,4},{6,7},{7,6},{8,9},{9,8},{10,11... | collective-permute-start | bytes 1179656 | tf_op jit(solution)/shard_map/ppermute | solution.py:790
  290.2 12.4 %collective-permute-start.24 = (bf16[512,384]{1,0:T(8,128)(2,1)}, bf16[512,384]{1,0:T(8,128)(2,1)S(1)}, u32[]{:S(2)}, u32[]{:S(2)}) collective-permute-start(bf16[512,384]{1,0:T(8,128)(2,1)} %get-tuple-element.142), channel_id=1, source_target_pairs={{4,0},{5,1},{6,2},{7,3},{12,8},{13,9},{14,10},{15,11},{20,16},{21,... | collective-permute-start | bytes 1179656 | tf_op jit(solution)/shard_map/ppermute | solution.py:994
  298.1 12.0 %collective-permute-start.33 = (bf16[192,1728]{1,0:T(8,128)(2,1)}, bf16[192,1728]{1,0:T(8,128)(2,1)}, u32[]{:S(2)}, u32[]{:S(2)}) collective-permute-start(bf16[192,1728]{1,0:T(8,128)(2,1)} %dynamic-slice_bitcast_fusion.1), channel_id=1, source_target_pairs={{0,8},{8,0},{16,24},{24,16},{1,9},{9,1},{17,25},{25,17},{2,10},{10... | collective-permute-start | bytes 1990664 | tf_op jit(solution)/shard_map/ppermute | solution.py:813
  299.2 21.1 %collective-permute-start.30 = (bf16[256,768]{1,0:T(8,128)(2,1)S(1)}, bf16[256,768]{1,0:T(8,128)(2,1)}, u32[]{:S(2)}, u32[]{:S(2)}) collective-permute-start(bf16[256,768]{1,0:T(8,128)(2,1)S(1)} %select_add_fusion.1.refs_6_), channel_id=1, source_target_pairs={{0,2},{2,0},{1,3},{3,1},{4,6},{6,4},{5,7},{7,5},{8,10},{10,8},{9,1... | collective-permute-start | bytes 1179656 | tf_op jit(solution)/shard_map/ppermute | solution.py:792
  307.7 19.7 %copy-start.1 = (bf16[512,768]{1,0:T(8,128)(2,1)S(1)}, bf16[512,768]{1,0:T(8,128)(2,1)}, u32[]{:S(2)}) copy-start(bf16[512,768]{1,0:T(8,128)(2,1)} %get-tuple-element.144.refs_0_) | copy-start | bytes 2359300
  308.9 18.4 %collective-permute-start.27 = (bf16[256,768]{1,0:T(8,128)(2,1)S(1)}, bf16[256,768]{1,0:T(8,128)(2,1)S(1)}, u32[]{:S(2)}, u32[]{:S(2)}) collective-permute-start(bf16[256,768]{1,0:T(8,128)(2,1)S(1)} %broadcast_select_fusion.2), channel_id=1, source_target_pairs={{0,1},{1,0},{2,3},{3,2},{4,5},{5,4},{6,7},{7,6},{8,9},{9,8},{10,11... | collective-permute-start | bytes 1179656 | tf_op jit(solution)/shard_map/ppermute | solution.py:790
  312.3 24.3 %collective-permute-start.34 = (bf16[192,1728]{1,0:T(8,128)(2,1)}, bf16[192,1728]{1,0:T(8,128)(2,1)}, u32[]{:S(2)}, u32[]{:S(2)}) collective-permute-start(bf16[192,1728]{1,0:T(8,128)(2,1)} %bitcast_add_fusion.1), channel_id=1, source_target_pairs={{0,4},{4,0},{1,5},{5,1},{2,6},{6,2},{3,7},{7,3},{8,12},{12,8},{9,1... | collective-permute-start | bytes 1990664 | tf_op jit(solution)/shard_map/ppermute | solution.py:798
  321.4 15.2 %copy-start.14 = (bf16[256,768]{1,0:T(8,128)(2,1)}, bf16[256,768]{1,0:T(8,128)(2,1)S(1)}, u32[]{:S(2)}) copy-start(bf16[256,768]{1,0:T(8,128)(2,1)S(1)} %add.121.done_ref) | copy-start | bytes 1179652
  321.4 1.3 collective-permute-start.39
  321.5 25.9 %collective-permute-start.31 = (bf16[256,768]{1,0:T(8,128)(2,1)S(1)}, bf16[256,768]{1,0:T(8,128)(2,1)}, u32[]{:S(2)}, u32[]{:S(2)}) collective-permute-start(bf16[256,768]{1,0:T(8,128)(2,1)S(1)} %add.121.done_ref), channel_id=1, source_target_pairs={{0,1},{1,0},{2,3},{3,2},{4,5},{5,4},{6,7},{7,6},{8,9},{9,8},{10,11... | collective-permute-start | bytes 1179656 | tf_op jit(solution)/shard_map/ppermute | solution.py:793
  322.7 6.4 %collective-permute-start.40 = (f32[8,1408]{1,0:T(8,128)S(1)}, f32[8,1408]{1,0:T(8,128)S(1)}, u32[]{:S(2)}, u32[]{:S(2)}) collective-permute-start(f32[8,1408]{1,0:T(8,128)S(1)} %add.142), channel_id=1, source_target_pairs={{0,16},{16,0},{8,24},{24,8},{1,17},{17,1},{9,25},{25,9},{2,18},{18... | collective-permute-start | bytes 135176 | tf_op jit(solution)/shard_map/ppermute | solution.py:829
  327.4 17.3 %collective-permute-start.28 = (bf16[256,768]{1,0:T(8,128)(2,1)S(1)}, bf16[256,768]{1,0:T(8,128)(2,1)}, u32[]{:S(2)}, u32[]{:S(2)}) collective-permute-start(bf16[256,768]{1,0:T(8,128)(2,1)S(1)} %select_add_fusion.refs_1_), channel_id=1, source_target_pairs={{0,2},{2,0},{1,3},{3,1},{4,6},{6,4},{5,7},{7,5},{8,10},{10,8},{9,1... | collective-permute-start | bytes 1179656 | tf_op jit(solution)/shard_map/ppermute | solution.py:792
  329.1 7.5 %collective-permute-start.41 = (f32[8,1408]{1,0:T(8,128)S(1)}, f32[8,1408]{1,0:T(8,128)S(1)}, u32[]{:S(2)}, u32[]{:S(2)}) collective-permute-start(f32[8,1408]{1,0:T(8,128)S(1)} %add.143), channel_id=1, source_target_pairs={{0,4},{4,0},{1,5},{5,1},{2,6},{6,2},{3,7},{7,3},{8,12},{12,8},{9,1... | collective-permute-start | bytes 135176 | tf_op jit(solution)/shard_map/ppermute | solution.py:798
  340.1 12.2 %collective-permute-start.35 = (bf16[192,640]{1,0:T(8,128)(2,1)}, bf16[192,640]{1,0:T(8,128)(2,1)}, u32[]{:S(2)}, u32[]{:S(2)}) collective-permute-start(bf16[192,640]{1,0:T(8,128)(2,1)} %get-tuple-element.169), channel_id=1, source_target_pairs={{0,8},{8,0},{16,24},{24,16},{1,9},{9,1},{17,25},{25,17},{2,10},{10... | collective-permute-start | bytes 737288 | tf_op jit(solution)/shard_map/ppermute | solution.py:823
  340.1 12.2 %collective-permute-start.36 = (bf16[192,640]{1,0:T(8,128)(2,1)}, bf16[192,640]{1,0:T(8,128)(2,1)}, u32[]{:S(2)}, u32[]{:S(2)}) collective-permute-start(bf16[192,640]{1,0:T(8,128)(2,1)} %get-tuple-element.171), channel_id=1, source_target_pairs={{0,16},{16,0},{8,24},{24,8},{1,17},{17,1},{9,25},{25,9},{2,18},{18... | collective-permute-start | bytes 737288 | tf_op jit(solution)/shard_map/ppermute | solution.py:823
  341.7 12.1 %collective-permute-start.37 = (bf16[192,640]{1,0:T(8,128)(2,1)}, bf16[192,640]{1,0:T(8,128)(2,1)}, u32[]{:S(2)}, u32[]{:S(2)}) collective-permute-start(bf16[192,640]{1,0:T(8,128)(2,1)} %get-tuple-element.170), channel_id=1, source_target_pairs={{0,24},{24,0},{8,16},{16,8},{1,25},{25,1},{9,17},{17,9},{2,26},{26... | collective-permute-start | bytes 737288 | tf_op jit(solution)/shard_map/ppermute | solution.py:823
  345.9 13.4 %collective-permute-start.29 = (bf16[256,768]{1,0:T(8,128)(2,1)S(1)}, bf16[256,768]{1,0:T(8,128)(2,1)}, u32[]{:S(2)}, u32[]{:S(2)}) collective-permute-start(bf16[256,768]{1,0:T(8,128)(2,1)S(1)} %add.120.done_ref), channel_id=1, source_target_pairs={{0,1},{1,0},{2,3},{3,2},{4,5},{5,4},{6,7},{7,6},{8,9},{9,8},{10,11... | collective-permute-start | bytes 1179656 | tf_op jit(solution)/shard_map/ppermute | solution.py:793
  355.1 8.4 %collective-permute-start.38 = (bf16[192,640]{1,0:T(8,128)(2,1)S(1)}, bf16[192,640]{1,0:T(8,128)(2,1)S(1)}, u32[]{:S(2)}, u32[]{:S(2)}) collective-permute-start(bf16[192,640]{1,0:T(8,128)(2,1)S(1)} %fusion.2), channel_id=1, source_target_pairs={{0,4},{4,0},{1,5},{5,1},{2,6},{6,2},{3,7},{7,3},{8,12},{12,8},{9,1... | collective-permute-start | bytes 737288 | tf_op jit(solution)/shard_map/ppermute | solution.py:798
  (31 other events, 132.0 us)
Sparse Core Ops, SparseCore 0:
  110.9 43.0 all-gather.2
  201.9 47.6 all-reduce.2

commit v6 on v5

--- a/solution.py
+++ b/solution.py
@@ -718,7 +718,7 @@
 
 def plain_call(dh1, at, total, first, rows, seqs, chain, after):
     d = total.shape[1]
-    tile = min(rows, 256)
+    tile = min(rows, 128)
     extra = ([] if chain is None else [chain]) + list(after)
     return pl.pallas_call(
         plain_kernel,
@@ -741,7 +741,7 @@
 
 def final_call(ids, dh1, at, done, other, first, rows, seqs, chain, after):
     half, d = done.shape
-    tile = min(half, 256)
+    tile = min(half, 128)
     per_half = half // tile
     per_seq = rows // tile
     extra = ([] if chain is None else [chain]) + list(after)

time: 376 us -> 381 us (1.013)
  Pallas kernels: 192 us -> 197 us
    pallas_call x3, Pallas kernels: 10.1 us -> 14.1 us  [final_call(): pl.pallas_call(final_kernel, out_shape=jax.ShapeDtypeStruct((seqs, rows,...]
  transfers between devices with their start and end apart: 44 -> 44, of which waited for: 17 -> 14; matrix products, arithmetic and copies ran while one was open for 12% -> 12% of each run, Pallas kernels for 51% -> 51%
where the time goes in v6:
time: 381 us; the launch traced here: 376 us
  Pallas kernels  197 us (52%)
  starting transfers between devices  57.5 us (15%)
  waiting for transfers between devices  52.8 us (14%)
  other arithmetic  30.5 us (8%)
  local copies, waits for them, and re-layouts  23 us (6%)
  between operations  15.1 us (4%)
    pallas_call x2, Pallas kernels, ffn_call(): pl.pallas_call(functools.partial(ffn_kernel, chained=bool(chained), final...  83 us
    pallas_call x4, Pallas kernels, attn_bwd_call(): pl.pallas_call(functools.partial(attn_bwd_kernel, heads=heads, size=size,...  36.8 us
    pallas_call x2, Pallas kernels, attn_fwd_call(): pl.pallas_call(functools.partial(attn_fwd_kernel, heads=heads, size=size,...  23.5 us
    pallas_call x4, Pallas kernels, dx_call(): pl.pallas_call(functools.partial(dx_kernel, nkv=len(dkvs)), out_shape=(ja...  16.7 us
    pallas_call x3, Pallas kernels, final_call(): pl.pallas_call(final_kernel, out_shape=jax.ShapeDtypeStruct((seqs, rows,...  14.1 us
    ppermute x3, waiting for transfers between devices, tp_reduce(): done = pair + lax.ppermute(pair, 'tp', FAR)  12.8 us
    pallas_call x2, Pallas kernels, qkv_call(): pl.pallas_call(functools.partial(qkv_kernel, scale=scale), out_shape=(jax...  12.6 us
    ppermute x3, waiting for transfers between devices, tp_gather(): return [value] + [lax.ppermute(value, 'tp', p) for p in (SWAP, FAR, ACROSS)]  10.5 us
  transfers between devices with their start and end apart: 44, of which 14 were waited for; matrix products, arithmetic and copies ran while one was open for 12% of the time, Pallas kernels for 51%

profile of v6, /device:TPU:0, one launch (start us, length us, event | category | flops | bytes accessed | tf_op | source)
XLA Modules:
  0.0 376.0 jit_solution(6026546796024699777)
XLA Ops:
  8.4 3.0 collective-permute-start.1
  22.4 6.3 %qkv.2 = (bf16[1024,192]{1,0:T(8,128)(2,1)}, bf16[1024,384]{1,0:T(8,128)(2,1)}, bf16[768,640]{1,0:T(8,128)(2,1)}) custom-call(s32[3]{0:T(128)} %pad_add_fusion.ids, bf16[4,512,768]{2,1,0:T(8,128)(2,1)} %x_ref.5, bf16[192,640]{1,0:T(8,128)(2,1)} %copy-done.13, bf16[192,640]{1,0:T(8,128)(2,1)} %copy-done.18, bf16[192,640]{1,0:T(8,128)(2,1)} %copy-done.17, ...), custom_call_target="tpu_custom_call" | custom-call | flops 1006632960 | bytes 5046272 | tf_op jit(solution)/shard_map/qkv/pallas_call | solution.py:83
  28.7 2.7 collective-permute-done.5
  31.4 2.8 collective-permute-done.7
  37.1 4.3 %collective-permute-start.4 = (bf16[1024,384]{1,0:T(8,128)(2,1)}, bf16[1024,384]{1,0:T(8,128)(2,1)}, u32[]{:S(2)}, u32[]{:S(2)}) collective-permute-start(bf16[1024,384]{1,0:T(8,128)(2,1)} %get-tuple-element.91.refs_3_.refs_7_), channel_id=1, source_target_pairs={{0,4},{1,5},{2,6},{3,7},{8,12},{9,13},{10,14},{11,15},{16,20},{17,... | collective-permute-start | bytes 2359304 | tf_op jit(solution)/shard_map/ppermute | solution.py:897
  42.1 6.3 %qkv.3 = (bf16[1024,192]{1,0:T(8,128)(2,1)}, bf16[1024,384]{1,0:T(8,128)(2,1)}, bf16[768,640]{1,0:T(8,128)(2,1)}) custom-call(s32[3]{0:T(128)} %pad_add_fusion.ids, bf16[4,512,768]{2,1,0:T(8,128)(2,1)} %x_ref.5, bf16[192,640]{1,0:T(8,128)(2,1)} %copy-done.13, bf16[192,640]{1,0:T(8,128)(2,1)} %copy-done.18, bf16[192,640]{1,0:T(8,128)(2,1)} %copy-done.17, ...), custom_call_target="tpu_custom_call" | custom-call | flops 1006632960 | bytes 5046272 | tf_op jit(solution)/shard_map/qkv/pallas_call | solution.py:83
  52.4 2.6 collective-permute-done.9
  55.0 2.0 broadcast_select_fusion.1.refs_6_
  58.8 11.8 %attn_fwd.2 = (bf16[4,3,512,1024]{3,2,1,0:T(8,128)(2,1)}, bf16[2,3,512,1024]{3,2,1,0:T(8,128)(2,1)}, bf16[528,384]{1,0:T(8,128)(2,1)}, f32[1024,128]{1,0:T(8,128)}) custom-call(s32[3]{0:T(128)} %pad_add_fusion.ids, bf16[1024,192]{1,0:T(8,128)(2,1)} %get-tuple-element.88.refs_0_, bf16[4,3,512,1024]{3,2,1,0:T(8,128)(2,1)} %refs_1_.3, ...), custom_call_target="tpu_custom_call" | custom-call | flops 2415919104 | bytes 18874368 | tf_op jit(solution)/shard_map/attn_fwd/pallas_call | solution.py:200
  70.6 2.0 broadcast_select_fusion
  74.0 4.4 %collective-permute-start.14 = (bf16[528,384]{1,0:T(8,128)(2,1)}, bf16[528,384]{1,0:T(8,128)(2,1)}, u32[]{:S(2)}, u32[]{:S(2)}) collective-permute-start(bf16[528,384]{1,0:T(8,128)(2,1)} %get-tuple-element.100.refs_6_.refs_1_.refs_7_.refs_4_), channel_id=1, source_target_pairs={{0,1},{1,0},{2,3},{3,2},{4,5},{5,4},{6,7},{7,6},{8,9},{9,8},{10,11... | collective-permute-start | bytes 1216520 | tf_op jit(solution)/shard_map/ppermute | solution.py:777
  81.2 3.0 pad_maximum_fusion.refs_7_.refs_11_
  84.2 11.7 %attn_fwd.3 = (bf16[4,3,512,1024]{3,2,1,0:T(8,128)(2,1)}, bf16[2,3,512,1024]{3,2,1,0:T(8,128)(2,1)}, bf16[528,384]{1,0:T(8,128)(2,1)}, f32[1024,128]{1,0:T(8,128)}) custom-call(s32[3]{0:T(128)} %pad_add_fusion.ids, bf16[1024,192]{1,0:T(8,128)(2,1)} %get-tuple-element.89.refs_5_.refs_0_, ...), custom_call_target="tpu_custom_call", output_to_operand_aliasing={{0}: (6, {})} | custom-call | flops 2415919104 | bytes 18874368 | tf_op jit(solution)/shard_map/attn_fwd/pallas_call | solution.py:200
  96.0 10.5 %collective-permute-done.15.refs_3_.refs_9_ = bf16[528,384]{1,0:T(8,128)(2,1)} collective-permute-done((bf16[528,384]{1,0:T(8,128)(2,1)}, bf16[528,384]{1,0:T(8,128)(2,1)}, u32[]{:S(2)}, u32[]{:S(2)}) %collective-permute-start.15) | collective-permute-done | bytes 405536 | tf_op jit(solution)/shard_map/ppermute | solution.py:777
  106.5 1.9 pad_maximum_fusion.1.refs_13_
  110.8 4.4 %collective-permute-done.18.refs_14_ = bf16[4,192,1728]{2,1,0:T(8,128)(2,1)} collective-permute-done((bf16[4,192,1728]{2,1,0:T(8,128)(2,1)S(1)}, bf16[4,192,1728]{2,1,0:T(8,128)(2,1)}, u32[]{:S(2)}, u32[]{:S(2)}) %collective-permute-start.18) | collective-permute-done | bytes 2654240 | tf_op jit(solution)/shard_map/ppermute | solution.py:936
  115.2 40.9 %ffn.2 = (bf16[4,512,768]{2,1,0:T(8,128)(2,1)}, f32[1024,768]{1,0:T(8,128)}, bf16[1024,192]{1,0:T(8,128)(2,1)}, f32[8,768]{1,0:T(8,128)}, f32[768,768]{1,0:T(8,1...) custom-call(s32[3]{0:T(128)} %pad_add_fusion.ids, bf16[4,512,768]{2,1,0:T(8,128)(2,1)} %x_ref.5, ...), custom_call_target="tpu_custom_call" | custom-call | flops 24159191040 | bytes 22020096 | tf_op jit(solution)/shard_map/ffn/pallas_call | solution.py:567
  156.1 9.2 %attn_bwd.4 = (bf16[4,3,512,1024]{3,2,1,0:T(8,128)(2,1)}, bf16[512,192]{1,0:T(8,128)(2,1)}, bf16[512,384]{1,0:T(8,128)(2,1)}, bf16[512,384]{1,0:T(8,128)(2,1)}) custom-call(s32[3]{0:T(128)} %pad_add_fusion.ids, bf16[1024,192]{1,0:T(8,128)(2,1)} %get-tuple-element.88.refs_0_, bf16[2,3,512,1024]{3,2,1,0:T(8,128)(2,1)} %get-tuple-element.112.refs_1_, ...), custom_call_target="tpu_custom_call" | custom-call | flops 8999999488 | bytes 1000 | tf_op jit(solution)/shard_map/attn_bwd/pallas_call | solution.py:331
  166.6 9.3 %attn_bwd.5 = (bf16[4,3,512,1024]{3,2,1,0:T(8,128)(2,1)}, bf16[512,192]{1,0:T(8,128)(2,1)}, bf16[512,384]{1,0:T(8,128)(2,1)}, bf16[512,384]{1,0:T(8,128)(2,1)}) custom-call(s32[3]{0:T(128)} %pad_add_fusion.ids, bf16[1024,192]{1,0:T(8,128)(2,1)} %get-tuple-element.88.refs_0_, ...), custom_call_target="tpu_custom_call", output_to_operand_aliasing={{0}: (9, {})} | custom-call | flops 8999999488 | bytes 1000 | tf_op jit(solution)/shard_map/attn_bwd/pallas_call | solution.py:331
  177.2 2.3 dynamic-slice_bitcast_fusion.2
  181.7 4.1 %dx.4 = (bf16[512,768]{1,0:T(8,128)(2,1)}, bf16[2048,640]{1,0:T(8,128)(2,1)}, f32[8,640]{1,0:T(8,128)}) custom-call(s32[3]{0:T(128)} %pad_add_fusion.ids, bf16[512,192]{1,0:T(8,128)(2,1)} %get-tuple-element.116.refs_9_.dq_ref, bf16[512,384]{1,0:T(8,128)(2,1)} %get-tuple-element.121.refs_0_, bf16[512,384]{1,0:T(8,128)(2,1)} %copy-done.33, ...), custom_call_target="tpu_custom_call" | custom-call | flops 3000000000 | bytes 1000 | tf_op jit(solution)/shard_map/dx/pallas_call | solution.py:640
  185.9 7.3 %collective-permute-done.19.refs_1_ = bf16[512,384]{1,0:T(8,128)(2,1)S(1)} collective-permute-done((bf16[512,384]{1,0:T(8,128)(2,1)}, bf16[512,384]{1,0:T(8,128)(2,1)S(1)}, u32[]{:S(2)}, u32[]{:S(2)}) %collective-permute-start.19) | collective-permute-done | bytes 393248 | tf_op jit(solution)/shard_map/ppermute | solution.py:994
  193.9 4.1 %dx.5 = (bf16[512,768]{1,0:T(8,128)(2,1)}, bf16[2048,640]{1,0:T(8,128)(2,1)}, f32[8,640]{1,0:T(8,128)}) custom-call(s32[3]{0:T(128)} %pad_add_fusion.ids, bf16[512,192]{1,0:T(8,128)(2,1)} %get-tuple-element.117.refs_3_.dq_ref, bf16[512,384]{1,0:T(8,128)(2,1)} %get-tuple-element.118.refs_0_, ...), custom_call_target="tpu_custom_call", output_to_operand_aliasing={{1}: (5, {})} | custom-call | flops 3000000000 | bytes 1000 | tf_op jit(solution)/shard_map/dx/pallas_call | solution.py:640
  200.0 5.1 %collective-permute-start.21 = (bf16[256,768]{1,0:T(8,128)(2,1)S(1)}, bf16[256,768]{1,0:T(8,128)(2,1)S(1)}, u32[]{:S(2)}, u32[]{:S(2)}) collective-permute-start(bf16[256,768]{1,0:T(8,128)(2,1)S(1)} %broadcast_select_fusion.4), channel_id=1, source_target_pairs={{0,1},{1,0},{2,3},{3,2},{4,5},{5,4},{6,7},{7,6},{8,9},{9,8},{10,11... | collective-permute-start | bytes 1179656 | tf_op jit(solution)/shard_map/ppermute | solution.py:790
  205.0 42.1 %ffn.3 = (bf16[4,512,768]{2,1,0:T(8,128)(2,1)}, f32[1024,768]{1,0:T(8,128)}, bf16[1024,192]{1,0:T(8,128)(2,1)}, f32[8,768]{1,0:T(8,128)}, bf16[768,1728]{1,0:T(8,128)(2,1)}) custom-call(s32[3]{0:T(128)} %pad_add_fusion.ids, bf16[4,512,768]{2,1,0:T(8,128)(2,1)} %x_ref.5, ...), custom_call_target="tpu_custom_call", output_to_operand_aliasing={{0}: (19, {})} | custom-call | flops 24159191040 | bytes 22020096 | tf_op jit(solution)/shard_map/ffn/pallas_call | solution.py:567
  249.8 9.1 %attn_bwd.6 = (bf16[4,3,512,1024]{3,2,1,0:T(8,128)(2,1)}, bf16[512,192]{1,0:T(8,128)(2,1)}, bf16[512,384]{1,0:T(8,128)(2,1)}, bf16[512,384]{1,0:T(8,128)(2,1)}) custom-call(s32[3]{0:T(128)} %pad_add_fusion.ids, bf16[1024,192]{1,0:T(8,128)(2,1)} %get-tuple-element.89.refs_5_.refs_0_, ...), custom_call_target="tpu_custom_call", output_to_operand_aliasing={{0}: (9, {})} | custom-call | flops 8999999488 | bytes 1000 | tf_op jit(solution)/shard_map/attn_bwd/pallas_call | solution.py:331
  260.4 2.5 dynamic-slice_bitcast_fusion
  264.2 4.0 %collective-permute-done.23 = bf16[256,768]{1,0:T(8,128)(2,1)} collective-permute-done((bf16[256,768]{1,0:T(8,128)(2,1)S(1)}, bf16[256,768]{1,0:T(8,128)(2,1)}, u32[]{:S(2)}, u32[]{:S(2)}) %collective-permute-start.23) | collective-permute-done | bytes 393248 | tf_op jit(solution)/shard_map/ppermute | solution.py:792
  269.4 3.9 %plain.1.refs_5_.refs_0_ = f32[4,512,768]{2,1,0:T(8,128)} custom-call(f32[1024,768]{1,0:T(8,128)} %get-tuple-element.138.dh1_ref, bf16[512,768]{1,0:T(8,128)(2,1)} %all-reduce.3.cloned.1.call-done.refs_10_.total_ref, bf16[512,192]{1,0:T(8,128)(2,1)} %get-tuple-element.134.refs_0_.dq_ref.refs_4_), custom_call_target="tpu_custom_call" | custom-call | flops 786432 | bytes 3932160 | tf_op jit(solution)/shard_map/plain/pallas_call | solution.py:723
  274.0 4.2 %dx.6 = (bf16[512,768]{1,0:T(8,128)(2,1)}, bf16[2048,640]{1,0:T(8,128)(2,1)}, f32[8,640]{1,0:T(8,128)}) custom-call(s32[3]{0:T(128)} %pad_add_fusion.ids, bf16[512,192]{1,0:T(8,128)(2,1)} %get-tuple-element.134.refs_0_.dq_ref.refs_4_, bf16[512,384]{1,0:T(8,128)(2,1)} %get-tuple-element.135.refs_0_, ...), custom_call_target="tpu_custom_call", output_to_operand_aliasing={{1}: (5, {})} | custom-call | flops 3000000000 | bytes 1000 | tf_op jit(solution)/shard_map/dx/pallas_call | solution.py:640
  278.2 1.9 broadcast_select_fusion.3
  280.1 2.0 collective-permute-start.26
  282.1 9.3 %attn_bwd.7 = (bf16[4,3,512,1024]{3,2,1,0:T(8,128)(2,1)}, bf16[512,192]{1,0:T(8,128)(2,1)}, bf16[512,384]{1,0:T(8,128)(2,1)}, bf16[512,384]{1,0:T(8,128)(2,1)}) custom-call(s32[3]{0:T(128)} %pad_add_fusion.ids, bf16[1024,192]{1,0:T(8,128)(2,1)} %get-tuple-element.89.refs_5_.refs_0_, ...), custom_call_target="tpu_custom_call", output_to_operand_aliasing={{0}: (9, {})} | custom-call | flops 8999999488 | bytes 1000 | tf_op jit(solution)/shard_map/attn_bwd/pallas_call | solution.py:331
  292.7 4.9 %final.3.refs_5_.refs_0_ = f32[4,512,768]{2,1,0:T(8,128)} custom-call(s32[3]{0:T(128)} %pad_add_fusion.ids, f32[1024,768]{1,0:T(8,128)} %get-tuple-element.138.dh1_ref, bf16[256,768]{1,0:T(8,128)(2,1)} %copy-done.9, bf16[256,768]{1,0:T(8,128)(2,1)} %collective-permute-done.25.other_ref, ...), custom_call_target="tpu_custom_call", output_to_operand_aliasing={{}: (4, {})} | custom-call | flops 786432 | bytes 4718592 | tf_op jit(solution)/shard_map/final/pallas_call | solution.py:750
  297.6 2.0 bitcast_add_fusion
  304.5 4.3 %dx.7 = (bf16[512,768]{1,0:T(8,128)(2,1)}, bf16[2048,640]{1,0:T(8,128)(2,1)}, f32[8,640]{1,0:T(8,128)}) custom-call(s32[3]{0:T(128)} %pad_add_fusion.ids, bf16[512,192]{1,0:T(8,128)(2,1)} %get-tuple-element.140.refs_1_.dq_ref.refs_4_, bf16[512,384]{1,0:T(8,128)(2,1)} %get-tuple-element.141.refs_0_, ...), custom_call_target="tpu_custom_call", output_to_operand_aliasing={{1}: (5, {})} | custom-call | flops 3000000000 | bytes 1000 | tf_op jit(solution)/shard_map/dx/pallas_call | solution.py:640
  312.0 2.2 bitcast_add_fusion.1
  314.2 2.7 collective-permute-start.34
  316.9 5.8 %collective-permute-done.30 = bf16[256,768]{1,0:T(8,128)(2,1)} collective-permute-done((bf16[256,768]{1,0:T(8,128)(2,1)S(1)}, bf16[256,768]{1,0:T(8,128)(2,1)}, u32[]{:S(2)}, u32[]{:S(2)}) %collective-permute-start.30) | collective-permute-done | bytes 393248 | tf_op jit(solution)/shard_map/ppermute | solution.py:792
  326.2 4.3 %collective-permute-done.27 = bf16[256,768]{1,0:T(8,128)(2,1)S(1)} collective-permute-done((bf16[256,768]{1,0:T(8,128)(2,1)S(1)}, bf16[256,768]{1,0:T(8,128)(2,1)S(1)}, u32[]{:S(2)}, u32[]{:S(2)}) %collective-permute-start.27) | collective-permute-done | bytes 393248 | tf_op jit(solution)/shard_map/ppermute | solution.py:790
  330.7 1.7 collective-permute-start.41
  332.4 6.4 %grad.1.refs_1_ = bf16[768,640]{1,0:T(8,128)(2,1)} custom-call(bf16[4,512,768]{2,1,0:T(8,128)(2,1)} %x_ref.5, bf16[2048,640]{1,0:T(8,128)(2,1)} %get-tuple-element.145.joined_ref, bf16[512,768]{1,0:T(8,128)(2,1)} %get-tuple-element.144.refs_0_, bf16[256,768]{1,0:T(8,128)(2,1)} %copy-done.10), custom_call_target="tpu_custom_call" | custom-call | flops 2013265920 | bytes 1966080 | tf_op jit(solution)/shard_map/grad/pallas_call | solution.py:687
  338.8 2.6 add_convert_fusion
  345.5 3.0 collective-permute-done.28
  349.6 4.6 %final.4.refs_0_ = f32[4,512,768]{2,1,0:T(8,128)} custom-call(s32[3]{0:T(128)} %pad_add_fusion.ids, f32[1024,768]{1,0:T(8,128)} %get-tuple-element.128.dh1_ref, bf16[256,768]{1,0:T(8,128)(2,1)} %copy-done.14, bf16[256,768]{1,0:T(8,128)(2,1)} %collective-permute-done.31.other_ref, ...), custom_call_target="tpu_custom_call", output_to_operand_aliasing={{}: (4, {})} | custom-call | flops 786432 | bytes 4718592 | tf_op jit(solution)/shard_map/final/pallas_call | solution.py:750
  357.3 3.8 %collective-permute-start.38 = (bf16[192,640]{1,0:T(8,128)(2,1)S(1)}, bf16[192,640]{1,0:T(8,128)(2,1)S(1)}, u32[]{:S(2)}, u32[]{:S(2)}) collective-permute-start(bf16[192,640]{1,0:T(8,128)(2,1)S(1)} %fusion.2), channel_id=1, source_target_pairs={{0,4},{4,0},{1,5},{5,1},{2,6},{6,2},{3,7},{7,3},{8,12},{12,8},{9,1... | collective-permute-start | bytes 737288 | tf_op jit(solution)/shard_map/ppermute | solution.py:798
  361.1 2.3 fusion.4
  363.4 4.6 %final.5 = f32[4,512,768]{2,1,0:T(8,128)} custom-call(s32[3]{0:T(128)} %pad_add_fusion.ids, f32[1024,768]{1,0:T(8,128)} %get-tuple-element.128.dh1_ref, bf16[256,768]{1,0:T(8,128)(2,1)} %copy-done.15, bf16[256,768]{1,0:T(8,128)(2,1)} %collective-permute-done.29.other_ref, f32[4,512,768]{2,1,0:T(8,128)} %final.4.refs_0_, ...), custom_call_target="tpu_custom_call", output_to_operand_aliasing={{}: (4, {})} | custom-call | flops 786432 | bytes 4718592 | tf_op jit(solution)/shard_map/final/pallas_call | solution.py:750
  (188 shorter events, 64.7 us)
Async XLA Ops:
  7.2 170.0 %all-gather.3.cloned.1.call-start = ((), (), s32[]{:S(2)}) async-start(), calls=%async_computation.1 | async-start | bytes 2027520 | tf_op jit(solution)/shard_map/all_gather | solution.py:920
  8.4 33.0 %copy-start.32 = (f32[768]{0:T(1024)S(1)}, f32[768]{0:T(1024)}, u32[]{:S(2)}) copy-start(f32[768]{0:T(1024)} %param.30) | copy-start | bytes 9220
  8.4 9.1 %collective-permute-start.1 = (bf16[192,640]{1,0:T(8,128)(2,1)S(1)}, bf16[192,640]{1,0:T(8,128)(2,1)S(1)}, u32[]{:S(2)}, u32[]{:S(2)}) collective-permute-start(bf16[192,640]{1,0:T(8,128)(2,1)S(1)} %pad_maximum_fusion.2.w0), channel_id=1, source_target_pairs={{0,16},{16,0},{8,24},{24,8},{1,17},{17,1},{9,25},{25,9},{2,18},{18... | collective-permute-start | bytes 737288 | tf_op jit(solution)/shard_map/ppermute | solution.py:781
  14.3 34.0 %copy-start.16 = (bf16[192,1728]{1,0:T(8,128)(2,1)}, bf16[192,1728]{1,0:T(8,128)(2,1)S(1)}, u32[]{:S(2)}) copy-start(bf16[192,1728]{1,0:T(8,128)(2,1)S(1)} %constant_dynamic-update-slice_fusion) | copy-start | bytes 1990660
  14.3 17.1 %collective-permute-start.5 = (bf16[192,1728]{1,0:T(8,128)(2,1)S(1)}, bf16[192,1728]{1,0:T(8,128)(2,1)}, u32[]{:S(2)}, u32[]{:S(2)}) collective-permute-start(bf16[192,1728]{1,0:T(8,128)(2,1)S(1)} %constant_dynamic-update-slice_fusion), channel_id=1, source_target_pairs={{0,1},{1,0},{2,3},{3,2},{4,5},{5,4},{6,7},{7,6},{8,9},{9,8},{10,11... | collective-permute-start | bytes 1990664 | tf_op jit(solution)/shard_map/ppermute | solution.py:872
  16.0 15.4 %collective-permute-start.6 = (bf16[192,1728]{1,0:T(8,128)(2,1)S(1)}, bf16[192,1728]{1,0:T(8,128)(2,1)}, u32[]{:S(2)}, u32[]{:S(2)}) collective-permute-start(bf16[192,1728]{1,0:T(8,128)(2,1)S(1)} %constant_dynamic-update-slice_fusion), channel_id=1, source_target_pairs={{1,2},{2,1},{5,6},{6,5},{9,10},{10,9},{13,14},{14,13},{17,18},{18,... | collective-permute-start | bytes 1990664 | tf_op jit(solution)/shard_map/ppermute | solution.py:873
  17.5 16.7 %collective-permute-start.7 = (bf16[192,1728]{1,0:T(8,128)(2,1)S(1)}, bf16[192,1728]{1,0:T(8,128)(2,1)}, u32[]{:S(2)}, u32[]{:S(2)}) collective-permute-start(bf16[192,1728]{1,0:T(8,128)(2,1)S(1)} %constant_dynamic-update-slice_fusion), channel_id=1, source_target_pairs={{0,16},{16,0},{8,24},{24,8},{1,17},{17,1},{9,25},{25,9},{2,18},{18... | collective-permute-start | bytes 1990664 | tf_op jit(solution)/shard_map/ppermute | solution.py:874
  19.2 2.5 collective-permute-start
  19.2 3.2 collective-permute-start.2
  34.2 16.9 %collective-permute-start.8 = (bf16[192,1728]{1,0:T(8,128)(2,1)}, bf16[192,1728]{1,0:T(8,128)(2,1)}, u32[]{:S(2)}, u32[]{:S(2)}) collective-permute-start(bf16[192,1728]{1,0:T(8,128)(2,1)} %collective-permute-done.5), channel_id=1, source_target_pairs={{1,2},{2,1},{5,6},{6,5},{9,10},{10,9},{13,14},{14,13},{17,18},{18,... | collective-permute-start | bytes 1990664 | tf_op jit(solution)/shard_map/ppermute | solution.py:893
  35.8 19.2 %collective-permute-start.9 = (bf16[192,1728]{1,0:T(8,128)(2,1)}, bf16[192,1728]{1,0:T(8,128)(2,1)}, u32[]{:S(2)}, u32[]{:S(2)}) collective-permute-start(bf16[192,1728]{1,0:T(8,128)(2,1)} %collective-permute-done.6), channel_id=1, source_target_pairs={{1,0},{2,3},{5,4},{6,7},{9,8},{10,11},{13,12},{14,15},{17,16},{18,... | collective-permute-start | bytes 1990664 | tf_op jit(solution)/shard_map/ppermute | solution.py:894
  37.1 21.7 %collective-permute-start.4 = (bf16[1024,384]{1,0:T(8,128)(2,1)}, bf16[1024,384]{1,0:T(8,128)(2,1)}, u32[]{:S(2)}, u32[]{:S(2)}) collective-permute-start(bf16[1024,384]{1,0:T(8,128)(2,1)} %get-tuple-element.91.refs_3_.refs_7_), channel_id=1, source_target_pairs={{0,4},{1,5},{2,6},{3,7},{8,12},{9,13},{10,14},{11,15},{16,20},{17,... | collective-permute-start | bytes 2359304 | tf_op jit(solution)/shard_map/ppermute | solution.py:897
  48.4 30.0 %collective-permute-start.3 = (bf16[1024,384]{1,0:T(8,128)(2,1)}, bf16[1024,384]{1,0:T(8,128)(2,1)S(1)}, u32[]{:S(2)}, u32[]{:S(2)}) collective-permute-start(bf16[1024,384]{1,0:T(8,128)(2,1)} %get-tuple-element.90.refs_3_.refs_7_), channel_id=1, source_target_pairs={{0,4},{1,5},{2,6},{3,7},{8,12},{9,13},{10,14},{11,15},{16,20},{17,... | collective-permute-start | bytes 2359304 | tf_op jit(solution)/shard_map/ppermute | solution.py:897
  49.7 30.0 %collective-permute-start.11 = (bf16[192,1728]{1,0:T(8,128)(2,1)}, bf16[192,1728]{1,0:T(8,128)(2,1)}, u32[]{:S(2)}, u32[]{:S(2)}) collective-permute-start(bf16[192,1728]{1,0:T(8,128)(2,1)} %collective-permute-done.5), channel_id=1, source_target_pairs={{0,16},{16,0},{8,24},{24,8},{1,17},{17,1},{9,25},{25,9},{2,18},{18... | collective-permute-start | bytes 1990664 | tf_op jit(solution)/shard_map/ppermute | solution.py:874
  51.1 19.5 %collective-permute-start.10 = (bf16[192,1728]{1,0:T(8,128)(2,1)}, bf16[192,1728]{1,0:T(8,128)(2,1)}, u32[]{:S(2)}, u32[]{:S(2)}) collective-permute-start(bf16[192,1728]{1,0:T(8,128)(2,1)} %collective-permute-done.8), channel_id=1, source_target_pairs={{1,0},{2,3},{5,4},{6,7},{9,8},{10,11},{13,12},{14,15},{17,16},{18,... | collective-permute-start | bytes 1990664 | tf_op jit(solution)/shard_map/ppermute | solution.py:904
  57.1 49.4 %collective-permute-start.12 = (bf16[192,1728]{1,0:T(8,128)(2,1)}, bf16[192,1728]{1,0:T(8,128)(2,1)}, u32[]{:S(2)}, u32[]{:S(2)}) collective-permute-start(bf16[192,1728]{1,0:T(8,128)(2,1)} %broadcast_select_fusion.1.refs_6_), channel_id=1, source_target_pairs={{0,16},{16,0},{8,24},{24,8},{1,17},{17,1},{9,25},{25,9},{2,18},{18... | collective-permute-start | bytes 1990664 | tf_op jit(solution)/shard_map/ppermute | solution.py:874
  72.7 33.8 %collective-permute-start.13 = (bf16[192,1728]{1,0:T(8,128)(2,1)}, bf16[192,1728]{1,0:T(8,128)(2,1)}, u32[]{:S(2)}, u32[]{:S(2)}) collective-permute-start(bf16[192,1728]{1,0:T(8,128)(2,1)} %broadcast_select_fusion), channel_id=1, source_target_pairs={{0,16},{16,0},{8,24},{24,8},{1,17},{17,1},{9,25},{25,9},{2,18},{18... | collective-permute-start | bytes 1990664 | tf_op jit(solution)/shard_map/ppermute | solution.py:874
  74.0 21.9 %collective-permute-start.14 = (bf16[528,384]{1,0:T(8,128)(2,1)}, bf16[528,384]{1,0:T(8,128)(2,1)}, u32[]{:S(2)}, u32[]{:S(2)}) collective-permute-start(bf16[528,384]{1,0:T(8,128)(2,1)} %get-tuple-element.100.refs_6_.refs_1_.refs_7_.refs_4_), channel_id=1, source_target_pairs={{0,1},{1,0},{2,3},{3,2},{4,5},{5,4},{6,7},{7,6},{8,9},{9,8},{10,11... | collective-permute-start | bytes 1216520 | tf_op jit(solution)/shard_map/ppermute | solution.py:777
  78.4 28.1 %collective-permute-start.15 = (bf16[528,384]{1,0:T(8,128)(2,1)}, bf16[528,384]{1,0:T(8,128)(2,1)}, u32[]{:S(2)}, u32[]{:S(2)}) collective-permute-start(bf16[528,384]{1,0:T(8,128)(2,1)} %get-tuple-element.100.refs_6_.refs_1_.refs_7_.refs_4_), channel_id=1, source_target_pairs={{0,2},{2,0},{1,3},{3,1},{4,6},{6,4},{5,7},{7,5},{8,10},{10,8},{9,1... | collective-permute-start | bytes 1216520 | tf_op jit(solution)/shard_map/ppermute | solution.py:777
  79.7 26.8 %collective-permute-start.16 = (bf16[528,384]{1,0:T(8,128)(2,1)}, bf16[528,384]{1,0:T(8,128)(2,1)}, u32[]{:S(2)}, u32[]{:S(2)}) collective-permute-start(bf16[528,384]{1,0:T(8,128)(2,1)} %get-tuple-element.100.refs_6_.refs_1_.refs_7_.refs_4_), channel_id=1, source_target_pairs={{0,3},{3,0},{1,2},{2,1},{4,7},{7,4},{5,6},{6,5},{8,11},{11,8},{9,1... | collective-permute-start | bytes 1216520 | tf_op jit(solution)/shard_map/ppermute | solution.py:777
  95.9 14.9 %collective-permute-start.17 = (bf16[4,192,1728]{2,1,0:T(8,128)(2,1)}, bf16[4,192,1728]{2,1,0:T(8,128)(2,1)}, u32[]{:S(2)}, u32[]{:S(2)}) collective-permute-start(bf16[4,192,1728]{2,1,0:T(8,128)(2,1)} %pad_maximum_fusion.refs_7_.refs_11_), channel_id=1, source_target_pairs={{0,8},{8,0},{16,24},{24,16},{1,9},{9,1},{17,25},{25,17},{2,10},{10... | collective-permute-start | bytes 7962632 | tf_op jit(solution)/shard_map/ppermute | solution.py:931
  110.0 5.2 %collective-permute-start.18 = (bf16[4,192,1728]{2,1,0:T(8,128)(2,1)S(1)}, bf16[4,192,1728]{2,1,0:T(8,128)(2,1)}, u32[]{:S(2)}, u32[]{:S(2)}) collective-permute-start(bf16[4,192,1728]{2,1,0:T(8,128)(2,1)S(1)} %pad_maximum_fusion.1.refs_13_), channel_id=1, source_target_pairs={{0,8},{8,0},{16,24},{24,16},{1,9},{9,1},{17,25},{25,17},{2,10},{10... | collective-permute-start | bytes 7962632 | tf_op jit(solution)/shard_map/ppermute | solution.py:936
  165.3 15.7 %collective-permute-start.20 = (bf16[512,384]{1,0:T(8,128)(2,1)}, bf16[512,384]{1,0:T(8,128)(2,1)S(1)}, u32[]{:S(2)}, u32[]{:S(2)}) collective-permute-start(bf16[512,384]{1,0:T(8,128)(2,1)} %get-tuple-element.122), channel_id=1, source_target_pairs={{4,0},{5,1},{6,2},{7,3},{12,8},{13,9},{14,10},{15,11},{20,16},{21,... | collective-permute-start | bytes 1179656 | tf_op jit(solution)/shard_map/ppermute | solution.py:994
  175.9 17.3 %collective-permute-start.19 = (bf16[512,384]{1,0:T(8,128)(2,1)}, bf16[512,384]{1,0:T(8,128)(2,1)S(1)}, u32[]{:S(2)}, u32[]{:S(2)}) collective-permute-start(bf16[512,384]{1,0:T(8,128)(2,1)} %get-tuple-element.119), channel_id=1, source_target_pairs={{4,0},{5,1},{6,2},{7,3},{12,8},{13,9},{14,10},{15,11},{20,16},{21,... | collective-permute-start | bytes 1179656 | tf_op jit(solution)/shard_map/ppermute | solution.py:994
  198.1 51.7 %all-reduce.3.cloned.1.call-start = ((), (), s32[]{:S(2)}) async-start(), calls=%async_computation | async-start | bytes 1572864 | tf_op jit(solution)/shard_map/psum | solution.py:1042
  200.0 47.2 %collective-permute-start.21 = (bf16[256,768]{1,0:T(8,128)(2,1)S(1)}, bf16[256,768]{1,0:T(8,128)(2,1)S(1)}, u32[]{:S(2)}, u32[]{:S(2)}) collective-permute-start(bf16[256,768]{1,0:T(8,128)(2,1)S(1)} %broadcast_select_fusion.4), channel_id=1, source_target_pairs={{0,1},{1,0},{2,3},{3,2},{4,5},{5,4},{6,7},{7,6},{8,9},{9,8},{10,11... | collective-permute-start | bytes 1179656 | tf_op jit(solution)/shard_map/ppermute | solution.py:790
  248.4 19.8 %collective-permute-start.23 = (bf16[256,768]{1,0:T(8,128)(2,1)S(1)}, bf16[256,768]{1,0:T(8,128)(2,1)}, u32[]{:S(2)}, u32[]{:S(2)}) collective-permute-start(bf16[256,768]{1,0:T(8,128)(2,1)S(1)} %select_add_fusion.2.refs_11_), channel_id=1, source_target_pairs={{0,2},{2,0},{1,3},{3,1},{4,6},{6,4},{5,7},{7,5},{8,10},{10,8},{9,1... | collective-permute-start | bytes 1179656 | tf_op jit(solution)/shard_map/ppermute | solution.py:792
  258.9 14.4 %collective-permute-start.22 = (bf16[512,384]{1,0:T(8,128)(2,1)}, bf16[512,384]{1,0:T(8,128)(2,1)S(1)}, u32[]{:S(2)}, u32[]{:S(2)}) collective-permute-start(bf16[512,384]{1,0:T(8,128)(2,1)} %get-tuple-element.136), channel_id=1, source_target_pairs={{4,0},{5,1},{6,2},{7,3},{12,8},{13,9},{14,10},{15,11},{20,16},{21,... | collective-permute-start | bytes 1179656 | tf_op jit(solution)/shard_map/ppermute | solution.py:994
  262.9 34.6 %collective-permute-start.32 = (bf16[2,192,1728]{2,1,0:T(8,128)(2,1)}, bf16[2,192,1728]{2,1,0:T(8,128)(2,1)}, u32[]{:S(2)}, u32[]{:S(2)}) collective-permute-start(bf16[2,192,1728]{2,1,0:T(8,128)(2,1)} %dynamic-slice_bitcast_fusion), channel_id=1, source_target_pairs={{0,16},{16,0},{8,24},{24,8},{1,17},{17,1},{9,25},{25,9},{2,18},{18... | collective-permute-start | bytes 3981320 | tf_op jit(solution)/shard_map/ppermute | solution.py:807
  269.3 23.4 %collective-permute-start.25 = (bf16[256,768]{1,0:T(8,128)(2,1)S(1)}, bf16[256,768]{1,0:T(8,128)(2,1)}, u32[]{:S(2)}, u32[]{:S(2)}) collective-permute-start(bf16[256,768]{1,0:T(8,128)(2,1)S(1)} %add.117.refs_6_.done_ref), channel_id=1, source_target_pairs={{0,1},{1,0},{2,3},{3,2},{4,5},{5,4},{6,7},{7,6},{8,9},{9,8},{10,11... | collective-permute-start | bytes 1179656 | tf_op jit(solution)/shard_map/ppermute | solution.py:793
  280.1 20.4 %collective-permute-start.26 = (bf16[256,768]{1,0:T(8,128)(2,1)}, bf16[256,768]{1,0:T(8,128)(2,1)}, u32[]{:S(2)}, u32[]{:S(2)}) collective-permute-start(bf16[256,768]{1,0:T(8,128)(2,1)} %broadcast_select_fusion.3), channel_id=1, source_target_pairs={{0,1},{1,0},{2,3},{3,2},{4,5},{5,4},{6,7},{7,6},{8,9},{9,8},{10,11... | collective-permute-start | bytes 1179656 | tf_op jit(solution)/shard_map/ppermute | solution.py:790
  291.4 12.4 %collective-permute-start.24 = (bf16[512,384]{1,0:T(8,128)(2,1)}, bf16[512,384]{1,0:T(8,128)(2,1)S(1)}, u32[]{:S(2)}, u32[]{:S(2)}) collective-permute-start(bf16[512,384]{1,0:T(8,128)(2,1)} %get-tuple-element.142), channel_id=1, source_target_pairs={{4,0},{5,1},{6,2},{7,3},{12,8},{13,9},{14,10},{15,11},{20,16},{21,... | collective-permute-start | bytes 1179656 | tf_op jit(solution)/shard_map/ppermute | solution.py:994
  300.6 11.4 %collective-permute-start.33 = (bf16[192,1728]{1,0:T(8,128)(2,1)}, bf16[192,1728]{1,0:T(8,128)(2,1)}, u32[]{:S(2)}, u32[]{:S(2)}) collective-permute-start(bf16[192,1728]{1,0:T(8,128)(2,1)} %dynamic-slice_bitcast_fusion.1), channel_id=1, source_target_pairs={{0,8},{8,0},{16,24},{24,16},{1,9},{9,1},{17,25},{25,17},{2,10},{10... | collective-permute-start | bytes 1990664 | tf_op jit(solution)/shard_map/ppermute | solution.py:813
  301.7 21.1 %collective-permute-start.30 = (bf16[256,768]{1,0:T(8,128)(2,1)S(1)}, bf16[256,768]{1,0:T(8,128)(2,1)}, u32[]{:S(2)}, u32[]{:S(2)}) collective-permute-start(bf16[256,768]{1,0:T(8,128)(2,1)S(1)} %select_add_fusion.1.refs_6_), channel_id=1, source_target_pairs={{0,2},{2,0},{1,3},{3,1},{4,6},{6,4},{5,7},{7,5},{8,10},{10,8},{9,1... | collective-permute-start | bytes 1179656 | tf_op jit(solution)/shard_map/ppermute | solution.py:792
  308.8 21.7 %copy-start.1 = (bf16[512,768]{1,0:T(8,128)(2,1)S(1)}, bf16[512,768]{1,0:T(8,128)(2,1)}, u32[]{:S(2)}) copy-start(bf16[512,768]{1,0:T(8,128)(2,1)} %get-tuple-element.144.refs_0_) | copy-start | bytes 2359300
  310.1 20.4 %collective-permute-start.27 = (bf16[256,768]{1,0:T(8,128)(2,1)S(1)}, bf16[256,768]{1,0:T(8,128)(2,1)S(1)}, u32[]{:S(2)}, u32[]{:S(2)}) collective-permute-start(bf16[256,768]{1,0:T(8,128)(2,1)S(1)} %broadcast_select_fusion.2), channel_id=1, source_target_pairs={{0,1},{1,0},{2,3},{3,2},{4,5},{5,4},{6,7},{7,6},{8,9},{9,8},{10,11... | collective-permute-start | bytes 1179656 | tf_op jit(solution)/shard_map/ppermute | solution.py:790
  314.2 24.6 %collective-permute-start.34 = (bf16[192,1728]{1,0:T(8,128)(2,1)}, bf16[192,1728]{1,0:T(8,128)(2,1)}, u32[]{:S(2)}, u32[]{:S(2)}) collective-permute-start(bf16[192,1728]{1,0:T(8,128)(2,1)} %bitcast_add_fusion.1), channel_id=1, source_target_pairs={{0,4},{4,0},{1,5},{5,1},{2,6},{6,2},{3,7},{7,3},{8,12},{12,8},{9,1... | collective-permute-start | bytes 1990664 | tf_op jit(solution)/shard_map/ppermute | solution.py:798
  323.8 15.0 %copy-start.14 = (bf16[256,768]{1,0:T(8,128)(2,1)}, bf16[256,768]{1,0:T(8,128)(2,1)S(1)}, u32[]{:S(2)}) copy-start(bf16[256,768]{1,0:T(8,128)(2,1)S(1)} %add.121.done_ref) | copy-start | bytes 1179652
  323.8 1.3 collective-permute-start.39
  323.9 25.7 %collective-permute-start.31 = (bf16[256,768]{1,0:T(8,128)(2,1)S(1)}, bf16[256,768]{1,0:T(8,128)(2,1)}, u32[]{:S(2)}, u32[]{:S(2)}) collective-permute-start(bf16[256,768]{1,0:T(8,128)(2,1)S(1)} %add.121.done_ref), channel_id=1, source_target_pairs={{0,1},{1,0},{2,3},{3,2},{4,5},{5,4},{6,7},{7,6},{8,9},{9,8},{10,11... | collective-permute-start | bytes 1179656 | tf_op jit(solution)/shard_map/ppermute | solution.py:793
  325.1 5.6 %collective-permute-start.40 = (f32[8,1408]{1,0:T(8,128)S(1)}, f32[8,1408]{1,0:T(8,128)S(1)}, u32[]{:S(2)}, u32[]{:S(2)}) collective-permute-start(f32[8,1408]{1,0:T(8,128)S(1)} %add.142), channel_id=1, source_target_pairs={{0,16},{16,0},{8,24},{24,8},{1,17},{17,1},{9,25},{25,9},{2,18},{18... | collective-permute-start | bytes 135176 | tf_op jit(solution)/shard_map/ppermute | solution.py:829
  330.6 17.8 %collective-permute-start.28 = (bf16[256,768]{1,0:T(8,128)(2,1)S(1)}, bf16[256,768]{1,0:T(8,128)(2,1)}, u32[]{:S(2)}, u32[]{:S(2)}) collective-permute-start(bf16[256,768]{1,0:T(8,128)(2,1)S(1)} %select_add_fusion.refs_1_), channel_id=1, source_target_pairs={{0,2},{2,0},{1,3},{3,1},{4,6},{6,4},{5,7},{7,5},{8,10},{10,8},{9,1... | collective-permute-start | bytes 1179656 | tf_op jit(solution)/shard_map/ppermute | solution.py:792
  330.7 8.1 %collective-permute-start.41 = (f32[8,1408]{1,0:T(8,128)S(1)}, f32[8,1408]{1,0:T(8,128)S(1)}, u32[]{:S(2)}, u32[]{:S(2)}) collective-permute-start(f32[8,1408]{1,0:T(8,128)S(1)} %add.143), channel_id=1, source_target_pairs={{0,4},{4,0},{1,5},{5,1},{2,6},{6,2},{3,7},{7,3},{8,12},{12,8},{9,1... | collective-permute-start | bytes 135176 | tf_op jit(solution)/shard_map/ppermute | solution.py:798
  342.3 13.6 %collective-permute-start.35 = (bf16[192,640]{1,0:T(8,128)(2,1)}, bf16[192,640]{1,0:T(8,128)(2,1)}, u32[]{:S(2)}, u32[]{:S(2)}) collective-permute-start(bf16[192,640]{1,0:T(8,128)(2,1)} %get-tuple-element.169), channel_id=1, source_target_pairs={{0,8},{8,0},{16,24},{24,16},{1,9},{9,1},{17,25},{25,17},{2,10},{10... | collective-permute-start | bytes 737288 | tf_op jit(solution)/shard_map/ppermute | solution.py:823
  342.3 13.6 %collective-permute-start.36 = (bf16[192,640]{1,0:T(8,128)(2,1)}, bf16[192,640]{1,0:T(8,128)(2,1)}, u32[]{:S(2)}, u32[]{:S(2)}) collective-permute-start(bf16[192,640]{1,0:T(8,128)(2,1)} %get-tuple-element.171), channel_id=1, source_target_pairs={{0,16},{16,0},{8,24},{24,8},{1,17},{17,1},{9,25},{25,9},{2,18},{18... | collective-permute-start | bytes 737288 | tf_op jit(solution)/shard_map/ppermute | solution.py:823
  343.4 12.5 %collective-permute-start.37 = (bf16[192,640]{1,0:T(8,128)(2,1)}, bf16[192,640]{1,0:T(8,128)(2,1)}, u32[]{:S(2)}, u32[]{:S(2)}) collective-permute-start(bf16[192,640]{1,0:T(8,128)(2,1)} %get-tuple-element.170), channel_id=1, source_target_pairs={{0,24},{24,0},{8,16},{16,8},{1,25},{25,1},{9,17},{17,9},{2,26},{26... | collective-permute-start | bytes 737288 | tf_op jit(solution)/shard_map/ppermute | solution.py:823
  349.5 13.9 %collective-permute-start.29 = (bf16[256,768]{1,0:T(8,128)(2,1)S(1)}, bf16[256,768]{1,0:T(8,128)(2,1)}, u32[]{:S(2)}, u32[]{:S(2)}) collective-permute-start(bf16[256,768]{1,0:T(8,128)(2,1)S(1)} %add.120.done_ref), channel_id=1, source_target_pairs={{0,1},{1,0},{2,3},{3,2},{4,5},{5,4},{6,7},{7,6},{8,9},{9,8},{10,11... | collective-permute-start | bytes 1179656 | tf_op jit(solution)/shard_map/ppermute | solution.py:793
  357.3 10.7 %collective-permute-start.38 = (bf16[192,640]{1,0:T(8,128)(2,1)S(1)}, bf16[192,640]{1,0:T(8,128)(2,1)S(1)}, u32[]{:S(2)}, u32[]{:S(2)}) collective-permute-start(bf16[192,640]{1,0:T(8,128)(2,1)S(1)} %fusion.2), channel_id=1, source_target_pairs={{0,4},{4,0},{1,5},{5,1},{2,6},{6,2},{3,7},{7,3},{8,12},{12,8},{9,1... | collective-permute-start | bytes 737288 | tf_op jit(solution)/shard_map/ppermute | solution.py:798
  (31 other events, 135.7 us)
Sparse Core Ops, SparseCore 0:
  110.9 43.0 all-gather.2
  201.9 47.6 all-reduce.2
